TPU v7x, 256 devices: a whole 4x4x8 slice. The times are simulated.
256 devices in a mesh: ctx: 64 (over x_hi, z, y), head: 4 (over x_lo, core).
Axes of the slice: x: 4 (x_hi: 2, x_lo: 2; x = x_hi * 2 + x_lo), y: 4, z: 8, core: 2. Of those that a mesh axis runs over, the one named last changes fastest.
Arguments:
- queries: bfloat16 [8192, 4096], P('ctx', 'head'), may hold values from -81 to 81
- key_states: bfloat16 [8192, 1024], P('ctx', 'head'), may hold values from -7 to 7
- value_states: bfloat16 [8192, 1024], P('ctx', 'head'), may hold values from -6 to 6
- out_weight: bfloat16 [4096, 4096], P('head'), may hold values from -0.09375 to 0.09375
- head_role: int32 [8], replicated, may hold values from 0 to 1, as said below
- sink_len: int32 [8], replicated, may hold values from 32 to 128, as said below
- window_len: int32 [8], replicated, may hold values from 256 to 1024, as said below
Outputs:
- mixed: bfloat16 [8192, 4096], P(('ctx', 'head'))
Inputs may be any that keep to these rules, and one draw needn't show every extreme that they name: `head_role`: exactly 4 heads are retrieval heads. `sink_len`: some head has exactly 128. `window_len`: some head has exactly 1024.
All inputs are finite; a program needn't handle non-finite values.
Results may differ from a plain program's by a relative error of at most 0.012.
Values may be sent and summed in bfloat16 or wider, within the bound.
A program may use at most 128 MiB of HBM per device.

v0:
```python
import jax
import jax.numpy as jnp
from jax import lax
from jax.sharding import PartitionSpec as P

HD = 128
GROUP = 4


NEGATIVE = -1e30


def online_update(running, query_heads, key_part, value_part, allowed):
    row_peak, row_total, weighted = running
    scores = jnp.einsum(
        "thgd,jhd->thgj", query_heads, key_part, preferred_element_type=jnp.float32
    ) * HD ** (-0.5)
    visible = allowed[:, :, None, :]
    block_peak = jnp.max(jnp.where(visible, scores, NEGATIVE), axis=-1)
    new_peak = jnp.maximum(row_peak, block_peak)
    weights = jnp.where(visible, jnp.exp(scores - new_peak[..., None]), 0.0)
    row_total = jnp.sum(weights, axis=-1)
    weighted = jnp.einsum(
        "thgj,jhd->thgd",
        weights.astype(jnp.bfloat16),
        value_part,
        preferred_element_type=jnp.float32,
    )
    return (new_peak, row_total, weighted)


def empty_state(row_count, head_count):
    return (
        jnp.full((row_count, head_count, GROUP), NEGATIVE, jnp.float32),
        jnp.zeros((row_count, head_count, GROUP), jnp.float32),
        jnp.zeros((row_count, head_count, GROUP, HD), jnp.float32),
    )


def finish(running, row_count):
    row_peak, row_total, weighted = running
    return (weighted / row_total[..., None]).astype(jnp.bfloat16).reshape(row_count, -1)


def per_device(queries, key_states, value_states, out_weight, head_role, sink_len, window_len):
    row_count = queries.shape[0]
    local_heads = key_states.shape[1] // HD
    row_base = lax.axis_index("ctx") * row_count
    query_pos = row_base + jnp.arange(row_count, dtype=jnp.int32)
    my_group = lax.axis_index("head")
    first_head = my_group * local_heads
    last_row = row_base + row_count - 1
    roles_here = lax.dynamic_slice_in_dim(head_role, first_head, local_heads)
    sinks_here = lax.dynamic_slice_in_dim(sink_len, first_head, local_heads)
    windows_here = lax.dynamic_slice_in_dim(window_len, first_head, local_heads)
    query_heads = queries.reshape(row_count, local_heads, GROUP, HD)
    key_part = lax.all_gather(key_states, "ctx", axis=0, tiled=True).reshape(-1, local_heads, HD)
    value_part = lax.all_gather(value_states, "ctx", axis=0, tiled=True).reshape(
        -1, local_heads, HD
    )
    key_pos = jnp.arange(key_part.shape[0], dtype=jnp.int32)

    def update(state):
        later = query_pos[:, None, None]
        earlier = key_pos[None, None, :]
        allowed = (earlier <= later) & (
            (roles_here[None, :, None] == 1)
            | (earlier < sinks_here[None, :, None])
            | (later - earlier < windows_here[None, :, None])
        )
        return online_update(state, query_heads, key_part, value_part, allowed)

    def unchanged(state):
        return state

    running = lax.cond(
        jnp.int32(0) <= last_row, update, unchanged, empty_state(row_count, local_heads)
    )
    attended = finish(running, row_count)
    mixed = lax.psum_scatter(
        jnp.dot(attended, out_weight, preferred_element_type=jnp.float32).astype(jnp.bfloat16),
        "head",
        scatter_dimension=0,
        tiled=True,
    )
    return mixed


def solution(mesh):
    in_specs = (
        P("ctx", "head"),
        P("ctx", "head"),
        P("ctx", "head"),
        P("head", None),
        P(),
        P(),
        P(),
    )
    out_specs = P(("ctx", "head"), None)
    return jax.shard_map(
        per_device, mesh=mesh, in_specs=in_specs, out_specs=out_specs, check_vma=False
    )
```

profile of v0, /device:TPU:1, one launch (start us, length us, event | category | flops | bytes accessed | tf_op | source)
XLA Modules:
  0.0 373.8 jit_solution(10370154354749702863)
XLA Ops:
  6.5 0.7 all-gather.3.cloned.1.call-update
  7.3 0.0 all-gather.5.cloned.1.call-start
  7.3 0.7 all-gather.5.cloned.1.call-update
  8.0 0.0 reduce-scatter.2.cloned.1.call-start
  8.1 131.3 %all-gather.3.cloned.1.call-done = bf16[8192,256]{1,0:T(8,128)(2,1)} async-done(((bf16[128,256]{1,0:T(8,128)(2,1)}), bf16[8192,256]{1,0:T(8,128)(2,1)}) %all-gather.3.cloned.1.call-update) | async-done | bytes 4194320 | tf_op jit(solution)/shard_map/all_gather | solution.py:57
  139.4 128.3 %all-gather.5.cloned.1.call-done = bf16[8192,256]{1,0:T(8,128)(2,1)} async-done(((bf16[128,256]{1,0:T(8,128)(2,1)}), bf16[8192,256]{1,0:T(8,128)(2,1)}) %all-gather.5.cloned.1.call-update) | async-done | bytes 4194320 | tf_op jit(solution)/shard_map/all_gather | solution.py:58
  267.6 70.6 %conditional.1 = (f32[128,2,4]{0,2,1:T(4,128)S(1)}, f32[128,2,4,128]{0,3,2,1:T(8,128)S(1)}) conditional(s32[]{:T(128)} %convert_element_type.15, () %tuple.22, (s32[8192]{0:T(1024)S(1)}, s32[8192]{0:T(1024)S(1)}, s32[]{:T(128)}, s32[128]{0:T(128)S(1)}, s32[]{:T(128)}, /*index=5*/s32[8]{0:T(128)}, s32[8192]{0:T(1024)S(1)}, s32[8]{0:T(128)}, ...), branch_computations={%region_0.0_spmd, %region_1.4_spmd} | conditional | flops 4395662336 | bytes 148269232 | solution.py:76
  267.6 0.7 dynamic-slice_compare_fusion
  268.4 0.7 dynamic_slice.19
  269.1 0.1 compare_or_fusion
  269.2 0.7 dynamic_slice.20
  269.9 1.2 broadcast_subtract_fusion
  271.2 3.7 broadcast_compare_fusion
  274.9 2.8 or_and_fusion
  277.7 6.9 %reshape.125 = bf16[8192,2,128]{2,1,0:T(2,128)(2,1)} reshape(bf16[8192,256]{1,0:T(8,128)(2,1)} %get-tuple-element.125) | data formatting | bytes 8388608 | tf_op jit(solution)/shard_map/reshape | solution.py:57
  284.6 0.2 reshape.126
  284.8 15.7 %fusion = (f32[128,2,4]{0,2,1:T(4,128)S(1)}, f32[2,8192,128,4]{2,1,3,0:T(8,128)}) fusion(pred[128,2,8192]{0,2,1:T(8,128)(4,1)S(1)} %or_and_fusion, bf16[128,2,4,128]{3,2,1,0:T(4,128)(2,1)S(1)} %reshape.126, bf16[8192,2,128,1]{2,1,0,3:T(2,128)(2,1)} %bitcast.23), kind=kOutput, calls=%fused_computation.2 | convolution fusion | flops 2172648448 | bytes 40112128 | tf_op jit(solution)/shard_map/cond/branch_1_fun/thgd,jhd->thgj/dot_general | solution.py:15
  300.5 6.9 %reshape.127 = bf16[8192,2,128]{2,1,0:T(2,128)(2,1)} reshape(bf16[8192,256]{1,0:T(8,128)(2,1)} %get-tuple-element.127) | data formatting | bytes 8388608 | tf_op jit(solution)/shard_map/reshape | solution.py:58
  307.4 16.3 %fusion.11 = f32[128,2,4,128]{3,0,2,1:T(8,128)S(1)} fusion(bf16[8192,2,128,1]{2,1,0,3:T(2,128)(2,1)} %bitcast.24, f32[2,8192,128,4]{2,1,3,0:T(8,128)} %get-tuple-element.142, f32[128,2,4]{0,2,1:T(4,128)S(1)} %broadcast_maximum_fusion, pred[128,2,8192]{0,2,1:T(8,128)(4,1)S(1)} %or_and_fusion), kind=kOutput, calls=%fused_computation.15 | convolution fusion | flops 2181038080 | bytes 40374272 | tf_op jit(solution)/shard_map/cond/branch_1_fun/thgj,jhd->thgd/dot_general | solution.py:23
  323.7 0.2 copy.36
  323.9 14.3 %fusion.4 = f32[128,2,4]{0,2,1:T(4,128)S(1)} fusion(f32[2,8192,128,4]{2,1,3,0:T(8,128)} %get-tuple-element.142, f32[128,2,4]{0,2,1:T(4,128)S(1)} %broadcast_maximum_fusion, pred[128,2,8192]{0,2,1:T(8,128)(4,1)S(1)} %or_and_fusion), kind=kLoop, calls=%fused_computation.6 | loop fusion | flops 33553408 | bytes 35659776 | tf_op jit(solution)/shard_map/cond/branch_1_fun/reduce_sum | solution.py:22
  338.3 0.1 divide_convert_fusion
  338.3 5.6 %convolution_convert_fusion = bf16[128,4096]{1,0:T(8,128)(2,1)} fusion(bf16[128,1024]{0,1:T(8,128)(2,1)S(1)} %bitcast.25, bf16[1024,4096]{1,0:T(8,128)(2,1)} %param.12), kind=kOutput, calls=%fused_computation.23 | convolution fusion | flops 1074266112 | bytes 9699328 | tf_op jit(solution)/shard_map/dot_general | solution.py:81
  344.0 23.3 %reduce-scatter.2.cloned.1.call-done = bf16[32,4096]{1,0:T(8,128)(2,1)} async-done(((bf16[128,4096]{1,0:T(8,128)(2,1)}), bf16[32,4096]{1,0:T(8,128)(2,1)}) %reduce-scatter.2.cloned.1.call-update) | async-done | bytes 262160 | tf_op jit(solution)/shard_map/reduce_scatter | solution.py:80
  (8 shorter events, 0.0 us)
Async XLA Ops:
  6.5 132.8 %all-gather.3.cloned.1.call-start = ((), (), s32[]{:S(2)}) async-start(), calls=%async_computation.1 | async-start | bytes 4259840 | tf_op jit(solution)/shard_map/all_gather | solution.py:57
  7.3 260.4 %all-gather.5.cloned.1.call-start = ((), (), s32[]{:S(2)}) async-start(), calls=%async_computation.2 | async-start | bytes 4259840 | tf_op jit(solution)/shard_map/all_gather | solution.py:58
  8.0 359.3 %reduce-scatter.2.cloned.1.call-start = ((), (), s32[]{:S(2)}) async-start(), calls=%async_computation.3 | async-start | bytes 1310720 | tf_op jit(solution)/shard_map/reduce_scatter | solution.py:80
  271.2 13.4 %copy-start = (bf16[128,1024]{1,0:T(8,128)(2,1)S(1)}, bf16[128,1024]{1,0:T(8,128)(2,1)}, u32[]{:S(2)}) copy-start(bf16[128,1024]{1,0:T(8,128)(2,1)} %get-tuple-element.139) | copy-start | bytes 786436 | tf_op jit(solution)/shard_map/cond
Sparse Core Ops, SparseCore 0:
  10.9 128.4 all-gather.2
  142.9 124.6 all-gather.4
  344.1 23.1 reduce-scatter.1
where the time goes:
time: 374 us
  waiting for transfers between devices  284 us (76%)
  matrix products  37.7 us (10%)
  other arithmetic  23 us (6%)
  local copies, waits for them, and re-layouts  15.6 us (4%)
  between operations  13.1 us (4%)
    all_gather x1, waiting for transfers between devices, per_device(): lax.all_gather(key_states, 'ctx', axis=0, tiled=True)  131 us
    all_gather x1, waiting for transfers between devices, per_device(): lax.all_gather(value_states, 'ctx', axis=0, tiled=True)  128 us
    reduce_scatter x1, waiting for transfers between devices, per_device(): lax.psum_scatter(jnp.dot(attended, out_weight, preferred_element_type=jnp...  23.3 us
    dot_general x1, matrix products, online_update(): jnp.einsum('thgj,jhd->thgd', weights.astype(jnp.bfloat16), value_part, pr...  16.3 us
    dot_general x1, matrix products, online_update(): jnp.einsum('thgd,jhd->thgj', query_heads, key_part, preferred_element_typ...  15.7 us
    reduce_sum x1, other arithmetic, online_update(): row_total = jnp.sum(weights, axis=-1)  14.3 us
  transfers between devices with their start and end apart: 3, of which 3 were waited for; matrix products, arithmetic and copies ran while one was open for 0% of the time, Pallas kernels for 0%

commit v1 on v0

--- a/solution.py
+++ b/solution.py
@@ -54,10 +54,12 @@
     sinks_here = lax.dynamic_slice_in_dim(sink_len, first_head, local_heads)
     windows_here = lax.dynamic_slice_in_dim(window_len, first_head, local_heads)
     query_heads = queries.reshape(row_count, local_heads, GROUP, HD)
-    key_part = lax.all_gather(key_states, "ctx", axis=0, tiled=True).reshape(-1, local_heads, HD)
-    value_part = lax.all_gather(value_states, "ctx", axis=0, tiled=True).reshape(
-        -1, local_heads, HD
+    width = key_states.shape[1]
+    both = lax.all_gather(
+        jnp.concatenate([key_states, value_states], axis=1), "ctx", axis=0, tiled=True
     )
+    key_part = both[:, :width].reshape(-1, local_heads, HD)
+    value_part = both[:, width:].reshape(-1, local_heads, HD)
     key_pos = jnp.arange(key_part.shape[0], dtype=jnp.int32)
 
     def update(state):

time: 374 us -> 276 us (0.74)
  waiting for transfers between devices: 284 us -> 196 us
  local copies, waits for them, and re-layouts: 15.6 us -> 6.97 us
    all_gather x2 -> x1, waiting for transfers between devices: 260 us -> 174 us  [per_device(): lax.all_gather(jnp.concatenate([key_states, value_states], axis=1), 'ctx'...]
    reshape x2 -> x0, local copies, waits for them, and re-layouts: 13.8 us -> none  [the longest x1 6.89 us: per_device(): lax.all_gather(key_states, 'ctx', axis=0, tiled=True)]
  transfers between devices with their start and end apart: 3 -> 2, of which waited for: 3 -> 2; matrix products, arithmetic and copies ran while one was open for 0% -> 0% of each run, Pallas kernels for 0% -> 0%
where the time goes in v1:
time: 276 us; the launch traced here: 275 us
  waiting for transfers between devices  196 us (71%)
  matrix products  35.1 us (13%)
  other arithmetic  23.7 us (9%)
  between operations  13.4 us (5%)
  local copies, waits for them, and re-layouts  6.97 us (3%)
    all_gather x1, waiting for transfers between devices, per_device(): lax.all_gather(jnp.concatenate([key_states, value_states], axis=1), 'ctx'...  174 us
    reduce_scatter x1, waiting for transfers between devices, per_device(): lax.psum_scatter(jnp.dot(attended, out_weight, preferred_element_type=jnp...  22.3 us
    dot_general x1, matrix products, online_update(): jnp.einsum('thgj,jhd->thgd', weights.astype(jnp.bfloat16), value_part, pr...  15.9 us
    reduce_sum x1, other arithmetic, online_update(): row_total = jnp.sum(weights, axis=-1)  14.4 us
    dot_general x1, matrix products, online_update(): jnp.einsum('thgd,jhd->thgj', query_heads, key_part, preferred_element_typ...  13.6 us
    dot_general x1, matrix products, per_device(): jnp.dot(attended, out_weight, preferred_element_type=jnp.float32)  5.65 us
  transfers between devices with their start and end apart: 2, of which 2 were waited for; matrix products, arithmetic and copies ran while one was open for 0% of the time, Pallas kernels for 0%

profile of v1, /device:TPU:1, one launch (start us, length us, event | category | flops | bytes accessed | tf_op | source)
XLA Modules:
  0.0 275.3 jit_solution(8369988572290120255)
XLA Ops:
  6.5 0.9 copy.27
  7.5 1.0 copy.28
  8.5 0.7 pad_maximum_fusion
  9.1 0.0 all-gather.2.cloned.1.call-update
  9.1 0.0 reduce-scatter.2.cloned.1.call-start
  9.2 173.6 %all-gather.2.cloned.1.call-done = bf16[8192,512]{0,1:T(8,128)(2,1)} async-done(((bf16[128,512]{0,1:T(8,128)(2,1)}), bf16[8192,512]{0,1:T(8,128)(2,1)}) %all-gather.2.cloned.1.call-update) | async-done | bytes 8388624 | tf_op jit(solution)/shard_map/all_gather | solution.py:58
  182.8 57.6 %conditional.1 = (f32[128,2,4]{0,2,1:T(4,128)S(1)}, f32[128,2,4,128]{0,3,2,1:T(8,128)S(1)}) conditional(s32[]{:T(128)} %convert_element_type.15, () %tuple.22, (s32[8192]{0:T(1024)S(1)}, s32[8192]{0:T(1024)S(1)}, s32[]{:T(128)}, s32[128]{0:T(128)S(1)}, s32[]{:T(128)}, /*index=5*/s32[8]{0:T(128)}, s32[8192]{0:T(1024)S(1)}, s32[8]{0:T(128)}, ...), branch_computations={%region_0.0_spmd, %region_1.4_spmd} | conditional | flops 4395662336 | bytes 180775088 | solution.py:78
  182.8 0.7 dynamic-slice_compare_fusion
  183.6 0.7 dynamic_slice.19
  184.3 0.7 dynamic_slice.20
  185.0 0.1 compare_or_fusion
  185.1 1.1 reshape.126
  186.3 3.7 %broadcast_compare_fusion = pred[128,8192]{0,1:T(8,128)(4,1)S(1)} fusion(s32[128]{0:T(128)S(1)} %broadcast_add_fusion, s32[8192]{0:T(1024)S(1)} %get-tuple-element.122), kind=kLoop, calls=%fused_computation.11 | loop fusion | flops 1048576 | bytes 1081856 | tf_op jit(solution)/shard_map/cond/branch_1_fun/le | solution.py:68
  190.0 1.2 broadcast_subtract_fusion
  191.2 2.8 %or_and_fusion = pred[128,2,8192]{0,2,1:T(8,128)(4,1)S(1)} fusion(s32[128,8192]{0,1:T(8,128)S(1)} %broadcast_subtract_fusion, s32[2]{0:T(128)S(1)} %dynamic_slice.20, pred[2,8192]{1,0:T(4,128)(4,1)S(1)} %compare_or_fusion, pred[128,8192]{0,1:T(8,128)(4,1)S(1)} %broadcast_compare_fusion), kind=kLoop, calls=%fused_computation.9 | loop fusion | flops 6291456 | bytes 7356424 | tf_op jit(solution)/shard_map/cond/branch_1_fun/and | solution.py:68
  194.1 2.3 fusion.15
  196.3 13.6 %fusion = (f32[128,2,4]{0,2,1:T(4,128)S(1)}, f32[2,8192,128,4]{2,1,3,0:T(8,128)}) fusion(pred[128,2,8192]{0,2,1:T(8,128)(4,1)S(1)} %or_and_fusion, bf16[8192,2,128,1]{0,2,3,1:T(8,128)(2,1)S(1)} %bitcast.33, bf16[128,2,4,128]{3,2,1,0:T(4,128)(2,1)S(1)} %reshape.126), kind=kOutput, calls=%fused_computation.2 | convolution fusion | flops 2172648448 | bytes 40112128 | tf_op jit(solution)/shard_map/cond/branch_1_fun/thgd,jhd->thgj/dot_general | solution.py:15
  209.9 15.9 %fusion.8 = f32[128,2,4,128]{3,0,2,1:T(8,128)S(1)} fusion(bf16[8192,2,128,1]{0,2,3,1:T(8,128)(2,1)} %bitcast.34, f32[2,8192,128,4]{2,1,3,0:T(8,128)} %get-tuple-element.144, f32[128,2,4]{0,2,1:T(4,128)S(1)} %broadcast_maximum_fusion, pred[128,2,8192]{0,2,1:T(8,128)(4,1)S(1)} %or_and_fusion), kind=kOutput, calls=%fused_computation.12 | convolution fusion | flops 2181038080 | bytes 40374272 | tf_op jit(solution)/shard_map/cond/branch_1_fun/thgj,jhd->thgd/dot_general | solution.py:23
  225.8 14.4 %fusion.4 = f32[128,2,4]{0,2,1:T(4,128)S(1)} fusion(f32[2,8192,128,4]{2,1,3,0:T(8,128)} %get-tuple-element.144, f32[128,2,4]{0,2,1:T(4,128)S(1)} %broadcast_maximum_fusion, pred[128,2,8192]{0,2,1:T(8,128)(4,1)S(1)} %or_and_fusion), kind=kLoop, calls=%fused_computation.6 | loop fusion | flops 33553408 | bytes 35659776 | tf_op jit(solution)/shard_map/cond/branch_1_fun/reduce_sum | solution.py:22
  240.2 0.2 copy.38
  240.4 0.1 divide_convert_fusion
  240.4 5.7 %convolution_convert_fusion = bf16[128,4096]{1,0:T(8,128)(2,1)} fusion(bf16[128,1024]{0,1:T(8,128)(2,1)S(1)} %bitcast.35, bf16[1024,4096]{1,0:T(8,128)(2,1)} %param.12), kind=kOutput, calls=%fused_computation.21 | convolution fusion | flops 1074266112 | bytes 9699328 | tf_op jit(solution)/shard_map/dot_general | solution.py:83
  246.1 0.0 reduce-scatter.2.cloned.1.call-update
  246.1 22.3 %reduce-scatter.2.cloned.1.call-done = bf16[32,4096]{1,0:T(8,128)(2,1)} async-done(((bf16[128,4096]{1,0:T(8,128)(2,1)}), bf16[32,4096]{1,0:T(8,128)(2,1)}) %reduce-scatter.2.cloned.1.call-update) | async-done | bytes 262160 | tf_op jit(solution)/shard_map/reduce_scatter | solution.py:82
  (7 shorter events, 0.0 us)
Async XLA Ops:
  6.5 176.3 %all-gather.2.cloned.1.call-start = ((), (), s32[]{:S(2)}) async-start(), calls=%async_computation.1 | async-start | bytes 8519680 | tf_op jit(solution)/shard_map/all_gather | solution.py:58
  9.1 259.3 %reduce-scatter.2.cloned.1.call-start = ((), (), s32[]{:S(2)}) async-start(), calls=%async_computation.2 | async-start | bytes 1310720 | tf_op jit(solution)/shard_map/reduce_scatter | solution.py:82
  186.2 7.8 %copy-start = (bf16[8192,512]{0,1:T(8,128)(2,1)S(1)}, bf16[8192,512]{0,1:T(8,128)(2,1)}, u32[]{:S(2)}) copy-start(bf16[8192,512]{0,1:T(8,128)(2,1)} %get-tuple-element.126) | copy-start | bytes 25165828 | tf_op jit(solution)/shard_map/cond
Sparse Core Ops, SparseCore 0:
  10.8 171.9 all-gather.1
  246.2 22.1 reduce-scatter.1

commit v2 on v1

v2 whole, which is shorter than its diff:
```python
import functools

import jax
import jax.numpy as jnp
from jax import lax
from jax.experimental import pallas as pl
from jax.experimental.pallas import tpu as pltpu
from jax.sharding import PartitionSpec as P

HD = 128
GROUP = 4
KEY_BLOCK = 512

NEGATIVE = -1e30


def attention_kernel(table_ref, meta_ref, q_ref, k_ref, v_ref, o_ref, peak_sc, total_sc, acc_sc):
    g = pl.program_id(0)
    step = pl.program_id(1)
    count = meta_ref[g, 0]
    is_retrieval = meta_ref[g, 1]
    sink = meta_ref[g, 2]
    window = meta_ref[g, 3]
    row_base = meta_ref[g, 4]
    rows = q_ref.shape[0]
    width = k_ref.shape[0]

    @pl.when(step == 0)
    def _():
        peak_sc[...] = jnp.full_like(peak_sc, NEGATIVE)
        total_sc[...] = jnp.zeros_like(total_sc)
        acc_sc[...] = jnp.zeros_like(acc_sc)

    @pl.when(step < count)
    def _():
        block = table_ref[g, step]
        key_base = block * width
        row = lax.broadcasted_iota(jnp.int32, (rows, width), 0)
        col = lax.broadcasted_iota(jnp.int32, (rows, width), 1)
        later_minus_earlier = (row - col) + (row_base - key_base)
        reach = jnp.where(is_retrieval == 1, jnp.int32(2**30), window)
        allowed = (later_minus_earlier >= 0) & (
            (later_minus_earlier < reach) | (col + key_base < sink)
        )
        keys = k_ref[...]
        values = v_ref[...]
        for i in range(GROUP):
            query = q_ref[:, i * HD:(i + 1) * HD]
            scores = lax.dot_general(
                query, keys, (((1,), (1,)), ((), ())), preferred_element_type=jnp.float32
            ) * HD ** (-0.5)
            old_peak = peak_sc[i]
            block_peak = jnp.max(jnp.where(allowed, scores, NEGATIVE), axis=-1, keepdims=True)
            new_peak = jnp.maximum(old_peak, block_peak)
            rescale = jnp.exp(old_peak - new_peak)
            weights = jnp.where(allowed, jnp.exp(scores - new_peak), 0.0)
            total_sc[i] = rescale * total_sc[i] + jnp.sum(weights, axis=-1, keepdims=True)
            acc_sc[i] = rescale * acc_sc[i] + jnp.dot(
                weights.astype(jnp.bfloat16), values, preferred_element_type=jnp.float32
            )
            peak_sc[i] = new_peak

    @pl.when(step == pl.num_programs(1) - 1)
    def _():
        for i in range(GROUP):
            o_ref[:, i * HD:(i + 1) * HD] = (acc_sc[i] / total_sc[i]).astype(o_ref.dtype)


def block_table(row_base, row_count, token_count, roles, sinks, windows):
    blocks = token_count // KEY_BLOCK
    first = jnp.arange(blocks, dtype=jnp.int32) * KEY_BLOCK
    last_key = first + KEY_BLOCK - 1
    causal = first <= row_base + row_count - 1
    reach = last_key[None, :] >= row_base - windows[:, None] + 1
    sunk = first[None, :] < sinks[:, None]
    needed = causal[None, :] & ((roles[:, None] == 1) | reach | sunk)
    order = jnp.argsort(jnp.logical_not(needed), axis=1, stable=True).astype(jnp.int32)
    count = jnp.sum(needed, axis=1).astype(jnp.int32)
    last = jnp.take_along_axis(order, (count - 1)[:, None], axis=1)
    steps = jnp.arange(blocks, dtype=jnp.int32)[None, :]
    table = jnp.where(steps < count[:, None], order, last)
    meta = jnp.stack(
        [count, roles, sinks, windows, jnp.broadcast_to(row_base, count.shape)], axis=1
    ).astype(jnp.int32)
    meta = jnp.pad(meta, ((0, 0), (0, 3)))
    return table, meta


def attend(queries, both, table, meta, local_heads):
    rows = queries.shape[0]
    blocks = table.shape[1]
    return pl.pallas_call(
        attention_kernel,
        out_shape=jax.ShapeDtypeStruct(queries.shape, jnp.bfloat16),
        grid_spec=pltpu.PrefetchScalarGridSpec(
            num_scalar_prefetch=2,
            grid=(local_heads, blocks),
            in_specs=[
                pl.BlockSpec((rows, GROUP * HD), lambda g, s, t, m: (0, g)),
                pl.BlockSpec((KEY_BLOCK, HD), lambda g, s, t, m: (t[g, s], g)),
                pl.BlockSpec((KEY_BLOCK, HD), lambda g, s, t, m: (t[g, s], local_heads + g)),
            ],
            out_specs=pl.BlockSpec((rows, GROUP * HD), lambda g, s, t, m: (0, g)),
            scratch_shapes=[
                pltpu.VMEM((GROUP, rows, 1), jnp.float32),
                pltpu.VMEM((GROUP, rows, 1), jnp.float32),
                pltpu.VMEM((GROUP, rows, HD), jnp.float32),
            ],
        ),
        compiler_params=pltpu.CompilerParams(
            dimension_semantics=("arbitrary", "arbitrary")
        ),
    )(table, meta, queries, both, both)


def per_device(queries, key_states, value_states, out_weight, head_role, sink_len, window_len):
    row_count = queries.shape[0]
    local_heads = key_states.shape[1] // HD
    row_base = lax.axis_index("ctx") * row_count
    first_head = lax.axis_index("head") * local_heads
    roles_here = lax.dynamic_slice_in_dim(head_role, first_head, local_heads)
    sinks_here = lax.dynamic_slice_in_dim(sink_len, first_head, local_heads)
    windows_here = lax.dynamic_slice_in_dim(window_len, first_head, local_heads)
    both = lax.all_gather(
        jnp.concatenate([key_states, value_states], axis=1), "ctx", axis=0, tiled=True
    )
    table, meta = block_table(
        row_base, row_count, both.shape[0], roles_here, sinks_here, windows_here
    )
    attended = attend(queries, both, table, meta, local_heads)
    mixed = lax.psum_scatter(
        jnp.dot(attended, out_weight, preferred_element_type=jnp.float32).astype(jnp.bfloat16),
        "head",
        scatter_dimension=0,
        tiled=True,
    )
    return mixed


def solution(mesh):
    in_specs = (
        P("ctx", "head"),
        P("ctx", "head"),
        P("ctx", "head"),
        P("head", None),
        P(),
        P(),
        P(),
    )
    out_specs = P(("ctx", "head"), None)
    return jax.shard_map(
        per_device, mesh=mesh, in_specs=in_specs, out_specs=out_specs, check_vma=False
    )
```

time: 276 us -> 251 us (0.909)
  matrix products: 35.1 us -> 5.74 us
  other arithmetic: 23.7 us -> 4.69 us
  waiting for transfers between devices: 196 us -> 214 us
  Pallas kernels: 0 us -> 9.34 us
  local copies, waits for them, and re-layouts: 6.97 us -> 4.1 us
    reduce_scatter x1, waiting for transfers between devices: 22.3 us -> 66 us  [per_device(): lax.psum_scatter(jnp.dot(attended, out_weight, preferred_element_type=jnp...]
    dot_general x2 -> x0, matrix products: 29.5 us -> none  [the longest x1 15.9 us: online_update(): jnp.einsum('thgj,jhd->thgd', weights.astype(jnp.bfloat16), value_part, pr...]
    all_gather x1, waiting for transfers between devices: 174 us -> 148 us  [per_device(): lax.all_gather(jnp.concatenate([key_states, value_states], axis=1), 'ctx'...]
    reduce_sum x1, other arithmetic: 14.4 us -> 0.19 us  [block_table(): count = jnp.sum(needed, axis=1).astype(jnp.int32)]
    pallas_call x0 -> x1, Pallas kernels: none -> 9.34 us  [attend(): pl.pallas_call(attention_kernel, out_shape=jax.ShapeDtypeStruct(queries.s...]
    le x1, other arithmetic: 3.72 us -> 0.01 us  [block_table(): causal = first <= row_base + row_count - 1]
    and x1 -> x0, other arithmetic: 2.8 us -> none  [update(): (earlier <= later) & ((roles_here[None, :, None] == 1) | (earlier < sinks...]
  transfers between devices with their start and end apart: 2 -> 2, of which waited for: 2 -> 2; matrix products, arithmetic and copies ran while one was open for 0% -> 3% of each run, Pallas kernels for 0% -> 0%
where the time goes in v2:
time: 251 us
  waiting for transfers between devices  214 us (85%)
  between operations  13.4 us (5%)
  Pallas kernels  9.34 us (4%)
  matrix products  5.74 us (2%)
  other arithmetic  4.69 us (2%)
  local copies, waits for them, and re-layouts  4.1 us (2%)
    all_gather x1, waiting for transfers between devices, per_device(): lax.all_gather(jnp.concatenate([key_states, value_states], axis=1), 'ctx'...  148 us
    reduce_scatter x1, waiting for transfers between devices, per_device(): lax.psum_scatter(jnp.dot(attended, out_weight, preferred_element_type=jnp...  66 us
    pallas_call x1, Pallas kernels, attend(): pl.pallas_call(attention_kernel, out_shape=jax.ShapeDtypeStruct(queries.s...  9.34 us
    dot_general x1, matrix products, per_device(): jnp.dot(attended, out_weight, preferred_element_type=jnp.float32)  5.74 us
  transfers between devices with their start and end apart: 2, of which 2 were waited for; matrix products, arithmetic and copies ran while one was open for 3% of the time, Pallas kernels for 0%

profile of v2, /device:TPU:1, one launch (start us, length us, event | category | flops | bytes accessed | tf_op | source)
XLA Modules:
  0.0 250.9 jit_solution(490101406791433072)
XLA Ops:
  6.5 1.5 pad_maximum_fusion
  8.2 0.7 dynamic-slice_bitcast_fusion.1
  8.9 0.1 copy.30
  9.0 0.7 dynamic_slice.11
  9.7 0.7 dynamic-slice_bitcast_fusion.2
  10.4 0.1 copy.31
  10.5 0.7 dynamic-slice_bitcast_fusion
  11.3 0.1 copy.32
  11.4 0.7 broadcast_compare_fusion
  12.1 0.2 convert_reduce_fusion
  12.3 0.1 copy.27
  12.4 0.1 copy.29
  12.5 0.1 stack.2
  12.6 0.5 pad.4.meta_ref
  13.1 0.1 copy.26
  13.3 0.7 sort.17
  13.9 0.1 copy.28
  14.0 0.2 or_reduce_fusion
  14.2 0.6 gather_fusion
  14.8 0.6 compare_select_fusion.2.table_ref
  15.4 147.5 %all-gather.2.cloned.1.call-done.k_ref.v_ref = bf16[8192,512]{1,0:T(8,128)(2,1)} async-done(((bf16[128,512]{1,0:T(8,128)(2,1)}), bf16[8192,512]{1,0:T(8,128)(2,1)}) %all-gather.2.cloned.1.call-update) | async-done | bytes 8388624 | tf_op jit(solution)/shard_map/all_gather | solution.py:124
  163.0 9.3 %shard_map.73 = bf16[128,1024]{1,0:T(8,128)(2,1)} custom-call(s32[2,16]{1,0:T(2,128)} %compare_select_fusion.2.table_ref, s32[2,8]{1,0:T(2,128)} %pad.4.meta_ref, bf16[128,1024]{1,0:T(8,128)(2,1)} %q_ref.1, bf16[8192,512]{1,0:T(8,128)(2,1)} %all-gather.2.cloned.1.call-done.k_ref.v_ref, bf16[8192,512]{1,0:T(8,128)(2,1)} %all-gather.2.cloned.1.call-done.k_ref.v_ref), custom_call_target="tpu_custom_call" | custom-call | tf_op jit(solution)/shard_map/pallas_call | solution.py:92
  172.3 5.7 %convolution_convert_fusion = bf16[128,4096]{1,0:T(8,128)(2,1)} fusion(bf16[128,1024]{1,0:T(8,128)(2,1)} %shard_map.73, bf16[1024,4096]{1,0:T(8,128)(2,1)} %param.10), kind=kOutput, calls=%fused_computation.1 | convolution fusion | flops 1074266112 | bytes 9699328 | tf_op jit(solution)/shard_map/dot_general | solution.py:132
  178.1 66.0 %reduce-scatter.2.cloned.1.call-done = bf16[32,4096]{1,0:T(8,128)(2,1)} async-done(((bf16[128,4096]{1,0:T(8,128)(2,1)}), bf16[32,4096]{1,0:T(8,128)(2,1)}) %reduce-scatter.2.cloned.1.call-update) | async-done | bytes 262160 | tf_op jit(solution)/shard_map/reduce_scatter | solution.py:131
  (13 shorter events, 0.1 us)
Async XLA Ops:
  6.5 156.4 %all-gather.2.cloned.1.call-start = ((), (), s32[]{:S(2)}) async-start(), calls=%async_computation.1 | async-start | bytes 8519680 | tf_op jit(solution)/shard_map/all_gather | solution.py:124
  8.1 236.0 %reduce-scatter.2.cloned.1.call-start = ((), (), s32[]{:S(2)}) async-start(), calls=%async_computation.2 | async-start | bytes 1310720 | tf_op jit(solution)/shard_map/reduce_scatter | solution.py:131
Sparse Core Ops, SparseCore 0:
  11.0 151.9 all-gather.1
  178.2 65.8 reduce-scatter.1

commit v3 on v2

v3 whole, which is shorter than its diff:
```python
import functools

import jax
import jax.numpy as jnp
from jax import lax
from jax.experimental import pallas as pl
from jax.experimental.pallas import tpu as pltpu
from jax.sharding import PartitionSpec as P

HD = 128
GROUP = 4
KEY_BLOCK = 512

NEGATIVE = -1e30


def attention_kernel(table_ref, meta_ref, q_ref, k_ref, v_ref, acc_ref, peak_ref, total_ref):
    g = pl.program_id(0)
    step = pl.program_id(1)
    count = meta_ref[g, 0]
    is_retrieval = meta_ref[g, 1]
    sink = meta_ref[g, 2]
    window = meta_ref[g, 3]
    row_base = meta_ref[g, 4]
    key_offset = meta_ref[g, 5]
    rows = q_ref.shape[0]
    width = k_ref.shape[0]

    @pl.when(step == 0)
    def _():
        peak_ref[...] = jnp.full_like(peak_ref, NEGATIVE)
        total_ref[...] = jnp.zeros_like(total_ref)
        acc_ref[...] = jnp.zeros_like(acc_ref)

    @pl.when(step < count)
    def _():
        block = table_ref[g, step]
        key_base = key_offset + block * width
        row = lax.broadcasted_iota(jnp.int32, (rows, width), 0)
        col = lax.broadcasted_iota(jnp.int32, (rows, width), 1)
        later_minus_earlier = (row - col) + (row_base - key_base)
        reach = jnp.where(is_retrieval == 1, jnp.int32(2**30), window)
        allowed = (later_minus_earlier >= 0) & (
            (later_minus_earlier < reach) | (col + key_base < sink)
        )
        keys = k_ref[...]
        values = v_ref[...]
        for i in range(GROUP):
            query = q_ref[:, i * HD:(i + 1) * HD]
            scores = lax.dot_general(
                query, keys, (((1,), (1,)), ((), ())), preferred_element_type=jnp.float32
            ) * HD ** (-0.5)
            old_peak = peak_ref[i]
            block_peak = jnp.max(jnp.where(allowed, scores, NEGATIVE), axis=-1, keepdims=True)
            new_peak = jnp.maximum(old_peak, block_peak)
            rescale = jnp.exp(old_peak - new_peak)
            weights = jnp.where(allowed, jnp.exp(scores - new_peak), 0.0)
            total_ref[i] = rescale * total_ref[i] + jnp.sum(weights, axis=-1, keepdims=True)
            acc_ref[:, i * HD:(i + 1) * HD] = rescale * acc_ref[:, i * HD:(i + 1) * HD] + jnp.dot(
                weights.astype(jnp.bfloat16), values, preferred_element_type=jnp.float32
            )
            peak_ref[i] = new_peak


def block_table(row_base, row_count, key_offset, key_count, roles, sinks, windows):
    blocks = key_count // KEY_BLOCK
    first = key_offset + jnp.arange(blocks, dtype=jnp.int32) * KEY_BLOCK
    last_key = first + KEY_BLOCK - 1
    causal = first <= row_base + row_count - 1
    reach = last_key[None, :] >= row_base - windows[:, None] + 1
    sunk = first[None, :] < sinks[:, None]
    needed = causal[None, :] & ((roles[:, None] == 1) | reach | sunk)
    order = jnp.argsort(jnp.logical_not(needed), axis=1, stable=True).astype(jnp.int32)
    count = jnp.sum(needed, axis=1).astype(jnp.int32)
    last = jnp.take_along_axis(order, jnp.maximum(count - 1, 0)[:, None], axis=1)
    steps = jnp.arange(blocks, dtype=jnp.int32)[None, :]
    table = jnp.where(steps < count[:, None], order, last)
    meta = jnp.stack(
        [
            count,
            roles,
            sinks,
            windows,
            jnp.broadcast_to(row_base, count.shape),
            jnp.broadcast_to(key_offset, count.shape),
        ],
        axis=1,
    ).astype(jnp.int32)
    meta = jnp.pad(meta, ((0, 0), (0, 2)))
    return table, meta


def attend(queries, both, table, meta, local_heads):
    rows = queries.shape[0]
    blocks = table.shape[1]
    heads = local_heads * GROUP
    return pl.pallas_call(
        attention_kernel,
        out_shape=(
            jax.ShapeDtypeStruct(queries.shape, jnp.float32),
            jax.ShapeDtypeStruct((heads, rows, 1), jnp.float32),
            jax.ShapeDtypeStruct((heads, rows, 1), jnp.float32),
        ),
        grid_spec=pltpu.PrefetchScalarGridSpec(
            num_scalar_prefetch=2,
            grid=(local_heads, blocks),
            in_specs=[
                pl.BlockSpec((rows, GROUP * HD), lambda g, s, t, m: (0, g)),
                pl.BlockSpec((KEY_BLOCK, HD), lambda g, s, t, m: (t[g, s], g)),
                pl.BlockSpec((KEY_BLOCK, HD), lambda g, s, t, m: (t[g, s], local_heads + g)),
            ],
            out_specs=(
                pl.BlockSpec((rows, GROUP * HD), lambda g, s, t, m: (0, g)),
                pl.BlockSpec((GROUP, rows, 1), lambda g, s, t, m: (g, 0, 0)),
                pl.BlockSpec((GROUP, rows, 1), lambda g, s, t, m: (g, 0, 0)),
            ),
        ),
        compiler_params=pltpu.CompilerParams(
            dimension_semantics=("arbitrary", "arbitrary")
        ),
    )(table, meta, queries, both, both)


def merge(own, other, row_count):
    acc_a, peak_a, total_a = own
    acc_b, peak_b, total_b = other
    heads = peak_a.shape[0]
    peak_a = peak_a.reshape(heads, row_count).T[:, :, None]
    peak_b = peak_b.reshape(heads, row_count).T[:, :, None]
    total_a = total_a.reshape(heads, row_count).T[:, :, None]
    total_b = total_b.reshape(heads, row_count).T[:, :, None]
    peak = jnp.maximum(peak_a, peak_b)
    scale_a = jnp.exp(peak_a - peak)
    scale_b = jnp.exp(peak_b - peak)
    acc = acc_a.reshape(row_count, heads, HD) * scale_a + acc_b.reshape(row_count, heads, HD) * scale_b
    total = total_a * scale_a + total_b * scale_b
    return (acc / total).astype(jnp.bfloat16).reshape(row_count, heads * HD)


def per_device(queries, key_states, value_states, out_weight, head_role, sink_len, window_len):
    row_count = queries.shape[0]
    local_heads = key_states.shape[1] // HD
    half = lax.axis_index("xh")
    ctx = half * lax.axis_size("zy") + lax.axis_index("zy")
    partner = (1 - half) * lax.axis_size("zy") + lax.axis_index("zy")
    first_head = lax.axis_index("head") * local_heads
    roles_here = lax.dynamic_slice_in_dim(head_role, first_head, local_heads)
    sinks_here = lax.dynamic_slice_in_dim(sink_len, first_head, local_heads)
    windows_here = lax.dynamic_slice_in_dim(window_len, first_head, local_heads)
    swap = [(0, 1), (1, 0)]
    partner_queries = lax.ppermute(queries, "xh", swap)
    both = lax.all_gather(
        jnp.concatenate([key_states, value_states], axis=1), "zy", axis=0, tiled=True
    )
    key_offset = half * both.shape[0]
    table, meta = block_table(
        partner * row_count, row_count, key_offset, both.shape[0],
        roles_here, sinks_here, windows_here,
    )
    for_partner = attend(partner_queries, both, table, meta, local_heads)
    from_partner = lax.ppermute(for_partner, "xh", swap)
    table, meta = block_table(
        ctx * row_count, row_count, key_offset, both.shape[0],
        roles_here, sinks_here, windows_here,
    )
    own = attend(queries, both, table, meta, local_heads)
    attended = merge(own, from_partner, row_count)
    mixed = lax.psum_scatter(
        jnp.dot(attended, out_weight, preferred_element_type=jnp.float32).astype(jnp.bfloat16),
        "head",
        scatter_dimension=0,
        tiled=True,
    )
    return mixed


def solution(mesh):
    ctx_size = mesh.shape["ctx"]
    devices = mesh.devices.reshape(2, ctx_size // 2, mesh.shape["head"])
    split = jax.sharding.Mesh(devices, ("xh", "zy", "head"))
    tokens = ("xh", "zy")
    in_specs = (
        P(tokens, "head"),
        P(tokens, "head"),
        P(tokens, "head"),
        P("head", None),
        P(),
        P(),
        P(),
    )
    out_specs = P(("xh", "zy", "head"), None)
    return jax.shard_map(
        per_device, mesh=split, in_specs=in_specs, out_specs=out_specs, check_vma=False
    )
```

time: 251 us -> 184 us (0.73)
  waiting for transfers between devices: 214 us -> 111 us
  Pallas kernels: 9.34 us -> 30.5 us
  starting transfers between devices: 0.04 us -> 6.78 us
  other arithmetic: 4.69 us -> 8.71 us
    all_gather x1, waiting for transfers between devices: 148 us -> 72.8 us  [per_device(): lax.all_gather(jnp.concatenate([key_states, value_states], axis=1), 'zy',...]
    reduce_scatter x1, waiting for transfers between devices: 66 us -> 18.2 us  [per_device(): lax.psum_scatter(jnp.dot(attended, out_weight, preferred_element_type=jnp...]
    pallas_call x1 -> x2, Pallas kernels: 9.34 us -> 30.5 us  [attend(): pl.pallas_call(attention_kernel, out_shape=(jax.ShapeDtypeStruct(queries....]
    ppermute x0 -> x4, waiting for transfers between devices: none -> 20.2 us  [the longest x3 20.2 us: per_device(): from_partner = lax.ppermute(for_partner, 'xh', swap)]
    ppermute x0 -> x4, starting transfers between devices: none -> 6.74 us  [the longest x1 3.66 us: per_device(): partner_queries = lax.ppermute(queries, 'xh', swap)]
  transfers between devices with their start and end apart: 2 -> 6, of which waited for: 2 -> 4; matrix products, arithmetic and copies ran while one was open for 3% -> 7% of each run, Pallas kernels for 0% -> 5%
where the time goes in v3:
time: 184 us; the launch traced here: 183 us
  waiting for transfers between devices  111 us (60%)
  Pallas kernels  30.5 us (17%)
  between operations  13.5 us (7%)
  other arithmetic  8.71 us (5%)
  starting transfers between devices  6.78 us (4%)
  local copies, waits for them, and re-layouts  6.5 us (4%)
  matrix products  6.09 us (3%)
    all_gather x1, waiting for transfers between devices, per_device(): lax.all_gather(jnp.concatenate([key_states, value_states], axis=1), 'zy',...  72.8 us
    pallas_call x2, Pallas kernels, attend(): pl.pallas_call(attention_kernel, out_shape=(jax.ShapeDtypeStruct(queries....  30.5 us
    ppermute x3, waiting for transfers between devices, per_device(): from_partner = lax.ppermute(for_partner, 'xh', swap)  20.2 us
    reduce_scatter x1, waiting for transfers between devices, per_device(): lax.psum_scatter(jnp.dot(attended, out_weight, preferred_element_type=jnp...  18.2 us
    dot_general x1, matrix products, per_device(): jnp.dot(attended, out_weight, preferred_element_type=jnp.float32)  6.09 us
  transfers between devices with their start and end apart: 6, of which 4 were waited for; matrix products, arithmetic and copies ran while one was open for 7% of the time, Pallas kernels for 5%

profile of v3, /device:TPU:1, one launch (start us, length us, event | category | flops | bytes accessed | tf_op | source)
XLA Modules:
  0.0 183.2 jit_solution(6059854021601889432)
XLA Ops:
  6.5 1.5 pad_maximum_fusion
  8.1 3.7 %collective-permute-start = (bf16[128,1024]{1,0:T(8,128)(2,1)}, bf16[128,1024]{1,0:T(8,128)(2,1)S(1)}, u32[]{:S(2)}, u32[]{:S(2)}) collective-permute-start(bf16[128,1024]{1,0:T(8,128)(2,1)} %q_ref.1), channel_id=1, source_target_pairs={{0,128},{128,0},{1,129},{129,1},{2,130},{130,2},{3,131},{131,3},{4... | collective-permute-start | bytes 786440 | tf_op jit(solution)/shard_map/ppermute | solution.py:151
  11.8 0.7 dynamic_slice.11
  12.5 0.7 broadcast_compare_fusion.1
  13.3 0.7 subtract_add_fusion.1
  14.3 0.6 sort.32
  15.0 0.6 gather_fusion.1
  15.6 0.7 dynamic-slice_bitcast_fusion
  16.3 0.7 dynamic-slice_bitcast_fusion.2
  18.3 0.6 sort.31
  18.9 0.6 gather_fusion
  19.5 0.7 compare_select_fusion.2.table_ref
  20.2 72.8 %all-gather.2.cloned.1.call-done.k_ref.v_ref = bf16[4096,512]{1,0:T(8,128)(2,1)} async-done(((bf16[128,512]{1,0:T(8,128)(2,1)}), bf16[4096,512]{1,0:T(8,128)(2,1)}) %all-gather.2.cloned.1.call-update) | async-done | bytes 4194320 | tf_op jit(solution)/shard_map/all_gather | solution.py:152
  93.0 22.1 %shard_map.74 = (f32[128,1024]{1,0:T(8,128)}, f32[8,128,1]{2,1,0:T(8,128)}, f32[8,128,1]{2,1,0:T(8,128)}) custom-call(s32[2,8]{1,0:T(2,128)} %compare_select_fusion.2.table_ref, s32[2,8]{1,0:T(2,128)} %pad.8.meta_ref, bf16[128,1024]{1,0:T(8,128)(2,1)} %copy-done, bf16[4096,512]{1,0:T(8,128)(2,1)} %all-gather.2.cloned.1.call-done.k_ref.v_ref, ...), custom_call_target="tpu_custom_call" | custom-call | tf_op jit(solution)/shard_map/pallas_call | solution.py:97
  115.2 3.0 %collective-permute-start.1 = (f32[8,128,1]{2,1,0:T(8,128)}, f32[8,128,1]{2,1,0:T(8,128)S(1)}, u32[]{:S(2)}, u32[]{:S(2)}) collective-permute-start(f32[8,128,1]{2,1,0:T(8,128)} %get-tuple-element.18), channel_id=1, source_target_pairs={{0,128},{128,0},{1,129},{129,1},{2,130},{130,2},{3,131},{131,3},{4... | collective-permute-start | bytes 12296 | tf_op jit(solution)/shard_map/ppermute | solution.py:161
  118.3 0.6 compare_select_fusion.3.table_ref
  119.1 0.6 pad.7.meta_ref
  119.7 8.3 %shard_map.73 = (f32[128,1024]{1,0:T(8,128)}, f32[8,128,1]{2,1,0:T(8,128)}, f32[8,128,1]{2,1,0:T(8,128)}) custom-call(s32[2,8]{1,0:T(2,128)} %compare_select_fusion.3.table_ref, s32[2,8]{1,0:T(2,128)} %pad.7.meta_ref, bf16[128,1024]{1,0:T(8,128)(2,1)} %q_ref.1, bf16[4096,512]{1,0:T(8,128)(2,1)} %all-gather.2.cloned.1.call-done.k_ref.v_ref, ...), custom_call_target="tpu_custom_call" | custom-call | tf_op jit(solution)/shard_map/pallas_call | solution.py:97
  128.0 1.2 reduce
  129.3 1.2 reduce.2
  130.5 9.2 %collective-permute-done.1 = f32[8,128,1]{2,1,0:T(8,128)S(1)} collective-permute-done((f32[8,128,1]{2,1,0:T(8,128)}, f32[8,128,1]{2,1,0:T(8,128)S(1)}, u32[]{:S(2)}, u32[]{:S(2)}) %collective-permute-start.1) | collective-permute-done | bytes 4128 | tf_op jit(solution)/shard_map/ppermute | solution.py:161
  139.9 11.0 %collective-permute-done.3 = f32[8,128,1]{2,1,0:T(8,128)S(1)} collective-permute-done((f32[8,128,1]{2,1,0:T(8,128)}, f32[8,128,1]{2,1,0:T(8,128)S(1)}, u32[]{:S(2)}, u32[]{:S(2)}) %collective-permute-start.3) | collective-permute-done | bytes 4128 | tf_op jit(solution)/shard_map/ppermute | solution.py:161
  152.1 6.1 %convolution_convert_fusion = bf16[128,4096]{1,0:T(8,128)(2,1)} fusion(bf16[1024,4096]{1,0:T(8,128)(2,1)} %param.12, f32[16,8,8,128]{3,2,1,0:T(8,128)S(1)} %bitcast.77, f32[128,1024]{1,0:T(8,128)S(1)} %collective-permute-done.2, f32[16,8,8,128]{3,2,1,0:T(8,128)S(1)} %bitcast.76, f32[128,1024]{1,0:T(8,128)} %get-tuple-element.15, ...), kind=kOutput, calls=%fused_computation.2 | convolution fusion | flops 1074921472 | bytes 12058624 | tf_op jit(solution)/shard_map/dot_general | solution.py:169
  158.2 18.2 %reduce-scatter.2.cloned.1.call-done = bf16[32,4096]{1,0:T(8,128)(2,1)} async-done(((bf16[128,4096]{1,0:T(8,128)(2,1)}), bf16[32,4096]{1,0:T(8,128)(2,1)}) %reduce-scatter.2.cloned.1.call-update) | async-done | bytes 262160 | tf_op jit(solution)/shard_map/reduce_scatter | solution.py:168
  (49 shorter events, 3.3 us)
Async XLA Ops:
  6.5 86.4 %all-gather.2.cloned.1.call-start = ((), (), s32[]{:S(2)}) async-start(), calls=%async_computation.1 | async-start | bytes 4325376 | tf_op jit(solution)/shard_map/all_gather | solution.py:152
  8.1 168.3 %reduce-scatter.2.cloned.1.call-start = ((), (), s32[]{:S(2)}) async-start(), calls=%async_computation.2 | async-start | bytes 1310720 | tf_op jit(solution)/shard_map/reduce_scatter | solution.py:168
  8.1 12.1 %collective-permute-start = (bf16[128,1024]{1,0:T(8,128)(2,1)}, bf16[128,1024]{1,0:T(8,128)(2,1)S(1)}, u32[]{:S(2)}, u32[]{:S(2)}) collective-permute-start(bf16[128,1024]{1,0:T(8,128)(2,1)} %q_ref.1), channel_id=1, source_target_pairs={{0,128},{128,0},{1,129},{129,1},{2,130},{130,2},{3,131},{131,3},{4... | collective-permute-start | bytes 786440 | tf_op jit(solution)/shard_map/ppermute | solution.py:151
  20.2 72.8 %copy-start = (bf16[128,1024]{1,0:T(8,128)(2,1)}, bf16[128,1024]{1,0:T(8,128)(2,1)S(1)}, u32[]{:S(2)}) copy-start(bf16[128,1024]{1,0:T(8,128)(2,1)S(1)} %collective-permute-done.q_ref) | copy-start | bytes 786436
  115.1 36.3 %collective-permute-start.2 = (f32[128,1024]{1,0:T(8,128)}, f32[128,1024]{1,0:T(8,128)S(1)}, u32[]{:S(2)}, u32[]{:S(2)}) collective-permute-start(f32[128,1024]{1,0:T(8,128)} %get-tuple-element.19), channel_id=1, source_target_pairs={{0,128},{128,0},{1,129},{129,1},{2,130},{130,2},{3,131},{131,3},{4... | collective-permute-start | bytes 1572872 | tf_op jit(solution)/shard_map/ppermute | solution.py:161
  115.2 24.5 %collective-permute-start.1 = (f32[8,128,1]{2,1,0:T(8,128)}, f32[8,128,1]{2,1,0:T(8,128)S(1)}, u32[]{:S(2)}, u32[]{:S(2)}) collective-permute-start(f32[8,128,1]{2,1,0:T(8,128)} %get-tuple-element.18), channel_id=1, source_target_pairs={{0,128},{128,0},{1,129},{129,1},{2,130},{130,2},{3,131},{131,3},{4... | collective-permute-start | bytes 12296 | tf_op jit(solution)/shard_map/ppermute | solution.py:161
  118.2 32.7 %collective-permute-start.3 = (f32[8,128,1]{2,1,0:T(8,128)}, f32[8,128,1]{2,1,0:T(8,128)S(1)}, u32[]{:S(2)}, u32[]{:S(2)}) collective-permute-start(f32[8,128,1]{2,1,0:T(8,128)} %get-tuple-element.21), channel_id=1, source_target_pairs={{0,128},{128,0},{1,129},{129,1},{2,130},{130,2},{3,131},{131,3},{4... | collective-permute-start | bytes 12296 | tf_op jit(solution)/shard_map/ppermute | solution.py:161
Sparse Core Ops, SparseCore 0:
  9.9 82.9 all-gather.1
  158.3 18.0 reduce-scatter.1

commit v4 on v3

v4 whole, which is shorter than its diff:
```python
import functools

import jax
import jax.numpy as jnp
from jax import lax
from jax.experimental import pallas as pl
from jax.experimental.pallas import tpu as pltpu
from jax.sharding import PartitionSpec as P

HD = 128
GROUP = 4
KEY_BLOCK = 512

NEGATIVE = -1e30


def attention_kernel(table_ref, meta_ref, q_ref, k_ref, v_ref, acc_ref, peak_ref, total_ref):
    g = pl.program_id(0)
    step = pl.program_id(1)
    blocks = pl.num_programs(1)
    count = meta_ref[g, 0]
    is_retrieval = meta_ref[g, 1]
    sink = meta_ref[g, 2]
    window = meta_ref[g, 3]
    row_base = meta_ref[g, 4]
    key_offset = meta_ref[g, 5]
    rows = q_ref.shape[1] // GROUP
    width = k_ref.shape[0]

    @pl.when(step == 0)
    def _():
        peak_ref[...] = jnp.full_like(peak_ref, NEGATIVE)
        total_ref[...] = jnp.zeros_like(total_ref)
        acc_ref[...] = jnp.zeros_like(acc_ref)

    def update(allowed):
        scores = lax.dot_general(
            q_ref[0], k_ref[...], (((1,), (1,)), ((), ())), preferred_element_type=jnp.float32
        ) * HD ** (-0.5)
        old_peak = peak_ref[0]
        if allowed is None:
            block_peak = jnp.max(scores, axis=-1, keepdims=True)
            new_peak = jnp.maximum(old_peak, block_peak)
            weights = jnp.exp(scores - new_peak)
        else:
            scores = scores.reshape(GROUP, rows, width)
            block_peak = jnp.max(
                jnp.where(allowed, scores, NEGATIVE), axis=-1, keepdims=True
            ).reshape(GROUP * rows, 1)
            new_peak = jnp.maximum(old_peak, block_peak)
            weights = jnp.where(
                allowed, jnp.exp(scores - new_peak.reshape(GROUP, rows, 1)), 0.0
            ).reshape(GROUP * rows, width)
        rescale = jnp.exp(old_peak - new_peak)
        total_ref[0] = rescale * total_ref[0] + jnp.sum(weights, axis=-1, keepdims=True)
        acc_ref[0] = rescale * acc_ref[0] + jnp.dot(
            weights.astype(jnp.bfloat16), v_ref[...], preferred_element_type=jnp.float32
        )
        peak_ref[0] = new_peak

    full = table_ref[g, blocks + step]

    @pl.when((step < count) & (full == 1))
    def _():
        update(None)

    @pl.when((step < count) & (full == 0))
    def _():
        block = table_ref[g, step]
        key_base = key_offset + block * width
        row = lax.broadcasted_iota(jnp.int32, (rows, width), 0)
        col = lax.broadcasted_iota(jnp.int32, (rows, width), 1)
        later_minus_earlier = (row - col) + (row_base - key_base)
        reach = jnp.where(is_retrieval == 1, jnp.int32(2**30), window)
        allowed = (later_minus_earlier >= 0) & (
            (later_minus_earlier < reach) | (col + key_base < sink)
        )
        update(allowed[None])


def block_table(row_base, row_count, key_offset, key_count, roles, sinks, windows):
    blocks = key_count // KEY_BLOCK
    first = key_offset + jnp.arange(blocks, dtype=jnp.int32) * KEY_BLOCK
    last_key = first + KEY_BLOCK - 1
    last_row = row_base + row_count - 1
    causal = first <= last_row
    reach = last_key[None, :] >= row_base - windows[:, None] + 1
    sunk = first[None, :] < sinks[:, None]
    retrieval = roles[:, None] == 1
    needed = causal[None, :] & (retrieval | reach | sunk)
    whole = (last_key <= row_base)[None, :] & (
        retrieval
        | (last_key[None, :] < sinks[:, None])
        | (last_row - first[None, :] < windows[:, None])
    )
    order = jnp.argsort(jnp.logical_not(needed), axis=1, stable=True).astype(jnp.int32)
    count = jnp.sum(needed, axis=1).astype(jnp.int32)
    last = jnp.take_along_axis(order, jnp.maximum(count - 1, 0)[:, None], axis=1)
    steps = jnp.arange(blocks, dtype=jnp.int32)[None, :]
    table = jnp.where(steps < count[:, None], order, last)
    full = jnp.take_along_axis(whole, table, axis=1).astype(jnp.int32)
    meta = jnp.stack(
        [
            count,
            roles,
            sinks,
            windows,
            jnp.broadcast_to(row_base, count.shape),
            jnp.broadcast_to(key_offset, count.shape),
        ],
        axis=1,
    ).astype(jnp.int32)
    meta = jnp.pad(meta, ((0, 0), (0, 2)))
    return jnp.concatenate([table, full], axis=1), meta


def attend(stacked, both, table, meta):
    local_heads, stack_rows, _ = stacked.shape
    blocks = table.shape[1] // 2
    return pl.pallas_call(
        attention_kernel,
        out_shape=(
            jax.ShapeDtypeStruct(stacked.shape, jnp.float32),
            jax.ShapeDtypeStruct((local_heads, stack_rows, 1), jnp.float32),
            jax.ShapeDtypeStruct((local_heads, stack_rows, 1), jnp.float32),
        ),
        grid_spec=pltpu.PrefetchScalarGridSpec(
            num_scalar_prefetch=2,
            grid=(local_heads, blocks),
            in_specs=[
                pl.BlockSpec((1, stack_rows, HD), lambda g, s, t, m: (g, 0, 0)),
                pl.BlockSpec((KEY_BLOCK, HD), lambda g, s, t, m: (t[g, s], g)),
                pl.BlockSpec((KEY_BLOCK, HD), lambda g, s, t, m: (t[g, s], local_heads + g)),
            ],
            out_specs=(
                pl.BlockSpec((1, stack_rows, HD), lambda g, s, t, m: (g, 0, 0)),
                pl.BlockSpec((1, stack_rows, 1), lambda g, s, t, m: (g, 0, 0)),
                pl.BlockSpec((1, stack_rows, 1), lambda g, s, t, m: (g, 0, 0)),
            ),
        ),
        compiler_params=pltpu.CompilerParams(
            dimension_semantics=("arbitrary", "arbitrary")
        ),
    )(table, meta, stacked, both, both)


def stack_heads(queries, local_heads):
    rows = queries.shape[0]
    return (
        queries.reshape(rows, local_heads, GROUP, HD)
        .transpose(1, 2, 0, 3)
        .reshape(local_heads, GROUP * rows, HD)
    )


def merge(own, other, row_count):
    acc_a, peak_a, total_a = own
    acc_b, peak_b, total_b = other
    peak = jnp.maximum(peak_a, peak_b)
    scale_a = jnp.exp(peak_a - peak)
    scale_b = jnp.exp(peak_b - peak)
    acc = acc_a * scale_a + acc_b * scale_b
    total = total_a * scale_a + total_b * scale_b
    local_heads = acc.shape[0]
    attended = (acc / total).astype(jnp.bfloat16)
    return (
        attended.reshape(local_heads, GROUP, row_count, HD)
        .transpose(2, 0, 1, 3)
        .reshape(row_count, local_heads * GROUP * HD)
    )


def per_device(queries, key_states, value_states, out_weight, head_role, sink_len, window_len):
    row_count = queries.shape[0]
    local_heads = key_states.shape[1] // HD
    half = lax.axis_index("xh")
    ctx = half * lax.axis_size("zy") + lax.axis_index("zy")
    partner = (1 - half) * lax.axis_size("zy") + lax.axis_index("zy")
    first_head = lax.axis_index("head") * local_heads
    roles_here = lax.dynamic_slice_in_dim(head_role, first_head, local_heads)
    sinks_here = lax.dynamic_slice_in_dim(sink_len, first_head, local_heads)
    windows_here = lax.dynamic_slice_in_dim(window_len, first_head, local_heads)
    swap = [(0, 1), (1, 0)]
    partner_queries = lax.ppermute(stack_heads(queries, local_heads), "xh", swap)
    both = lax.all_gather(
        jnp.concatenate([key_states, value_states], axis=1), "zy", axis=0, tiled=True
    )
    key_offset = half * both.shape[0]
    table, meta = block_table(
        partner * row_count, row_count, key_offset, both.shape[0],
        roles_here, sinks_here, windows_here,
    )
    for_partner = attend(partner_queries, both, table, meta)
    from_partner = lax.ppermute(for_partner, "xh", swap)
    table, meta = block_table(
        ctx * row_count, row_count, key_offset, both.shape[0],
        roles_here, sinks_here, windows_here,
    )
    own = attend(stack_heads(queries, local_heads), both, table, meta)
    attended = merge(own, from_partner, row_count)
    mixed = lax.psum_scatter(
        jnp.dot(attended, out_weight, preferred_element_type=jnp.float32).astype(jnp.bfloat16),
        "head",
        scatter_dimension=0,
        tiled=True,
    )
    return mixed


def solution(mesh):
    ctx_size = mesh.shape["ctx"]
    devices = mesh.devices.reshape(2, ctx_size // 2, mesh.shape["head"])
    split = jax.sharding.Mesh(devices, ("xh", "zy", "head"))
    tokens = ("xh", "zy")
    in_specs = (
        P(tokens, "head"),
        P(tokens, "head"),
        P(tokens, "head"),
        P("head", None),
        P(),
        P(),
        P(),
    )
    out_specs = P(("xh", "zy", "head"), None)
    return jax.shard_map(
        per_device, mesh=split, in_specs=in_specs, out_specs=out_specs, check_vma=False
    )
```

time: 184 us -> 191 us (1.038)
  waiting for transfers between devices: 111 us -> 127 us
  Pallas kernels: 30.5 us -> 19.7 us
  local copies, waits for them, and re-layouts: 6.5 us -> 8.63 us
    reduce_scatter x1, waiting for transfers between devices: 18.2 us -> 35.7 us  [per_device(): lax.psum_scatter(jnp.dot(attended, out_weight, preferred_element_type=jnp...]
    pallas_call x2, Pallas kernels: 30.5 us -> 19.7 us  [attend(): pl.pallas_call(attention_kernel, out_shape=(jax.ShapeDtypeStruct(stacked....]
    all_gather x1, waiting for transfers between devices: 72.8 us -> 69.5 us  [per_device(): lax.all_gather(jnp.concatenate([key_states, value_states], axis=1), 'zy',...]
    pallas_call x2 -> x0, other arithmetic: 2.49 us -> none  [attend(): pl.pallas_call(attention_kernel, out_shape=(jax.ShapeDtypeStruct(queries....]
  transfers between devices with their start and end apart: 6 -> 6, of which waited for: 4 -> 4; matrix products, arithmetic and copies ran while one was open for 7% -> 8% of each run, Pallas kernels for 5% -> 4%
where the time goes in v4:
time: 191 us
  waiting for transfers between devices  127 us (66%)
  Pallas kernels  19.7 us (10%)
  between operations  13.5 us (7%)
  other arithmetic  9.32 us (5%)
  local copies, waits for them, and re-layouts  8.63 us (5%)
  starting transfers between devices  6.76 us (4%)
  matrix products  5.66 us (3%)
    all_gather x1, waiting for transfers between devices, per_device(): lax.all_gather(jnp.concatenate([key_states, value_states], axis=1), 'zy',...  69.5 us
    reduce_scatter x1, waiting for transfers between devices, per_device(): lax.psum_scatter(jnp.dot(attended, out_weight, preferred_element_type=jnp...  35.7 us
    ppermute x3, waiting for transfers between devices, per_device(): from_partner = lax.ppermute(for_partner, 'xh', swap)  21.8 us
    pallas_call x2, Pallas kernels, attend(): pl.pallas_call(attention_kernel, out_shape=(jax.ShapeDtypeStruct(stacked....  19.7 us
    dot_general x1, matrix products, per_device(): jnp.dot(attended, out_weight, preferred_element_type=jnp.float32)  5.66 us
  transfers between devices with their start and end apart: 6, of which 4 were waited for; matrix products, arithmetic and copies ran while one was open for 8% of the time, Pallas kernels for 4%

profile of v4, /device:TPU:1, one launch (start us, length us, event | category | flops | bytes accessed | tf_op | source)
XLA Modules:
  0.0 190.6 jit_solution(7673681291731494379)
XLA Ops:
  6.5 1.5 pad_maximum_fusion
  8.1 1.1 reshape.98
  9.3 3.7 %collective-permute-start = (bf16[2,512,128]{2,1,0:T(8,128)(2,1)S(1)}, bf16[2,512,128]{2,1,0:T(8,128)(2,1)S(1)}, u32[]{:S(2)}, u32[]{:S(2)}) collective-permute-start(bf16[2,512,128]{2,1,0:T(8,128)(2,1)S(1)} %bitcast.53), channel_id=1, source_target_pairs={{0,128},{128,0},{1,129},{129,1},{2,130},{130,2},{3,131},{131,3},{4... | collective-permute-start | bytes 786440 | tf_op jit(solution)/shard_map/ppermute | solution.py:184
  13.0 0.7 dynamic_slice.11
  13.7 0.7 dynamic-slice_bitcast_fusion
  14.5 0.7 dynamic-slice_bitcast_fusion.1
  15.3 0.7 subtract_add_fusion.1
  16.2 0.7 broadcast_compare_fusion.3
  18.1 0.6 sort.32
  19.7 0.7 gather_fusion.3
  20.5 0.6 sort.31
  22.0 0.7 gather_fusion.1
  22.8 0.7 pad_add_fusion.3.table_ref
  23.5 69.5 %all-gather.2.cloned.1.call-done.k_ref.v_ref = bf16[4096,512]{1,0:T(8,128)(2,1)} async-done(((bf16[128,512]{1,0:T(8,128)(2,1)}), bf16[4096,512]{1,0:T(8,128)(2,1)}) %all-gather.2.cloned.1.call-update) | async-done | bytes 4194320 | tf_op jit(solution)/shard_map/all_gather | solution.py:185
  93.0 11.8 %shard_map.74 = (f32[2,512,128]{2,1,0:T(8,128)}, f32[2,512,1]{2,1,0:T(8,128)}, f32[2,512,1]{2,1,0:T(8,128)}) custom-call(s32[2,16]{1,0:T(2,128)} %pad_add_fusion.3.table_ref, s32[2,8]{1,0:T(2,128)} %pad.8.meta_ref, bf16[2,512,128]{2,1,0:T(8,128)(2,1)} %copy-done.1, bf16[4096,512]{1,0:T(8,128)(2,1)} %all-gather.2.cloned.1.call-done.k_ref.v_ref, ...), custom_call_target="tpu_custom_call" | custom-call | tf_op jit(solution)/shard_map/pallas_call | solution.py:120
  104.7 3.0 %collective-permute-start.1 = (f32[2,512,1]{2,1,0:T(8,128)}, f32[2,512,1]{2,1,0:T(8,128)S(1)}, u32[]{:S(2)}, u32[]{:S(2)}) collective-permute-start(f32[2,512,1]{2,1,0:T(8,128)} %get-tuple-element.19), channel_id=1, source_target_pairs={{0,128},{128,0},{1,129},{129,1},{2,130},{130,2},{3,131},{131,3},{4... | collective-permute-start | bytes 12296 | tf_op jit(solution)/shard_map/ppermute | solution.py:194
  107.8 0.6 pad_add_fusion.2.table_ref
  109.2 8.0 %shard_map.73 = (f32[2,512,128]{2,1,0:T(8,128)}, f32[2,512,1]{2,1,0:T(8,128)}, f32[2,512,1]{2,1,0:T(8,128)}) custom-call(s32[2,16]{1,0:T(2,128)} %pad_add_fusion.2.table_ref, s32[2,8]{1,0:T(2,128)} %pad.7.meta_ref, bf16[2,512,128]{2,1,0:T(8,128)(2,1)} %bitcast.54, bf16[4096,512]{1,0:T(8,128)(2,1)} %all-gather.2.cloned.1.call-done.k_ref.v_ref, ...), custom_call_target="tpu_custom_call" | custom-call | tf_op jit(solution)/shard_map/pallas_call | solution.py:120
  117.2 10.6 %collective-permute-done.1 = f32[2,512,1]{2,1,0:T(8,128)S(1)} collective-permute-done((f32[2,512,1]{2,1,0:T(8,128)}, f32[2,512,1]{2,1,0:T(8,128)S(1)}, u32[]{:S(2)}, u32[]{:S(2)}) %collective-permute-start.1) | collective-permute-done | bytes 4128 | tf_op jit(solution)/shard_map/ppermute | solution.py:194
  127.8 11.2 %collective-permute-done.3 = f32[2,512,1]{2,1,0:T(8,128)S(1)} collective-permute-done((f32[2,512,1]{2,1,0:T(8,128)}, f32[2,512,1]{2,1,0:T(8,128)S(1)}, u32[]{:S(2)}, u32[]{:S(2)}) %collective-permute-start.3) | collective-permute-done | bytes 4128 | tf_op jit(solution)/shard_map/ppermute | solution.py:194
  139.0 1.7 fusion.3
  140.7 1.5 divide_convert_fusion
  142.4 5.7 %convolution_convert_fusion = bf16[128,4096]{1,0:T(8,128)(2,1)} fusion(bf16[128,1024]{0,1:T(8,128)(2,1)S(1)} %bitcast.52, bf16[1024,4096]{1,0:T(8,128)(2,1)} %param.14), kind=kOutput, calls=%fused_computation.4 | convolution fusion | flops 1074266112 | bytes 9699328 | tf_op jit(solution)/shard_map/dot_general | solution.py:202
  148.1 35.7 %reduce-scatter.2.cloned.1.call-done = bf16[32,4096]{1,0:T(8,128)(2,1)} async-done(((bf16[128,4096]{1,0:T(8,128)(2,1)}), bf16[32,4096]{1,0:T(8,128)(2,1)}) %reduce-scatter.2.cloned.1.call-update) | async-done | bytes 262160 | tf_op jit(solution)/shard_map/reduce_scatter | solution.py:201
  (59 shorter events, 4.7 us)
Async XLA Ops:
  6.5 86.4 %all-gather.2.cloned.1.call-start = ((), (), s32[]{:S(2)}) async-start(), calls=%async_computation.1 | async-start | bytes 4325376 | tf_op jit(solution)/shard_map/all_gather | solution.py:185
  8.1 175.7 %reduce-scatter.2.cloned.1.call-start = ((), (), s32[]{:S(2)}) async-start(), calls=%async_computation.2 | async-start | bytes 1310720 | tf_op jit(solution)/shard_map/reduce_scatter | solution.py:201
  9.3 99.9 %copy-start = (bf16[128,2,4,128]{3,0,2,1:T(8,128)(2,1)}, bf16[128,2,4,128]{3,0,2,1:T(8,128)(2,1)S(1)}, u32[]{:S(2)}) copy-start(bf16[128,2,4,128]{3,0,2,1:T(8,128)(2,1)S(1)} %copy.54) | copy-start | bytes 786436
  9.3 14.2 %collective-permute-start = (bf16[2,512,128]{2,1,0:T(8,128)(2,1)S(1)}, bf16[2,512,128]{2,1,0:T(8,128)(2,1)S(1)}, u32[]{:S(2)}, u32[]{:S(2)}) collective-permute-start(bf16[2,512,128]{2,1,0:T(8,128)(2,1)S(1)} %bitcast.53), channel_id=1, source_target_pairs={{0,128},{128,0},{1,129},{129,1},{2,130},{130,2},{3,131},{131,3},{4... | collective-permute-start | bytes 786440 | tf_op jit(solution)/shard_map/ppermute | solution.py:184
  23.5 69.5 %copy-start.1 = (bf16[2,512,128]{2,1,0:T(8,128)(2,1)}, bf16[2,512,128]{2,1,0:T(8,128)(2,1)S(1)}, u32[]{:S(2)}) copy-start(bf16[2,512,128]{2,1,0:T(8,128)(2,1)S(1)} %collective-permute-done.q_ref) | copy-start | bytes 786436
  104.7 36.0 %collective-permute-start.2 = (f32[2,512,128]{2,1,0:T(8,128)}, f32[2,512,128]{2,1,0:T(8,128)S(1)}, u32[]{:S(2)}, u32[]{:S(2)}) collective-permute-start(f32[2,512,128]{2,1,0:T(8,128)} %get-tuple-element.20), channel_id=1, source_target_pairs={{0,128},{128,0},{1,129},{129,1},{2,130},{130,2},{3,131},{131,3},{4... | collective-permute-start | bytes 1572872 | tf_op jit(solution)/shard_map/ppermute | solution.py:194
  104.7 23.0 %collective-permute-start.1 = (f32[2,512,1]{2,1,0:T(8,128)}, f32[2,512,1]{2,1,0:T(8,128)S(1)}, u32[]{:S(2)}, u32[]{:S(2)}) collective-permute-start(f32[2,512,1]{2,1,0:T(8,128)} %get-tuple-element.19), channel_id=1, source_target_pairs={{0,128},{128,0},{1,129},{129,1},{2,130},{130,2},{3,131},{131,3},{4... | collective-permute-start | bytes 12296 | tf_op jit(solution)/shard_map/ppermute | solution.py:194
  107.7 31.3 %collective-permute-start.3 = (f32[2,512,1]{2,1,0:T(8,128)}, f32[2,512,1]{2,1,0:T(8,128)S(1)}, u32[]{:S(2)}, u32[]{:S(2)}) collective-permute-start(f32[2,512,1]{2,1,0:T(8,128)} %get-tuple-element.22), channel_id=1, source_target_pairs={{0,128},{128,0},{1,129},{129,1},{2,130},{130,2},{3,131},{131,3},{4... | collective-permute-start | bytes 12296 | tf_op jit(solution)/shard_map/ppermute | solution.py:194
Sparse Core Ops, SparseCore 0:
  9.9 82.9 all-gather.1
  148.2 35.5 reduce-scatter.1

commit v5 on v4

--- a/solution.py
+++ b/solution.py
@@ -173,31 +173,40 @@
 def per_device(queries, key_states, value_states, out_weight, head_role, sink_len, window_len):
     row_count = queries.shape[0]
     local_heads = key_states.shape[1] // HD
+    half_size = lax.axis_size("z") * lax.axis_size("y")
     half = lax.axis_index("xh")
-    ctx = half * lax.axis_size("zy") + lax.axis_index("zy")
-    partner = (1 - half) * lax.axis_size("zy") + lax.axis_index("zy")
+    place = lax.axis_index("z") * lax.axis_size("y") + lax.axis_index("y")
+    ctx = half * half_size + place
+    partner = (1 - half) * half_size + place
     first_head = lax.axis_index("head") * local_heads
     roles_here = lax.dynamic_slice_in_dim(head_role, first_head, local_heads)
     sinks_here = lax.dynamic_slice_in_dim(sink_len, first_head, local_heads)
     windows_here = lax.dynamic_slice_in_dim(window_len, first_head, local_heads)
-    swap = [(0, 1), (1, 0)]
-    partner_queries = lax.ppermute(stack_heads(queries, local_heads), "xh", swap)
-    both = lax.all_gather(
-        jnp.concatenate([key_states, value_states], axis=1), "zy", axis=0, tiled=True
-    )
+    partner_queries = lax.ppermute(stack_heads(queries, local_heads), "xh", [(1, 0)])
+    both = jnp.concatenate([key_states, value_states], axis=1)
+    both = lax.all_gather(both, "y", axis=0, tiled=True)
+    both = lax.all_gather(both, "z", axis=0, tiled=True)
     key_offset = half * both.shape[0]
     table, meta = block_table(
         partner * row_count, row_count, key_offset, both.shape[0],
         roles_here, sinks_here, windows_here,
     )
-    for_partner = attend(partner_queries, both, table, meta)
-    from_partner = lax.ppermute(for_partner, "xh", swap)
+    acc_p, peak_p, total_p = attend(partner_queries, both, table, meta)
+    stats_p = jnp.concatenate(
+        [peak_p.reshape(local_heads, -1), total_p.reshape(local_heads, -1)], axis=0
+    )
+    acc_p = lax.ppermute(acc_p.astype(jnp.bfloat16), "xh", [(0, 1)])
+    stats_p = lax.ppermute(stats_p, "xh", [(0, 1)])
     table, meta = block_table(
         ctx * row_count, row_count, key_offset, both.shape[0],
         roles_here, sinks_here, windows_here,
     )
     own = attend(stack_heads(queries, local_heads), both, table, meta)
-    attended = merge(own, from_partner, row_count)
+    received = half == 1
+    peak_b = jnp.where(received, stats_p[:local_heads], NEGATIVE)[:, :, None]
+    total_b = jnp.where(received, stats_p[local_heads:], 0.0)[:, :, None]
+    acc_b = jnp.where(received, acc_p.astype(jnp.float32), 0.0)
+    attended = merge(own, (acc_b, peak_b, total_b), row_count)
     mixed = lax.psum_scatter(
         jnp.dot(attended, out_weight, preferred_element_type=jnp.float32).astype(jnp.bfloat16),
         "head",
@@ -209,9 +218,12 @@
 
 def solution(mesh):
     ctx_size = mesh.shape["ctx"]
-    devices = mesh.devices.reshape(2, ctx_size // 2, mesh.shape["head"])
-    split = jax.sharding.Mesh(devices, ("xh", "zy", "head"))
-    tokens = ("xh", "zy")
+    y_size = 4
+    devices = mesh.devices.reshape(
+        2, ctx_size // (2 * y_size), y_size, mesh.shape["head"]
+    )
+    split = jax.sharding.Mesh(devices, ("xh", "z", "y", "head"))
+    tokens = ("xh", "z", "y")
     in_specs = (
         P(tokens, "head"),
         P(tokens, "head"),
@@ -221,7 +233,7 @@
         P(),
         P(),
     )
-    out_specs = P(("xh", "zy", "head"), None)
+    out_specs = P(("xh", "z", "y", "head"), None)
     return jax.shard_map(
         per_device, mesh=split, in_specs=in_specs, out_specs=out_specs, check_vma=False
     )

time: 191 us -> 173 us (0.906)
  waiting for transfers between devices: 127 us -> 93.6 us
  blocking collectives: 0 us -> 13 us
  other arithmetic: 9.32 us -> 12.2 us
  starting transfers between devices: 6.76 us -> 3.93 us
    all_gather x1, waiting for transfers between devices: 69.5 us -> 46.7 us  [per_device(): both = lax.all_gather(both, 'z', axis=0, tiled=True)]
    ppermute x4 -> x3, waiting for transfers between devices: 21.8 us -> 0.01 us  [the longest x1 0.01 us: per_device(): lax.ppermute(stack_heads(queries, local_heads), 'xh', [(1, 0)])]
    all_gather x0 -> x1, blocking collectives: none -> 13 us  [per_device(): both = lax.all_gather(both, 'y', axis=0, tiled=True)]
    reduce_scatter x1, waiting for transfers between devices: 35.7 us -> 46.8 us  [per_device(): lax.psum_scatter(jnp.dot(attended, out_weight, preferred_element_type=jnp...]
    ppermute x4 -> x3, starting transfers between devices: 6.72 us -> 3.89 us  [the longest x1 1.31 us: per_device(): acc_p = lax.ppermute(acc_p.astype(jnp.bfloat16), 'xh', [(0, 1)])]
    pallas_call x0 -> x2, other arithmetic: none -> 2.51 us  [attend(): pl.pallas_call(attention_kernel, out_shape=(jax.ShapeDtypeStruct(stacked....]
  transfers between devices with their start and end apart: 6 -> 5, of which waited for: 4 -> 2; matrix products, arithmetic and copies ran while one was open for 8% -> 9% of each run, Pallas kernels for 4% -> 5%
where the time goes in v5:
time: 173 us; the launch traced here: 172 us
  waiting for transfers between devices  93.6 us (54%)
  Pallas kernels  21 us (12%)
  between operations  13.6 us (8%)
  blocking collectives  13 us (8%)
  other arithmetic  12.2 us (7%)
  local copies, waits for them, and re-layouts  9.09 us (5%)
  matrix products  5.66 us (3%)
  starting transfers between devices  3.93 us (2%)
    reduce_scatter x1, waiting for transfers between devices, per_device(): lax.psum_scatter(jnp.dot(attended, out_weight, preferred_element_type=jnp...  46.8 us
    all_gather x1, waiting for transfers between devices, per_device(): both = lax.all_gather(both, 'z', axis=0, tiled=True)  46.7 us
    pallas_call x2, Pallas kernels, attend(): pl.pallas_call(attention_kernel, out_shape=(jax.ShapeDtypeStruct(stacked....  21 us
    all_gather x1, blocking collectives, per_device(): both = lax.all_gather(both, 'y', axis=0, tiled=True)  13 us
    dot_general x1, matrix products, per_device(): jnp.dot(attended, out_weight, preferred_element_type=jnp.float32)  5.66 us
  transfers between devices with their start and end apart: 5, of which 2 were waited for; matrix products, arithmetic and copies ran while one was open for 9% of the time, Pallas kernels for 5%

profile of v5, /device:TPU:1, one launch (start us, length us, event | category | flops | bytes accessed | tf_op | source)
XLA Modules:
  0.0 172.1 jit_solution(1051608667960349407)
XLA Ops:
  6.5 0.9 pad_maximum_fusion
  7.4 13.0 %all_gather.6 = bf16[512,512]{1,0:T(8,128)(2,1)} all-gather(bf16[128,512]{1,0:T(8,128)(2,1)S(1)} %pad_maximum_fusion), channel_id=1, replica_groups=mesh['xh'=2,'z'=8,'y'=4,'head'=4] {'y'}, dimensions={0}, use_global_device_ids=true | all-gather | bytes 655360 | tf_op jit(solution)/shard_map/all_gather | solution.py:187
  20.5 1.1 reshape.104
  21.7 1.3 collective-permute-start
  23.0 0.7 dynamic_slice.11
  23.7 0.7 broadcast_compare_fusion.3
  24.5 0.7 subtract_add_fusion.1
  27.2 0.7 gather_fusion.3
  28.1 0.6 sort.31
  29.4 0.7 dynamic-slice_bitcast_fusion
  30.8 0.7 dynamic-slice_bitcast_fusion.1
  32.7 0.7 gather_fusion.1
  33.5 46.7 %all-gather.2.cloned.1.call-done.k_ref.v_ref = bf16[4096,512]{1,0:T(8,128)(2,1)} async-done(((bf16[512,512]{1,0:T(8,128)(2,1)}), bf16[4096,512]{1,0:T(8,128)(2,1)}) %all-gather.2.cloned.1.call-update) | async-done | bytes 4194320 | tf_op jit(solution)/shard_map/all_gather | solution.py:188
  80.2 13.0 %shard_map.74 = (f32[2,512,128]{2,1,0:T(8,128)}, f32[2,512,1]{2,1,0:T(8,128)}, f32[2,512,1]{2,1,0:T(8,128)}) custom-call(s32[2,16]{1,0:T(2,128)} %pad_add_fusion.3.table_ref, s32[2,8]{1,0:T(2,128)} %pad.8.meta_ref, bf16[2,512,128]{2,1,0:T(8,128)(2,1)} %copy-done.1, bf16[4096,512]{1,0:T(8,128)(2,1)} %all-gather.2.cloned.1.call-done.k_ref.v_ref, ...), custom_call_target="tpu_custom_call" | custom-call | tf_op jit(solution)/shard_map/pallas_call | solution.py:120
  93.3 1.2 reduce.1
  94.5 1.3 reduce
  95.8 1.3 collective-permute-start.1
  98.5 1.1 convert_element_type.28
  99.5 1.3 collective-permute-start.2
  100.9 8.0 %shard_map.73 = (f32[2,512,128]{2,1,0:T(8,128)}, f32[2,512,1]{2,1,0:T(8,128)}, f32[2,512,1]{2,1,0:T(8,128)}) custom-call(s32[2,16]{1,0:T(2,128)} %pad_add_fusion.2.table_ref, s32[2,8]{1,0:T(2,128)} %pad.7.meta_ref, bf16[2,512,128]{2,1,0:T(8,128)(2,1)} %bitcast.58, bf16[4096,512]{1,0:T(8,128)(2,1)} %all-gather.2.cloned.1.call-done.k_ref.v_ref, ...), custom_call_target="tpu_custom_call" | custom-call | tf_op jit(solution)/shard_map/pallas_call | solution.py:120
  109.3 1.7 fusion.3
  111.0 1.5 divide_convert_fusion
  112.7 5.7 %convolution_convert_fusion = bf16[128,4096]{1,0:T(8,128)(2,1)} fusion(bf16[128,1024]{0,1:T(8,128)(2,1)S(1)} %bitcast.56, bf16[1024,4096]{1,0:T(8,128)(2,1)} %param.14), kind=kOutput, calls=%fused_computation.4 | convolution fusion | flops 1074266112 | bytes 9699328 | tf_op jit(solution)/shard_map/dot_general | solution.py:211
  118.4 46.8 %reduce-scatter.2.cloned.1.call-done = bf16[32,4096]{1,0:T(8,128)(2,1)} async-done(((bf16[128,4096]{1,0:T(8,128)(2,1)}), bf16[32,4096]{1,0:T(8,128)(2,1)}) %reduce-scatter.2.cloned.1.call-update) | async-done | bytes 262160 | tf_op jit(solution)/shard_map/reduce_scatter | solution.py:210
  (65 shorter events, 6.9 us)
Async XLA Ops:
  6.5 73.7 %all-gather.2.cloned.1.call-start = ((), (), s32[]{:S(2)}) async-start(), calls=%async_computation.1 | async-start | bytes 4718592 | tf_op jit(solution)/shard_map/all_gather | solution.py:188
  20.4 144.8 %reduce-scatter.2.cloned.1.call-start = ((), (), s32[]{:S(2)}) async-start(), calls=%async_computation.2 | async-start | bytes 1310720 | tf_op jit(solution)/shard_map/reduce_scatter | solution.py:210
  21.6 79.2 %copy-start = (bf16[128,2,4,128]{3,0,2,1:T(8,128)(2,1)}, bf16[128,2,4,128]{3,0,2,1:T(8,128)(2,1)S(1)}, u32[]{:S(2)}) copy-start(bf16[128,2,4,128]{3,0,2,1:T(8,128)(2,1)S(1)} %copy.80) | copy-start | bytes 786436
  21.7 11.8 %collective-permute-start = (bf16[2,512,128]{2,1,0:T(8,128)(2,1)S(1)}, bf16[2,512,128]{2,1,0:T(8,128)(2,1)S(1)}, u32[]{:S(2)}, u32[]{:S(2)}) collective-permute-start(bf16[2,512,128]{2,1,0:T(8,128)(2,1)S(1)} %bitcast.57), channel_id=1, source_target_pairs={{128,0},{129,1},{130,2},{131,3},{132,4},{133,5},{134,6},{135,7},{1... | collective-permute-start | bytes 786440 | tf_op jit(solution)/shard_map/ppermute | solution.py:185
  33.5 46.7 %copy-start.1 = (bf16[2,512,128]{2,1,0:T(8,128)(2,1)}, bf16[2,512,128]{2,1,0:T(8,128)(2,1)S(1)}, u32[]{:S(2)}) copy-start(bf16[2,512,128]{2,1,0:T(8,128)(2,1)S(1)} %collective-permute-done.q_ref) | copy-start | bytes 786436
  95.8 13.0 %collective-permute-start.1 = (f32[4,512]{1,0:T(4,128)S(1)}, f32[4,512]{1,0:T(4,128)S(1)}, u32[]{:S(2)}, u32[]{:S(2)}) collective-permute-start(f32[4,512]{1,0:T(4,128)S(1)} %pad_maximum_fusion.1), channel_id=1, source_target_pairs={{0,128},{1,129},{2,130},{3,131},{4,132},{5,133},{6,134},{7,135},{8... | collective-permute-start | bytes 24584 | tf_op jit(solution)/shard_map/ppermute | solution.py:199
  99.5 11.5 %collective-permute-start.2 = (bf16[2,512,128]{2,1,0:T(8,128)(2,1)S(1)}, bf16[2,512,128]{2,1,0:T(8,128)(2,1)S(1)}, u32[]{:S(2)}, u32[]{:S(2)}) collective-permute-start(bf16[2,512,128]{2,1,0:T(8,128)(2,1)S(1)} %convert_element_type.28), channel_id=1, source_target_pairs={{0,128},{1,129},{2,130},{3,131},{4,132},{5,133},{6,134},{7,135},{8... | collective-permute-start | bytes 786440 | tf_op jit(solution)/shard_map/ppermute | solution.py:198
Sparse Core Ops, SparseCore 0:
  20.6 59.6 all-gather.1
  118.5 46.6 reduce-scatter.1

commit v6 on v5

--- a/solution.py
+++ b/solution.py
@@ -9,7 +9,7 @@
 
 HD = 128
 GROUP = 4
-KEY_BLOCK = 512
+KEY_BLOCK = 1024
 
 NEGATIVE = -1e30
 

time: 173 us -> 161 us (0.931)
  waiting for transfers between devices: 93.6 us -> 77.6 us
  Pallas kernels: 21 us -> 25 us
    reduce_scatter x1, waiting for transfers between devices: 46.8 us -> 30.7 us  [per_device(): lax.psum_scatter(jnp.dot(attended, out_weight, preferred_element_type=jnp...]
    pallas_call x2, Pallas kernels: 21 us -> 25 us  [attend(): pl.pallas_call(attention_kernel, out_shape=(jax.ShapeDtypeStruct(stacked....]
  transfers between devices with their start and end apart: 5 -> 5, of which waited for: 2 -> 2; matrix products, arithmetic and copies ran while one was open for 9% -> 10% of each run, Pallas kernels for 5% -> 5%
where the time goes in v6:
time: 161 us; the launch traced here: 160 us
  waiting for transfers between devices  77.6 us (48%)
  Pallas kernels  25 us (16%)
  between operations  13.6 us (8%)
  blocking collectives  13 us (8%)
  other arithmetic  12.1 us (8%)
  local copies, waits for them, and re-layouts  9.11 us (6%)
  matrix products  5.66 us (4%)
  starting transfers between devices  3.93 us (2%)
    all_gather x1, waiting for transfers between devices, per_device(): both = lax.all_gather(both, 'z', axis=0, tiled=True)  46.9 us
    reduce_scatter x1, waiting for transfers between devices, per_device(): lax.psum_scatter(jnp.dot(attended, out_weight, preferred_element_type=jnp...  30.7 us
    pallas_call x2, Pallas kernels, attend(): pl.pallas_call(attention_kernel, out_shape=(jax.ShapeDtypeStruct(stacked....  25 us
    all_gather x1, blocking collectives, per_device(): both = lax.all_gather(both, 'y', axis=0, tiled=True)  13 us
    dot_general x1, matrix products, per_device(): jnp.dot(attended, out_weight, preferred_element_type=jnp.float32)  5.66 us
  transfers between devices with their start and end apart: 5, of which 2 were waited for; matrix products, arithmetic and copies ran while one was open for 10% of the time, Pallas kernels for 5%

profile of v6, /device:TPU:1, one launch (start us, length us, event | category | flops | bytes accessed | tf_op | source)
XLA Modules:
  0.0 159.9 jit_solution(16449192827030326545)
XLA Ops:
  6.5 0.9 pad_maximum_fusion
  7.4 13.0 %all_gather.6 = bf16[512,512]{1,0:T(8,128)(2,1)} all-gather(bf16[128,512]{1,0:T(8,128)(2,1)S(1)} %pad_maximum_fusion), channel_id=1, replica_groups=mesh['xh'=2,'z'=8,'y'=4,'head'=4] {'y'}, dimensions={0}, use_global_device_ids=true | all-gather | bytes 655360 | tf_op jit(solution)/shard_map/all_gather | solution.py:187
  20.5 1.1 reshape.104
  21.7 1.3 collective-permute-start
  23.0 0.7 dynamic_slice.11
  23.7 0.7 broadcast_compare_fusion.3
  24.5 0.7 subtract_add_fusion.1
  26.3 0.6 gather_fusion.2
  27.1 0.7 gather_fusion.3
  29.3 0.7 dynamic-slice_bitcast_fusion
  30.7 0.7 dynamic-slice_bitcast_fusion.1
  32.6 0.7 gather_fusion.1
  33.4 46.9 %all-gather.2.cloned.1.call-done.k_ref.v_ref = bf16[4096,512]{1,0:T(8,128)(2,1)} async-done(((bf16[512,512]{1,0:T(8,128)(2,1)}), bf16[4096,512]{1,0:T(8,128)(2,1)}) %all-gather.2.cloned.1.call-update) | async-done | bytes 4194320 | tf_op jit(solution)/shard_map/all_gather | solution.py:188
  80.3 16.2 %shard_map.74 = (f32[2,512,128]{2,1,0:T(8,128)}, f32[2,512,1]{2,1,0:T(8,128)}, f32[2,512,1]{2,1,0:T(8,128)}) custom-call(s32[2,8]{1,0:T(2,128)} %pad_add_fusion.3.table_ref, s32[2,8]{1,0:T(2,128)} %pad.8.meta_ref, bf16[2,512,128]{2,1,0:T(8,128)(2,1)} %copy-done.1, bf16[4096,512]{1,0:T(8,128)(2,1)} %all-gather.2.cloned.1.call-done.k_ref.v_ref, ...), custom_call_target="tpu_custom_call" | custom-call | tf_op jit(solution)/shard_map/pallas_call | solution.py:120
  96.5 1.2 reduce.1
  97.7 1.3 reduce
  99.0 1.3 collective-permute-start.1
  101.7 1.1 convert_element_type.28
  102.7 1.3 collective-permute-start.2
  104.1 8.8 %shard_map.73 = (f32[2,512,128]{2,1,0:T(8,128)}, f32[2,512,1]{2,1,0:T(8,128)}, f32[2,512,1]{2,1,0:T(8,128)}) custom-call(s32[2,8]{1,0:T(2,128)} %pad_add_fusion.2.table_ref, s32[2,8]{1,0:T(2,128)} %pad.7.meta_ref, bf16[2,512,128]{2,1,0:T(8,128)(2,1)} %bitcast.58, bf16[4096,512]{1,0:T(8,128)(2,1)} %all-gather.2.cloned.1.call-done.k_ref.v_ref, ...), custom_call_target="tpu_custom_call" | custom-call | tf_op jit(solution)/shard_map/pallas_call | solution.py:120
  113.3 1.7 %fusion.3 = (f32[2,512]{1,0:T(2,128)S(1)}, f32[2,512]{1,0:T(2,128)S(1)}, f32[2,512]{1,0:T(2,128)S(1)}) fusion(f32[2,512,1]{2,1,0:T(8,128)} %get-tuple-element.17, f32[2,512,1]{2,1,0:T(8,128)S(1)} %copy.90, f32[2,512,1]{2,1,0:T(8,128)S(1)} %copy.92, f32[2,512,1]{2,1,0:T(8,128)} %get-tuple-element.22), kind=kLoop, calls=%fused_computation.12 | loop fusion | flops 6144 | bytes 28672 | tf_op jit(solution)/shard_map/exp | solution.py:160
  115.0 1.5 divide_convert_fusion
  116.7 5.7 %convolution_convert_fusion = bf16[128,4096]{1,0:T(8,128)(2,1)} fusion(bf16[128,1024]{0,1:T(8,128)(2,1)S(1)} %bitcast.56, bf16[1024,4096]{1,0:T(8,128)(2,1)} %param.14), kind=kOutput, calls=%fused_computation.4 | convolution fusion | flops 1074266112 | bytes 9699328 | tf_op jit(solution)/shard_map/dot_general | solution.py:211
  122.4 30.7 %reduce-scatter.2.cloned.1.call-done = bf16[32,4096]{1,0:T(8,128)(2,1)} async-done(((bf16[128,4096]{1,0:T(8,128)(2,1)}), bf16[32,4096]{1,0:T(8,128)(2,1)}) %reduce-scatter.2.cloned.1.call-update) | async-done | bytes 262160 | tf_op jit(solution)/shard_map/reduce_scatter | solution.py:210
  (65 shorter events, 6.9 us)
Async XLA Ops:
  6.5 73.7 %all-gather.2.cloned.1.call-start = ((), (), s32[]{:S(2)}) async-start(), calls=%async_computation.1 | async-start | bytes 4718592 | tf_op jit(solution)/shard_map/all_gather | solution.py:188
  20.4 132.6 %reduce-scatter.2.cloned.1.call-start = ((), (), s32[]{:S(2)}) async-start(), calls=%async_computation.2 | async-start | bytes 1310720 | tf_op jit(solution)/shard_map/reduce_scatter | solution.py:210
  21.6 82.4 %copy-start = (bf16[128,2,4,128]{3,0,2,1:T(8,128)(2,1)}, bf16[128,2,4,128]{3,0,2,1:T(8,128)(2,1)S(1)}, u32[]{:S(2)}) copy-start(bf16[128,2,4,128]{3,0,2,1:T(8,128)(2,1)S(1)} %copy.80) | copy-start | bytes 786436
  21.7 11.7 %collective-permute-start = (bf16[2,512,128]{2,1,0:T(8,128)(2,1)S(1)}, bf16[2,512,128]{2,1,0:T(8,128)(2,1)S(1)}, u32[]{:S(2)}, u32[]{:S(2)}) collective-permute-start(bf16[2,512,128]{2,1,0:T(8,128)(2,1)S(1)} %bitcast.57), channel_id=1, source_target_pairs={{128,0},{129,1},{130,2},{131,3},{132,4},{133,5},{134,6},{135,7},{1... | collective-permute-start | bytes 786440 | tf_op jit(solution)/shard_map/ppermute | solution.py:185
  33.4 46.9 %copy-start.1 = (bf16[2,512,128]{2,1,0:T(8,128)(2,1)}, bf16[2,512,128]{2,1,0:T(8,128)(2,1)S(1)}, u32[]{:S(2)}) copy-start(bf16[2,512,128]{2,1,0:T(8,128)(2,1)S(1)} %collective-permute-done.q_ref) | copy-start | bytes 786436
  99.0 13.8 %collective-permute-start.1 = (f32[4,512]{1,0:T(4,128)S(1)}, f32[4,512]{1,0:T(4,128)S(1)}, u32[]{:S(2)}, u32[]{:S(2)}) collective-permute-start(f32[4,512]{1,0:T(4,128)S(1)} %pad_maximum_fusion.1), channel_id=1, source_target_pairs={{0,128},{1,129},{2,130},{3,131},{4,132},{5,133},{6,134},{7,135},{8... | collective-permute-start | bytes 24584 | tf_op jit(solution)/shard_map/ppermute | solution.py:199
  102.7 12.3 %collective-permute-start.2 = (bf16[2,512,128]{2,1,0:T(8,128)(2,1)S(1)}, bf16[2,512,128]{2,1,0:T(8,128)(2,1)S(1)}, u32[]{:S(2)}, u32[]{:S(2)}) collective-permute-start(bf16[2,512,128]{2,1,0:T(8,128)(2,1)S(1)} %convert_element_type.28), channel_id=1, source_target_pairs={{0,128},{1,129},{2,130},{3,131},{4,132},{5,133},{6,134},{7,135},{8... | collective-permute-start | bytes 786440 | tf_op jit(solution)/shard_map/ppermute | solution.py:198
Sparse Core Ops, SparseCore 0:
  20.6 59.6 all-gather.1
  122.5 30.5 reduce-scatter.1

commit v7 on v6

--- a/solution.py
+++ b/solution.py
@@ -170,6 +170,35 @@
     )
 
 
+def gather_ring(block, axis):
+    size = lax.axis_size(axis)
+    here = lax.axis_index(axis)
+    pieces = [block]
+    for shift in range(1, size):
+        pieces.append(
+            lax.ppermute(block, axis, [(i, (i + shift) % size) for i in range(size)])
+        )
+    stacked = jnp.stack(pieces)
+    order = (here - jnp.arange(size, dtype=jnp.int32)) % size
+    return jnp.take(stacked, order, axis=0).reshape(size * block.shape[0], block.shape[1])
+
+
+def scatter_sum(partial):
+    rows, width = partial.shape
+    quarter = rows // 4
+    parts = partial.reshape(2, 2, quarter, width)
+    core = lax.axis_index("core")
+    keep = jnp.take(parts, core, axis=1)
+    give = jnp.take(parts, 1 - core, axis=1)
+    got = lax.ppermute(give.astype(jnp.bfloat16), "core", [(0, 1), (1, 0)])
+    summed = keep + got.astype(jnp.float32)
+    xl = lax.axis_index("xl")
+    keep = jnp.take(summed, xl, axis=0)
+    give = jnp.take(summed, 1 - xl, axis=0)
+    got = lax.ppermute(give.astype(jnp.bfloat16), "xl", [(0, 1), (1, 0)])
+    return (keep + got.astype(jnp.float32)).astype(jnp.bfloat16)
+
+
 def per_device(queries, key_states, value_states, out_weight, head_role, sink_len, window_len):
     row_count = queries.shape[0]
     local_heads = key_states.shape[1] // HD
@@ -178,13 +207,14 @@
     place = lax.axis_index("z") * lax.axis_size("y") + lax.axis_index("y")
     ctx = half * half_size + place
     partner = (1 - half) * half_size + place
-    first_head = lax.axis_index("head") * local_heads
+    head_index = lax.axis_index("xl") * lax.axis_size("core") + lax.axis_index("core")
+    first_head = head_index * local_heads
     roles_here = lax.dynamic_slice_in_dim(head_role, first_head, local_heads)
     sinks_here = lax.dynamic_slice_in_dim(sink_len, first_head, local_heads)
     windows_here = lax.dynamic_slice_in_dim(window_len, first_head, local_heads)
     partner_queries = lax.ppermute(stack_heads(queries, local_heads), "xh", [(1, 0)])
     both = jnp.concatenate([key_states, value_states], axis=1)
-    both = lax.all_gather(both, "y", axis=0, tiled=True)
+    both = gather_ring(both, "y")
     both = lax.all_gather(both, "z", axis=0, tiled=True)
     key_offset = half * both.shape[0]
     table, meta = block_table(
@@ -207,33 +237,27 @@
     total_b = jnp.where(received, stats_p[local_heads:], 0.0)[:, :, None]
     acc_b = jnp.where(received, acc_p.astype(jnp.float32), 0.0)
     attended = merge(own, (acc_b, peak_b, total_b), row_count)
-    mixed = lax.psum_scatter(
-        jnp.dot(attended, out_weight, preferred_element_type=jnp.float32).astype(jnp.bfloat16),
-        "head",
-        scatter_dimension=0,
-        tiled=True,
-    )
-    return mixed
+    partial = jnp.dot(attended, out_weight, preferred_element_type=jnp.float32)
+    return scatter_sum(partial)
 
 
 def solution(mesh):
     ctx_size = mesh.shape["ctx"]
     y_size = 4
-    devices = mesh.devices.reshape(
-        2, ctx_size // (2 * y_size), y_size, mesh.shape["head"]
-    )
-    split = jax.sharding.Mesh(devices, ("xh", "z", "y", "head"))
+    devices = mesh.devices.reshape(2, ctx_size // (2 * y_size), y_size, 2, mesh.shape["head"] // 2)
+    split = jax.sharding.Mesh(devices, ("xh", "z", "y", "xl", "core"))
     tokens = ("xh", "z", "y")
+    heads = ("xl", "core")
     in_specs = (
-        P(tokens, "head"),
-        P(tokens, "head"),
-        P(tokens, "head"),
-        P("head", None),
+        P(tokens, heads),
+        P(tokens, heads),
+        P(tokens, heads),
+        P(heads, None),
         P(),
         P(),
         P(),
     )
-    out_specs = P(("xh", "z", "y", "head"), None)
+    out_specs = P(("xh", "z", "y", "xl", "core"), None)
     return jax.shard_map(
         per_device, mesh=split, in_specs=in_specs, out_specs=out_specs, check_vma=False
     )

time: 161 us -> 143 us (0.89)
  the two profiles are of different devices: /device:TPU:1 before, /device:TPU:192 now
where the time goes in v7:
time: 143 us; the launch traced here: 142 us
  waiting for transfers between devices  58.1 us (41%)
  Pallas kernels  32.5 us (23%)
  between operations  13.7 us (10%)
  other arithmetic  13 us (9%)
  starting transfers between devices  10.3 us (7%)
  local copies, waits for them, and re-layouts  9.74 us (7%)
  matrix products  4.64 us (3%)
    all_gather x1, waiting for transfers between devices, per_device(): both = lax.all_gather(both, 'z', axis=0, tiled=True)  38.6 us
    pallas_call x2, Pallas kernels, attend(): pl.pallas_call(attention_kernel, out_shape=(jax.ShapeDtypeStruct(stacked....  32.5 us
    ppermute x3, waiting for transfers between devices, gather_ring(): lax.ppermute(block, axis, [(i, (i + shift) % size) for i in range(size)])  7.55 us
    ppermute x1, waiting for transfers between devices, scatter_sum(): got = lax.ppermute(give.astype(jnp.bfloat16), 'xl', [(0, 1), (1, 0)])  6.87 us
    dot_general x1, matrix products, per_device(): partial = jnp.dot(attended, out_weight, preferred_element_type=jnp.float32)  4.64 us
    ppermute x3, starting transfers between devices, gather_ring(): lax.ppermute(block, axis, [(i, (i + shift) % size) for i in range(size)])  4.61 us
    ppermute x1, waiting for transfers between devices, per_device(): lax.ppermute(stack_heads(queries, local_heads), 'xh', [(1, 0)])  3.05 us
  transfers between devices with their start and end apart: 9, of which 7 were waited for; matrix products, arithmetic and copies ran while one was open for 9% of the time, Pallas kernels for 13%

profile of v7, /device:TPU:192, one launch (start us, length us, event | category | flops | bytes accessed | tf_op | source)
XLA Modules:
  0.0 141.9 jit_solution(2875664193408806190)
XLA Ops:
  8.3 3.0 %collective-permute-start.2 = (bf16[128,512]{1,0:T(8,128)(2,1)S(1)}, bf16[128,512]{1,0:T(8,128)(2,1)S(1)}, u32[]{:S(2)}, u32[]{:S(2)}) collective-permute-start(bf16[128,512]{1,0:T(8,128)(2,1)S(1)} %constant_dynamic-update-slice_fusion), channel_id=1, source_target_pairs={{0,12},{4,0},{8,4},{12,8},{1,13},{5,1},{9,5},{13,9},{2,14},{6,2},{... | collective-permute-start | bytes 393224 | tf_op jit(solution)/shard_map/ppermute | solution.py:179
  11.9 1.0 collective-permute-start
  13.0 3.8 %collective-permute-done.2 = bf16[128,512]{1,0:T(8,128)(2,1)S(1)} collective-permute-done((bf16[128,512]{1,0:T(8,128)(2,1)S(1)}, bf16[128,512]{1,0:T(8,128)(2,1)S(1)}, u32[]{:S(2)}, u32[]{:S(2)}) %collective-permute-start.2) | collective-permute-done | bytes 131104 | tf_op jit(solution)/shard_map/ppermute | solution.py:179
  16.9 2.3 %collective-permute-done.1 = bf16[128,512]{1,0:T(8,128)(2,1)S(1)} collective-permute-done((bf16[128,512]{1,0:T(8,128)(2,1)S(1)}, bf16[128,512]{1,0:T(8,128)(2,1)S(1)}, u32[]{:S(2)}, u32[]{:S(2)}) %collective-permute-start.1) | collective-permute-done | bytes 131104 | tf_op jit(solution)/shard_map/ppermute | solution.py:179
  19.2 1.4 collective-permute-done
  21.2 0.9 bitcast_select_fusion.1
  22.2 1.1 reshape.164
  23.4 1.3 collective-permute-start.3
  31.8 3.0 %collective-permute-done.3.q_ref = bf16[2,512,128]{2,1,0:T(8,128)(2,1)S(1)} collective-permute-done((bf16[2,512,128]{2,1,0:T(8,128)(2,1)S(1)}, bf16[2,512,128]{2,1,0:T(8,128)(2,1)S(1)}, u32[]{:S(2)}, u32[]{:S(2)}) %collective-permute-start.3) | collective-permute-done | bytes 262176 | tf_op jit(solution)/shard_map/ppermute | solution.py:215
  34.9 38.6 %all-gather.2.cloned.1.call-done.k_ref.v_ref = bf16[4096,512]{1,0:T(8,128)(2,1)} async-done(((bf16[512,512]{1,0:T(8,128)(2,1)}), bf16[4096,512]{1,0:T(8,128)(2,1)}) %all-gather.2.cloned.1.call-update) | async-done | bytes 4194320 | tf_op jit(solution)/shard_map/all_gather | solution.py:218
  73.4 14.2 %shard_map.74 = (f32[2,512,128]{2,1,0:T(8,128)}, f32[2,512,1]{2,1,0:T(8,128)}, f32[2,512,1]{2,1,0:T(8,128)}) custom-call(s32[2,8]{1,0:T(2,128)} %pad_add_fusion.3.table_ref, s32[2,8]{1,0:T(2,128)} %pad.8.meta_ref, bf16[2,512,128]{2,1,0:T(8,128)(2,1)} %copy-done.1, bf16[4096,512]{1,0:T(8,128)(2,1)} %all-gather.2.cloned.1.call-done.k_ref.v_ref, ...), custom_call_target="tpu_custom_call" | custom-call | tf_op jit(solution)/shard_map/pallas_call | solution.py:120
  87.7 1.2 reduce.1
  88.9 1.3 reduce
  90.2 1.3 collective-permute-start.4
  92.8 1.1 convert_element_type.40
  93.9 1.5 %collective-permute-start.5 = (bf16[2,512,128]{2,1,0:T(8,128)(2,1)S(1)}, bf16[2,512,128]{2,1,0:T(8,128)(2,1)S(1)}, u32[]{:S(2)}, u32[]{:S(2)}) collective-permute-start(bf16[2,512,128]{2,1,0:T(8,128)(2,1)S(1)} %convert_element_type.40), channel_id=1, source_target_pairs={{0,128},{1,129},{2,130},{3,131},{4,132},{5,133},{6,134},{7,135},{8... | collective-permute-start | bytes 786440 | tf_op jit(solution)/shard_map/ppermute | solution.py:228
  95.4 18.3 %shard_map.73 = (f32[2,512,128]{2,1,0:T(8,128)}, f32[2,512,1]{2,1,0:T(8,128)}, f32[2,512,1]{2,1,0:T(8,128)}) custom-call(s32[2,8]{1,0:T(2,128)} %pad_add_fusion.2.table_ref, s32[2,8]{1,0:T(2,128)} %pad.7.meta_ref, bf16[2,512,128]{2,1,0:T(8,128)(2,1)} %bitcast.88, bf16[4096,512]{1,0:T(8,128)(2,1)} %all-gather.2.cloned.1.call-done.k_ref.v_ref, ...), custom_call_target="tpu_custom_call" | custom-call | tf_op jit(solution)/shard_map/pallas_call | solution.py:120
  114.2 1.7 %fusion.8 = (f32[2,512]{1,0:T(2,128)S(1)}, f32[2,512]{1,0:T(2,128)S(1)}, f32[2,512]{1,0:T(2,128)S(1)}) fusion(f32[2,512,1]{2,1,0:T(8,128)} %get-tuple-element.19, f32[2,512,1]{2,1,0:T(8,128)S(1)} %copy.94, f32[2,512,1]{2,1,0:T(8,128)S(1)} %copy.96, f32[2,512,1]{2,1,0:T(8,128)} %get-tuple-element.24), kind=kLoop, calls=%fused_computation.23 | loop fusion | flops 6144 | bytes 28672 | tf_op jit(solution)/shard_map/exp | solution.py:160
  115.9 1.5 %divide_convert_fusion = bf16[2,512,128]{2,1,0:T(8,128)(2,1)S(1)} fusion(bf16[2,512,128]{2,1,0:T(8,128)(2,1)S(1)} %collective-permute-done.5, f32[2,512,128]{2,1,0:T(8,128)} %get-tuple-element.18, f32[2,512]{1,0:T(2,128)S(1)} %get-tuple-element.48, f32[2,512]{1,0:T(2,128)S(1)} %get-tuple-element.49, f32[2,512]{1,0:T(2,128)S(1)} %get-tuple-element.47, pred[]{:T(512)S(6)} %eq.11), kind=kLoop, calls=%fused_computation.20 | loop fusion | flops 917504 | bytes 1060865 | tf_op jit(solution)/shard_map/convert_element_type | solution.py:165
  117.8 4.6 %fusion = f32[2,2,32,4096]{3,2,1,0:T(8,128)S(1)} fusion(bf16[2,2,32,1024]{3,2,1,0:T(8,128)(2,1)S(1)} %dot_general.5, bf16[1024,4096]{1,0:T(8,128)(2,1)} %param.18), kind=kOutput, calls=%fused_computation.5 | convolution fusion | flops 1073741824 | bytes 10747904 | tf_op jit(solution)/shard_map/dot_general | solution.py:240
  122.7 2.0 %collective-permute-done.6 = bf16[2,32,4096]{2,1,0:T(8,128)(2,1)} collective-permute-done((bf16[2,32,4096]{2,1,0:T(8,128)(2,1)S(1)}, bf16[2,32,4096]{2,1,0:T(8,128)(2,1)}, u32[]{:S(2)}, u32[]{:S(2)}) %collective-permute-start.6) | collective-permute-done | bytes 524320 | tf_op jit(solution)/shard_map/ppermute | solution.py:193
  124.7 1.1 fusion.3
  125.9 1.6 %collective-permute-start.7 = (bf16[32,4096]{1,0:T(8,128)(2,1)S(1)}, bf16[32,4096]{1,0:T(8,128)(2,1)S(1)}, u32[]{:S(2)}, u32[]{:S(2)}) collective-permute-start(bf16[32,4096]{1,0:T(8,128)(2,1)S(1)} %bitcast_convert_fusion.1), channel_id=1, source_target_pairs={{0,2},{2,0},{1,3},{3,1},{4,6},{6,4},{5,7},{7,5},{8,10},{10,8},{9,1... | collective-permute-start | bytes 786440 | tf_op jit(solution)/shard_map/ppermute | solution.py:198
  127.5 6.9 %collective-permute-done.7 = bf16[32,4096]{1,0:T(8,128)(2,1)S(1)} collective-permute-done((bf16[32,4096]{1,0:T(8,128)(2,1)S(1)}, bf16[32,4096]{1,0:T(8,128)(2,1)S(1)}, u32[]{:S(2)}, u32[]{:S(2)}) %collective-permute-start.7) | collective-permute-done | bytes 262176 | tf_op jit(solution)/shard_map/ppermute | solution.py:198
  (90 shorter events, 13.4 us)
Async XLA Ops:
  6.5 18.1 %copy-start.4 = (s32[8]{0:T(128)S(1)}, s32[8]{0:T(128)}, u32[]{:S(2)}) copy-start(s32[8]{0:T(128)} %param.20) | copy-start | bytes 100
  6.5 18.2 %copy-start.3 = (s32[8]{0:T(128)S(1)}, s32[8]{0:T(128)}, u32[]{:S(2)}) copy-start(s32[8]{0:T(128)} %param.19) | copy-start | bytes 100
  6.5 18.4 %copy-start.2 = (s32[8]{0:T(128)S(1)}, s32[8]{0:T(128)}, u32[]{:S(2)}) copy-start(s32[8]{0:T(128)} %param.21) | copy-start | bytes 100
  6.5 66.9 %all-gather.2.cloned.1.call-start = ((), (), s32[]{:S(2)}) async-start(), calls=%async_computation | async-start | bytes 4718592 | tf_op jit(solution)/shard_map/all_gather | solution.py:218
  8.3 8.6 %collective-permute-start.2 = (bf16[128,512]{1,0:T(8,128)(2,1)S(1)}, bf16[128,512]{1,0:T(8,128)(2,1)S(1)}, u32[]{:S(2)}, u32[]{:S(2)}) collective-permute-start(bf16[128,512]{1,0:T(8,128)(2,1)S(1)} %constant_dynamic-update-slice_fusion), channel_id=1, source_target_pairs={{0,12},{4,0},{8,4},{12,8},{1,13},{5,1},{9,5},{13,9},{2,14},{6,2},{... | collective-permute-start | bytes 393224 | tf_op jit(solution)/shard_map/ppermute | solution.py:179
  11.3 7.9 %collective-permute-start.1 = (bf16[128,512]{1,0:T(8,128)(2,1)S(1)}, bf16[128,512]{1,0:T(8,128)(2,1)S(1)}, u32[]{:S(2)}, u32[]{:S(2)}) collective-permute-start(bf16[128,512]{1,0:T(8,128)(2,1)S(1)} %constant_dynamic-update-slice_fusion), channel_id=1, source_target_pairs={{0,8},{4,12},{8,0},{12,4},{1,9},{5,13},{9,1},{13,5},{2,10},{6,14},... | collective-permute-start | bytes 393224 | tf_op jit(solution)/shard_map/ppermute | solution.py:179
  11.9 8.6 %collective-permute-start = (bf16[128,512]{1,0:T(8,128)(2,1)S(1)}, bf16[128,512]{1,0:T(8,128)(2,1)S(1)}, u32[]{:S(2)}, u32[]{:S(2)}) collective-permute-start(bf16[128,512]{1,0:T(8,128)(2,1)S(1)} %constant_dynamic-update-slice_fusion), channel_id=1, source_target_pairs={{0,4},{4,8},{8,12},{12,0},{1,5},{5,9},{9,13},{13,1},{2,6},{6,10},{... | collective-permute-start | bytes 393224 | tf_op jit(solution)/shard_map/ppermute | solution.py:179
  23.3 64.3 %copy-start = (bf16[128,2,4,128]{3,0,2,1:T(8,128)(2,1)}, bf16[128,2,4,128]{3,0,2,1:T(8,128)(2,1)S(1)}, u32[]{:S(2)}) copy-start(bf16[128,2,4,128]{3,0,2,1:T(8,128)(2,1)S(1)} %copy.84) | copy-start | bytes 786436
  23.4 11.5 %collective-permute-start.3 = (bf16[2,512,128]{2,1,0:T(8,128)(2,1)S(1)}, bf16[2,512,128]{2,1,0:T(8,128)(2,1)S(1)}, u32[]{:S(2)}, u32[]{:S(2)}) collective-permute-start(bf16[2,512,128]{2,1,0:T(8,128)(2,1)S(1)} %bitcast.87), channel_id=1, source_target_pairs={{128,0},{129,1},{130,2},{131,3},{132,4},{133,5},{134,6},{135,7},{1... | collective-permute-start | bytes 786440 | tf_op jit(solution)/shard_map/ppermute | solution.py:215
  34.9 38.6 %copy-start.1 = (bf16[2,512,128]{2,1,0:T(8,128)(2,1)}, bf16[2,512,128]{2,1,0:T(8,128)(2,1)S(1)}, u32[]{:S(2)}) copy-start(bf16[2,512,128]{2,1,0:T(8,128)(2,1)S(1)} %collective-permute-done.3.q_ref) | copy-start | bytes 786436
  90.2 23.6 %collective-permute-start.4 = (f32[4,512]{1,0:T(4,128)S(1)}, f32[4,512]{1,0:T(4,128)S(1)}, u32[]{:S(2)}, u32[]{:S(2)}) collective-permute-start(f32[4,512]{1,0:T(4,128)S(1)} %pad_maximum_fusion.1), channel_id=1, source_target_pairs={{0,128},{1,129},{2,130},{3,131},{4,132},{5,133},{6,134},{7,135},{8... | collective-permute-start | bytes 24584 | tf_op jit(solution)/shard_map/ppermute | solution.py:229
  93.9 22.0 %collective-permute-start.5 = (bf16[2,512,128]{2,1,0:T(8,128)(2,1)S(1)}, bf16[2,512,128]{2,1,0:T(8,128)(2,1)S(1)}, u32[]{:S(2)}, u32[]{:S(2)}) collective-permute-start(bf16[2,512,128]{2,1,0:T(8,128)(2,1)S(1)} %convert_element_type.40), channel_id=1, source_target_pairs={{0,128},{1,129},{2,130},{3,131},{4,132},{5,133},{6,134},{7,135},{8... | collective-permute-start | bytes 786440 | tf_op jit(solution)/shard_map/ppermute | solution.py:228
  122.6 2.1 %collective-permute-start.6 = (bf16[2,32,4096]{2,1,0:T(8,128)(2,1)S(1)}, bf16[2,32,4096]{2,1,0:T(8,128)(2,1)}, u32[]{:S(2)}, u32[]{:S(2)}) collective-permute-start(bf16[2,32,4096]{2,1,0:T(8,128)(2,1)S(1)} %bitcast_convert_fusion), channel_id=1, source_target_pairs={{0,1},{1,0},{2,3},{3,2},{4,5},{5,4},{6,7},{7,6},{8,9},{9,8},{10,11... | collective-permute-start | bytes 1572872 | tf_op jit(solution)/shard_map/ppermute | solution.py:193
  125.9 8.4 %collective-permute-start.7 = (bf16[32,4096]{1,0:T(8,128)(2,1)S(1)}, bf16[32,4096]{1,0:T(8,128)(2,1)S(1)}, u32[]{:S(2)}, u32[]{:S(2)}) collective-permute-start(bf16[32,4096]{1,0:T(8,128)(2,1)S(1)} %bitcast_convert_fusion.1), channel_id=1, source_target_pairs={{0,2},{2,0},{1,3},{3,1},{4,6},{6,4},{5,7},{7,5},{8,10},{10,8},{9,1... | collective-permute-start | bytes 786440 | tf_op jit(solution)/shard_map/ppermute | solution.py:198
Sparse Core Ops, SparseCore 0:
  22.3 51.0 all-gather.1

commit v8 on v7

--- a/solution.py
+++ b/solution.py
@@ -215,23 +215,42 @@
     partner_queries = lax.ppermute(stack_heads(queries, local_heads), "xh", [(1, 0)])
     both = jnp.concatenate([key_states, value_states], axis=1)
     both = gather_ring(both, "y")
-    both = lax.all_gather(both, "z", axis=0, tiled=True)
-    key_offset = half * both.shape[0]
-    table, meta = block_table(
-        partner * row_count, row_count, key_offset, both.shape[0],
+    per_head = [
+        lax.all_gather(
+            jnp.concatenate(
+                [both[:, g * HD:(g + 1) * HD], both[:, (local_heads + g) * HD:(local_heads + g + 1) * HD]],
+                axis=1,
+            ),
+            "z",
+            axis=0,
+            tiled=True,
+        )
+        for g in range(local_heads)
+    ]
+    key_count = per_head[0].shape[0]
+    key_offset = half * key_count
+    table_p, meta_p = block_table(
+        partner * row_count, row_count, key_offset, key_count,
         roles_here, sinks_here, windows_here,
     )
-    acc_p, peak_p, total_p = attend(partner_queries, both, table, meta)
+    table_o, meta_o = block_table(
+        ctx * row_count, row_count, key_offset, key_count,
+        roles_here, sinks_here, windows_here,
+    )
+    own_queries = stack_heads(queries, local_heads)
+    for_partner = []
+    own_parts = []
+    for g in range(local_heads):
+        one = slice(g, g + 1)
+        for_partner.append(attend(partner_queries[one], per_head[g], table_p[one], meta_p[one]))
+        own_parts.append(attend(own_queries[one], per_head[g], table_o[one], meta_o[one]))
+    acc_p, peak_p, total_p = (jnp.concatenate(x, axis=0) for x in zip(*for_partner))
+    own = tuple(jnp.concatenate(x, axis=0) for x in zip(*own_parts))
     stats_p = jnp.concatenate(
         [peak_p.reshape(local_heads, -1), total_p.reshape(local_heads, -1)], axis=0
     )
     acc_p = lax.ppermute(acc_p.astype(jnp.bfloat16), "xh", [(0, 1)])
     stats_p = lax.ppermute(stats_p, "xh", [(0, 1)])
-    table, meta = block_table(
-        ctx * row_count, row_count, key_offset, both.shape[0],
-        roles_here, sinks_here, windows_here,
-    )
-    own = attend(stack_heads(queries, local_heads), both, table, meta)
     received = half == 1
     peak_b = jnp.where(received, stats_p[:local_heads], NEGATIVE)[:, :, None]
     total_b = jnp.where(received, stats_p[local_heads:], 0.0)[:, :, None]

time: 143 us -> 169 us (1.18)
  the two profiles are of different devices: /device:TPU:192 before, /device:TPU:226 now
where the time goes in v8:
time: 169 us
  waiting for transfers between devices  78.3 us (46%)
  Pallas kernels  34.8 us (21%)
  local copies, waits for them, and re-layouts  14.4 us (9%)
  between operations  13.8 us (8%)
  other arithmetic  12.6 us (7%)
  starting transfers between devices  10.1 us (6%)
  matrix products  4.64 us (3%)
    all_gather x2, waiting for transfers between devices, per_device(): lax.all_gather(jnp.concatenate([both[:, g * HD:(g + 1) * HD], both[:, (lo...  63.3 us
    pallas_call x4, Pallas kernels, attend(): pl.pallas_call(attention_kernel, out_shape=(jax.ShapeDtypeStruct(stacked....  34.8 us
    ppermute x1, waiting for transfers between devices, scatter_sum(): got = lax.ppermute(give.astype(jnp.bfloat16), 'xl', [(0, 1), (1, 0)])  8.33 us
    ppermute x3, starting transfers between devices, gather_ring(): lax.ppermute(block, axis, [(i, (i + shift) % size) for i in range(size)])  5.83 us
    dot_general x1, matrix products, per_device(): partial = jnp.dot(attended, out_weight, preferred_element_type=jnp.float32)  4.64 us
    ppermute x3, waiting for transfers between devices, gather_ring(): lax.ppermute(block, axis, [(i, (i + shift) % size) for i in range(size)])  4.56 us
    pallas_call x4, other arithmetic, attend(): pl.pallas_call(attention_kernel, out_shape=(jax.ShapeDtypeStruct(stacked....  4.38 us
  transfers between devices with their start and end apart: 10, of which 6 were waited for; matrix products, arithmetic and copies ran while one was open for 10% of the time, Pallas kernels for 14%

profile of v8, /device:TPU:226, one launch (start us, length us, event | category | flops | bytes accessed | tf_op | source)
XLA Modules:
  0.0 168.6 jit_solution(12375730833844691116)
XLA Ops:
  8.2 1.6 collective-permute-start
  9.8 2.9 %collective-permute-start.1 = (bf16[128,512]{1,0:T(8,128)(2,1)S(1)}, bf16[128,512]{1,0:T(8,128)(2,1)S(1)}, u32[]{:S(2)}, u32[]{:S(2)}) collective-permute-start(bf16[128,512]{1,0:T(8,128)(2,1)S(1)} %constant_dynamic-update-slice_fusion), channel_id=1, source_target_pairs={{0,8},{4,12},{8,0},{12,4},{1,9},{5,13},{9,1},{13,5},{2,10},{6,14},... | collective-permute-start | bytes 393224 | tf_op jit(solution)/shard_map/ppermute | solution.py:179
  12.7 1.3 collective-permute-start.2
  14.7 4.0 %collective-permute-done.1 = bf16[128,512]{1,0:T(8,128)(2,1)S(1)} collective-permute-done((bf16[128,512]{1,0:T(8,128)(2,1)S(1)}, bf16[128,512]{1,0:T(8,128)(2,1)S(1)}, u32[]{:S(2)}, u32[]{:S(2)}) %collective-permute-start.1) | collective-permute-done | bytes 131104 | tf_op jit(solution)/shard_map/ppermute | solution.py:179
  20.7 1.3 collective-permute-start.3
  32.3 27.8 %all-gather.3.cloned.1.call-done.k_ref.v_ref = bf16[4096,256]{1,0:T(8,128)(2,1)} async-done(((bf16[512,256]{1,0:T(8,128)(2,1)}), bf16[4096,256]{1,0:T(8,128)(2,1)}) %all-gather.3.cloned.1.call-update) | async-done | bytes 2097168 | tf_op jit(solution)/shard_map/all_gather | solution.py:219
  60.1 4.9 %shard_map.75 = (f32[1,512,128]{2,1,0:T(8,128)}, f32[1,512,1]{2,1,0:T(8,128)}, f32[1,512,1]{2,1,0:T(8,128)}) custom-call(s32[1,8]{1,0:T(1,128)} %get-tuple-element.92.table_ref, s32[1,8]{1,0:T(1,128)} %get-tuple-element.90.meta_ref, bf16[1,512,128]{2,1,0:T(8,128)(2,1)} %get-tuple-element.80.q_ref, ...), custom_call_target="tpu_custom_call" | custom-call | tf_op jit(solution)/shard_map/pallas_call | solution.py:120
  66.1 35.5 %all-gather.5.cloned.1.call-done.k_ref.v_ref = bf16[4096,256]{1,0:T(8,128)(2,1)} async-done(((bf16[512,256]{1,0:T(8,128)(2,1)}), bf16[4096,256]{1,0:T(8,128)(2,1)}) %all-gather.5.cloned.1.call-update) | async-done | bytes 2097168 | tf_op jit(solution)/shard_map/all_gather | solution.py:219
  101.6 10.5 %shard_map.76 = (f32[1,512,128]{2,1,0:T(8,128)}, f32[1,512,1]{2,1,0:T(8,128)}, f32[1,512,1]{2,1,0:T(8,128)}) custom-call(s32[1,8]{1,0:T(1,128)} %get-tuple-element.93.table_ref, s32[1,8]{1,0:T(1,128)} %get-tuple-element.91.meta_ref, bf16[1,512,128]{2,1,0:T(8,128)(2,1)} %get-tuple-element.81.q_ref, ...), custom_call_target="tpu_custom_call" | custom-call | tf_op jit(solution)/shard_map/pallas_call | solution.py:120
  112.1 1.1 copy.91
  113.3 1.1 copy.93
  114.4 1.3 collective-permute-start.4
  116.7 1.5 collective-permute-start.5
  118.8 8.8 %shard_map.73 = (f32[1,512,128]{2,1,0:T(8,128)}, f32[1,512,1]{2,1,0:T(8,128)}, f32[1,512,1]{2,1,0:T(8,128)}) custom-call(s32[1,8]{1,0:T(1,128)} %get-tuple-element.88.table_ref, s32[1,8]{1,0:T(1,128)} %get-tuple-element.86.meta_ref, bf16[1,512,128]{2,1,0:T(8,128)(2,1)} %bitcast.99, bf16[4096,256]{1,0:T(8,128)(2,1)} %all-gather.3.cloned.1.call-done.k_ref.v_ref, ...), custom_call_target="tpu_custom_call" | custom-call | tf_op jit(solution)/shard_map/pallas_call | solution.py:120
  127.7 1.1 reduce
  128.8 1.1 reduce.2
  129.9 10.6 %shard_map.74 = (f32[1,512,128]{2,1,0:T(8,128)}, f32[1,512,1]{2,1,0:T(8,128)}, f32[1,512,1]{2,1,0:T(8,128)}) custom-call(s32[1,8]{1,0:T(1,128)} %get-tuple-element.89.table_ref, s32[1,8]{1,0:T(1,128)} %get-tuple-element.87.meta_ref, bf16[1,512,128]{2,1,0:T(8,128)(2,1)} %bitcast.98, bf16[4096,256]{1,0:T(8,128)(2,1)} %all-gather.5.cloned.1.call-done.k_ref.v_ref, ...), custom_call_target="tpu_custom_call" | custom-call | tf_op jit(solution)/shard_map/pallas_call | solution.py:120
  140.5 1.1 reduce.1
  141.6 1.1 reduce.3
  142.7 1.4 fusion.7
  144.5 4.6 %fusion = f32[2,2,32,4096]{3,2,1,0:T(8,128)S(1)} fusion(bf16[2,2,32,1024]{3,2,1,0:T(8,128)(2,1)S(1)} %dot_general.5, bf16[1024,4096]{1,0:T(8,128)(2,1)} %param.18), kind=kOutput, calls=%fused_computation.5 | convolution fusion | flops 1073741824 | bytes 10747904 | tf_op jit(solution)/shard_map/dot_general | solution.py:259
  149.4 2.0 %collective-permute-done.6 = bf16[2,32,4096]{2,1,0:T(8,128)(2,1)} collective-permute-done((bf16[2,32,4096]{2,1,0:T(8,128)(2,1)S(1)}, bf16[2,32,4096]{2,1,0:T(8,128)(2,1)}, u32[]{:S(2)}, u32[]{:S(2)}) %collective-permute-start.6) | collective-permute-done | bytes 524320 | tf_op jit(solution)/shard_map/ppermute | solution.py:193
  151.4 1.1 fusion.3
  152.7 8.3 %collective-permute-done.7 = bf16[32,4096]{1,0:T(8,128)(2,1)S(1)} collective-permute-done((bf16[32,4096]{1,0:T(8,128)(2,1)S(1)}, bf16[32,4096]{1,0:T(8,128)(2,1)S(1)}, u32[]{:S(2)}, u32[]{:S(2)}) %collective-permute-start.7) | collective-permute-done | bytes 262176 | tf_op jit(solution)/shard_map/ppermute | solution.py:198
  (113 shorter events, 18.7 us)
Async XLA Ops:
  6.5 53.6 %all-gather.3.cloned.1.call-start = ((), (), s32[]{:S(2)}) async-start(), calls=%async_computation | async-start | bytes 2359296 | tf_op jit(solution)/shard_map/all_gather | solution.py:219
  8.2 6.5 %collective-permute-start = (bf16[128,512]{1,0:T(8,128)(2,1)S(1)}, bf16[128,512]{1,0:T(8,128)(2,1)S(1)}, u32[]{:S(2)}, u32[]{:S(2)}) collective-permute-start(bf16[128,512]{1,0:T(8,128)(2,1)S(1)} %constant_dynamic-update-slice_fusion), channel_id=1, source_target_pairs={{0,4},{4,8},{8,12},{12,0},{1,5},{5,9},{9,13},{13,1},{2,6},{6,10},{... | collective-permute-start | bytes 393224 | tf_op jit(solution)/shard_map/ppermute | solution.py:179
  9.8 8.9 %collective-permute-start.1 = (bf16[128,512]{1,0:T(8,128)(2,1)S(1)}, bf16[128,512]{1,0:T(8,128)(2,1)S(1)}, u32[]{:S(2)}, u32[]{:S(2)}) collective-permute-start(bf16[128,512]{1,0:T(8,128)(2,1)S(1)} %constant_dynamic-update-slice_fusion), channel_id=1, source_target_pairs={{0,8},{4,12},{8,0},{12,4},{1,9},{5,13},{9,1},{13,5},{2,10},{6,14},... | collective-permute-start | bytes 393224 | tf_op jit(solution)/shard_map/ppermute | solution.py:179
  12.7 6.0 %collective-permute-start.2 = (bf16[128,512]{1,0:T(8,128)(2,1)S(1)}, bf16[128,512]{1,0:T(8,128)(2,1)S(1)}, u32[]{:S(2)}, u32[]{:S(2)}) collective-permute-start(bf16[128,512]{1,0:T(8,128)(2,1)S(1)} %constant_dynamic-update-slice_fusion), channel_id=1, source_target_pairs={{0,12},{4,0},{8,4},{12,8},{1,13},{5,1},{9,5},{13,9},{2,14},{6,2},{... | collective-permute-start | bytes 393224 | tf_op jit(solution)/shard_map/ppermute | solution.py:179
  18.8 1.7 copy-start.1
  19.4 2.6 %copy-start.6 = (s32[8]{0:T(128)S(1)}, s32[8]{0:T(128)}, u32[]{:S(2)}) copy-start(s32[8]{0:T(128)} %param.20) | copy-start | bytes 100
  19.4 2.7 %copy-start.5 = (s32[8]{0:T(128)S(1)}, s32[8]{0:T(128)}, u32[]{:S(2)}) copy-start(s32[8]{0:T(128)} %param.19) | copy-start | bytes 100
  19.4 2.8 %copy-start.4 = (s32[8]{0:T(128)S(1)}, s32[8]{0:T(128)}, u32[]{:S(2)}) copy-start(s32[8]{0:T(128)} %param.21) | copy-start | bytes 100
  20.4 81.2 %all-gather.5.cloned.1.call-start = ((), (), s32[]{:S(2)}) async-start(), calls=%async_computation.1 | async-start | bytes 2359296 | tf_op jit(solution)/shard_map/all_gather | solution.py:219
  20.7 10.9 %collective-permute-start.3 = (bf16[2,512,128]{2,1,0:T(8,128)(2,1)S(1)}, bf16[2,512,128]{2,1,0:T(8,128)(2,1)S(1)}, u32[]{:S(2)}, u32[]{:S(2)}) collective-permute-start(bf16[2,512,128]{2,1,0:T(8,128)(2,1)S(1)} %bitcast.95), channel_id=1, source_target_pairs={{128,0},{129,1},{130,2},{131,3},{132,4},{133,5},{134,6},{135,7},{1... | collective-permute-start | bytes 786440 | tf_op jit(solution)/shard_map/ppermute | solution.py:215
  101.6 11.5 %copy-start.2 = (f32[1,512,1]{2,1,0:T(8,128)S(1)}, f32[1,512,1]{2,1,0:T(8,128)}, u32[]{:S(2)}) copy-start(f32[1,512,1]{2,1,0:T(8,128)} %get-tuple-element.31) | copy-start | bytes 6148
  101.6 14.1 %copy-start = (f32[1,512,128]{2,1,0:T(8,128)S(1)}, f32[1,512,128]{2,1,0:T(8,128)}, u32[]{:S(2)}) copy-start(f32[1,512,128]{2,1,0:T(8,128)} %get-tuple-element.33) | copy-start | bytes 786436
  114.4 28.3 %collective-permute-start.4 = (f32[4,512]{1,0:T(4,128)S(1)}, f32[4,512]{1,0:T(4,128)S(1)}, u32[]{:S(2)}, u32[]{:S(2)}) collective-permute-start(f32[4,512]{1,0:T(4,128)S(1)} %pad_maximum_fusion.4), channel_id=1, source_target_pairs={{0,128},{1,129},{2,130},{3,131},{4,132},{5,133},{6,134},{7,135},{8... | collective-permute-start | bytes 24584 | tf_op jit(solution)/shard_map/ppermute | solution.py:253
  116.7 26.0 %collective-permute-start.5 = (bf16[2,512,128]{2,1,0:T(8,128)(2,1)S(1)}, bf16[2,512,128]{2,1,0:T(8,128)(2,1)S(1)}, u32[]{:S(2)}, u32[]{:S(2)}) collective-permute-start(bf16[2,512,128]{2,1,0:T(8,128)(2,1)S(1)} %pad_maximum_fusion.3), channel_id=1, source_target_pairs={{0,128},{1,129},{2,130},{3,131},{4,132},{5,133},{6,134},{7,135},{8... | collective-permute-start | bytes 786440 | tf_op jit(solution)/shard_map/ppermute | solution.py:252
  129.9 12.9 %copy-start.3 = (f32[1,512,128]{2,1,0:T(8,128)S(1)}, f32[1,512,128]{2,1,0:T(8,128)}, u32[]{:S(2)}) copy-start(f32[1,512,128]{2,1,0:T(8,128)} %get-tuple-element.24) | copy-start | bytes 786436
  149.3 2.1 %collective-permute-start.6 = (bf16[2,32,4096]{2,1,0:T(8,128)(2,1)S(1)}, bf16[2,32,4096]{2,1,0:T(8,128)(2,1)}, u32[]{:S(2)}, u32[]{:S(2)}) collective-permute-start(bf16[2,32,4096]{2,1,0:T(8,128)(2,1)S(1)} %bitcast_convert_fusion), channel_id=1, source_target_pairs={{0,1},{1,0},{2,3},{3,2},{4,5},{5,4},{6,7},{7,6},{8,9},{9,8},{10,11... | collective-permute-start | bytes 1572872 | tf_op jit(solution)/shard_map/ppermute | solution.py:193
  152.6 8.4 %collective-permute-start.7 = (bf16[32,4096]{1,0:T(8,128)(2,1)S(1)}, bf16[32,4096]{1,0:T(8,128)(2,1)S(1)}, u32[]{:S(2)}, u32[]{:S(2)}) collective-permute-start(bf16[32,4096]{1,0:T(8,128)(2,1)S(1)} %bitcast_convert_fusion.1), channel_id=1, source_target_pairs={{0,2},{2,0},{1,3},{3,1},{4,6},{6,4},{5,7},{7,5},{8,10},{10,8},{9,1... | collective-permute-start | bytes 786440 | tf_op jit(solution)/shard_map/ppermute | solution.py:198
Sparse Core Ops, SparseCore 0:
  20.6 39.5 all-gather.2
  61.9 39.6 all-gather.4

commit v9 on v7

--- a/solution.py
+++ b/solution.py
@@ -9,7 +9,7 @@
 
 HD = 128
 GROUP = 4
-KEY_BLOCK = 1024
+KEY_BLOCK = 2048
 
 NEGATIVE = -1e30
 

time: 143 us -> 140 us (0.979)
  the two profiles are of different devices: /device:TPU:192 before, /device:TPU:1 now
where the time goes in v9:
time: 140 us; the launch traced here: 139 us
  waiting for transfers between devices  62.5 us (45%)
  Pallas kernels  22.3 us (16%)
  between operations  13.7 us (10%)
  starting transfers between devices  13.1 us (9%)
  other arithmetic  12.9 us (9%)
  local copies, waits for them, and re-layouts  9.72 us (7%)
  matrix products  4.64 us (3%)
    all_gather x1, waiting for transfers between devices, per_device(): both = lax.all_gather(both, 'z', axis=0, tiled=True)  43.5 us
    pallas_call x2, Pallas kernels, attend(): pl.pallas_call(attention_kernel, out_shape=(jax.ShapeDtypeStruct(stacked....  22.3 us
    ppermute x3, waiting for transfers between devices, gather_ring(): lax.ppermute(block, axis, [(i, (i + shift) % size) for i in range(size)])  8.46 us
    ppermute x1, waiting for transfers between devices, scatter_sum(): got = lax.ppermute(give.astype(jnp.bfloat16), 'xl', [(0, 1), (1, 0)])  6.55 us
    dot_general x1, matrix products, per_device(): partial = jnp.dot(attended, out_weight, preferred_element_type=jnp.float32)  4.64 us
    ppermute x3, starting transfers between devices, gather_ring(): lax.ppermute(block, axis, [(i, (i + shift) % size) for i in range(size)])  4.6 us
  transfers between devices with their start and end apart: 9, of which 7 were waited for; matrix products, arithmetic and copies ran while one was open for 9% of the time, Pallas kernels for 7%

profile of v9, /device:TPU:1, one launch (start us, length us, event | category | flops | bytes accessed | tf_op | source)
XLA Modules:
  0.0 138.9 jit_solution(10746407070030087647)
XLA Ops:
  8.3 3.6 %collective-permute-start.2 = (bf16[128,512]{1,0:T(8,128)(2,1)S(1)}, bf16[128,512]{1,0:T(8,128)(2,1)S(1)}, u32[]{:S(2)}, u32[]{:S(2)}) collective-permute-start(bf16[128,512]{1,0:T(8,128)(2,1)S(1)} %constant_dynamic-update-slice_fusion), channel_id=1, source_target_pairs={{0,12},{4,0},{8,4},{12,8},{1,13},{5,1},{9,5},{13,9},{2,14},{6,2},{... | collective-permute-start | bytes 393224 | tf_op jit(solution)/shard_map/ppermute | solution.py:179
  13.0 2.4 %collective-permute-done.2 = bf16[128,512]{1,0:T(8,128)(2,1)S(1)} collective-permute-done((bf16[128,512]{1,0:T(8,128)(2,1)S(1)}, bf16[128,512]{1,0:T(8,128)(2,1)S(1)}, u32[]{:S(2)}, u32[]{:S(2)}) %collective-permute-start.2) | collective-permute-done | bytes 131104 | tf_op jit(solution)/shard_map/ppermute | solution.py:179
  15.4 1.8 %collective-permute-done.1 = bf16[128,512]{1,0:T(8,128)(2,1)S(1)} collective-permute-done((bf16[128,512]{1,0:T(8,128)(2,1)S(1)}, bf16[128,512]{1,0:T(8,128)(2,1)S(1)}, u32[]{:S(2)}, u32[]{:S(2)}) %collective-permute-start.1) | collective-permute-done | bytes 131104 | tf_op jit(solution)/shard_map/ppermute | solution.py:179
  17.3 4.2 %collective-permute-done = bf16[128,512]{1,0:T(8,128)(2,1)S(1)} collective-permute-done((bf16[128,512]{1,0:T(8,128)(2,1)S(1)}, bf16[128,512]{1,0:T(8,128)(2,1)S(1)}, u32[]{:S(2)}, u32[]{:S(2)}) %collective-permute-start) | collective-permute-done | bytes 131104 | tf_op jit(solution)/shard_map/ppermute | solution.py:179
  22.1 0.9 bitcast_select_fusion.1
  23.1 1.1 reshape.164
  24.3 1.3 collective-permute-start.3
  32.7 2.2 %collective-permute-done.3.q_ref = bf16[2,512,128]{2,1,0:T(8,128)(2,1)S(1)} collective-permute-done((bf16[2,512,128]{2,1,0:T(8,128)(2,1)S(1)}, bf16[2,512,128]{2,1,0:T(8,128)(2,1)S(1)}, u32[]{:S(2)}, u32[]{:S(2)}) %collective-permute-start.3) | collective-permute-done | bytes 262176 | tf_op jit(solution)/shard_map/ppermute | solution.py:215
  34.9 43.5 %all-gather.2.cloned.1.call-done.k_ref.v_ref = bf16[4096,512]{1,0:T(8,128)(2,1)} async-done(((bf16[512,512]{1,0:T(8,128)(2,1)}), bf16[4096,512]{1,0:T(8,128)(2,1)}) %all-gather.2.cloned.1.call-update) | async-done | bytes 4194320 | tf_op jit(solution)/shard_map/all_gather | solution.py:218
  78.4 12.0 %shard_map.74 = (f32[2,512,128]{2,1,0:T(8,128)}, f32[2,512,1]{2,1,0:T(8,128)}, f32[2,512,1]{2,1,0:T(8,128)}) custom-call(s32[2,4]{1,0:T(2,128)} %pad_add_fusion.3.table_ref, s32[2,8]{1,0:T(2,128)} %pad.8.meta_ref, bf16[2,512,128]{2,1,0:T(8,128)(2,1)} %copy-done.1, bf16[4096,512]{1,0:T(8,128)(2,1)} %all-gather.2.cloned.1.call-done.k_ref.v_ref, ...), custom_call_target="tpu_custom_call" | custom-call | tf_op jit(solution)/shard_map/pallas_call | solution.py:120
  90.4 1.2 reduce.1
  91.7 1.3 reduce
  92.9 1.3 collective-permute-start.4
  95.6 1.1 convert_element_type.40
  96.7 1.5 %collective-permute-start.5 = (bf16[2,512,128]{2,1,0:T(8,128)(2,1)S(1)}, bf16[2,512,128]{2,1,0:T(8,128)(2,1)S(1)}, u32[]{:S(2)}, u32[]{:S(2)}) collective-permute-start(bf16[2,512,128]{2,1,0:T(8,128)(2,1)S(1)} %convert_element_type.40), channel_id=1, source_target_pairs={{0,128},{1,129},{2,130},{3,131},{4,132},{5,133},{6,134},{7,135},{8... | collective-permute-start | bytes 786440 | tf_op jit(solution)/shard_map/ppermute | solution.py:228
  98.2 10.4 %shard_map.73 = (f32[2,512,128]{2,1,0:T(8,128)}, f32[2,512,1]{2,1,0:T(8,128)}, f32[2,512,1]{2,1,0:T(8,128)}) custom-call(s32[2,4]{1,0:T(2,128)} %pad_add_fusion.2.table_ref, s32[2,8]{1,0:T(2,128)} %pad.7.meta_ref, bf16[2,512,128]{2,1,0:T(8,128)(2,1)} %bitcast.88, bf16[4096,512]{1,0:T(8,128)(2,1)} %all-gather.2.cloned.1.call-done.k_ref.v_ref, ...), custom_call_target="tpu_custom_call" | custom-call | tf_op jit(solution)/shard_map/pallas_call | solution.py:120
  109.0 1.7 %fusion.8 = (f32[2,512]{1,0:T(2,128)S(1)}, f32[2,512]{1,0:T(2,128)S(1)}, f32[2,512]{1,0:T(2,128)S(1)}) fusion(f32[2,512,1]{2,1,0:T(8,128)} %get-tuple-element.19, f32[2,512,1]{2,1,0:T(8,128)S(1)} %copy.94, f32[2,512,1]{2,1,0:T(8,128)S(1)} %copy.96, f32[2,512,1]{2,1,0:T(8,128)} %get-tuple-element.24), kind=kLoop, calls=%fused_computation.23 | loop fusion | flops 6144 | bytes 28672 | tf_op jit(solution)/shard_map/exp | solution.py:160
  110.7 1.5 %divide_convert_fusion = bf16[2,512,128]{2,1,0:T(8,128)(2,1)S(1)} fusion(bf16[2,512,128]{2,1,0:T(8,128)(2,1)S(1)} %collective-permute-done.5, f32[2,512,128]{2,1,0:T(8,128)} %get-tuple-element.18, f32[2,512]{1,0:T(2,128)S(1)} %get-tuple-element.48, f32[2,512]{1,0:T(2,128)S(1)} %get-tuple-element.49, f32[2,512]{1,0:T(2,128)S(1)} %get-tuple-element.47, pred[]{:T(512)S(6)} %eq.11), kind=kLoop, calls=%fused_computation.20 | loop fusion | flops 917504 | bytes 1060865 | tf_op jit(solution)/shard_map/convert_element_type | solution.py:165
  112.7 4.6 %fusion = f32[2,2,32,4096]{3,2,1,0:T(8,128)S(1)} fusion(bf16[2,2,32,1024]{3,2,1,0:T(8,128)(2,1)S(1)} %dot_general.5, bf16[1024,4096]{1,0:T(8,128)(2,1)} %param.18), kind=kOutput, calls=%fused_computation.5 | convolution fusion | flops 1073741824 | bytes 10747904 | tf_op jit(solution)/shard_map/dot_general | solution.py:240
  117.4 2.1 %collective-permute-start.6 = (bf16[2,32,4096]{2,1,0:T(8,128)(2,1)S(1)}, bf16[2,32,4096]{2,1,0:T(8,128)(2,1)}, u32[]{:S(2)}, u32[]{:S(2)}) collective-permute-start(bf16[2,32,4096]{2,1,0:T(8,128)(2,1)S(1)} %bitcast_convert_fusion), channel_id=1, source_target_pairs={{0,1},{1,0},{2,3},{3,2},{4,5},{5,4},{6,7},{7,6},{8,9},{9,8},{10,11... | collective-permute-start | bytes 1572872 | tf_op jit(solution)/shard_map/ppermute | solution.py:193
  119.4 1.7 %collective-permute-done.6 = bf16[2,32,4096]{2,1,0:T(8,128)(2,1)} collective-permute-done((bf16[2,32,4096]{2,1,0:T(8,128)(2,1)S(1)}, bf16[2,32,4096]{2,1,0:T(8,128)(2,1)}, u32[]{:S(2)}, u32[]{:S(2)}) %collective-permute-start.6) | collective-permute-done | bytes 524320 | tf_op jit(solution)/shard_map/ppermute | solution.py:193
  121.1 1.1 fusion.3
  122.3 2.4 %collective-permute-start.7 = (bf16[32,4096]{1,0:T(8,128)(2,1)S(1)}, bf16[32,4096]{1,0:T(8,128)(2,1)S(1)}, u32[]{:S(2)}, u32[]{:S(2)}) collective-permute-start(bf16[32,4096]{1,0:T(8,128)(2,1)S(1)} %bitcast_convert_fusion.1), channel_id=1, source_target_pairs={{0,2},{2,0},{1,3},{3,1},{4,6},{6,4},{5,7},{7,5},{8,10},{10,8},{9,1... | collective-permute-start | bytes 786440 | tf_op jit(solution)/shard_map/ppermute | solution.py:198
  124.7 6.5 %collective-permute-done.7 = bf16[32,4096]{1,0:T(8,128)(2,1)S(1)} collective-permute-done((bf16[32,4096]{1,0:T(8,128)(2,1)S(1)}, bf16[32,4096]{1,0:T(8,128)(2,1)S(1)}, u32[]{:S(2)}, u32[]{:S(2)}) %collective-permute-start.7) | collective-permute-done | bytes 262176 | tf_op jit(solution)/shard_map/ppermute | solution.py:198
  (90 shorter events, 13.7 us)
Async XLA Ops:
  6.5 19.0 %copy-start.4 = (s32[8]{0:T(128)S(1)}, s32[8]{0:T(128)}, u32[]{:S(2)}) copy-start(s32[8]{0:T(128)} %param.20) | copy-start | bytes 100
  6.5 19.1 %copy-start.3 = (s32[8]{0:T(128)S(1)}, s32[8]{0:T(128)}, u32[]{:S(2)}) copy-start(s32[8]{0:T(128)} %param.19) | copy-start | bytes 100
  6.5 19.3 %copy-start.2 = (s32[8]{0:T(128)S(1)}, s32[8]{0:T(128)}, u32[]{:S(2)}) copy-start(s32[8]{0:T(128)} %param.21) | copy-start | bytes 100
  6.5 71.9 %all-gather.2.cloned.1.call-start = ((), (), s32[]{:S(2)}) async-start(), calls=%async_computation | async-start | bytes 4718592 | tf_op jit(solution)/shard_map/all_gather | solution.py:218
  8.3 7.2 %collective-permute-start.2 = (bf16[128,512]{1,0:T(8,128)(2,1)S(1)}, bf16[128,512]{1,0:T(8,128)(2,1)S(1)}, u32[]{:S(2)}, u32[]{:S(2)}) collective-permute-start(bf16[128,512]{1,0:T(8,128)(2,1)S(1)} %constant_dynamic-update-slice_fusion), channel_id=1, source_target_pairs={{0,12},{4,0},{8,4},{12,8},{1,13},{5,1},{9,5},{13,9},{2,14},{6,2},{... | collective-permute-start | bytes 393224 | tf_op jit(solution)/shard_map/ppermute | solution.py:179
  11.8 5.4 %collective-permute-start.1 = (bf16[128,512]{1,0:T(8,128)(2,1)S(1)}, bf16[128,512]{1,0:T(8,128)(2,1)S(1)}, u32[]{:S(2)}, u32[]{:S(2)}) collective-permute-start(bf16[128,512]{1,0:T(8,128)(2,1)S(1)} %constant_dynamic-update-slice_fusion), channel_id=1, source_target_pairs={{0,8},{4,12},{8,0},{12,4},{1,9},{5,13},{9,1},{13,5},{2,10},{6,14},... | collective-permute-start | bytes 393224 | tf_op jit(solution)/shard_map/ppermute | solution.py:179
  12.2 9.3 %collective-permute-start = (bf16[128,512]{1,0:T(8,128)(2,1)S(1)}, bf16[128,512]{1,0:T(8,128)(2,1)S(1)}, u32[]{:S(2)}, u32[]{:S(2)}) collective-permute-start(bf16[128,512]{1,0:T(8,128)(2,1)S(1)} %constant_dynamic-update-slice_fusion), channel_id=1, source_target_pairs={{0,4},{4,8},{8,12},{12,0},{1,5},{5,9},{9,13},{13,1},{2,6},{6,10},{... | collective-permute-start | bytes 393224 | tf_op jit(solution)/shard_map/ppermute | solution.py:179
  24.2 66.2 %copy-start = (bf16[128,2,4,128]{3,0,2,1:T(8,128)(2,1)}, bf16[128,2,4,128]{3,0,2,1:T(8,128)(2,1)S(1)}, u32[]{:S(2)}) copy-start(bf16[128,2,4,128]{3,0,2,1:T(8,128)(2,1)S(1)} %copy.84) | copy-start | bytes 786436
  24.3 10.7 %collective-permute-start.3 = (bf16[2,512,128]{2,1,0:T(8,128)(2,1)S(1)}, bf16[2,512,128]{2,1,0:T(8,128)(2,1)S(1)}, u32[]{:S(2)}, u32[]{:S(2)}) collective-permute-start(bf16[2,512,128]{2,1,0:T(8,128)(2,1)S(1)} %bitcast.87), channel_id=1, source_target_pairs={{128,0},{129,1},{130,2},{131,3},{132,4},{133,5},{134,6},{135,7},{1... | collective-permute-start | bytes 786440 | tf_op jit(solution)/shard_map/ppermute | solution.py:215
  34.9 43.5 %copy-start.1 = (bf16[2,512,128]{2,1,0:T(8,128)(2,1)}, bf16[2,512,128]{2,1,0:T(8,128)(2,1)S(1)}, u32[]{:S(2)}) copy-start(bf16[2,512,128]{2,1,0:T(8,128)(2,1)S(1)} %collective-permute-done.3.q_ref) | copy-start | bytes 786436
  92.9 15.6 %collective-permute-start.4 = (f32[4,512]{1,0:T(4,128)S(1)}, f32[4,512]{1,0:T(4,128)S(1)}, u32[]{:S(2)}, u32[]{:S(2)}) collective-permute-start(f32[4,512]{1,0:T(4,128)S(1)} %pad_maximum_fusion.1), channel_id=1, source_target_pairs={{0,128},{1,129},{2,130},{3,131},{4,132},{5,133},{6,134},{7,135},{8... | collective-permute-start | bytes 24584 | tf_op jit(solution)/shard_map/ppermute | solution.py:229
  96.7 14.1 %collective-permute-start.5 = (bf16[2,512,128]{2,1,0:T(8,128)(2,1)S(1)}, bf16[2,512,128]{2,1,0:T(8,128)(2,1)S(1)}, u32[]{:S(2)}, u32[]{:S(2)}) collective-permute-start(bf16[2,512,128]{2,1,0:T(8,128)(2,1)S(1)} %convert_element_type.40), channel_id=1, source_target_pairs={{0,128},{1,129},{2,130},{3,131},{4,132},{5,133},{6,134},{7,135},{8... | collective-permute-start | bytes 786440 | tf_op jit(solution)/shard_map/ppermute | solution.py:228
  117.4 3.7 %collective-permute-start.6 = (bf16[2,32,4096]{2,1,0:T(8,128)(2,1)S(1)}, bf16[2,32,4096]{2,1,0:T(8,128)(2,1)}, u32[]{:S(2)}, u32[]{:S(2)}) collective-permute-start(bf16[2,32,4096]{2,1,0:T(8,128)(2,1)S(1)} %bitcast_convert_fusion), channel_id=1, source_target_pairs={{0,1},{1,0},{2,3},{3,2},{4,5},{5,4},{6,7},{7,6},{8,9},{9,8},{10,11... | collective-permute-start | bytes 1572872 | tf_op jit(solution)/shard_map/ppermute | solution.py:193
  122.3 8.9 %collective-permute-start.7 = (bf16[32,4096]{1,0:T(8,128)(2,1)S(1)}, bf16[32,4096]{1,0:T(8,128)(2,1)S(1)}, u32[]{:S(2)}, u32[]{:S(2)}) collective-permute-start(bf16[32,4096]{1,0:T(8,128)(2,1)S(1)} %bitcast_convert_fusion.1), channel_id=1, source_target_pairs={{0,2},{2,0},{1,3},{3,1},{4,6},{6,4},{5,7},{7,5},{8,10},{10,8},{9,1... | collective-permute-start | bytes 786440 | tf_op jit(solution)/shard_map/ppermute | solution.py:198
Sparse Core Ops, SparseCore 0:
  23.2 55.1 all-gather.1

commit v10 on v9

--- a/solution.py
+++ b/solution.py
@@ -183,6 +183,26 @@
     return jnp.take(stacked, order, axis=0).reshape(size * block.shape[0], block.shape[1])
 
 
+def gather_both_ways(block, axis):
+    size = lax.axis_size(axis)
+    here = lax.axis_index(axis)
+    right = [(i, (i + 1) % size) for i in range(size)]
+    left = [(i, (i - 1) % size) for i in range(size)]
+    pieces = [None] * size
+    pieces[0] = block
+    forward = block
+    backward = block
+    for step in range(1, size // 2 + 1):
+        forward = lax.ppermute(forward, axis, right)
+        pieces[size - step] = forward
+        if step < size - size // 2:
+            backward = lax.ppermute(backward, axis, left)
+            pieces[step] = backward
+    stacked = jnp.stack(pieces)
+    order = (jnp.arange(size, dtype=jnp.int32) - here) % size
+    return jnp.take(stacked, order, axis=0).reshape(size * block.shape[0], block.shape[1])
+
+
 def scatter_sum(partial):
     rows, width = partial.shape
     quarter = rows // 4
@@ -215,7 +235,7 @@
     partner_queries = lax.ppermute(stack_heads(queries, local_heads), "xh", [(1, 0)])
     both = jnp.concatenate([key_states, value_states], axis=1)
     both = gather_ring(both, "y")
-    both = lax.all_gather(both, "z", axis=0, tiled=True)
+    both = gather_both_ways(both, "z")
     key_offset = half * both.shape[0]
     table, meta = block_table(
         partner * row_count, row_count, key_offset, both.shape[0],

time: 140 us -> 139 us (level)
  waiting for transfers between devices: 62.5 us -> 41.4 us
  starting transfers between devices: 13.1 us -> 27.6 us
  between operations: 13.7 us -> 0.33 us
  local copies, waits for them, and re-layouts: 9.72 us -> 21.9 us
  other arithmetic: 12.9 us -> 18.4 us
    all_gather x1 -> x0, waiting for transfers between devices: 43.5 us -> none  [per_device(): both = lax.all_gather(both, 'z', axis=0, tiled=True)]
    ppermute x0 -> x7, waiting for transfers between devices: none -> 33.4 us  [the longest x4 33.4 us: gather_both_ways(): forward = lax.ppermute(forward, axis, right)]
    ppermute x0 -> x7, starting transfers between devices: none -> 11.4 us  [the longest x3 9.64 us: gather_both_ways(): backward = lax.ppermute(backward, axis, left)]
    ppermute x3, waiting for transfers between devices: 8.46 us -> 0.01 us  [gather_ring(): lax.ppermute(block, axis, [(i, (i + shift) % size) for i in range(size)])]
    unnamed x11 -> x13, local copies, waits for them, and re-layouts: 0.9 us -> 5.99 us
    gather x0 -> x1, local copies, waits for them, and re-layouts: none -> 4.97 us  [gather_both_ways(): jnp.take(stacked, order, axis=0)]
    select_n x0 -> x2, other arithmetic: none -> 3.87 us  [gather_both_ways(): jnp.take(stacked, order, axis=0)]
    ppermute x1, starting transfers between devices: 2.07 us -> 5.01 us  [scatter_sum(): got = lax.ppermute(give.astype(jnp.bfloat16), 'core', [(0, 1), (1, 0)])]
  transfers between devices with their start and end apart: 9 -> 15, of which waited for: 7 -> 6; matrix products, arithmetic and copies ran while one was open for 9% -> 23% of each run, Pallas kernels for 7% -> 8%
where the time goes in v10:
time: 139 us; the launch traced here: 138 us
  waiting for transfers between devices  41.4 us (30%)
  starting transfers between devices  27.6 us (20%)
  Pallas kernels  23.7 us (17%)
  local copies, waits for them, and re-layouts  21.9 us (16%)
  other arithmetic  18.4 us (13%)
  matrix products  4.64 us (3%)
    ppermute x4, waiting for transfers between devices, gather_both_ways(): forward = lax.ppermute(forward, axis, right)  33.4 us
    pallas_call x2, Pallas kernels, attend(): pl.pallas_call(attention_kernel, out_shape=(jax.ShapeDtypeStruct(stacked....  23.7 us
    ppermute x3, starting transfers between devices, gather_both_ways(): backward = lax.ppermute(backward, axis, left)  9.64 us
    ppermute x1, waiting for transfers between devices, scatter_sum(): got = lax.ppermute(give.astype(jnp.bfloat16), 'xl', [(0, 1), (1, 0)])  6.31 us
    unnamed x13, local copies, waits for them, and re-layouts  5.99 us
    ppermute x3, starting transfers between devices, gather_ring(): lax.ppermute(block, axis, [(i, (i + shift) % size) for i in range(size)])  5.81 us
    ppermute x1, starting transfers between devices, scatter_sum(): got = lax.ppermute(give.astype(jnp.bfloat16), 'core', [(0, 1), (1, 0)])  5.01 us
    gather x1, local copies, waits for them, and re-layouts, gather_both_ways(): jnp.take(stacked, order, axis=0)  4.97 us
  transfers between devices with their start and end apart: 15, of which 6 were waited for; matrix products, arithmetic and copies ran while one was open for 23% of the time, Pallas kernels for 8%

profile of v10, /device:TPU:1, one launch (start us, length us, event | category | flops | bytes accessed | tf_op | source)
XLA Modules:
  0.0 138.0 jit_solution(485688691661664846)
XLA Ops:
  1.7 2.1 %collective-permute-start = (bf16[128,512]{1,0:T(8,128)(2,1)S(1)}, bf16[128,512]{1,0:T(8,128)(2,1)S(1)}, u32[]{:S(2)}, u32[]{:S(2)}) collective-permute-start(bf16[128,512]{1,0:T(8,128)(2,1)S(1)} %constant_dynamic-update-slice_fusion), channel_id=1, source_target_pairs={{0,4},{4,8},{8,12},{12,0},{1,5},{5,9},{9,13},{13,1},{2,6},{6,10},{... | collective-permute-start | bytes 393224 | tf_op jit(solution)/shard_map/ppermute | solution.py:179
  3.8 2.6 %collective-permute-start.1 = (bf16[128,512]{1,0:T(8,128)(2,1)S(1)}, bf16[128,512]{1,0:T(8,128)(2,1)S(1)}, u32[]{:S(2)}, u32[]{:S(2)}) collective-permute-start(bf16[128,512]{1,0:T(8,128)(2,1)S(1)} %constant_dynamic-update-slice_fusion), channel_id=1, source_target_pairs={{0,8},{4,12},{8,0},{12,4},{1,9},{5,13},{9,1},{13,5},{2,10},{6,14},... | collective-permute-start | bytes 393224 | tf_op jit(solution)/shard_map/ppermute | solution.py:179
  8.7 1.3 collective-permute-start.10
  18.2 1.7 %collective-permute-start.6 = (bf16[512,512]{1,0:T(8,128)(2,1)S(1)}, bf16[512,512]{1,0:T(8,128)(2,1)S(1)}, u32[]{:S(2)}, u32[]{:S(2)}) collective-permute-start(bf16[512,512]{1,0:T(8,128)(2,1)S(1)} %bitcast_select_fusion.2), channel_id=1, source_target_pairs={{0,16},{16,32},{32,48},{48,64},{64,80},{80,96},{96,112},{112,0},{1... | collective-permute-start | bytes 1572872 | tf_op jit(solution)/shard_map/ppermute | solution.py:196
  20.5 4.0 %collective-permute-start.3 = (bf16[512,512]{1,0:T(8,128)(2,1)S(1)}, bf16[512,512]{1,0:T(8,128)(2,1)S(1)}, u32[]{:S(2)}, u32[]{:S(2)}) collective-permute-start(bf16[512,512]{1,0:T(8,128)(2,1)S(1)} %bitcast_select_fusion.2), channel_id=1, source_target_pairs={{0,112},{16,0},{32,16},{48,32},{64,48},{80,64},{96,80},{112,96},{1... | collective-permute-start | bytes 1572872 | tf_op jit(solution)/shard_map/ppermute | solution.py:199
  24.5 10.1 %collective-permute-done.6 = bf16[512,512]{1,0:T(8,128)(2,1)S(1)} collective-permute-done((bf16[512,512]{1,0:T(8,128)(2,1)S(1)}, bf16[512,512]{1,0:T(8,128)(2,1)S(1)}, u32[]{:S(2)}, u32[]{:S(2)}) %collective-permute-start.6) | collective-permute-done | bytes 524320 | tf_op jit(solution)/shard_map/ppermute | solution.py:196
  34.7 2.9 %collective-permute-start.4 = (bf16[512,512]{1,0:T(8,128)(2,1)S(1)}, bf16[512,512]{1,0:T(8,128)(2,1)S(1)}, u32[]{:S(2)}, u32[]{:S(2)}) collective-permute-start(bf16[512,512]{1,0:T(8,128)(2,1)S(1)} %collective-permute-done.3), channel_id=1, source_target_pairs={{0,112},{16,0},{32,16},{48,32},{64,48},{80,64},{96,80},{112,96},{1... | collective-permute-start | bytes 1572872 | tf_op jit(solution)/shard_map/ppermute | solution.py:199
  37.7 9.4 %collective-permute-done.7 = bf16[512,512]{1,0:T(8,128)(2,1)S(1)} collective-permute-done((bf16[512,512]{1,0:T(8,128)(2,1)S(1)}, bf16[512,512]{1,0:T(8,128)(2,1)S(1)}, u32[]{:S(2)}, u32[]{:S(2)}) %collective-permute-start.7) | collective-permute-done | bytes 524320 | tf_op jit(solution)/shard_map/ppermute | solution.py:196
  49.0 2.7 %collective-permute-start.5 = (bf16[512,512]{1,0:T(8,128)(2,1)S(1)}, bf16[512,512]{1,0:T(8,128)(2,1)S(1)}, u32[]{:S(2)}, u32[]{:S(2)}) collective-permute-start(bf16[512,512]{1,0:T(8,128)(2,1)S(1)} %collective-permute-done.4), channel_id=1, source_target_pairs={{0,112},{16,0},{32,16},{48,32},{64,48},{80,64},{96,80},{112,96},{1... | collective-permute-start | bytes 1572872 | tf_op jit(solution)/shard_map/ppermute | solution.py:199
  52.7 5.9 %collective-permute-done.8 = bf16[512,512]{1,0:T(8,128)(2,1)S(1)} collective-permute-done((bf16[512,512]{1,0:T(8,128)(2,1)S(1)}, bf16[512,512]{1,0:T(8,128)(2,1)S(1)}, u32[]{:S(2)}, u32[]{:S(2)}) %collective-permute-start.8) | collective-permute-done | bytes 524320 | tf_op jit(solution)/shard_map/ppermute | solution.py:196
  61.1 8.1 %collective-permute-done.9 = bf16[512,512]{1,0:T(8,128)(2,1)S(1)} collective-permute-done((bf16[512,512]{1,0:T(8,128)(2,1)S(1)}, bf16[512,512]{1,0:T(8,128)(2,1)S(1)}, u32[]{:S(2)}, u32[]{:S(2)}) %collective-permute-start.9) | collective-permute-done | bytes 524320 | tf_op jit(solution)/shard_map/ppermute | solution.py:196
  72.5 5.0 %gather_fusion.1 = bf16[8,512,512]{2,1,0:T(8,128)(2,1)} fusion(bf16[8,512,512]{2,1,0:T(8,128)(2,1)} %bitcast_dynamic-update-slice_fusion, s32[1024]{0:T(1024)S(1)} %pad_clamp_fusion), kind=kCustom, calls=%fused_computation.5 | custom fusion | bytes 8388640 | tf_op jit(solution)/shard_map/jit(_take)/gather | solution.py:203
  77.5 3.9 %bitcast_select_fusion.k_ref.v_ref = bf16[4096,512]{1,0:T(8,128)(2,1)} fusion(bf16[8,512,512]{2,1,0:T(8,128)(2,1)} %gather_fusion.1, pred[4096]{0:T(1024)(128)(4,1)S(1)} %bitcast.121), kind=kLoop, calls=%fused_computation.8 | loop fusion | flops 2097152 | bytes 8392704 | tf_op jit(solution)/shard_map/jit(_take)/select_n | solution.py:203
  81.4 13.3 %shard_map.74 = (f32[2,512,128]{2,1,0:T(8,128)}, f32[2,512,1]{2,1,0:T(8,128)}, f32[2,512,1]{2,1,0:T(8,128)}) custom-call(s32[2,4]{1,0:T(2,128)} %pad_add_fusion.3.table_ref, s32[2,8]{1,0:T(2,128)} %pad.8.meta_ref, bf16[2,512,128]{2,1,0:T(8,128)(2,1)} %collective-permute-done.10.q_ref, bf16[4096,512]{1,0:T(8,128)(2,1)} %bitcast_select_fusion.k_ref.v_ref, ...), custom_call_target="tpu_custom_call" | custom-call | tf_op jit(solution)/shard_map/pallas_call | solution.py:120
  97.2 1.3 collective-permute-start.11
  101.0 1.5 %collective-permute-start.12 = (bf16[2,512,128]{2,1,0:T(8,128)(2,1)S(1)}, bf16[2,512,128]{2,1,0:T(8,128)(2,1)S(1)}, u32[]{:S(2)}, u32[]{:S(2)}) collective-permute-start(bf16[2,512,128]{2,1,0:T(8,128)(2,1)S(1)} %convert_element_type.40), channel_id=1, source_target_pairs={{0,128},{1,129},{2,130},{3,131},{4,132},{5,133},{6,134},{7,135},{8... | collective-permute-start | bytes 786440 | tf_op jit(solution)/shard_map/ppermute | solution.py:248
  102.5 10.4 %shard_map.73 = (f32[2,512,128]{2,1,0:T(8,128)}, f32[2,512,1]{2,1,0:T(8,128)}, f32[2,512,1]{2,1,0:T(8,128)}) custom-call(s32[2,4]{1,0:T(2,128)} %pad_add_fusion.2.table_ref, s32[2,8]{1,0:T(2,128)} %pad.7.meta_ref, bf16[2,512,128]{2,1,0:T(8,128)(2,1)} %bitcast.115, bf16[4096,512]{1,0:T(8,128)(2,1)} %bitcast_select_fusion.k_ref.v_ref, ...), custom_call_target="tpu_custom_call" | custom-call | tf_op jit(solution)/shard_map/pallas_call | solution.py:120
  113.4 1.7 %fusion.9 = (f32[2,512]{1,0:T(2,128)S(1)}, f32[2,512]{1,0:T(2,128)S(1)}, f32[2,512]{1,0:T(2,128)S(1)}) fusion(f32[2,512,1]{2,1,0:T(8,128)} %get-tuple-element.19, f32[2,512,1]{2,1,0:T(8,128)S(1)} %copy.94, f32[2,512,1]{2,1,0:T(8,128)S(1)} %copy.96, f32[2,512,1]{2,1,0:T(8,128)} %get-tuple-element.24), kind=kLoop, calls=%fused_computation.34 | loop fusion | flops 6144 | bytes 28672 | tf_op jit(solution)/shard_map/exp | solution.py:160
  115.1 1.5 %divide_convert_fusion = bf16[2,512,128]{2,1,0:T(8,128)(2,1)S(1)} fusion(bf16[2,512,128]{2,1,0:T(8,128)(2,1)S(1)} %collective-permute-done.12, f32[2,512,128]{2,1,0:T(8,128)} %get-tuple-element.18, f32[2,512]{1,0:T(2,128)S(1)} %get-tuple-element.48, f32[2,512]{1,0:T(2,128)S(1)} %get-tuple-element.49, f32[2,512]{1,0:T(2,128)S(1)} %get-tuple-element.47, ...), kind=kLoop, calls=%fused_computation.31 | loop fusion | flops 917504 | bytes 1060865 | tf_op jit(solution)/shard_map/convert_element_type | solution.py:165
  117.0 4.6 %fusion = f32[2,2,32,4096]{3,2,1,0:T(8,128)S(1)} fusion(bf16[2,2,32,1024]{3,2,1,0:T(8,128)(2,1)S(1)} %dot_general.5, bf16[1024,4096]{1,0:T(8,128)(2,1)} %param.18), kind=kOutput, calls=%fused_computation.6 | convolution fusion | flops 1073741824 | bytes 10747904 | tf_op jit(solution)/shard_map/dot_general | solution.py:260
  121.7 5.0 %collective-permute-start.13 = (bf16[2,32,4096]{2,1,0:T(8,128)(2,1)S(1)}, bf16[2,32,4096]{2,1,0:T(8,128)(2,1)}, u32[]{:S(2)}, u32[]{:S(2)}) collective-permute-start(bf16[2,32,4096]{2,1,0:T(8,128)(2,1)S(1)} %bitcast_convert_fusion), channel_id=1, source_target_pairs={{0,1},{1,0},{2,3},{3,2},{4,5},{5,4},{6,7},{7,6},{8,9},{9,8},{10,11... | collective-permute-start | bytes 1572872 | tf_op jit(solution)/shard_map/ppermute | solution.py:213
  126.7 1.7 %collective-permute-done.13 = bf16[2,32,4096]{2,1,0:T(8,128)(2,1)} collective-permute-done((bf16[2,32,4096]{2,1,0:T(8,128)(2,1)S(1)}, bf16[2,32,4096]{2,1,0:T(8,128)(2,1)}, u32[]{:S(2)}, u32[]{:S(2)}) %collective-permute-start.13) | collective-permute-done | bytes 524320 | tf_op jit(solution)/shard_map/ppermute | solution.py:213
  129.6 1.3 collective-permute-start.14
  130.9 6.3 %collective-permute-done.14 = bf16[32,4096]{1,0:T(8,128)(2,1)S(1)} collective-permute-done((bf16[32,4096]{1,0:T(8,128)(2,1)S(1)}, bf16[32,4096]{1,0:T(8,128)(2,1)S(1)}, u32[]{:S(2)}, u32[]{:S(2)}) %collective-permute-start.14) | collective-permute-done | bytes 262176 | tf_op jit(solution)/shard_map/ppermute | solution.py:218
  (110 shorter events, 29.4 us)
Async XLA Ops:
  0.0 47.0 %copy-start.1 = (s32[8]{0:T(128)S(1)}, s32[8]{0:T(128)}, u32[]{:S(2)}) copy-start(s32[8]{0:T(128)} %param.20) | copy-start | bytes 100
  1.7 15.6 %collective-permute-start = (bf16[128,512]{1,0:T(8,128)(2,1)S(1)}, bf16[128,512]{1,0:T(8,128)(2,1)S(1)}, u32[]{:S(2)}, u32[]{:S(2)}) collective-permute-start(bf16[128,512]{1,0:T(8,128)(2,1)S(1)} %constant_dynamic-update-slice_fusion), channel_id=1, source_target_pairs={{0,4},{4,8},{8,12},{12,0},{1,5},{5,9},{9,13},{13,1},{2,6},{6,10},{... | collective-permute-start | bytes 393224 | tf_op jit(solution)/shard_map/ppermute | solution.py:179
  3.8 13.5 %collective-permute-start.1 = (bf16[128,512]{1,0:T(8,128)(2,1)S(1)}, bf16[128,512]{1,0:T(8,128)(2,1)S(1)}, u32[]{:S(2)}, u32[]{:S(2)}) collective-permute-start(bf16[128,512]{1,0:T(8,128)(2,1)S(1)} %constant_dynamic-update-slice_fusion), channel_id=1, source_target_pairs={{0,8},{4,12},{8,0},{12,4},{1,9},{5,13},{9,1},{13,5},{2,10},{6,14},... | collective-permute-start | bytes 393224 | tf_op jit(solution)/shard_map/ppermute | solution.py:179
  6.5 10.9 %collective-permute-start.2 = (bf16[128,512]{1,0:T(8,128)(2,1)S(1)}, bf16[128,512]{1,0:T(8,128)(2,1)S(1)}, u32[]{:S(2)}, u32[]{:S(2)}) collective-permute-start(bf16[128,512]{1,0:T(8,128)(2,1)S(1)} %constant_dynamic-update-slice_fusion), channel_id=1, source_target_pairs={{0,12},{4,0},{8,4},{12,8},{1,13},{5,1},{9,5},{13,9},{2,14},{6,2},{... | collective-permute-start | bytes 393224 | tf_op jit(solution)/shard_map/ppermute | solution.py:179
  8.7 51.6 %copy-start = (bf16[128,2,4,128]{3,0,2,1:T(8,128)(2,1)}, bf16[128,2,4,128]{3,0,2,1:T(8,128)(2,1)S(1)}, u32[]{:S(2)}) copy-start(bf16[128,2,4,128]{3,0,2,1:T(8,128)(2,1)S(1)} %copy.84) | copy-start | bytes 786436
  8.7 72.7 %collective-permute-start.10 = (bf16[2,512,128]{2,1,0:T(8,128)(2,1)S(1)}, bf16[2,512,128]{2,1,0:T(8,128)(2,1)}, u32[]{:S(2)}, u32[]{:S(2)}) collective-permute-start(bf16[2,512,128]{2,1,0:T(8,128)(2,1)S(1)} %bitcast.114), channel_id=1, source_target_pairs={{128,0},{129,1},{130,2},{131,3},{132,4},{133,5},{134,6},{135,7},{1... | collective-permute-start | bytes 786440 | tf_op jit(solution)/shard_map/ppermute | solution.py:235
  18.2 16.4 %collective-permute-start.6 = (bf16[512,512]{1,0:T(8,128)(2,1)S(1)}, bf16[512,512]{1,0:T(8,128)(2,1)S(1)}, u32[]{:S(2)}, u32[]{:S(2)}) collective-permute-start(bf16[512,512]{1,0:T(8,128)(2,1)S(1)} %bitcast_select_fusion.2), channel_id=1, source_target_pairs={{0,16},{16,32},{32,48},{48,64},{64,80},{80,96},{96,112},{112,0},{1... | collective-permute-start | bytes 1572872 | tf_op jit(solution)/shard_map/ppermute | solution.py:196
  20.5 14.1 %collective-permute-start.3 = (bf16[512,512]{1,0:T(8,128)(2,1)S(1)}, bf16[512,512]{1,0:T(8,128)(2,1)S(1)}, u32[]{:S(2)}, u32[]{:S(2)}) collective-permute-start(bf16[512,512]{1,0:T(8,128)(2,1)S(1)} %bitcast_select_fusion.2), channel_id=1, source_target_pairs={{0,112},{16,0},{32,16},{48,32},{64,48},{80,64},{96,80},{112,96},{1... | collective-permute-start | bytes 1572872 | tf_op jit(solution)/shard_map/ppermute | solution.py:199
  34.6 12.5 %collective-permute-start.7 = (bf16[512,512]{1,0:T(8,128)(2,1)S(1)}, bf16[512,512]{1,0:T(8,128)(2,1)S(1)}, u32[]{:S(2)}, u32[]{:S(2)}) collective-permute-start(bf16[512,512]{1,0:T(8,128)(2,1)S(1)} %collective-permute-done.6), channel_id=1, source_target_pairs={{0,16},{16,32},{32,48},{48,64},{64,80},{80,96},{96,112},{112,0},{1... | collective-permute-start | bytes 1572872 | tf_op jit(solution)/shard_map/ppermute | solution.py:196
  34.7 14.3 %collective-permute-start.4 = (bf16[512,512]{1,0:T(8,128)(2,1)S(1)}, bf16[512,512]{1,0:T(8,128)(2,1)S(1)}, u32[]{:S(2)}, u32[]{:S(2)}) collective-permute-start(bf16[512,512]{1,0:T(8,128)(2,1)S(1)} %collective-permute-done.3), channel_id=1, source_target_pairs={{0,112},{16,0},{32,16},{48,32},{64,48},{80,64},{96,80},{112,96},{1... | collective-permute-start | bytes 1572872 | tf_op jit(solution)/shard_map/ppermute | solution.py:199
  47.0 11.5 %collective-permute-start.8 = (bf16[512,512]{1,0:T(8,128)(2,1)S(1)}, bf16[512,512]{1,0:T(8,128)(2,1)S(1)}, u32[]{:S(2)}, u32[]{:S(2)}) collective-permute-start(bf16[512,512]{1,0:T(8,128)(2,1)S(1)} %collective-permute-done.7), channel_id=1, source_target_pairs={{0,16},{16,32},{32,48},{48,64},{64,80},{80,96},{96,112},{112,0},{1... | collective-permute-start | bytes 1572872 | tf_op jit(solution)/shard_map/ppermute | solution.py:196
  49.0 11.3 %collective-permute-start.5 = (bf16[512,512]{1,0:T(8,128)(2,1)S(1)}, bf16[512,512]{1,0:T(8,128)(2,1)S(1)}, u32[]{:S(2)}, u32[]{:S(2)}) collective-permute-start(bf16[512,512]{1,0:T(8,128)(2,1)S(1)} %collective-permute-done.4), channel_id=1, source_target_pairs={{0,112},{16,0},{32,16},{48,32},{64,48},{80,64},{96,80},{112,96},{1... | collective-permute-start | bytes 1572872 | tf_op jit(solution)/shard_map/ppermute | solution.py:199
  58.6 10.6 %collective-permute-start.9 = (bf16[512,512]{1,0:T(8,128)(2,1)S(1)}, bf16[512,512]{1,0:T(8,128)(2,1)S(1)}, u32[]{:S(2)}, u32[]{:S(2)}) collective-permute-start(bf16[512,512]{1,0:T(8,128)(2,1)S(1)} %collective-permute-done.8), channel_id=1, source_target_pairs={{0,16},{16,32},{32,48},{48,64},{64,80},{80,96},{96,112},{112,0},{1... | collective-permute-start | bytes 1572872 | tf_op jit(solution)/shard_map/ppermute | solution.py:196
  97.2 15.7 %collective-permute-start.11 = (f32[4,512]{1,0:T(4,128)S(1)}, f32[4,512]{1,0:T(4,128)S(1)}, u32[]{:S(2)}, u32[]{:S(2)}) collective-permute-start(f32[4,512]{1,0:T(4,128)S(1)} %pad_maximum_fusion.1), channel_id=1, source_target_pairs={{0,128},{1,129},{2,130},{3,131},{4,132},{5,133},{6,134},{7,135},{8... | collective-permute-start | bytes 24584 | tf_op jit(solution)/shard_map/ppermute | solution.py:249
  101.0 14.1 %collective-permute-start.12 = (bf16[2,512,128]{2,1,0:T(8,128)(2,1)S(1)}, bf16[2,512,128]{2,1,0:T(8,128)(2,1)S(1)}, u32[]{:S(2)}, u32[]{:S(2)}) collective-permute-start(bf16[2,512,128]{2,1,0:T(8,128)(2,1)S(1)} %convert_element_type.40), channel_id=1, source_target_pairs={{0,128},{1,129},{2,130},{3,131},{4,132},{5,133},{6,134},{7,135},{8... | collective-permute-start | bytes 786440 | tf_op jit(solution)/shard_map/ppermute | solution.py:248
  121.7 6.7 %collective-permute-start.13 = (bf16[2,32,4096]{2,1,0:T(8,128)(2,1)S(1)}, bf16[2,32,4096]{2,1,0:T(8,128)(2,1)}, u32[]{:S(2)}, u32[]{:S(2)}) collective-permute-start(bf16[2,32,4096]{2,1,0:T(8,128)(2,1)S(1)} %bitcast_convert_fusion), channel_id=1, source_target_pairs={{0,1},{1,0},{2,3},{3,2},{4,5},{5,4},{6,7},{7,6},{8,9},{9,8},{10,11... | collective-permute-start | bytes 1572872 | tf_op jit(solution)/shard_map/ppermute | solution.py:213
  129.6 7.6 %collective-permute-start.14 = (bf16[32,4096]{1,0:T(8,128)(2,1)S(1)}, bf16[32,4096]{1,0:T(8,128)(2,1)S(1)}, u32[]{:S(2)}, u32[]{:S(2)}) collective-permute-start(bf16[32,4096]{1,0:T(8,128)(2,1)S(1)} %bitcast_convert_fusion.1), channel_id=1, source_target_pairs={{0,2},{2,0},{1,3},{3,1},{4,6},{6,4},{5,7},{7,5},{8,10},{10,8},{9,1... | collective-permute-start | bytes 786440 | tf_op jit(solution)/shard_map/ppermute | solution.py:218

commit v11 on v10

--- a/solution.py
+++ b/solution.py
@@ -170,17 +170,19 @@
     )
 
 
+def place(result, piece, origin):
+    return lax.dynamic_update_slice(result, piece, (origin * piece.shape[0], 0))
+
+
 def gather_ring(block, axis):
     size = lax.axis_size(axis)
     here = lax.axis_index(axis)
-    pieces = [block]
+    result = jnp.zeros((size * block.shape[0], block.shape[1]), block.dtype)
+    result = place(result, block, here)
     for shift in range(1, size):
-        pieces.append(
-            lax.ppermute(block, axis, [(i, (i + shift) % size) for i in range(size)])
-        )
-    stacked = jnp.stack(pieces)
-    order = (here - jnp.arange(size, dtype=jnp.int32)) % size
-    return jnp.take(stacked, order, axis=0).reshape(size * block.shape[0], block.shape[1])
+        piece = lax.ppermute(block, axis, [(i, (i + shift) % size) for i in range(size)])
+        result = place(result, piece, (here - shift) % size)
+    return result
 
 
 def gather_both_ways(block, axis):
@@ -188,19 +190,17 @@
     here = lax.axis_index(axis)
     right = [(i, (i + 1) % size) for i in range(size)]
     left = [(i, (i - 1) % size) for i in range(size)]
-    pieces = [None] * size
-    pieces[0] = block
+    result = jnp.zeros((size * block.shape[0], block.shape[1]), block.dtype)
+    result = place(result, block, here)
     forward = block
     backward = block
     for step in range(1, size // 2 + 1):
         forward = lax.ppermute(forward, axis, right)
-        pieces[size - step] = forward
+        result = place(result, forward, (here - step) % size)
         if step < size - size // 2:
             backward = lax.ppermute(backward, axis, left)
-            pieces[step] = backward
-    stacked = jnp.stack(pieces)
-    order = (jnp.arange(size, dtype=jnp.int32) - here) % size
-    return jnp.take(stacked, order, axis=0).reshape(size * block.shape[0], block.shape[1])
+            result = place(result, backward, (here + step) % size)
+    return result
 
 
 def scatter_sum(partial):

time: 139 us -> 127 us (0.914)
  other arithmetic: 18.4 us -> 13.4 us
  waiting for transfers between devices: 41.4 us -> 37.2 us
  local copies, waits for them, and re-layouts: 21.9 us -> 18.7 us
    dynamic_update_slice x0 -> x12, local copies, waits for them, and re-layouts: none -> 6.77 us  [place(): return lax.dynamic_update_slice(result, piece, (origin * piece.shape[0], 0))]
    ppermute x4, waiting for transfers between devices: 33.4 us -> 27.3 us  [gather_both_ways(): forward = lax.ppermute(forward, axis, right)]
    gather x2 -> x0, local copies, waits for them, and re-layouts: 5.55 us -> none  [the longest x1 4.97 us: gather_both_ways(): jnp.take(stacked, order, axis=0)]
    unnamed x13 -> x7, local copies, waits for them, and re-layouts: 5.99 us -> 0.88 us
    select_n x4 -> x0, other arithmetic: 4.02 us -> none  [the longest x2 3.87 us: gather_both_ways(): jnp.take(stacked, order, axis=0)]
    broadcast_in_dim x1 -> x2, local copies, waits for them, and re-layouts: 0.07 us -> 2.24 us  [the longest x1 2.2 us: gather_both_ways(): result = jnp.zeros((size * block.shape[0], block.shape[1]), block.dtype)]
  transfers between devices with their start and end apart: 15 -> 15, of which waited for: 6 -> 7; matrix products, arithmetic and copies ran while one was open for 23% -> 19% of each run, Pallas kernels for 8% -> 8%
where the time goes in v11:
time: 127 us; the launch traced here: 126 us
  waiting for transfers between devices  37.2 us (29%)
  starting transfers between devices  27.9 us (22%)
  Pallas kernels  23.7 us (19%)
  local copies, waits for them, and re-layouts  18.7 us (15%)
  other arithmetic  13.4 us (11%)
  matrix products  4.65 us (4%)
    ppermute x4, waiting for transfers between devices, gather_both_ways(): forward = lax.ppermute(forward, axis, right)  27.3 us
    pallas_call x2, Pallas kernels, attend(): pl.pallas_call(attention_kernel, out_shape=(jax.ShapeDtypeStruct(stacked....  23.7 us
    ppermute x3, starting transfers between devices, gather_both_ways(): backward = lax.ppermute(backward, axis, left)  9.77 us
    ppermute x1, waiting for transfers between devices, scatter_sum(): got = lax.ppermute(give.astype(jnp.bfloat16), 'xl', [(0, 1), (1, 0)])  7.5 us
    dynamic_update_slice x12, local copies, waits for them, and re-layouts, place(): return lax.dynamic_update_slice(result, piece, (origin * piece.shape[0], 0))  6.77 us
    ppermute x1, starting transfers between devices, scatter_sum(): got = lax.ppermute(give.astype(jnp.bfloat16), 'core', [(0, 1), (1, 0)])  6.35 us
    ppermute x3, starting transfers between devices, gather_ring(): lax.ppermute(block, axis, [(i, (i + shift) % size) for i in range(size)])  5.81 us
    dot_general x1, matrix products, per_device(): partial = jnp.dot(attended, out_weight, preferred_element_type=jnp.float32)  4.65 us
  transfers between devices with their start and end apart: 15, of which 7 were waited for; matrix products, arithmetic and copies ran while one was open for 19% of the time, Pallas kernels for 8%

profile of v11, /device:TPU:1, one launch (start us, length us, event | category | flops | bytes accessed | tf_op | source)
XLA Modules:
  0.0 125.9 jit_solution(10503825044152110475)
XLA Ops:
  1.7 2.1 %collective-permute-start = (bf16[128,512]{1,0:T(8,128)(2,1)S(1)}, bf16[128,512]{1,0:T(8,128)(2,1)S(1)}, u32[]{:S(2)}, u32[]{:S(2)}) collective-permute-start(bf16[128,512]{1,0:T(8,128)(2,1)S(1)} %constant_dynamic-update-slice_fusion), channel_id=1, source_target_pairs={{0,4},{4,8},{8,12},{12,0},{1,5},{5,9},{9,13},{13,1},{2,6},{6,10},{... | collective-permute-start | bytes 393224 | tf_op jit(solution)/shard_map/ppermute | solution.py:183
  3.8 2.6 %collective-permute-start.1 = (bf16[128,512]{1,0:T(8,128)(2,1)S(1)}, bf16[128,512]{1,0:T(8,128)(2,1)S(1)}, u32[]{:S(2)}, u32[]{:S(2)}) collective-permute-start(bf16[128,512]{1,0:T(8,128)(2,1)S(1)} %constant_dynamic-update-slice_fusion), channel_id=1, source_target_pairs={{0,8},{4,12},{8,0},{12,4},{1,9},{5,13},{9,1},{13,5},{2,10},{6,14},... | collective-permute-start | bytes 393224 | tf_op jit(solution)/shard_map/ppermute | solution.py:183
  8.7 1.3 %collective-permute-start.10 = (bf16[2,512,128]{2,1,0:T(8,128)(2,1)S(1)}, bf16[2,512,128]{2,1,0:T(8,128)(2,1)}, u32[]{:S(2)}, u32[]{:S(2)}) collective-permute-start(bf16[2,512,128]{2,1,0:T(8,128)(2,1)S(1)} %bitcast.77), channel_id=1, source_target_pairs={{128,0},{129,1},{130,2},{131,3},{132,4},{133,5},{134,6},{135,7},{1... | collective-permute-start | bytes 786440 | tf_op jit(solution)/shard_map/ppermute | solution.py:235
  16.1 1.7 %collective-permute-start.3 = (bf16[512,512]{1,0:T(8,128)(2,1)S(1)}, bf16[512,512]{1,0:T(8,128)(2,1)S(1)}, u32[]{:S(2)}, u32[]{:S(2)}) collective-permute-start(bf16[512,512]{1,0:T(8,128)(2,1)S(1)} %constant_dynamic-update-slice_fusion.10), channel_id=1, source_target_pairs={{0,16},{16,32},{32,48},{48,64},{64,80},{80,96},{96,112},{112,0},{1... | collective-permute-start | bytes 1572872 | tf_op jit(solution)/shard_map/ppermute | solution.py:198
  18.4 4.0 %collective-permute-start.4 = (bf16[512,512]{1,0:T(8,128)(2,1)S(1)}, bf16[512,512]{1,0:T(8,128)(2,1)S(1)}, u32[]{:S(2)}, u32[]{:S(2)}) collective-permute-start(bf16[512,512]{1,0:T(8,128)(2,1)S(1)} %constant_dynamic-update-slice_fusion.10), channel_id=1, source_target_pairs={{0,112},{16,0},{32,16},{48,32},{64,48},{80,64},{96,80},{112,96},{1... | collective-permute-start | bytes 1572872 | tf_op jit(solution)/shard_map/ppermute | solution.py:201
  23.1 9.4 %collective-permute-done.3 = bf16[512,512]{1,0:T(8,128)(2,1)S(1)} collective-permute-done((bf16[512,512]{1,0:T(8,128)(2,1)S(1)}, bf16[512,512]{1,0:T(8,128)(2,1)S(1)}, u32[]{:S(2)}, u32[]{:S(2)}) %collective-permute-start.3) | collective-permute-done | bytes 524320 | tf_op jit(solution)/shard_map/ppermute | solution.py:198
  32.5 3.0 %collective-permute-start.6 = (bf16[512,512]{1,0:T(8,128)(2,1)S(1)}, bf16[512,512]{1,0:T(8,128)(2,1)S(1)}, u32[]{:S(2)}, u32[]{:S(2)}) collective-permute-start(bf16[512,512]{1,0:T(8,128)(2,1)S(1)} %collective-permute-done.4), channel_id=1, source_target_pairs={{0,112},{16,0},{32,16},{48,32},{64,48},{80,64},{96,80},{112,96},{1... | collective-permute-start | bytes 1572872 | tf_op jit(solution)/shard_map/ppermute | solution.py:201
  35.6 9.3 %collective-permute-done.5 = bf16[512,512]{1,0:T(8,128)(2,1)S(1)} collective-permute-done((bf16[512,512]{1,0:T(8,128)(2,1)S(1)}, bf16[512,512]{1,0:T(8,128)(2,1)S(1)}, u32[]{:S(2)}, u32[]{:S(2)}) %collective-permute-start.5) | collective-permute-done | bytes 524320 | tf_op jit(solution)/shard_map/ppermute | solution.py:198
  46.9 2.2 %broadcast_in_dim.97 = bf16[4096,512]{1,0:T(8,128)(2,1)} broadcast(bf16[]{:T(256)} %constant.155.clone.1), dimensions={} | broadcast | bytes 4194306 | tf_op jit(solution)/shard_map/broadcast_in_dim | solution.py:193
  50.0 2.7 %collective-permute-start.8 = (bf16[512,512]{1,0:T(8,128)(2,1)S(1)}, bf16[512,512]{1,0:T(8,128)(2,1)S(1)}, u32[]{:S(2)}, u32[]{:S(2)}) collective-permute-start(bf16[512,512]{1,0:T(8,128)(2,1)S(1)} %collective-permute-done.6), channel_id=1, source_target_pairs={{0,112},{16,0},{32,16},{48,32},{64,48},{80,64},{96,80},{112,96},{1... | collective-permute-start | bytes 1572872 | tf_op jit(solution)/shard_map/ppermute | solution.py:201
  53.5 2.9 %collective-permute-done.7 = bf16[512,512]{1,0:T(8,128)(2,1)S(1)} collective-permute-done((bf16[512,512]{1,0:T(8,128)(2,1)S(1)}, bf16[512,512]{1,0:T(8,128)(2,1)S(1)}, u32[]{:S(2)}, u32[]{:S(2)}) %collective-permute-start.7) | collective-permute-done | bytes 524320 | tf_op jit(solution)/shard_map/ppermute | solution.py:198
  61.4 5.7 %collective-permute-done.9 = bf16[512,512]{1,0:T(8,128)(2,1)S(1)} collective-permute-done((bf16[512,512]{1,0:T(8,128)(2,1)S(1)}, bf16[512,512]{1,0:T(8,128)(2,1)S(1)}, u32[]{:S(2)}, u32[]{:S(2)}) %collective-permute-start.9) | collective-permute-done | bytes 524320 | tf_op jit(solution)/shard_map/ppermute | solution.py:198
  67.9 13.3 %shard_map.74 = (f32[2,512,128]{2,1,0:T(8,128)}, f32[2,512,1]{2,1,0:T(8,128)}, f32[2,512,1]{2,1,0:T(8,128)}) custom-call(s32[2,4]{1,0:T(2,128)} %pad_add_fusion.3.table_ref, s32[2,8]{1,0:T(2,128)} %pad.8.meta_ref, bf16[2,512,128]{2,1,0:T(8,128)(2,1)} %collective-permute-done.10.q_ref, bf16[4096,512]{1,0:T(8,128)(2,1)} %constant_dynamic-update-slice_fusion.2.k_ref.v_ref, ...), custom_call_target="tpu_custom_call" | custom-call | tf_op jit(solution)/shard_map/pallas_call | solution.py:120
  81.2 1.2 reduce
  82.5 1.3 reduce.1
  83.7 1.3 %collective-permute-start.11 = (f32[4,512]{1,0:T(4,128)S(1)}, f32[4,512]{1,0:T(4,128)S(1)}, u32[]{:S(2)}, u32[]{:S(2)}) collective-permute-start(f32[4,512]{1,0:T(4,128)S(1)} %pad_maximum_fusion), channel_id=1, source_target_pairs={{0,128},{1,129},{2,130},{3,131},{4,132},{5,133},{6,134},{7,135},{8... | collective-permute-start | bytes 24584 | tf_op jit(solution)/shard_map/ppermute | solution.py:249
  87.5 1.5 %collective-permute-start.12 = (bf16[2,512,128]{2,1,0:T(8,128)(2,1)S(1)}, bf16[2,512,128]{2,1,0:T(8,128)(2,1)S(1)}, u32[]{:S(2)}, u32[]{:S(2)}) collective-permute-start(bf16[2,512,128]{2,1,0:T(8,128)(2,1)S(1)} %convert_element_type.40), channel_id=1, source_target_pairs={{0,128},{1,129},{2,130},{3,131},{4,132},{5,133},{6,134},{7,135},{8... | collective-permute-start | bytes 786440 | tf_op jit(solution)/shard_map/ppermute | solution.py:248
  89.0 10.4 %shard_map.73 = (f32[2,512,128]{2,1,0:T(8,128)}, f32[2,512,1]{2,1,0:T(8,128)}, f32[2,512,1]{2,1,0:T(8,128)}) custom-call(s32[2,4]{1,0:T(2,128)} %pad_add_fusion.2.table_ref, s32[2,8]{1,0:T(2,128)} %pad.7.meta_ref, bf16[2,512,128]{2,1,0:T(8,128)(2,1)} %bitcast.78, bf16[4096,512]{1,0:T(8,128)(2,1)} %constant_dynamic-update-slice_fusion.2.k_ref.v_ref, ...), custom_call_target="tpu_custom_call" | custom-call | tf_op jit(solution)/shard_map/pallas_call | solution.py:120
  99.9 1.8 %fusion.8 = (f32[2,512]{1,0:T(2,128)S(1)}, f32[2,512]{1,0:T(2,128)S(1)}, f32[2,512]{1,0:T(2,128)S(1)}) fusion(f32[2,512,1]{2,1,0:T(8,128)} %get-tuple-element.19, f32[2,512,1]{2,1,0:T(8,128)S(1)} %copy.94, f32[2,512,1]{2,1,0:T(8,128)S(1)} %copy.96, f32[2,512,1]{2,1,0:T(8,128)} %get-tuple-element.24), kind=kLoop, calls=%fused_computation.20 | loop fusion | flops 6144 | bytes 28672 | tf_op jit(solution)/shard_map/exp | solution.py:160
  101.6 1.5 %divide_convert_fusion = bf16[2,512,128]{2,1,0:T(8,128)(2,1)S(1)} fusion(bf16[2,512,128]{2,1,0:T(8,128)(2,1)S(1)} %collective-permute-done.12, f32[2,512,128]{2,1,0:T(8,128)} %get-tuple-element.18, f32[2,512]{1,0:T(2,128)S(1)} %get-tuple-element.48, f32[2,512]{1,0:T(2,128)S(1)} %get-tuple-element.49, f32[2,512]{1,0:T(2,128)S(1)} %get-tuple-element.47, ...), kind=kLoop, calls=%fused_computation.17 | loop fusion | flops 917504 | bytes 1060865 | tf_op jit(solution)/shard_map/convert_element_type | solution.py:165
  103.5 4.7 %fusion = f32[2,2,32,4096]{3,2,1,0:T(8,128)S(1)} fusion(bf16[2,2,32,1024]{3,2,1,0:T(8,128)(2,1)S(1)} %dot_general.5, bf16[1024,4096]{1,0:T(8,128)(2,1)} %param.18), kind=kOutput, calls=%fused_computation.4 | convolution fusion | flops 1073741824 | bytes 10747904 | tf_op jit(solution)/shard_map/dot_general | solution.py:260
  108.3 6.4 %collective-permute-start.13 = (bf16[2,32,4096]{2,1,0:T(8,128)(2,1)S(1)}, bf16[2,32,4096]{2,1,0:T(8,128)(2,1)}, u32[]{:S(2)}, u32[]{:S(2)}) collective-permute-start(bf16[2,32,4096]{2,1,0:T(8,128)(2,1)S(1)} %bitcast_convert_fusion), channel_id=1, source_target_pairs={{0,1},{1,0},{2,3},{3,2},{4,5},{5,4},{6,7},{7,6},{8,9},{9,8},{10,11... | collective-permute-start | bytes 1572872 | tf_op jit(solution)/shard_map/ppermute | solution.py:213
  114.6 1.7 %collective-permute-done.13 = bf16[2,32,4096]{2,1,0:T(8,128)(2,1)} collective-permute-done((bf16[2,32,4096]{2,1,0:T(8,128)(2,1)S(1)}, bf16[2,32,4096]{2,1,0:T(8,128)(2,1)}, u32[]{:S(2)}, u32[]{:S(2)}) %collective-permute-start.13) | collective-permute-done | bytes 524320 | tf_op jit(solution)/shard_map/ppermute | solution.py:213
  117.6 7.5 %collective-permute-done.14 = bf16[32,4096]{1,0:T(8,128)(2,1)S(1)} collective-permute-done((bf16[32,4096]{1,0:T(8,128)(2,1)S(1)}, bf16[32,4096]{1,0:T(8,128)(2,1)S(1)}, u32[]{:S(2)}, u32[]{:S(2)}) %collective-permute-start.14) | collective-permute-done | bytes 262176 | tf_op jit(solution)/shard_map/ppermute | solution.py:218
  (104 shorter events, 26.0 us)
Async XLA Ops:
  0.0 35.6 %copy-start.1 = (s32[8]{0:T(128)S(1)}, s32[8]{0:T(128)}, u32[]{:S(2)}) copy-start(s32[8]{0:T(128)} %param.19) | copy-start | bytes 100
  0.0 44.9 %copy-start.2 = (s32[8]{0:T(128)S(1)}, s32[8]{0:T(128)}, u32[]{:S(2)}) copy-start(s32[8]{0:T(128)} %param.20) | copy-start | bytes 100
  1.7 14.3 %collective-permute-start = (bf16[128,512]{1,0:T(8,128)(2,1)S(1)}, bf16[128,512]{1,0:T(8,128)(2,1)S(1)}, u32[]{:S(2)}, u32[]{:S(2)}) collective-permute-start(bf16[128,512]{1,0:T(8,128)(2,1)S(1)} %constant_dynamic-update-slice_fusion), channel_id=1, source_target_pairs={{0,4},{4,8},{8,12},{12,0},{1,5},{5,9},{9,13},{13,1},{2,6},{6,10},{... | collective-permute-start | bytes 393224 | tf_op jit(solution)/shard_map/ppermute | solution.py:183
  3.8 12.1 %collective-permute-start.1 = (bf16[128,512]{1,0:T(8,128)(2,1)S(1)}, bf16[128,512]{1,0:T(8,128)(2,1)S(1)}, u32[]{:S(2)}, u32[]{:S(2)}) collective-permute-start(bf16[128,512]{1,0:T(8,128)(2,1)S(1)} %constant_dynamic-update-slice_fusion), channel_id=1, source_target_pairs={{0,8},{4,12},{8,0},{12,4},{1,9},{5,13},{9,1},{13,5},{2,10},{6,14},... | collective-permute-start | bytes 393224 | tf_op jit(solution)/shard_map/ppermute | solution.py:183
  6.5 9.6 %collective-permute-start.2 = (bf16[128,512]{1,0:T(8,128)(2,1)S(1)}, bf16[128,512]{1,0:T(8,128)(2,1)S(1)}, u32[]{:S(2)}, u32[]{:S(2)}) collective-permute-start(bf16[128,512]{1,0:T(8,128)(2,1)S(1)} %constant_dynamic-update-slice_fusion), channel_id=1, source_target_pairs={{0,12},{4,0},{8,4},{12,8},{1,13},{5,1},{9,5},{13,9},{2,14},{6,2},{... | collective-permute-start | bytes 393224 | tf_op jit(solution)/shard_map/ppermute | solution.py:183
  8.7 40.4 %copy-start = (bf16[128,2,4,128]{3,0,2,1:T(8,128)(2,1)}, bf16[128,2,4,128]{3,0,2,1:T(8,128)(2,1)S(1)}, u32[]{:S(2)}) copy-start(bf16[128,2,4,128]{3,0,2,1:T(8,128)(2,1)S(1)} %copy.84) | copy-start | bytes 786436
  8.7 59.2 %collective-permute-start.10 = (bf16[2,512,128]{2,1,0:T(8,128)(2,1)S(1)}, bf16[2,512,128]{2,1,0:T(8,128)(2,1)}, u32[]{:S(2)}, u32[]{:S(2)}) collective-permute-start(bf16[2,512,128]{2,1,0:T(8,128)(2,1)S(1)} %bitcast.77), channel_id=1, source_target_pairs={{128,0},{129,1},{130,2},{131,3},{132,4},{133,5},{134,6},{135,7},{1... | collective-permute-start | bytes 786440 | tf_op jit(solution)/shard_map/ppermute | solution.py:235
  16.1 16.4 %collective-permute-start.3 = (bf16[512,512]{1,0:T(8,128)(2,1)S(1)}, bf16[512,512]{1,0:T(8,128)(2,1)S(1)}, u32[]{:S(2)}, u32[]{:S(2)}) collective-permute-start(bf16[512,512]{1,0:T(8,128)(2,1)S(1)} %constant_dynamic-update-slice_fusion.10), channel_id=1, source_target_pairs={{0,16},{16,32},{32,48},{48,64},{64,80},{80,96},{96,112},{112,0},{1... | collective-permute-start | bytes 1572872 | tf_op jit(solution)/shard_map/ppermute | solution.py:198
  18.4 14.1 %collective-permute-start.4 = (bf16[512,512]{1,0:T(8,128)(2,1)S(1)}, bf16[512,512]{1,0:T(8,128)(2,1)S(1)}, u32[]{:S(2)}, u32[]{:S(2)}) collective-permute-start(bf16[512,512]{1,0:T(8,128)(2,1)S(1)} %constant_dynamic-update-slice_fusion.10), channel_id=1, source_target_pairs={{0,112},{16,0},{32,16},{48,32},{64,48},{80,64},{96,80},{112,96},{1... | collective-permute-start | bytes 1572872 | tf_op jit(solution)/shard_map/ppermute | solution.py:201
  32.4 12.5 %collective-permute-start.5 = (bf16[512,512]{1,0:T(8,128)(2,1)S(1)}, bf16[512,512]{1,0:T(8,128)(2,1)S(1)}, u32[]{:S(2)}, u32[]{:S(2)}) collective-permute-start(bf16[512,512]{1,0:T(8,128)(2,1)S(1)} %collective-permute-done.3), channel_id=1, source_target_pairs={{0,16},{16,32},{32,48},{48,64},{64,80},{80,96},{96,112},{112,0},{1... | collective-permute-start | bytes 1572872 | tf_op jit(solution)/shard_map/ppermute | solution.py:198
  32.5 17.4 %collective-permute-start.6 = (bf16[512,512]{1,0:T(8,128)(2,1)S(1)}, bf16[512,512]{1,0:T(8,128)(2,1)S(1)}, u32[]{:S(2)}, u32[]{:S(2)}) collective-permute-start(bf16[512,512]{1,0:T(8,128)(2,1)S(1)} %collective-permute-done.4), channel_id=1, source_target_pairs={{0,112},{16,0},{32,16},{48,32},{64,48},{80,64},{96,80},{112,96},{1... | collective-permute-start | bytes 1572872 | tf_op jit(solution)/shard_map/ppermute | solution.py:201
  44.9 11.5 %collective-permute-start.7 = (bf16[512,512]{1,0:T(8,128)(2,1)S(1)}, bf16[512,512]{1,0:T(8,128)(2,1)S(1)}, u32[]{:S(2)}, u32[]{:S(2)}) collective-permute-start(bf16[512,512]{1,0:T(8,128)(2,1)S(1)} %collective-permute-done.5), channel_id=1, source_target_pairs={{0,16},{16,32},{32,48},{48,64},{64,80},{80,96},{96,112},{112,0},{1... | collective-permute-start | bytes 1572872 | tf_op jit(solution)/shard_map/ppermute | solution.py:198
  50.0 10.5 %collective-permute-start.8 = (bf16[512,512]{1,0:T(8,128)(2,1)S(1)}, bf16[512,512]{1,0:T(8,128)(2,1)S(1)}, u32[]{:S(2)}, u32[]{:S(2)}) collective-permute-start(bf16[512,512]{1,0:T(8,128)(2,1)S(1)} %collective-permute-done.6), channel_id=1, source_target_pairs={{0,112},{16,0},{32,16},{48,32},{64,48},{80,64},{96,80},{112,96},{1... | collective-permute-start | bytes 1572872 | tf_op jit(solution)/shard_map/ppermute | solution.py:201
  56.4 10.6 %collective-permute-start.9 = (bf16[512,512]{1,0:T(8,128)(2,1)S(1)}, bf16[512,512]{1,0:T(8,128)(2,1)S(1)}, u32[]{:S(2)}, u32[]{:S(2)}) collective-permute-start(bf16[512,512]{1,0:T(8,128)(2,1)S(1)} %collective-permute-done.7), channel_id=1, source_target_pairs={{0,16},{16,32},{32,48},{48,64},{64,80},{80,96},{96,112},{112,0},{1... | collective-permute-start | bytes 1572872 | tf_op jit(solution)/shard_map/ppermute | solution.py:198
  83.7 15.7 %collective-permute-start.11 = (f32[4,512]{1,0:T(4,128)S(1)}, f32[4,512]{1,0:T(4,128)S(1)}, u32[]{:S(2)}, u32[]{:S(2)}) collective-permute-start(f32[4,512]{1,0:T(4,128)S(1)} %pad_maximum_fusion), channel_id=1, source_target_pairs={{0,128},{1,129},{2,130},{3,131},{4,132},{5,133},{6,134},{7,135},{8... | collective-permute-start | bytes 24584 | tf_op jit(solution)/shard_map/ppermute | solution.py:249
  87.5 14.1 %collective-permute-start.12 = (bf16[2,512,128]{2,1,0:T(8,128)(2,1)S(1)}, bf16[2,512,128]{2,1,0:T(8,128)(2,1)S(1)}, u32[]{:S(2)}, u32[]{:S(2)}) collective-permute-start(bf16[2,512,128]{2,1,0:T(8,128)(2,1)S(1)} %convert_element_type.40), channel_id=1, source_target_pairs={{0,128},{1,129},{2,130},{3,131},{4,132},{5,133},{6,134},{7,135},{8... | collective-permute-start | bytes 786440 | tf_op jit(solution)/shard_map/ppermute | solution.py:248
  108.3 8.0 %collective-permute-start.13 = (bf16[2,32,4096]{2,1,0:T(8,128)(2,1)S(1)}, bf16[2,32,4096]{2,1,0:T(8,128)(2,1)}, u32[]{:S(2)}, u32[]{:S(2)}) collective-permute-start(bf16[2,32,4096]{2,1,0:T(8,128)(2,1)S(1)} %bitcast_convert_fusion), channel_id=1, source_target_pairs={{0,1},{1,0},{2,3},{3,2},{4,5},{5,4},{6,7},{7,6},{8,9},{9,8},{10,11... | collective-permute-start | bytes 1572872 | tf_op jit(solution)/shard_map/ppermute | solution.py:213
  117.5 7.6 %collective-permute-start.14 = (bf16[32,4096]{1,0:T(8,128)(2,1)S(1)}, bf16[32,4096]{1,0:T(8,128)(2,1)S(1)}, u32[]{:S(2)}, u32[]{:S(2)}) collective-permute-start(bf16[32,4096]{1,0:T(8,128)(2,1)S(1)} %bitcast_convert_fusion.1), channel_id=1, source_target_pairs={{0,2},{2,0},{1,3},{3,1},{4,6},{6,4},{5,7},{7,5},{8,10},{10,8},{9,1... | collective-permute-start | bytes 786440 | tf_op jit(solution)/shard_map/ppermute | solution.py:218

commit v12 on v11

--- a/solution.py
+++ b/solution.py
@@ -78,6 +78,118 @@
         update(allowed[None])
 
 
+def piece_kernel(meta_ref, q_ref, k_ref, v_ref, acc_in, peak_in, total_in,
+                 acc_ref, peak_ref, total_ref):
+    i = pl.program_id(0)
+    needed = meta_ref[i, 0]
+    full = meta_ref[i, 1]
+    is_retrieval = meta_ref[i, 2]
+    sink = meta_ref[i, 3]
+    window = meta_ref[i, 4]
+    row_base = meta_ref[i, 5]
+    key_base = meta_ref[i, 6]
+    rows = q_ref.shape[1] // GROUP
+    width = k_ref.shape[0]
+    acc_ref[...] = acc_in[...]
+    peak_ref[...] = peak_in[...]
+    total_ref[...] = total_in[...]
+
+    def update(allowed):
+        scores = lax.dot_general(
+            q_ref[0], k_ref[...], (((1,), (1,)), ((), ())), preferred_element_type=jnp.float32
+        ) * HD ** (-0.5)
+        old_peak = peak_ref[0]
+        if allowed is None:
+            new_peak = jnp.maximum(old_peak, jnp.max(scores, axis=-1, keepdims=True))
+            weights = jnp.exp(scores - new_peak)
+        else:
+            scores = scores.reshape(GROUP, rows, width)
+            block_peak = jnp.max(
+                jnp.where(allowed, scores, NEGATIVE), axis=-1, keepdims=True
+            ).reshape(GROUP * rows, 1)
+            new_peak = jnp.maximum(old_peak, block_peak)
+            weights = jnp.where(
+                allowed, jnp.exp(scores - new_peak.reshape(GROUP, rows, 1)), 0.0
+            ).reshape(GROUP * rows, width)
+        rescale = jnp.exp(old_peak - new_peak)
+        total_ref[0] = rescale * total_ref[0] + jnp.sum(weights, axis=-1, keepdims=True)
+        acc_ref[0] = rescale * acc_ref[0] + jnp.dot(
+            weights.astype(jnp.bfloat16), v_ref[...], preferred_element_type=jnp.float32
+        )
+        peak_ref[0] = new_peak
+
+    @pl.when((needed == 1) & (full == 1))
+    def _():
+        update(None)
+
+    @pl.when((needed == 1) & (full == 0))
+    def _():
+        row = lax.broadcasted_iota(jnp.int32, (rows, width), 0)
+        col = lax.broadcasted_iota(jnp.int32, (rows, width), 1)
+        later_minus_earlier = (row - col) + (row_base - key_base)
+        reach = jnp.where(is_retrieval == 1, jnp.int32(2**30), window)
+        allowed = (later_minus_earlier >= 0) & (
+            (later_minus_earlier < reach) | (col + key_base < sink)
+        )
+        update(allowed[None])
+
+
+def piece_meta(row_bases, key_base, width, rows, roles, sinks, windows):
+    last_key = key_base + width - 1
+    last_rows = row_bases + rows - 1
+    retrieval = roles == 1
+    needed = (key_base <= last_rows) & (
+        retrieval | (last_key >= row_bases - windows + 1) | (key_base < sinks)
+    )
+    full = (last_key <= row_bases) & (
+        retrieval | (last_key < sinks) | (last_rows - key_base < windows)
+    )
+    zeros = jnp.zeros_like(row_bases)
+    return jnp.stack(
+        [needed.astype(jnp.int32), full.astype(jnp.int32), roles, sinks, windows,
+         row_bases, zeros + key_base, zeros],
+        axis=1,
+    ).astype(jnp.int32)
+
+
+def attend_piece(meta, stacked, piece, state):
+    count, stack_rows, _ = stacked.shape
+    local_heads = piece.shape[1] // (2 * HD)
+    width = piece.shape[0]
+    acc, peak, total = state
+    return pl.pallas_call(
+        piece_kernel,
+        out_shape=(
+            jax.ShapeDtypeStruct(acc.shape, jnp.float32),
+            jax.ShapeDtypeStruct(peak.shape, jnp.float32),
+            jax.ShapeDtypeStruct(total.shape, jnp.float32),
+        ),
+        grid_spec=pltpu.PrefetchScalarGridSpec(
+            num_scalar_prefetch=1,
+            grid=(count,),
+            in_specs=[
+                pl.BlockSpec((1, stack_rows, HD), lambda i, m: (i, 0, 0)),
+                pl.BlockSpec((width, HD), lambda i, m: (0, i % local_heads)),
+                pl.BlockSpec((width, HD), lambda i, m: (0, local_heads + i % local_heads)),
+                pl.BlockSpec((1, stack_rows, HD), lambda i, m: (i, 0, 0)),
+                pl.BlockSpec((1, stack_rows, 1), lambda i, m: (i, 0, 0)),
+                pl.BlockSpec((1, stack_rows, 1), lambda i, m: (i, 0, 0)),
+            ],
+            out_specs=(
+                pl.BlockSpec((1, stack_rows, HD), lambda i, m: (i, 0, 0)),
+                pl.BlockSpec((1, stack_rows, 1), lambda i, m: (i, 0, 0)),
+                pl.BlockSpec((1, stack_rows, 1), lambda i, m: (i, 0, 0)),
+            ),
+        ),
+        compiler_params=pltpu.CompilerParams(dimension_semantics=("arbitrary",)),
+        cost_estimate=pl.CostEstimate(
+            flops=4 * count * stack_rows * width * HD,
+            transcendentals=count * stack_rows * width,
+            bytes_accessed=2 * piece.size + 2 * stacked.size + 8 * acc.size,
+        ),
+    )(meta, stacked, piece, piece, acc, peak, total)
+
+
 def block_table(row_base, row_count, key_offset, key_count, roles, sinks, windows):
     blocks = key_count // KEY_BLOCK
     first = key_offset + jnp.arange(blocks, dtype=jnp.int32) * KEY_BLOCK
@@ -235,23 +347,62 @@
     partner_queries = lax.ppermute(stack_heads(queries, local_heads), "xh", [(1, 0)])
     both = jnp.concatenate([key_states, value_states], axis=1)
     both = gather_ring(both, "y")
-    both = gather_both_ways(both, "z")
-    key_offset = half * both.shape[0]
-    table, meta = block_table(
-        partner * row_count, row_count, key_offset, both.shape[0],
-        roles_here, sinks_here, windows_here,
-    )
-    acc_p, peak_p, total_p = attend(partner_queries, both, table, meta)
+    stacked = jnp.concatenate([partner_queries, stack_heads(queries, local_heads)], axis=0)
+    row_bases = jnp.concatenate(
+        [jnp.broadcast_to(partner * row_count, (local_heads,)),
+         jnp.broadcast_to(ctx * row_count, (local_heads,))]
+    ).astype(jnp.int32)
+    roles2 = jnp.concatenate([roles_here, roles_here])
+    sinks2 = jnp.concatenate([sinks_here, sinks_here])
+    windows2 = jnp.concatenate([windows_here, windows_here])
+    width = both.shape[0]
+    key_start = half * width * lax.axis_size("z")
+    heads2 = 2 * local_heads
+    state = (
+        jnp.zeros((heads2, GROUP * row_count, HD), jnp.float32),
+        jnp.full((heads2, GROUP * row_count, 1), NEGATIVE, jnp.float32),
+        jnp.zeros((heads2, GROUP * row_count, 1), jnp.float32),
+    )
+
+    def take(state, piece, origin):
+        meta = piece_meta(
+            row_bases, key_start + origin * width, width, row_count, roles2, sinks2, windows2
+        )
+        return attend_piece(meta, stacked, piece, state)
+
+    size = lax.axis_size("z")
+    here = lax.axis_index("z")
+    right = [(i, (i + 1) % size) for i in range(size)]
+    left = [(i, (i - 1) % size) for i in range(size)]
+    steps = size // 2
+    forward = lax.ppermute(both, "z", right)
+    backward = lax.ppermute(both, "z", left)
+    state = take(state, both, here)
+    state, forward, backward = lax.optimization_barrier((state, forward, backward))
+    for step in range(1, steps + 1):
+        sends_back = step + 1 < size - steps
+        if step < steps:
+            next_forward = lax.ppermute(forward, "z", right)
+        if sends_back:
+            next_backward = lax.ppermute(backward, "z", left)
+        state = take(state, forward, (here - step) % size)
+        if step < size - steps:
+            state = take(state, backward, (here + step) % size)
+        if step < steps:
+            forward = next_forward
+            if sends_back:
+                backward = next_backward
+                state, forward, backward = lax.optimization_barrier((state, forward, backward))
+            else:
+                state, forward = lax.optimization_barrier((state, forward))
+    acc_all, peak_all, total_all = state
+    acc_p, peak_p, total_p = acc_all[:local_heads], peak_all[:local_heads], total_all[:local_heads]
+    own = (acc_all[local_heads:], peak_all[local_heads:], total_all[local_heads:])
     stats_p = jnp.concatenate(
         [peak_p.reshape(local_heads, -1), total_p.reshape(local_heads, -1)], axis=0
     )
     acc_p = lax.ppermute(acc_p.astype(jnp.bfloat16), "xh", [(0, 1)])
     stats_p = lax.ppermute(stats_p, "xh", [(0, 1)])
-    table, meta = block_table(
-        ctx * row_count, row_count, key_offset, both.shape[0],
-        roles_here, sinks_here, windows_here,
-    )
-    own = attend(stack_heads(queries, local_heads), both, table, meta)
     received = half == 1
     peak_b = jnp.where(received, stats_p[:local_heads], NEGATIVE)[:, :, None]
     total_b = jnp.where(received, stats_p[local_heads:], 0.0)[:, :, None]

time: 127 us -> 135 us (1.063)
  the two profiles are of different devices: /device:TPU:1 before, /device:TPU:166 now
where the time goes in v12:
time: 135 us; the launch traced here: 133 us
  Pallas kernels  52.8 us (39%)
  waiting for transfers between devices  25.9 us (19%)
  starting transfers between devices  21.2 us (16%)
  local copies, waits for them, and re-layouts  20.8 us (15%)
  other arithmetic  7.5 us (6%)
  matrix products  4.64 us (3%)
    pallas_call x8, Pallas kernels, attend_piece(): pl.pallas_call(piece_kernel, out_shape=(jax.ShapeDtypeStruct(acc.shape, j...  52.8 us
    ppermute x1, waiting for transfers between devices, per_device(): stats_p = lax.ppermute(stats_p, 'xh', [(0, 1)])  9.97 us
    ppermute x1, waiting for transfers between devices, scatter_sum(): got = lax.ppermute(give.astype(jnp.bfloat16), 'xl', [(0, 1), (1, 0)])  8.33 us
    another operation x37, local copies, waits for them, and re-layouts, piece_meta(): jnp.stack([needed.astype(jnp.int32), full.astype(jnp.int32), roles, sinks...  7.3 us
    ppermute x3, starting transfers between devices, gather_ring(): lax.ppermute(block, axis, [(i, (i + shift) % size) for i in range(size)])  5.83 us
    ppermute x1, waiting for transfers between devices, per_device(): acc_p = lax.ppermute(acc_p.astype(jnp.bfloat16), 'xh', [(0, 1)])  5.65 us
    dot_general x1, matrix products, per_device(): partial = jnp.dot(attended, out_weight, preferred_element_type=jnp.float32)  4.64 us
    ppermute x2, starting transfers between devices, per_device(): next_backward = lax.ppermute(backward, 'z', left)  3.97 us
  transfers between devices with their start and end apart: 15, of which 4 were waited for; matrix products, arithmetic and copies ran while one was open for 15% of the time, Pallas kernels for 35%

profile of v12, /device:TPU:166, one launch (start us, length us, event | category | flops | bytes accessed | tf_op | source)
XLA Modules:
  0.0 133.3 jit_solution(13137214322532948156)
XLA Ops:
  1.7 1.6 %collective-permute-start.1 = (bf16[128,512]{1,0:T(8,128)(2,1)S(1)}, bf16[128,512]{1,0:T(8,128)(2,1)S(1)}, u32[]{:S(2)}, u32[]{:S(2)}) collective-permute-start(bf16[128,512]{1,0:T(8,128)(2,1)S(1)} %constant_dynamic-update-slice_fusion), channel_id=1, source_target_pairs={{0,4},{4,8},{8,12},{12,0},{1,5},{5,9},{9,13},{13,1},{2,6},{6,10},{... | collective-permute-start | bytes 393224 | tf_op jit(solution)/shard_map/ppermute | solution.py:295
  3.3 2.9 %collective-permute-start.2 = (bf16[128,512]{1,0:T(8,128)(2,1)S(1)}, bf16[128,512]{1,0:T(8,128)(2,1)S(1)}, u32[]{:S(2)}, u32[]{:S(2)}) collective-permute-start(bf16[128,512]{1,0:T(8,128)(2,1)S(1)} %constant_dynamic-update-slice_fusion), channel_id=1, source_target_pairs={{0,8},{4,12},{8,0},{12,4},{1,9},{5,13},{9,1},{13,5},{2,10},{6,14},... | collective-permute-start | bytes 393224 | tf_op jit(solution)/shard_map/ppermute | solution.py:295
  6.2 1.3 %collective-permute-start.3 = (bf16[128,512]{1,0:T(8,128)(2,1)S(1)}, bf16[128,512]{1,0:T(8,128)(2,1)S(1)}, u32[]{:S(2)}, u32[]{:S(2)}) collective-permute-start(bf16[128,512]{1,0:T(8,128)(2,1)S(1)} %constant_dynamic-update-slice_fusion), channel_id=1, source_target_pairs={{0,12},{4,0},{8,4},{12,8},{1,13},{5,1},{9,5},{13,9},{2,14},{6,2},{... | collective-permute-start | bytes 393224 | tf_op jit(solution)/shard_map/ppermute | solution.py:295
  8.7 3.3 %collective-permute-start = (bf16[2,512,128]{2,1,0:T(8,128)(2,1)S(1)}, bf16[2,512,128]{2,1,0:T(8,128)(2,1)S(1)}, u32[]{:S(2)}, u32[]{:S(2)}) collective-permute-start(bf16[2,512,128]{2,1,0:T(8,128)(2,1)S(1)} %bitcast.74), channel_id=1, source_target_pairs={{128,0},{129,1},{130,2},{131,3},{132,4},{133,5},{134,6},{135,7},{1... | collective-permute-start | bytes 786440 | tf_op jit(solution)/shard_map/ppermute | solution.py:347
  22.4 7.5 %shard_map.73 = (f32[4,512,128]{2,1,0:T(8,128)}, f32[4,512,1]{2,1,0:T(8,128)}, f32[4,512,1]{2,1,0:T(8,128)}) custom-call(s32[4,8]{1,0:T(4,128)} %stack.217.meta_ref, bf16[4,512,128]{2,1,0:T(8,128)(2,1)} %pad_maximum_fusion.q_ref, bf16[512,512]{1,0:T(8,128)(2,1)} %copy-done, bf16[512,512]{1,0:T(8,128)(2,1)} %copy-done, ...), custom_call_target="tpu_custom_call" | custom-call | flops 536870912 | bytes 3145728 | tf_op jit(solution)/shard_map/pallas_call | solution.py:160
  31.1 1.5 %collective-permute-start.7 = (bf16[512,512]{1,0:T(8,128)(2,1)S(1)}, bf16[512,512]{1,0:T(8,128)(2,1)S(1)}, u32[]{:S(2)}, u32[]{:S(2)}) collective-permute-start(bf16[512,512]{1,0:T(8,128)(2,1)S(1)} %collective-permute-done.5.k_ref.v_ref), channel_id=1, source_target_pairs={{0,112},{16,0},{32,16},{48,32},{64,48},{80,64},{96,80},{112,96},{1... | collective-permute-start | bytes 1572872 | tf_op jit(solution)/shard_map/ppermute | solution.py:387
  34.6 7.6 %shard_map.74 = (f32[4,512,128]{2,1,0:T(8,128)}, f32[4,512,1]{2,1,0:T(8,128)}, f32[4,512,1]{2,1,0:T(8,128)}) custom-call(s32[4,8]{1,0:T(4,128)} %stack.223.meta_ref, bf16[4,512,128]{2,1,0:T(8,128)(2,1)} %pad_maximum_fusion.q_ref, bf16[512,512]{1,0:T(8,128)(2,1)} %copy-done.1, bf16[512,512]{1,0:T(8,128)(2,1)} %copy-done.1, ...), custom_call_target="tpu_custom_call" | custom-call | flops 536870912 | bytes 3145728 | tf_op jit(solution)/shard_map/pallas_call | solution.py:160
  42.2 5.2 %shard_map.75 = (f32[4,512,128]{2,1,0:T(8,128)}, f32[4,512,1]{2,1,0:T(8,128)}, f32[4,512,1]{2,1,0:T(8,128)}) custom-call(s32[4,8]{1,0:T(4,128)} %stack.211.meta_ref, bf16[4,512,128]{2,1,0:T(8,128)(2,1)} %pad_maximum_fusion.q_ref, bf16[512,512]{1,0:T(8,128)(2,1)} %copy-done.2, bf16[512,512]{1,0:T(8,128)(2,1)} %copy-done.2, ...), custom_call_target="tpu_custom_call" | custom-call | flops 536870912 | bytes 3145728 | tf_op jit(solution)/shard_map/pallas_call | solution.py:160
  48.2 2.5 %collective-permute-start.9 = (bf16[512,512]{1,0:T(8,128)(2,1)S(1)}, bf16[512,512]{1,0:T(8,128)(2,1)S(1)}, u32[]{:S(2)}, u32[]{:S(2)}) collective-permute-start(bf16[512,512]{1,0:T(8,128)(2,1)S(1)} %collective-permute-done.7.k_ref.v_ref), channel_id=1, source_target_pairs={{0,112},{16,0},{32,16},{48,32},{64,48},{80,64},{96,80},{112,96},{1... | collective-permute-start | bytes 1572872 | tf_op jit(solution)/shard_map/ppermute | solution.py:387
  52.7 7.6 %shard_map.76 = (f32[4,512,128]{2,1,0:T(8,128)}, f32[4,512,1]{2,1,0:T(8,128)}, f32[4,512,1]{2,1,0:T(8,128)}) custom-call(s32[4,8]{1,0:T(4,128)} %stack.229.meta_ref, bf16[4,512,128]{2,1,0:T(8,128)(2,1)} %pad_maximum_fusion.q_ref, bf16[512,512]{1,0:T(8,128)(2,1)} %copy-done.4, bf16[512,512]{1,0:T(8,128)(2,1)} %copy-done.4, ...), custom_call_target="tpu_custom_call" | custom-call | flops 536870912 | bytes 3145728 | tf_op jit(solution)/shard_map/pallas_call | solution.py:160
  60.3 5.2 %shard_map.77 = (f32[4,512,128]{2,1,0:T(8,128)}, f32[4,512,1]{2,1,0:T(8,128)}, f32[4,512,1]{2,1,0:T(8,128)}) custom-call(s32[4,8]{1,0:T(4,128)} %stack.205.meta_ref, bf16[4,512,128]{2,1,0:T(8,128)(2,1)} %pad_maximum_fusion.q_ref, bf16[512,512]{1,0:T(8,128)(2,1)} %copy-done.5, bf16[512,512]{1,0:T(8,128)(2,1)} %copy-done.5, ...), custom_call_target="tpu_custom_call" | custom-call | flops 536870912 | bytes 3145728 | tf_op jit(solution)/shard_map/pallas_call | solution.py:160
  65.6 1.4 %collective-permute-start.10 = (bf16[512,512]{1,0:T(8,128)(2,1)S(1)}, bf16[512,512]{1,0:T(8,128)(2,1)S(1)}, u32[]{:S(2)}, u32[]{:S(2)}) collective-permute-start(bf16[512,512]{1,0:T(8,128)(2,1)S(1)} %collective-permute-done.8.k_ref.v_ref), channel_id=1, source_target_pairs={{0,16},{16,32},{32,48},{48,64},{64,80},{80,96},{96,112},{112,0},{1... | collective-permute-start | bytes 1572872 | tf_op jit(solution)/shard_map/ppermute | solution.py:385
  69.7 6.5 %shard_map.78 = (f32[4,512,128]{2,1,0:T(8,128)}, f32[4,512,1]{2,1,0:T(8,128)}, f32[4,512,1]{2,1,0:T(8,128)}) custom-call(s32[4,8]{1,0:T(4,128)} %stack.235.meta_ref, bf16[4,512,128]{2,1,0:T(8,128)(2,1)} %pad_maximum_fusion.q_ref, bf16[512,512]{1,0:T(8,128)(2,1)} %copy-done.3, bf16[512,512]{1,0:T(8,128)(2,1)} %copy-done.3, ...), custom_call_target="tpu_custom_call" | custom-call | flops 536870912 | bytes 3145728 | tf_op jit(solution)/shard_map/pallas_call | solution.py:160
  76.2 6.5 %shard_map.79 = (f32[4,512,128]{2,1,0:T(8,128)}, f32[4,512,1]{2,1,0:T(8,128)}, f32[4,512,1]{2,1,0:T(8,128)}) custom-call(s32[4,8]{1,0:T(4,128)} %stack.199.meta_ref, bf16[4,512,128]{2,1,0:T(8,128)(2,1)} %pad_maximum_fusion.q_ref, bf16[512,512]{1,0:T(8,128)(2,1)} %copy-done.6, bf16[512,512]{1,0:T(8,128)(2,1)} %copy-done.6, ...), custom_call_target="tpu_custom_call" | custom-call | flops 536870912 | bytes 3145728 | tf_op jit(solution)/shard_map/pallas_call | solution.py:160
  83.6 6.5 %shard_map.80 = (f32[4,512,128]{2,1,0:T(8,128)}, f32[4,512,1]{2,1,0:T(8,128)}, f32[4,512,1]{2,1,0:T(8,128)}) custom-call(s32[4,8]{1,0:T(4,128)} %stack.193.meta_ref, bf16[4,512,128]{2,1,0:T(8,128)(2,1)} %pad_maximum_fusion.q_ref, bf16[512,512]{1,0:T(8,128)(2,1)} %copy-done.7, bf16[512,512]{1,0:T(8,128)(2,1)} %copy-done.7, ...), custom_call_target="tpu_custom_call" | custom-call | flops 536870912 | bytes 3145728 | tf_op jit(solution)/shard_map/pallas_call | solution.py:160
  92.6 1.3 collective-permute-start.11
  95.0 1.3 collective-permute-start.12
  96.3 10.0 %collective-permute-done.11 = f32[4,512]{1,0:T(4,128)S(1)} collective-permute-done((f32[4,512]{1,0:T(4,128)S(1)}, f32[4,512]{1,0:T(4,128)S(1)}, u32[]{:S(2)}, u32[]{:S(2)}) %collective-permute-start.11) | collective-permute-done | bytes 8224 | tf_op jit(solution)/shard_map/ppermute | solution.py:405
  106.8 1.7 %fusion.8 = (f32[2,512]{1,0:T(2,128)S(1)}, f32[2,512]{1,0:T(2,128)S(1)}, f32[2,512]{1,0:T(2,128)S(1)}) fusion(f32[2,512,1]{2,1,0:T(8,128)S(1)} %copy.329, f32[4,512,1]{2,1,0:T(8,128)} %get-tuple-element.91, f32[2,512,1]{2,1,0:T(8,128)S(1)} %copy.331, f32[4,512,1]{2,1,0:T(8,128)} %get-tuple-element.92), kind=kLoop, calls=%fused_computation.20 | loop fusion | flops 6144 | bytes 28672 | tf_op jit(solution)/shard_map/exp | solution.py:272
  108.5 5.6 %collective-permute-done.12 = bf16[2,512,128]{2,1,0:T(8,128)(2,1)S(1)} collective-permute-done((bf16[2,512,128]{2,1,0:T(8,128)(2,1)S(1)}, bf16[2,512,128]{2,1,0:T(8,128)(2,1)S(1)}, u32[]{:S(2)}, u32[]{:S(2)}) %collective-permute-start.12) | collective-permute-done | bytes 262176 | tf_op jit(solution)/shard_map/ppermute | solution.py:404
  114.1 1.5 %divide_convert_fusion = bf16[2,512,128]{2,1,0:T(8,128)(2,1)S(1)} fusion(bf16[2,512,128]{2,1,0:T(8,128)(2,1)S(1)} %collective-permute-done.12, f32[4,512,128]{2,1,0:T(8,128)} %get-tuple-element.90, f32[2,512]{1,0:T(2,128)S(1)} %get-tuple-element.116, f32[2,512]{1,0:T(2,128)S(1)} %get-tuple-element.117, f32[2,512]{1,0:T(2,128)S(1)} %get-tuple-element.115, ...), kind=kLoop, calls=%fused_computation.15 | loop fusion | flops 917504 | bytes 1060865 | tf_op jit(solution)/shard_map/convert_element_type | solution.py:277
  116.0 4.6 %fusion = f32[2,2,32,4096]{3,2,1,0:T(8,128)S(1)} fusion(bf16[2,2,32,1024]{3,2,1,0:T(8,128)(2,1)S(1)} %dot_general.5, bf16[1024,4096]{1,0:T(8,128)(2,1)} %param.14), kind=kOutput, calls=%fused_computation | convolution fusion | flops 1073741824 | bytes 10747904 | tf_op jit(solution)/shard_map/dot_general | solution.py:411
  121.0 1.9 %collective-permute-done.13 = bf16[2,32,4096]{2,1,0:T(8,128)(2,1)} collective-permute-done((bf16[2,32,4096]{2,1,0:T(8,128)(2,1)S(1)}, bf16[2,32,4096]{2,1,0:T(8,128)(2,1)}, u32[]{:S(2)}, u32[]{:S(2)}) %collective-permute-start.13) | collective-permute-done | bytes 524320 | tf_op jit(solution)/shard_map/ppermute | solution.py:325
  124.2 8.3 %collective-permute-done.14 = bf16[32,4096]{1,0:T(8,128)(2,1)S(1)} collective-permute-done((bf16[32,4096]{1,0:T(8,128)(2,1)S(1)}, bf16[32,4096]{1,0:T(8,128)(2,1)S(1)}, u32[]{:S(2)}, u32[]{:S(2)}) %collective-permute-start.14) | collective-permute-done | bytes 262176 | tf_op jit(solution)/shard_map/ppermute | solution.py:330
  (119 shorter events, 29.3 us)
Async XLA Ops:
  1.7 12.8 %collective-permute-start.1 = (bf16[128,512]{1,0:T(8,128)(2,1)S(1)}, bf16[128,512]{1,0:T(8,128)(2,1)S(1)}, u32[]{:S(2)}, u32[]{:S(2)}) collective-permute-start(bf16[128,512]{1,0:T(8,128)(2,1)S(1)} %constant_dynamic-update-slice_fusion), channel_id=1, source_target_pairs={{0,4},{4,8},{8,12},{12,0},{1,5},{5,9},{9,13},{13,1},{2,6},{6,10},{... | collective-permute-start | bytes 393224 | tf_op jit(solution)/shard_map/ppermute | solution.py:295
  3.3 11.3 %collective-permute-start.2 = (bf16[128,512]{1,0:T(8,128)(2,1)S(1)}, bf16[128,512]{1,0:T(8,128)(2,1)S(1)}, u32[]{:S(2)}, u32[]{:S(2)}) collective-permute-start(bf16[128,512]{1,0:T(8,128)(2,1)S(1)} %constant_dynamic-update-slice_fusion), channel_id=1, source_target_pairs={{0,8},{4,12},{8,0},{12,4},{1,9},{5,13},{9,1},{13,5},{2,10},{6,14},... | collective-permute-start | bytes 393224 | tf_op jit(solution)/shard_map/ppermute | solution.py:295
  6.2 8.4 %collective-permute-start.3 = (bf16[128,512]{1,0:T(8,128)(2,1)S(1)}, bf16[128,512]{1,0:T(8,128)(2,1)S(1)}, u32[]{:S(2)}, u32[]{:S(2)}) collective-permute-start(bf16[128,512]{1,0:T(8,128)(2,1)S(1)} %constant_dynamic-update-slice_fusion), channel_id=1, source_target_pairs={{0,12},{4,0},{8,4},{12,8},{1,13},{5,1},{9,5},{13,9},{2,14},{6,2},{... | collective-permute-start | bytes 393224 | tf_op jit(solution)/shard_map/ppermute | solution.py:295
  8.7 9.7 %collective-permute-start = (bf16[2,512,128]{2,1,0:T(8,128)(2,1)S(1)}, bf16[2,512,128]{2,1,0:T(8,128)(2,1)S(1)}, u32[]{:S(2)}, u32[]{:S(2)}) collective-permute-start(bf16[2,512,128]{2,1,0:T(8,128)(2,1)S(1)} %bitcast.74), channel_id=1, source_target_pairs={{128,0},{129,1},{130,2},{131,3},{132,4},{133,5},{134,6},{135,7},{1... | collective-permute-start | bytes 786440 | tf_op jit(solution)/shard_map/ppermute | solution.py:347
  14.6 7.8 %copy-start = (bf16[512,512]{1,0:T(8,128)(2,1)}, bf16[512,512]{1,0:T(8,128)(2,1)S(1)}, u32[]{:S(2)}) copy-start(bf16[512,512]{1,0:T(8,128)(2,1)S(1)} %constant_dynamic-update-slice_fusion.2.k_ref.v_ref) | copy-start | bytes 1572868
  14.6 15.4 %collective-permute-start.4 = (bf16[512,512]{1,0:T(8,128)(2,1)S(1)}, bf16[512,512]{1,0:T(8,128)(2,1)S(1)}, u32[]{:S(2)}, u32[]{:S(2)}) collective-permute-start(bf16[512,512]{1,0:T(8,128)(2,1)S(1)} %constant_dynamic-update-slice_fusion.2.k_ref.v_ref), channel_id=1, source_target_pairs={{0,16},{16,32},{32,48},{48,64},{64,80},{80,96},{96,112},{112,0},{1... | collective-permute-start | bytes 1572872 | tf_op jit(solution)/shard_map/ppermute | solution.py:378
  15.7 14.3 %collective-permute-start.5 = (bf16[512,512]{1,0:T(8,128)(2,1)S(1)}, bf16[512,512]{1,0:T(8,128)(2,1)S(1)}, u32[]{:S(2)}, u32[]{:S(2)}) collective-permute-start(bf16[512,512]{1,0:T(8,128)(2,1)S(1)} %constant_dynamic-update-slice_fusion.2.k_ref.v_ref), channel_id=1, source_target_pairs={{0,112},{16,0},{32,16},{48,32},{64,48},{80,64},{96,80},{112,96},{1... | collective-permute-start | bytes 1572872 | tf_op jit(solution)/shard_map/ppermute | solution.py:379
  30.0 4.6 %copy-start.1 = (bf16[512,512]{1,0:T(8,128)(2,1)}, bf16[512,512]{1,0:T(8,128)(2,1)S(1)}, u32[]{:S(2)}) copy-start(bf16[512,512]{1,0:T(8,128)(2,1)S(1)} %collective-permute-done.4.k_ref.v_ref) | copy-start | bytes 1572868
  30.0 12.2 %copy-start.2 = (bf16[512,512]{1,0:T(8,128)(2,1)}, bf16[512,512]{1,0:T(8,128)(2,1)S(1)}, u32[]{:S(2)}) copy-start(bf16[512,512]{1,0:T(8,128)(2,1)S(1)} %collective-permute-done.5.k_ref.v_ref) | copy-start | bytes 1572868
  30.0 17.5 %collective-permute-start.6 = (bf16[512,512]{1,0:T(8,128)(2,1)S(1)}, bf16[512,512]{1,0:T(8,128)(2,1)S(1)}, u32[]{:S(2)}, u32[]{:S(2)}) collective-permute-start(bf16[512,512]{1,0:T(8,128)(2,1)S(1)} %collective-permute-done.4.k_ref.v_ref), channel_id=1, source_target_pairs={{0,16},{16,32},{32,48},{48,64},{64,80},{80,96},{96,112},{112,0},{1... | collective-permute-start | bytes 1572872 | tf_op jit(solution)/shard_map/ppermute | solution.py:385
  31.1 16.4 %collective-permute-start.7 = (bf16[512,512]{1,0:T(8,128)(2,1)S(1)}, bf16[512,512]{1,0:T(8,128)(2,1)S(1)}, u32[]{:S(2)}, u32[]{:S(2)}) collective-permute-start(bf16[512,512]{1,0:T(8,128)(2,1)S(1)} %collective-permute-done.5.k_ref.v_ref), channel_id=1, source_target_pairs={{0,112},{16,0},{32,16},{48,32},{64,48},{80,64},{96,80},{112,96},{1... | collective-permute-start | bytes 1572872 | tf_op jit(solution)/shard_map/ppermute | solution.py:387
  47.5 5.2 %copy-start.4 = (bf16[512,512]{1,0:T(8,128)(2,1)}, bf16[512,512]{1,0:T(8,128)(2,1)S(1)}, u32[]{:S(2)}) copy-start(bf16[512,512]{1,0:T(8,128)(2,1)S(1)} %collective-permute-done.6.k_ref.v_ref) | copy-start | bytes 1572868
  47.5 12.8 %copy-start.5 = (bf16[512,512]{1,0:T(8,128)(2,1)}, bf16[512,512]{1,0:T(8,128)(2,1)S(1)}, u32[]{:S(2)}) copy-start(bf16[512,512]{1,0:T(8,128)(2,1)S(1)} %collective-permute-done.7.k_ref.v_ref) | copy-start | bytes 1572868
  47.5 18.0 %collective-permute-start.8 = (bf16[512,512]{1,0:T(8,128)(2,1)S(1)}, bf16[512,512]{1,0:T(8,128)(2,1)S(1)}, u32[]{:S(2)}, u32[]{:S(2)}) collective-permute-start(bf16[512,512]{1,0:T(8,128)(2,1)S(1)} %collective-permute-done.6.k_ref.v_ref), channel_id=1, source_target_pairs={{0,16},{16,32},{32,48},{48,64},{64,80},{80,96},{96,112},{112,0},{1... | collective-permute-start | bytes 1572872 | tf_op jit(solution)/shard_map/ppermute | solution.py:385
  48.2 17.4 %collective-permute-start.9 = (bf16[512,512]{1,0:T(8,128)(2,1)S(1)}, bf16[512,512]{1,0:T(8,128)(2,1)S(1)}, u32[]{:S(2)}, u32[]{:S(2)}) collective-permute-start(bf16[512,512]{1,0:T(8,128)(2,1)S(1)} %collective-permute-done.7.k_ref.v_ref), channel_id=1, source_target_pairs={{0,112},{16,0},{32,16},{48,32},{64,48},{80,64},{96,80},{112,96},{1... | collective-permute-start | bytes 1572872 | tf_op jit(solution)/shard_map/ppermute | solution.py:387
  65.5 4.1 %copy-start.3 = (bf16[512,512]{1,0:T(8,128)(2,1)}, bf16[512,512]{1,0:T(8,128)(2,1)S(1)}, u32[]{:S(2)}) copy-start(bf16[512,512]{1,0:T(8,128)(2,1)S(1)} %collective-permute-done.8.k_ref.v_ref) | copy-start | bytes 1572868
  65.6 10.7 %copy-start.6 = (bf16[512,512]{1,0:T(8,128)(2,1)}, bf16[512,512]{1,0:T(8,128)(2,1)S(1)}, u32[]{:S(2)}) copy-start(bf16[512,512]{1,0:T(8,128)(2,1)S(1)} %collective-permute-done.9.k_ref.v_ref) | copy-start | bytes 1572868
  65.6 17.2 %collective-permute-start.10 = (bf16[512,512]{1,0:T(8,128)(2,1)S(1)}, bf16[512,512]{1,0:T(8,128)(2,1)S(1)}, u32[]{:S(2)}, u32[]{:S(2)}) collective-permute-start(bf16[512,512]{1,0:T(8,128)(2,1)S(1)} %collective-permute-done.8.k_ref.v_ref), channel_id=1, source_target_pairs={{0,16},{16,32},{32,48},{48,64},{64,80},{80,96},{96,112},{112,0},{1... | collective-permute-start | bytes 1572872 | tf_op jit(solution)/shard_map/ppermute | solution.py:385
  82.8 0.8 copy-start.7
  92.6 13.7 %collective-permute-start.11 = (f32[4,512]{1,0:T(4,128)S(1)}, f32[4,512]{1,0:T(4,128)S(1)}, u32[]{:S(2)}, u32[]{:S(2)}) collective-permute-start(f32[4,512]{1,0:T(4,128)S(1)} %pad_maximum_fusion.1), channel_id=1, source_target_pairs={{0,128},{1,129},{2,130},{3,131},{4,132},{5,133},{6,134},{7,135},{8... | collective-permute-start | bytes 24584 | tf_op jit(solution)/shard_map/ppermute | solution.py:405
  95.0 19.1 %collective-permute-start.12 = (bf16[2,512,128]{2,1,0:T(8,128)(2,1)S(1)}, bf16[2,512,128]{2,1,0:T(8,128)(2,1)S(1)}, u32[]{:S(2)}, u32[]{:S(2)}) collective-permute-start(bf16[2,512,128]{2,1,0:T(8,128)(2,1)S(1)} %slice.77), channel_id=1, source_target_pairs={{0,128},{1,129},{2,130},{3,131},{4,132},{5,133},{6,134},{7,135},{8... | collective-permute-start | bytes 786440 | tf_op jit(solution)/shard_map/ppermute | solution.py:404
  120.8 2.1 %collective-permute-start.13 = (bf16[2,32,4096]{2,1,0:T(8,128)(2,1)S(1)}, bf16[2,32,4096]{2,1,0:T(8,128)(2,1)}, u32[]{:S(2)}, u32[]{:S(2)}) collective-permute-start(bf16[2,32,4096]{2,1,0:T(8,128)(2,1)S(1)} %bitcast_convert_fusion), channel_id=1, source_target_pairs={{0,1},{1,0},{2,3},{3,2},{4,5},{5,4},{6,7},{7,6},{8,9},{9,8},{10,11... | collective-permute-start | bytes 1572872 | tf_op jit(solution)/shard_map/ppermute | solution.py:325
  124.1 8.4 %collective-permute-start.14 = (bf16[32,4096]{1,0:T(8,128)(2,1)S(1)}, bf16[32,4096]{1,0:T(8,128)(2,1)S(1)}, u32[]{:S(2)}, u32[]{:S(2)}) collective-permute-start(bf16[32,4096]{1,0:T(8,128)(2,1)S(1)} %bitcast_convert_fusion.1), channel_id=1, source_target_pairs={{0,2},{2,0},{1,3},{3,1},{4,6},{6,4},{5,7},{7,5},{8,10},{10,8},{9,1... | collective-permute-start | bytes 786440 | tf_op jit(solution)/shard_map/ppermute | solution.py:330

commit v13 on v11

--- a/solution.py
+++ b/solution.py
@@ -203,14 +203,18 @@
     return result
 
 
-def scatter_sum(partial):
-    rows, width = partial.shape
+def scatter_sum(attended, out_weight):
+    rows = attended.shape[0]
     quarter = rows // 4
-    parts = partial.reshape(2, 2, quarter, width)
+    parts = attended.reshape(2, 2, quarter, attended.shape[1])
     core = lax.axis_index("core")
-    keep = jnp.take(parts, core, axis=1)
-    give = jnp.take(parts, 1 - core, axis=1)
+
+    def project(x):
+        return jnp.einsum("aqf,fd->aqd", x, out_weight, preferred_element_type=jnp.float32)
+
+    give = project(jnp.take(parts, 1 - core, axis=1))
     got = lax.ppermute(give.astype(jnp.bfloat16), "core", [(0, 1), (1, 0)])
+    keep = lax.optimization_barrier(project(jnp.take(parts, core, axis=1)))
     summed = keep + got.astype(jnp.float32)
     xl = lax.axis_index("xl")
     keep = jnp.take(summed, xl, axis=0)
@@ -257,8 +261,7 @@
     total_b = jnp.where(received, stats_p[local_heads:], 0.0)[:, :, None]
     acc_b = jnp.where(received, acc_p.astype(jnp.float32), 0.0)
     attended = merge(own, (acc_b, peak_b, total_b), row_count)
-    partial = jnp.dot(attended, out_weight, preferred_element_type=jnp.float32)
-    return scatter_sum(partial)
+    return scatter_sum(attended, out_weight)
 
 
 def solution(mesh):

time: 127 us -> 129 us (1.016)
  matrix products: 4.65 us -> 9.91 us
  waiting for transfers between devices: 37.2 us -> 35.9 us
    dot_general x1 -> x2, matrix products: 4.65 us -> 9.91 us  [project(): jnp.einsum('aqf,fd->aqd', x, out_weight, preferred_element_type=jnp.float32)]
    ppermute x1, waiting for transfers between devices: 1.67 us -> 0.01 us  [scatter_sum(): got = lax.ppermute(give.astype(jnp.bfloat16), 'core', [(0, 1), (1, 0)])]
  transfers between devices with their start and end apart: 15 -> 15, of which waited for: 7 -> 6; matrix products, arithmetic and copies ran while one was open for 19% -> 22% of each run, Pallas kernels for 8% -> 8%
where the time goes in v13:
time: 129 us
  waiting for transfers between devices  35.9 us (28%)
  starting transfers between devices  27.9 us (22%)
  Pallas kernels  23.7 us (18%)
  local copies, waits for them, and re-layouts  18.7 us (14%)
  other arithmetic  12.3 us (10%)
  matrix products  9.91 us (8%)
    ppermute x4, waiting for transfers between devices, gather_both_ways(): forward = lax.ppermute(forward, axis, right)  27.3 us
    pallas_call x2, Pallas kernels, attend(): pl.pallas_call(attention_kernel, out_shape=(jax.ShapeDtypeStruct(stacked....  23.7 us
    dot_general x2, matrix products, project(): jnp.einsum('aqf,fd->aqd', x, out_weight, preferred_element_type=jnp.float32)  9.91 us
    ppermute x3, starting transfers between devices, gather_both_ways(): backward = lax.ppermute(backward, axis, left)  9.77 us
    ppermute x1, waiting for transfers between devices, scatter_sum(): got = lax.ppermute(give.astype(jnp.bfloat16), 'xl', [(0, 1), (1, 0)])  7.9 us
    dynamic_update_slice x12, local copies, waits for them, and re-layouts, place(): return lax.dynamic_update_slice(result, piece, (origin * piece.shape[0], 0))  6.77 us
    ppermute x1, starting transfers between devices, scatter_sum(): got = lax.ppermute(give.astype(jnp.bfloat16), 'core', [(0, 1), (1, 0)])  6.35 us
    ppermute x3, starting transfers between devices, gather_ring(): lax.ppermute(block, axis, [(i, (i + shift) % size) for i in range(size)])  5.81 us
  transfers between devices with their start and end apart: 15, of which 6 were waited for; matrix products, arithmetic and copies ran while one was open for 22% of the time, Pallas kernels for 8%

profile of v13, /device:TPU:1, one launch (start us, length us, event | category | flops | bytes accessed | tf_op | source)
XLA Modules:
  0.0 128.8 jit_solution(4126380331284637187)
XLA Ops:
  1.7 2.1 %collective-permute-start = (bf16[128,512]{1,0:T(8,128)(2,1)S(1)}, bf16[128,512]{1,0:T(8,128)(2,1)S(1)}, u32[]{:S(2)}, u32[]{:S(2)}) collective-permute-start(bf16[128,512]{1,0:T(8,128)(2,1)S(1)} %constant_dynamic-update-slice_fusion), channel_id=1, source_target_pairs={{0,4},{4,8},{8,12},{12,0},{1,5},{5,9},{9,13},{13,1},{2,6},{6,10},{... | collective-permute-start | bytes 393224 | tf_op jit(solution)/shard_map/ppermute | solution.py:183
  3.8 2.6 %collective-permute-start.1 = (bf16[128,512]{1,0:T(8,128)(2,1)S(1)}, bf16[128,512]{1,0:T(8,128)(2,1)S(1)}, u32[]{:S(2)}, u32[]{:S(2)}) collective-permute-start(bf16[128,512]{1,0:T(8,128)(2,1)S(1)} %constant_dynamic-update-slice_fusion), channel_id=1, source_target_pairs={{0,8},{4,12},{8,0},{12,4},{1,9},{5,13},{9,1},{13,5},{2,10},{6,14},... | collective-permute-start | bytes 393224 | tf_op jit(solution)/shard_map/ppermute | solution.py:183
  8.7 1.3 %collective-permute-start.10 = (bf16[2,512,128]{2,1,0:T(8,128)(2,1)S(1)}, bf16[2,512,128]{2,1,0:T(8,128)(2,1)}, u32[]{:S(2)}, u32[]{:S(2)}) collective-permute-start(bf16[2,512,128]{2,1,0:T(8,128)(2,1)S(1)} %bitcast.83), channel_id=1, source_target_pairs={{128,0},{129,1},{130,2},{131,3},{132,4},{133,5},{134,6},{135,7},{1... | collective-permute-start | bytes 786440 | tf_op jit(solution)/shard_map/ppermute | solution.py:239
  16.1 1.7 %collective-permute-start.3 = (bf16[512,512]{1,0:T(8,128)(2,1)S(1)}, bf16[512,512]{1,0:T(8,128)(2,1)S(1)}, u32[]{:S(2)}, u32[]{:S(2)}) collective-permute-start(bf16[512,512]{1,0:T(8,128)(2,1)S(1)} %constant_dynamic-update-slice_fusion.10), channel_id=1, source_target_pairs={{0,16},{16,32},{32,48},{48,64},{64,80},{80,96},{96,112},{112,0},{1... | collective-permute-start | bytes 1572872 | tf_op jit(solution)/shard_map/ppermute | solution.py:198
  18.4 4.0 %collective-permute-start.4 = (bf16[512,512]{1,0:T(8,128)(2,1)S(1)}, bf16[512,512]{1,0:T(8,128)(2,1)S(1)}, u32[]{:S(2)}, u32[]{:S(2)}) collective-permute-start(bf16[512,512]{1,0:T(8,128)(2,1)S(1)} %constant_dynamic-update-slice_fusion.10), channel_id=1, source_target_pairs={{0,112},{16,0},{32,16},{48,32},{64,48},{80,64},{96,80},{112,96},{1... | collective-permute-start | bytes 1572872 | tf_op jit(solution)/shard_map/ppermute | solution.py:201
  23.1 9.4 %collective-permute-done.3 = bf16[512,512]{1,0:T(8,128)(2,1)S(1)} collective-permute-done((bf16[512,512]{1,0:T(8,128)(2,1)S(1)}, bf16[512,512]{1,0:T(8,128)(2,1)S(1)}, u32[]{:S(2)}, u32[]{:S(2)}) %collective-permute-start.3) | collective-permute-done | bytes 524320 | tf_op jit(solution)/shard_map/ppermute | solution.py:198
  32.5 3.0 %collective-permute-start.6 = (bf16[512,512]{1,0:T(8,128)(2,1)S(1)}, bf16[512,512]{1,0:T(8,128)(2,1)S(1)}, u32[]{:S(2)}, u32[]{:S(2)}) collective-permute-start(bf16[512,512]{1,0:T(8,128)(2,1)S(1)} %collective-permute-done.4), channel_id=1, source_target_pairs={{0,112},{16,0},{32,16},{48,32},{64,48},{80,64},{96,80},{112,96},{1... | collective-permute-start | bytes 1572872 | tf_op jit(solution)/shard_map/ppermute | solution.py:201
  35.6 9.3 %collective-permute-done.5 = bf16[512,512]{1,0:T(8,128)(2,1)S(1)} collective-permute-done((bf16[512,512]{1,0:T(8,128)(2,1)S(1)}, bf16[512,512]{1,0:T(8,128)(2,1)S(1)}, u32[]{:S(2)}, u32[]{:S(2)}) %collective-permute-start.5) | collective-permute-done | bytes 524320 | tf_op jit(solution)/shard_map/ppermute | solution.py:198
  46.9 2.2 %broadcast_in_dim.97 = bf16[4096,512]{1,0:T(8,128)(2,1)} broadcast(bf16[]{:T(256)} %constant.155.clone.1), dimensions={} | broadcast | bytes 4194306 | tf_op jit(solution)/shard_map/broadcast_in_dim | solution.py:193
  50.0 2.7 %collective-permute-start.8 = (bf16[512,512]{1,0:T(8,128)(2,1)S(1)}, bf16[512,512]{1,0:T(8,128)(2,1)S(1)}, u32[]{:S(2)}, u32[]{:S(2)}) collective-permute-start(bf16[512,512]{1,0:T(8,128)(2,1)S(1)} %collective-permute-done.6), channel_id=1, source_target_pairs={{0,112},{16,0},{32,16},{48,32},{64,48},{80,64},{96,80},{112,96},{1... | collective-permute-start | bytes 1572872 | tf_op jit(solution)/shard_map/ppermute | solution.py:201
  53.5 2.9 %collective-permute-done.7 = bf16[512,512]{1,0:T(8,128)(2,1)S(1)} collective-permute-done((bf16[512,512]{1,0:T(8,128)(2,1)S(1)}, bf16[512,512]{1,0:T(8,128)(2,1)S(1)}, u32[]{:S(2)}, u32[]{:S(2)}) %collective-permute-start.7) | collective-permute-done | bytes 524320 | tf_op jit(solution)/shard_map/ppermute | solution.py:198
  61.4 5.7 %collective-permute-done.9 = bf16[512,512]{1,0:T(8,128)(2,1)S(1)} collective-permute-done((bf16[512,512]{1,0:T(8,128)(2,1)S(1)}, bf16[512,512]{1,0:T(8,128)(2,1)S(1)}, u32[]{:S(2)}, u32[]{:S(2)}) %collective-permute-start.9) | collective-permute-done | bytes 524320 | tf_op jit(solution)/shard_map/ppermute | solution.py:198
  67.9 13.3 %shard_map.74 = (f32[2,512,128]{2,1,0:T(8,128)}, f32[2,512,1]{2,1,0:T(8,128)}, f32[2,512,1]{2,1,0:T(8,128)}) custom-call(s32[2,4]{1,0:T(2,128)} %pad_add_fusion.3.table_ref, s32[2,8]{1,0:T(2,128)} %pad.8.meta_ref, bf16[2,512,128]{2,1,0:T(8,128)(2,1)} %collective-permute-done.10.q_ref, bf16[4096,512]{1,0:T(8,128)(2,1)} %constant_dynamic-update-slice_fusion.2.k_ref.v_ref, ...), custom_call_target="tpu_custom_call" | custom-call | tf_op jit(solution)/shard_map/pallas_call | solution.py:120
  81.2 1.2 reduce
  82.5 1.3 reduce.1
  83.7 1.3 %collective-permute-start.11 = (f32[4,512]{1,0:T(4,128)S(1)}, f32[4,512]{1,0:T(4,128)S(1)}, u32[]{:S(2)}, u32[]{:S(2)}) collective-permute-start(f32[4,512]{1,0:T(4,128)S(1)} %pad_maximum_fusion), channel_id=1, source_target_pairs={{0,128},{1,129},{2,130},{3,131},{4,132},{5,133},{6,134},{7,135},{8... | collective-permute-start | bytes 24584 | tf_op jit(solution)/shard_map/ppermute | solution.py:253
  87.5 1.5 %collective-permute-start.12 = (bf16[2,512,128]{2,1,0:T(8,128)(2,1)S(1)}, bf16[2,512,128]{2,1,0:T(8,128)(2,1)S(1)}, u32[]{:S(2)}, u32[]{:S(2)}) collective-permute-start(bf16[2,512,128]{2,1,0:T(8,128)(2,1)S(1)} %convert_element_type.40), channel_id=1, source_target_pairs={{0,128},{1,129},{2,130},{3,131},{4,132},{5,133},{6,134},{7,135},{8... | collective-permute-start | bytes 786440 | tf_op jit(solution)/shard_map/ppermute | solution.py:252
  89.0 10.4 %shard_map.73 = (f32[2,512,128]{2,1,0:T(8,128)}, f32[2,512,1]{2,1,0:T(8,128)}, f32[2,512,1]{2,1,0:T(8,128)}) custom-call(s32[2,4]{1,0:T(2,128)} %pad_add_fusion.2.table_ref, s32[2,8]{1,0:T(2,128)} %pad.7.meta_ref, bf16[2,512,128]{2,1,0:T(8,128)(2,1)} %bitcast.84, bf16[4096,512]{1,0:T(8,128)(2,1)} %constant_dynamic-update-slice_fusion.2.k_ref.v_ref, ...), custom_call_target="tpu_custom_call" | custom-call | tf_op jit(solution)/shard_map/pallas_call | solution.py:120
  99.9 1.8 %fusion.11 = (f32[2,512]{1,0:T(2,128)S(1)}, f32[2,512]{1,0:T(2,128)S(1)}, f32[2,512]{1,0:T(2,128)S(1)}) fusion(f32[2,512,1]{2,1,0:T(8,128)} %get-tuple-element.19, f32[2,512,1]{2,1,0:T(8,128)S(1)} %copy.94, f32[2,512,1]{2,1,0:T(8,128)S(1)} %copy.96, f32[2,512,1]{2,1,0:T(8,128)} %get-tuple-element.24), kind=kLoop, calls=%fused_computation.21 | loop fusion | flops 6144 | bytes 28672 | tf_op jit(solution)/shard_map/exp | solution.py:160
  101.6 1.5 %divide_convert_fusion = bf16[2,512,128]{2,1,0:T(8,128)(2,1)S(1)} fusion(bf16[2,512,128]{2,1,0:T(8,128)(2,1)S(1)} %collective-permute-done.12, f32[2,512,128]{2,1,0:T(8,128)} %get-tuple-element.18, f32[2,512]{1,0:T(2,128)S(1)} %get-tuple-element.48, f32[2,512]{1,0:T(2,128)S(1)} %get-tuple-element.49, f32[2,512]{1,0:T(2,128)S(1)} %get-tuple-element.47, ...), kind=kLoop, calls=%fused_computation.17 | loop fusion | flops 917504 | bytes 1060865 | tf_op jit(solution)/shard_map/convert_element_type | solution.py:165
  103.5 5.0 %fusion.4 = bf16[2,32,4096]{2,1,0:T(8,128)(2,1)S(1)} fusion(bf16[1024,4096]{1,0:T(8,128)(2,1)} %param.18, bf16[2,2,32,1024]{3,2,1,0:T(8,128)(2,1)S(1)} %reshape_reshape.3, s32[]{:T(128)S(6)} %select_n.191, pred[]{:T(512)S(6)} %and.150), kind=kOutput, calls=%fused_computation.8 | convolution fusion | flops 537198592 | bytes 9043973 | tf_op jit(solution)/shard_map/aqf,fd->aqd/dot_general | solution.py:213
  108.5 6.3 %collective-permute-start.13 = (bf16[2,32,4096]{2,1,0:T(8,128)(2,1)S(1)}, bf16[2,32,4096]{2,1,0:T(8,128)(2,1)S(1)}, u32[]{:S(2)}, u32[]{:S(2)}) collective-permute-start(bf16[2,32,4096]{2,1,0:T(8,128)(2,1)S(1)} %fusion.4), channel_id=1, source_target_pairs={{0,1},{1,0},{2,3},{3,2},{4,5},{5,4},{6,7},{7,6},{8,9},{9,8},{10,11... | collective-permute-start | bytes 1572872 | tf_op jit(solution)/shard_map/ppermute | solution.py:216
  114.9 4.9 %fusion.2 = f32[2,32,4096]{2,1,0:T(8,128)S(1)} fusion(bf16[1024,4096]{1,0:T(8,128)(2,1)} %param.18, bf16[2,2,32,1024]{3,2,1,0:T(8,128)(2,1)S(1)} %reshape_reshape.3, s32[]{:T(128)S(6)} %select_n.189, pred[]{:T(512)S(6)} %and.149), kind=kOutput, calls=%fused_computation.6 | convolution fusion | flops 536936448 | bytes 9568261 | tf_op jit(solution)/shard_map/aqf,fd->aqd/dot_general | solution.py:213
  120.1 7.9 %collective-permute-done.14 = bf16[32,4096]{1,0:T(8,128)(2,1)S(1)} collective-permute-done((bf16[32,4096]{1,0:T(8,128)(2,1)S(1)}, bf16[32,4096]{1,0:T(8,128)(2,1)S(1)}, u32[]{:S(2)}, u32[]{:S(2)}) %collective-permute-start.14) | collective-permute-done | bytes 262176 | tf_op jit(solution)/shard_map/ppermute | solution.py:222
  (104 shorter events, 24.9 us)
Async XLA Ops:
  0.0 35.6 %copy-start.1 = (s32[8]{0:T(128)S(1)}, s32[8]{0:T(128)}, u32[]{:S(2)}) copy-start(s32[8]{0:T(128)} %param.19) | copy-start | bytes 100
  0.0 44.9 %copy-start.2 = (s32[8]{0:T(128)S(1)}, s32[8]{0:T(128)}, u32[]{:S(2)}) copy-start(s32[8]{0:T(128)} %param.20) | copy-start | bytes 100
  1.7 14.3 %collective-permute-start = (bf16[128,512]{1,0:T(8,128)(2,1)S(1)}, bf16[128,512]{1,0:T(8,128)(2,1)S(1)}, u32[]{:S(2)}, u32[]{:S(2)}) collective-permute-start(bf16[128,512]{1,0:T(8,128)(2,1)S(1)} %constant_dynamic-update-slice_fusion), channel_id=1, source_target_pairs={{0,4},{4,8},{8,12},{12,0},{1,5},{5,9},{9,13},{13,1},{2,6},{6,10},{... | collective-permute-start | bytes 393224 | tf_op jit(solution)/shard_map/ppermute | solution.py:183
  3.8 12.1 %collective-permute-start.1 = (bf16[128,512]{1,0:T(8,128)(2,1)S(1)}, bf16[128,512]{1,0:T(8,128)(2,1)S(1)}, u32[]{:S(2)}, u32[]{:S(2)}) collective-permute-start(bf16[128,512]{1,0:T(8,128)(2,1)S(1)} %constant_dynamic-update-slice_fusion), channel_id=1, source_target_pairs={{0,8},{4,12},{8,0},{12,4},{1,9},{5,13},{9,1},{13,5},{2,10},{6,14},... | collective-permute-start | bytes 393224 | tf_op jit(solution)/shard_map/ppermute | solution.py:183
  6.5 9.6 %collective-permute-start.2 = (bf16[128,512]{1,0:T(8,128)(2,1)S(1)}, bf16[128,512]{1,0:T(8,128)(2,1)S(1)}, u32[]{:S(2)}, u32[]{:S(2)}) collective-permute-start(bf16[128,512]{1,0:T(8,128)(2,1)S(1)} %constant_dynamic-update-slice_fusion), channel_id=1, source_target_pairs={{0,12},{4,0},{8,4},{12,8},{1,13},{5,1},{9,5},{13,9},{2,14},{6,2},{... | collective-permute-start | bytes 393224 | tf_op jit(solution)/shard_map/ppermute | solution.py:183
  8.7 40.4 %copy-start = (bf16[128,2,4,128]{3,0,2,1:T(8,128)(2,1)}, bf16[128,2,4,128]{3,0,2,1:T(8,128)(2,1)S(1)}, u32[]{:S(2)}) copy-start(bf16[128,2,4,128]{3,0,2,1:T(8,128)(2,1)S(1)} %copy.84) | copy-start | bytes 786436
  8.7 59.2 %collective-permute-start.10 = (bf16[2,512,128]{2,1,0:T(8,128)(2,1)S(1)}, bf16[2,512,128]{2,1,0:T(8,128)(2,1)}, u32[]{:S(2)}, u32[]{:S(2)}) collective-permute-start(bf16[2,512,128]{2,1,0:T(8,128)(2,1)S(1)} %bitcast.83), channel_id=1, source_target_pairs={{128,0},{129,1},{130,2},{131,3},{132,4},{133,5},{134,6},{135,7},{1... | collective-permute-start | bytes 786440 | tf_op jit(solution)/shard_map/ppermute | solution.py:239
  16.1 16.4 %collective-permute-start.3 = (bf16[512,512]{1,0:T(8,128)(2,1)S(1)}, bf16[512,512]{1,0:T(8,128)(2,1)S(1)}, u32[]{:S(2)}, u32[]{:S(2)}) collective-permute-start(bf16[512,512]{1,0:T(8,128)(2,1)S(1)} %constant_dynamic-update-slice_fusion.10), channel_id=1, source_target_pairs={{0,16},{16,32},{32,48},{48,64},{64,80},{80,96},{96,112},{112,0},{1... | collective-permute-start | bytes 1572872 | tf_op jit(solution)/shard_map/ppermute | solution.py:198
  18.4 14.1 %collective-permute-start.4 = (bf16[512,512]{1,0:T(8,128)(2,1)S(1)}, bf16[512,512]{1,0:T(8,128)(2,1)S(1)}, u32[]{:S(2)}, u32[]{:S(2)}) collective-permute-start(bf16[512,512]{1,0:T(8,128)(2,1)S(1)} %constant_dynamic-update-slice_fusion.10), channel_id=1, source_target_pairs={{0,112},{16,0},{32,16},{48,32},{64,48},{80,64},{96,80},{112,96},{1... | collective-permute-start | bytes 1572872 | tf_op jit(solution)/shard_map/ppermute | solution.py:201
  32.4 12.5 %collective-permute-start.5 = (bf16[512,512]{1,0:T(8,128)(2,1)S(1)}, bf16[512,512]{1,0:T(8,128)(2,1)S(1)}, u32[]{:S(2)}, u32[]{:S(2)}) collective-permute-start(bf16[512,512]{1,0:T(8,128)(2,1)S(1)} %collective-permute-done.3), channel_id=1, source_target_pairs={{0,16},{16,32},{32,48},{48,64},{64,80},{80,96},{96,112},{112,0},{1... | collective-permute-start | bytes 1572872 | tf_op jit(solution)/shard_map/ppermute | solution.py:198
  32.5 17.4 %collective-permute-start.6 = (bf16[512,512]{1,0:T(8,128)(2,1)S(1)}, bf16[512,512]{1,0:T(8,128)(2,1)S(1)}, u32[]{:S(2)}, u32[]{:S(2)}) collective-permute-start(bf16[512,512]{1,0:T(8,128)(2,1)S(1)} %collective-permute-done.4), channel_id=1, source_target_pairs={{0,112},{16,0},{32,16},{48,32},{64,48},{80,64},{96,80},{112,96},{1... | collective-permute-start | bytes 1572872 | tf_op jit(solution)/shard_map/ppermute | solution.py:201
  44.9 11.5 %collective-permute-start.7 = (bf16[512,512]{1,0:T(8,128)(2,1)S(1)}, bf16[512,512]{1,0:T(8,128)(2,1)S(1)}, u32[]{:S(2)}, u32[]{:S(2)}) collective-permute-start(bf16[512,512]{1,0:T(8,128)(2,1)S(1)} %collective-permute-done.5), channel_id=1, source_target_pairs={{0,16},{16,32},{32,48},{48,64},{64,80},{80,96},{96,112},{112,0},{1... | collective-permute-start | bytes 1572872 | tf_op jit(solution)/shard_map/ppermute | solution.py:198
  50.0 10.5 %collective-permute-start.8 = (bf16[512,512]{1,0:T(8,128)(2,1)S(1)}, bf16[512,512]{1,0:T(8,128)(2,1)S(1)}, u32[]{:S(2)}, u32[]{:S(2)}) collective-permute-start(bf16[512,512]{1,0:T(8,128)(2,1)S(1)} %collective-permute-done.6), channel_id=1, source_target_pairs={{0,112},{16,0},{32,16},{48,32},{64,48},{80,64},{96,80},{112,96},{1... | collective-permute-start | bytes 1572872 | tf_op jit(solution)/shard_map/ppermute | solution.py:201
  56.4 10.6 %collective-permute-start.9 = (bf16[512,512]{1,0:T(8,128)(2,1)S(1)}, bf16[512,512]{1,0:T(8,128)(2,1)S(1)}, u32[]{:S(2)}, u32[]{:S(2)}) collective-permute-start(bf16[512,512]{1,0:T(8,128)(2,1)S(1)} %collective-permute-done.7), channel_id=1, source_target_pairs={{0,16},{16,32},{32,48},{48,64},{64,80},{80,96},{96,112},{112,0},{1... | collective-permute-start | bytes 1572872 | tf_op jit(solution)/shard_map/ppermute | solution.py:198
  83.7 15.7 %collective-permute-start.11 = (f32[4,512]{1,0:T(4,128)S(1)}, f32[4,512]{1,0:T(4,128)S(1)}, u32[]{:S(2)}, u32[]{:S(2)}) collective-permute-start(f32[4,512]{1,0:T(4,128)S(1)} %pad_maximum_fusion), channel_id=1, source_target_pairs={{0,128},{1,129},{2,130},{3,131},{4,132},{5,133},{6,134},{7,135},{8... | collective-permute-start | bytes 24584 | tf_op jit(solution)/shard_map/ppermute | solution.py:253
  87.5 14.1 %collective-permute-start.12 = (bf16[2,512,128]{2,1,0:T(8,128)(2,1)S(1)}, bf16[2,512,128]{2,1,0:T(8,128)(2,1)S(1)}, u32[]{:S(2)}, u32[]{:S(2)}) collective-permute-start(bf16[2,512,128]{2,1,0:T(8,128)(2,1)S(1)} %convert_element_type.40), channel_id=1, source_target_pairs={{0,128},{1,129},{2,130},{3,131},{4,132},{5,133},{6,134},{7,135},{8... | collective-permute-start | bytes 786440 | tf_op jit(solution)/shard_map/ppermute | solution.py:252
  108.5 11.3 %collective-permute-start.13 = (bf16[2,32,4096]{2,1,0:T(8,128)(2,1)S(1)}, bf16[2,32,4096]{2,1,0:T(8,128)(2,1)S(1)}, u32[]{:S(2)}, u32[]{:S(2)}) collective-permute-start(bf16[2,32,4096]{2,1,0:T(8,128)(2,1)S(1)} %fusion.4), channel_id=1, source_target_pairs={{0,1},{1,0},{2,3},{3,2},{4,5},{5,4},{6,7},{7,6},{8,9},{9,8},{10,11... | collective-permute-start | bytes 1572872 | tf_op jit(solution)/shard_map/ppermute | solution.py:216
  120.0 8.0 %collective-permute-start.14 = (bf16[32,4096]{1,0:T(8,128)(2,1)S(1)}, bf16[32,4096]{1,0:T(8,128)(2,1)S(1)}, u32[]{:S(2)}, u32[]{:S(2)}) collective-permute-start(bf16[32,4096]{1,0:T(8,128)(2,1)S(1)} %bitcast_convert_fusion), channel_id=1, source_target_pairs={{0,2},{2,0},{1,3},{3,1},{4,6},{6,4},{5,7},{7,5},{8,10},{10,8},{9,1... | collective-permute-start | bytes 786440 | tf_op jit(solution)/shard_map/ppermute | solution.py:222

commit v14 on v11

--- a/solution.py
+++ b/solution.py
@@ -114,7 +114,7 @@
     return jnp.concatenate([table, full], axis=1), meta
 
 
-def attend(stacked, both, table, meta):
+def attend(stacked, keys, values, table, meta):
     local_heads, stack_rows, _ = stacked.shape
     blocks = table.shape[1] // 2
     return pl.pallas_call(
@@ -130,7 +130,7 @@
             in_specs=[
                 pl.BlockSpec((1, stack_rows, HD), lambda g, s, t, m: (g, 0, 0)),
                 pl.BlockSpec((KEY_BLOCK, HD), lambda g, s, t, m: (t[g, s], g)),
-                pl.BlockSpec((KEY_BLOCK, HD), lambda g, s, t, m: (t[g, s], local_heads + g)),
+                pl.BlockSpec((KEY_BLOCK, HD), lambda g, s, t, m: (t[g, s], g)),
             ],
             out_specs=(
                 pl.BlockSpec((1, stack_rows, HD), lambda g, s, t, m: (g, 0, 0)),
@@ -141,7 +141,7 @@
         compiler_params=pltpu.CompilerParams(
             dimension_semantics=("arbitrary", "arbitrary")
         ),
-    )(table, meta, stacked, both, both)
+    )(table, meta, stacked, keys, values)
 
 
 def stack_heads(queries, local_heads):
@@ -185,22 +185,39 @@
     return result
 
 
-def gather_both_ways(block, axis):
+def gather_both_ways(block, axis, result=None, put=place):
     size = lax.axis_size(axis)
     here = lax.axis_index(axis)
     right = [(i, (i + 1) % size) for i in range(size)]
     left = [(i, (i - 1) % size) for i in range(size)]
-    result = jnp.zeros((size * block.shape[0], block.shape[1]), block.dtype)
-    result = place(result, block, here)
+    if result is None:
+        result = jnp.zeros((size * block.shape[0], block.shape[1]), block.dtype)
+    result = put(result, block, here)
     forward = block
     backward = block
     for step in range(1, size // 2 + 1):
         forward = lax.ppermute(forward, axis, right)
-        result = place(result, forward, (here - step) % size)
+        result = put(result, forward, (here - step) % size)
         if step < size - size // 2:
             backward = lax.ppermute(backward, axis, left)
-            result = place(result, backward, (here + step) % size)
+            result = put(result, backward, (here + step) % size)
     return result
+
+
+def place_strided(result, piece, origin):
+    outer = result.shape[0]
+    return lax.dynamic_update_slice(
+        result, piece.reshape(outer, 1, -1, piece.shape[1]), (0, origin, 0, 0)
+    )
+
+
+def gather_values(block, outer_axis, inner_axis):
+    column = gather_both_ways(block, outer_axis)
+    outer = lax.axis_size(outer_axis)
+    inner = lax.axis_size(inner_axis)
+    result = jnp.zeros((outer, inner, block.shape[0], block.shape[1]), block.dtype)
+    result = gather_both_ways(column, inner_axis, result, place_strided)
+    return result.reshape(outer * inner * block.shape[0], block.shape[1])
 
 
 def scatter_sum(partial):
@@ -233,25 +250,24 @@
     sinks_here = lax.dynamic_slice_in_dim(sink_len, first_head, local_heads)
     windows_here = lax.dynamic_slice_in_dim(window_len, first_head, local_heads)
     partner_queries = lax.ppermute(stack_heads(queries, local_heads), "xh", [(1, 0)])
-    both = jnp.concatenate([key_states, value_states], axis=1)
-    both = gather_ring(both, "y")
-    both = gather_both_ways(both, "z")
-    key_offset = half * both.shape[0]
+    keys = gather_both_ways(gather_ring(key_states, "y"), "z")
+    values = gather_values(value_states, "z", "y")
+    key_offset = half * keys.shape[0]
     table, meta = block_table(
-        partner * row_count, row_count, key_offset, both.shape[0],
+        partner * row_count, row_count, key_offset, keys.shape[0],
         roles_here, sinks_here, windows_here,
     )
-    acc_p, peak_p, total_p = attend(partner_queries, both, table, meta)
+    acc_p, peak_p, total_p = attend(partner_queries, keys, values, table, meta)
     stats_p = jnp.concatenate(
         [peak_p.reshape(local_heads, -1), total_p.reshape(local_heads, -1)], axis=0
     )
     acc_p = lax.ppermute(acc_p.astype(jnp.bfloat16), "xh", [(0, 1)])
     stats_p = lax.ppermute(stats_p, "xh", [(0, 1)])
     table, meta = block_table(
-        ctx * row_count, row_count, key_offset, both.shape[0],
+        ctx * row_count, row_count, key_offset, keys.shape[0],
         roles_here, sinks_here, windows_here,
     )
-    own = attend(stack_heads(queries, local_heads), both, table, meta)
+    own = attend(stack_heads(queries, local_heads), keys, values, table, meta)
     received = half == 1
     peak_b = jnp.where(received, stats_p[:local_heads], NEGATIVE)[:, :, None]
     total_b = jnp.where(received, stats_p[local_heads:], 0.0)[:, :, None]

time: 127 us -> 131 us (1.031)
  starting transfers between devices: 27.9 us -> 41 us
  local copies, waits for them, and re-layouts: 18.7 us -> 12.8 us
  waiting for transfers between devices: 37.2 us -> 34.6 us
    ppermute x3 -> x7, starting transfers between devices: 9.77 us -> 19.9 us  [gather_both_ways(): backward = lax.ppermute(backward, axis, left)]
    dynamic_update_slice x12 -> x20, local copies, waits for them, and re-layouts: 6.77 us -> 0.32 us  [place(): return lax.dynamic_update_slice(result, piece, (origin * piece.shape[0], 0))]
    ppermute x1, starting transfers between devices: 0.09 us -> 2.63 us  [scatter_sum(): got = lax.ppermute(give.astype(jnp.bfloat16), 'xl', [(0, 1), (1, 0)])]
    broadcast_in_dim x1 -> x2, local copies, waits for them, and re-layouts: 2.2 us -> 0.17 us  [gather_both_ways(): result = jnp.zeros((size * block.shape[0], block.shape[1]), block.dtype)]
    unnamed x7 -> x14, local copies, waits for them, and re-layouts: 0.88 us -> 2.67 us
    ppermute x4 -> x10, starting transfers between devices: 1.72 us -> 3.12 us  [gather_both_ways(): forward = lax.ppermute(forward, axis, right)]
    ppermute x4 -> x10, waiting for transfers between devices: 27.3 us -> 26.5 us  [gather_both_ways(): forward = lax.ppermute(forward, axis, right)]
  transfers between devices with their start and end apart: 15 -> 25, of which waited for: 7 -> 8; matrix products, arithmetic and copies ran while one was open for 19% -> 13% of each run, Pallas kernels for 8% -> 8%
where the time goes in v14:
time: 131 us
  starting transfers between devices  41 us (31%)
  waiting for transfers between devices  34.6 us (26%)
  Pallas kernels  24.9 us (19%)
  local copies, waits for them, and re-layouts  12.8 us (10%)
  other arithmetic  12.2 us (9%)
  matrix products  4.64 us (4%)
    ppermute x10, waiting for transfers between devices, gather_both_ways(): forward = lax.ppermute(forward, axis, right)  26.5 us
    pallas_call x2, Pallas kernels, attend(): pl.pallas_call(attention_kernel, out_shape=(jax.ShapeDtypeStruct(stacked....  24.9 us
    ppermute x7, starting transfers between devices, gather_both_ways(): backward = lax.ppermute(backward, axis, left)  19.9 us
    ppermute x1, waiting for transfers between devices, scatter_sum(): got = lax.ppermute(give.astype(jnp.bfloat16), 'xl', [(0, 1), (1, 0)])  6.38 us
    ppermute x1, starting transfers between devices, scatter_sum(): got = lax.ppermute(give.astype(jnp.bfloat16), 'core', [(0, 1), (1, 0)])  6.22 us
    ppermute x3, starting transfers between devices, gather_ring(): lax.ppermute(block, axis, [(i, (i + shift) % size) for i in range(size)])  4.99 us
    dot_general x1, matrix products, per_device(): partial = jnp.dot(attended, out_weight, preferred_element_type=jnp.float32)  4.64 us
    ppermute x10, starting transfers between devices, gather_both_ways(): forward = lax.ppermute(forward, axis, right)  3.12 us
  transfers between devices with their start and end apart: 25, of which 8 were waited for; matrix products, arithmetic and copies ran while one was open for 13% of the time, Pallas kernels for 8%

profile of v14, /device:TPU:1, one launch (start us, length us, event | category | flops | bytes accessed | tf_op | source)
XLA Modules:
  0.0 130.7 jit_solution(14403094429871734861)
XLA Ops:
  0.0 2.5 %collective-permute-start.10 = (bf16[128,256]{1,0:T(8,128)(2,1)}, bf16[128,256]{1,0:T(8,128)(2,1)S(1)}, u32[]{:S(2)}, u32[]{:S(2)}) collective-permute-start(bf16[128,256]{1,0:T(8,128)(2,1)} %param.17), channel_id=1, source_target_pairs={{0,16},{16,32},{32,48},{48,64},{64,80},{80,96},{96,112},{112,0},{1... | collective-permute-start | bytes 196616 | tf_op jit(solution)/shard_map/ppermute | solution.py:199
  2.5 3.9 %collective-permute-start.11 = (bf16[128,256]{1,0:T(8,128)(2,1)}, bf16[128,256]{1,0:T(8,128)(2,1)S(1)}, u32[]{:S(2)}, u32[]{:S(2)}) collective-permute-start(bf16[128,256]{1,0:T(8,128)(2,1)} %param.17), channel_id=1, source_target_pairs={{0,112},{16,0},{32,16},{48,32},{64,48},{80,64},{96,80},{112,96},{1... | collective-permute-start | bytes 196616 | tf_op jit(solution)/shard_map/ppermute | solution.py:202
  7.7 2.6 %collective-permute-start.1 = (bf16[128,256]{1,0:T(8,128)(2,1)}, bf16[128,256]{1,0:T(8,128)(2,1)S(1)}, u32[]{:S(2)}, u32[]{:S(2)}) collective-permute-start(bf16[128,256]{1,0:T(8,128)(2,1)} %param.16), channel_id=1, source_target_pairs={{0,8},{4,12},{8,0},{12,4},{1,9},{5,13},{9,1},{13,5},{2,10},{6,14},... | collective-permute-start | bytes 196616 | tf_op jit(solution)/shard_map/ppermute | solution.py:183
  24.6 2.7 %collective-permute-start.4 = (bf16[512,256]{1,0:T(8,128)(2,1)S(1)}, bf16[512,256]{1,0:T(8,128)(2,1)S(1)}, u32[]{:S(2)}, u32[]{:S(2)}) collective-permute-start(bf16[512,256]{1,0:T(8,128)(2,1)S(1)} %constant_dynamic-update-slice_fusion.20), channel_id=1, source_target_pairs={{0,112},{16,0},{32,16},{48,32},{64,48},{80,64},{96,80},{112,96},{1... | collective-permute-start | bytes 786440 | tf_op jit(solution)/shard_map/ppermute | solution.py:202
  27.5 2.7 %collective-permute-start.13 = (bf16[128,256]{1,0:T(8,128)(2,1)S(1)}, bf16[128,256]{1,0:T(8,128)(2,1)S(1)}, u32[]{:S(2)}, u32[]{:S(2)}) collective-permute-start(bf16[128,256]{1,0:T(8,128)(2,1)S(1)} %collective-permute-done.11), channel_id=1, source_target_pairs={{0,112},{16,0},{32,16},{48,32},{64,48},{80,64},{96,80},{112,96},{1... | collective-permute-start | bytes 196616 | tf_op jit(solution)/shard_map/ppermute | solution.py:202
  30.2 3.0 %collective-permute-done.12 = bf16[128,256]{1,0:T(8,128)(2,1)S(1)} collective-permute-done((bf16[128,256]{1,0:T(8,128)(2,1)S(1)}, bf16[128,256]{1,0:T(8,128)(2,1)S(1)}, u32[]{:S(2)}, u32[]{:S(2)}) %collective-permute-start.12) | collective-permute-done | bytes 65568 | tf_op jit(solution)/shard_map/ppermute | solution.py:199
  33.2 2.7 %collective-permute-start.15 = (bf16[128,256]{1,0:T(8,128)(2,1)S(1)}, bf16[128,256]{1,0:T(8,128)(2,1)S(1)}, u32[]{:S(2)}, u32[]{:S(2)}) collective-permute-start(bf16[128,256]{1,0:T(8,128)(2,1)S(1)} %collective-permute-done.13), channel_id=1, source_target_pairs={{0,112},{16,0},{32,16},{48,32},{64,48},{80,64},{96,80},{112,96},{1... | collective-permute-start | bytes 196616 | tf_op jit(solution)/shard_map/ppermute | solution.py:202
  35.9 1.6 %collective-permute-done.14 = bf16[128,256]{1,0:T(8,128)(2,1)S(1)} collective-permute-done((bf16[128,256]{1,0:T(8,128)(2,1)S(1)}, bf16[128,256]{1,0:T(8,128)(2,1)S(1)}, u32[]{:S(2)}, u32[]{:S(2)}) %collective-permute-start.14) | collective-permute-done | bytes 65568 | tf_op jit(solution)/shard_map/ppermute | solution.py:199
  37.6 4.3 %collective-permute-done.16 = bf16[128,256]{1,0:T(8,128)(2,1)S(1)} collective-permute-done((bf16[128,256]{1,0:T(8,128)(2,1)S(1)}, bf16[128,256]{1,0:T(8,128)(2,1)S(1)}, u32[]{:S(2)}, u32[]{:S(2)}) %collective-permute-start.16) | collective-permute-done | bytes 65568 | tf_op jit(solution)/shard_map/ppermute | solution.py:199
  42.3 2.3 %collective-permute-start.18 = (bf16[1024,256]{1,0:T(8,128)(2,1)S(1)}, bf16[1024,256]{1,0:T(8,128)(2,1)S(1)}, u32[]{:S(2)}, u32[]{:S(2)}) collective-permute-start(bf16[1024,256]{1,0:T(8,128)(2,1)S(1)} %constant_dynamic-update-slice_fusion.4), channel_id=1, source_target_pairs={{0,12},{4,0},{8,4},{12,8},{1,13},{5,1},{9,5},{13,9},{2,14},{6,2},{... | collective-permute-start | bytes 1572872 | tf_op jit(solution)/shard_map/ppermute | solution.py:202
  44.6 2.7 %collective-permute-start.6 = (bf16[512,256]{1,0:T(8,128)(2,1)S(1)}, bf16[512,256]{1,0:T(8,128)(2,1)S(1)}, u32[]{:S(2)}, u32[]{:S(2)}) collective-permute-start(bf16[512,256]{1,0:T(8,128)(2,1)S(1)} %collective-permute-done.4), channel_id=1, source_target_pairs={{0,112},{16,0},{32,16},{48,32},{64,48},{80,64},{96,80},{112,96},{1... | collective-permute-start | bytes 786440 | tf_op jit(solution)/shard_map/ppermute | solution.py:202
  47.6 3.4 %collective-permute-done.5 = bf16[512,256]{1,0:T(8,128)(2,1)S(1)} collective-permute-done((bf16[512,256]{1,0:T(8,128)(2,1)S(1)}, bf16[512,256]{1,0:T(8,128)(2,1)S(1)}, u32[]{:S(2)}, u32[]{:S(2)}) %collective-permute-start.5) | collective-permute-done | bytes 262176 | tf_op jit(solution)/shard_map/ppermute | solution.py:199
  51.1 3.0 %collective-permute-start.8 = (bf16[512,256]{1,0:T(8,128)(2,1)S(1)}, bf16[512,256]{1,0:T(8,128)(2,1)S(1)}, u32[]{:S(2)}, u32[]{:S(2)}) collective-permute-start(bf16[512,256]{1,0:T(8,128)(2,1)S(1)} %collective-permute-done.6), channel_id=1, source_target_pairs={{0,112},{16,0},{32,16},{48,32},{64,48},{80,64},{96,80},{112,96},{1... | collective-permute-start | bytes 786440 | tf_op jit(solution)/shard_map/ppermute | solution.py:202
  54.2 5.7 %collective-permute-done.7 = bf16[512,256]{1,0:T(8,128)(2,1)S(1)} collective-permute-done((bf16[512,256]{1,0:T(8,128)(2,1)S(1)}, bf16[512,256]{1,0:T(8,128)(2,1)S(1)}, u32[]{:S(2)}, u32[]{:S(2)}) %collective-permute-start.7) | collective-permute-done | bytes 262176 | tf_op jit(solution)/shard_map/ppermute | solution.py:199
  60.0 8.6 %collective-permute-done.9 = bf16[512,256]{1,0:T(8,128)(2,1)S(1)} collective-permute-done((bf16[512,256]{1,0:T(8,128)(2,1)S(1)}, bf16[512,256]{1,0:T(8,128)(2,1)S(1)}, u32[]{:S(2)}, u32[]{:S(2)}) %collective-permute-start.9) | collective-permute-done | bytes 262176 | tf_op jit(solution)/shard_map/ppermute | solution.py:199
  71.4 14.6 %shard_map.74 = (f32[2,512,128]{2,1,0:T(8,128)}, f32[2,512,1]{2,1,0:T(8,128)}, f32[2,512,1]{2,1,0:T(8,128)}) custom-call(s32[2,4]{1,0:T(2,128)} %pad_add_fusion.3.table_ref, s32[2,8]{1,0:T(2,128)} %pad.8.meta_ref, bf16[2,512,128]{2,1,0:T(8,128)(2,1)} %copy-done.4, bf16[4096,256]{1,0:T(8,128)(2,1)} %copy-done.1, bf16[4096,256]{1,0:T(8,128)(2,1)} %bitcast.82), custom_call_target="tpu_custom_call" | custom-call | tf_op jit(solution)/shard_map/pallas_call | solution.py:120
  92.2 1.5 %collective-permute-start.22 = (bf16[2,512,128]{2,1,0:T(8,128)(2,1)S(1)}, bf16[2,512,128]{2,1,0:T(8,128)(2,1)S(1)}, u32[]{:S(2)}, u32[]{:S(2)}) collective-permute-start(bf16[2,512,128]{2,1,0:T(8,128)(2,1)S(1)} %convert_element_type.40), channel_id=1, source_target_pairs={{0,128},{1,129},{2,130},{3,131},{4,132},{5,133},{6,134},{7,135},{8... | collective-permute-start | bytes 786440 | tf_op jit(solution)/shard_map/ppermute | solution.py:264
  93.8 10.3 %shard_map.73 = (f32[2,512,128]{2,1,0:T(8,128)}, f32[2,512,1]{2,1,0:T(8,128)}, f32[2,512,1]{2,1,0:T(8,128)}) custom-call(s32[2,4]{1,0:T(2,128)} %pad_add_fusion.2.table_ref, s32[2,8]{1,0:T(2,128)} %pad.7.meta_ref, bf16[2,512,128]{2,1,0:T(8,128)(2,1)} %bitcast.86, bf16[4096,256]{1,0:T(8,128)(2,1)} %copy-done.1, bf16[4096,256]{1,0:T(8,128)(2,1)} %bitcast.83), custom_call_target="tpu_custom_call" | custom-call | tf_op jit(solution)/shard_map/pallas_call | solution.py:120
  104.6 1.7 %fusion.8 = (f32[2,512]{1,0:T(2,128)S(1)}, f32[2,512]{1,0:T(2,128)S(1)}, f32[2,512]{1,0:T(2,128)S(1)}) fusion(f32[2,512,1]{2,1,0:T(8,128)} %get-tuple-element.19, f32[2,512,1]{2,1,0:T(8,128)S(1)} %copy.94, f32[2,512,1]{2,1,0:T(8,128)S(1)} %copy.96, f32[2,512,1]{2,1,0:T(8,128)} %get-tuple-element.24), kind=kLoop, calls=%fused_computation.20 | loop fusion | flops 6144 | bytes 28672 | tf_op jit(solution)/shard_map/exp | solution.py:160
  107.2 4.6 %fusion = f32[2,2,32,4096]{3,2,1,0:T(8,128)S(1)} fusion(bf16[2,2,32,1024]{3,2,1,0:T(8,128)(2,1)S(1)} %dot_general.5, bf16[1024,4096]{1,0:T(8,128)(2,1)} %param.18), kind=kOutput, calls=%fused_computation.4 | convolution fusion | flops 1073741824 | bytes 10747904 | tf_op jit(solution)/shard_map/dot_general | solution.py:276
  111.9 6.2 %collective-permute-start.23 = (bf16[2,32,4096]{2,1,0:T(8,128)(2,1)S(1)}, bf16[2,32,4096]{2,1,0:T(8,128)(2,1)}, u32[]{:S(2)}, u32[]{:S(2)}) collective-permute-start(bf16[2,32,4096]{2,1,0:T(8,128)(2,1)S(1)} %bitcast_convert_fusion), channel_id=1, source_target_pairs={{0,1},{1,0},{2,3},{3,2},{4,5},{5,4},{6,7},{7,6},{8,9},{9,8},{10,11... | collective-permute-start | bytes 1572872 | tf_op jit(solution)/shard_map/ppermute | solution.py:230
  118.1 1.7 %collective-permute-done.23 = bf16[2,32,4096]{2,1,0:T(8,128)(2,1)} collective-permute-done((bf16[2,32,4096]{2,1,0:T(8,128)(2,1)S(1)}, bf16[2,32,4096]{2,1,0:T(8,128)(2,1)}, u32[]{:S(2)}, u32[]{:S(2)}) %collective-permute-start.23) | collective-permute-done | bytes 524320 | tf_op jit(solution)/shard_map/ppermute | solution.py:230
  121.0 2.6 %collective-permute-start.24 = (bf16[32,4096]{1,0:T(8,128)(2,1)S(1)}, bf16[32,4096]{1,0:T(8,128)(2,1)S(1)}, u32[]{:S(2)}, u32[]{:S(2)}) collective-permute-start(bf16[32,4096]{1,0:T(8,128)(2,1)S(1)} %bitcast_convert_fusion.1), channel_id=1, source_target_pairs={{0,2},{2,0},{1,3},{3,1},{4,6},{6,4},{5,7},{7,5},{8,10},{10,8},{9,1... | collective-permute-start | bytes 786440 | tf_op jit(solution)/shard_map/ppermute | solution.py:235
  123.6 6.4 %collective-permute-done.24 = bf16[32,4096]{1,0:T(8,128)(2,1)S(1)} collective-permute-done((bf16[32,4096]{1,0:T(8,128)(2,1)S(1)}, bf16[32,4096]{1,0:T(8,128)(2,1)S(1)}, u32[]{:S(2)}, u32[]{:S(2)}) %collective-permute-start.24) | collective-permute-done | bytes 262176 | tf_op jit(solution)/shard_map/ppermute | solution.py:235
  (144 shorter events, 28.9 us)
Async XLA Ops:
  0.0 27.3 %collective-permute-start.10 = (bf16[128,256]{1,0:T(8,128)(2,1)}, bf16[128,256]{1,0:T(8,128)(2,1)S(1)}, u32[]{:S(2)}, u32[]{:S(2)}) collective-permute-start(bf16[128,256]{1,0:T(8,128)(2,1)} %param.17), channel_id=1, source_target_pairs={{0,16},{16,32},{32,48},{48,64},{64,80},{80,96},{96,112},{112,0},{1... | collective-permute-start | bytes 196616 | tf_op jit(solution)/shard_map/ppermute | solution.py:199
  2.5 25.0 %collective-permute-start.11 = (bf16[128,256]{1,0:T(8,128)(2,1)}, bf16[128,256]{1,0:T(8,128)(2,1)S(1)}, u32[]{:S(2)}, u32[]{:S(2)}) collective-permute-start(bf16[128,256]{1,0:T(8,128)(2,1)} %param.17), channel_id=1, source_target_pairs={{0,112},{16,0},{32,16},{48,32},{64,48},{80,64},{96,80},{112,96},{1... | collective-permute-start | bytes 196616 | tf_op jit(solution)/shard_map/ppermute | solution.py:202
  6.4 16.7 %collective-permute-start = (bf16[128,256]{1,0:T(8,128)(2,1)}, bf16[128,256]{1,0:T(8,128)(2,1)S(1)}, u32[]{:S(2)}, u32[]{:S(2)}) collective-permute-start(bf16[128,256]{1,0:T(8,128)(2,1)} %param.16), channel_id=1, source_target_pairs={{0,4},{4,8},{8,12},{12,0},{1,5},{5,9},{9,13},{13,1},{2,6},{6,10},{... | collective-permute-start | bytes 196616 | tf_op jit(solution)/shard_map/ppermute | solution.py:183
  7.7 16.7 %collective-permute-start.1 = (bf16[128,256]{1,0:T(8,128)(2,1)}, bf16[128,256]{1,0:T(8,128)(2,1)S(1)}, u32[]{:S(2)}, u32[]{:S(2)}) collective-permute-start(bf16[128,256]{1,0:T(8,128)(2,1)} %param.16), channel_id=1, source_target_pairs={{0,8},{4,12},{8,0},{12,4},{1,9},{5,13},{9,1},{13,5},{2,10},{6,14},... | collective-permute-start | bytes 196616 | tf_op jit(solution)/shard_map/ppermute | solution.py:183
  10.3 14.1 %collective-permute-start.2 = (bf16[128,256]{1,0:T(8,128)(2,1)}, bf16[128,256]{1,0:T(8,128)(2,1)S(1)}, u32[]{:S(2)}, u32[]{:S(2)}) collective-permute-start(bf16[128,256]{1,0:T(8,128)(2,1)} %param.16), channel_id=1, source_target_pairs={{0,12},{4,0},{8,4},{12,8},{1,13},{5,1},{9,5},{13,9},{2,14},{6,2},{... | collective-permute-start | bytes 196616 | tf_op jit(solution)/shard_map/ppermute | solution.py:183
  23.1 46.9 %collective-permute-start.20 = (bf16[2,512,128]{2,1,0:T(8,128)(2,1)S(1)}, bf16[2,512,128]{2,1,0:T(8,128)(2,1)S(1)}, u32[]{:S(2)}, u32[]{:S(2)}) collective-permute-start(bf16[2,512,128]{2,1,0:T(8,128)(2,1)S(1)} %bitcast.85), channel_id=1, source_target_pairs={{128,0},{129,1},{130,2},{131,3},{132,4},{133,5},{134,6},{135,7},{1... | collective-permute-start | bytes 786440 | tf_op jit(solution)/shard_map/ppermute | solution.py:252
  24.5 20.1 %collective-permute-start.3 = (bf16[512,256]{1,0:T(8,128)(2,1)S(1)}, bf16[512,256]{1,0:T(8,128)(2,1)S(1)}, u32[]{:S(2)}, u32[]{:S(2)}) collective-permute-start(bf16[512,256]{1,0:T(8,128)(2,1)S(1)} %constant_dynamic-update-slice_fusion.20), channel_id=1, source_target_pairs={{0,16},{16,32},{32,48},{48,64},{64,80},{80,96},{96,112},{112,0},{1... | collective-permute-start | bytes 786440 | tf_op jit(solution)/shard_map/ppermute | solution.py:199
  24.6 20.0 %collective-permute-start.4 = (bf16[512,256]{1,0:T(8,128)(2,1)S(1)}, bf16[512,256]{1,0:T(8,128)(2,1)S(1)}, u32[]{:S(2)}, u32[]{:S(2)}) collective-permute-start(bf16[512,256]{1,0:T(8,128)(2,1)S(1)} %constant_dynamic-update-slice_fusion.20), channel_id=1, source_target_pairs={{0,112},{16,0},{32,16},{48,32},{64,48},{80,64},{96,80},{112,96},{1... | collective-permute-start | bytes 786440 | tf_op jit(solution)/shard_map/ppermute | solution.py:202
  27.3 5.9 %collective-permute-start.12 = (bf16[128,256]{1,0:T(8,128)(2,1)S(1)}, bf16[128,256]{1,0:T(8,128)(2,1)S(1)}, u32[]{:S(2)}, u32[]{:S(2)}) collective-permute-start(bf16[128,256]{1,0:T(8,128)(2,1)S(1)} %collective-permute-done.10), channel_id=1, source_target_pairs={{0,16},{16,32},{32,48},{48,64},{64,80},{80,96},{96,112},{112,0},{1... | collective-permute-start | bytes 196616 | tf_op jit(solution)/shard_map/ppermute | solution.py:199
  27.5 5.7 %collective-permute-start.13 = (bf16[128,256]{1,0:T(8,128)(2,1)S(1)}, bf16[128,256]{1,0:T(8,128)(2,1)S(1)}, u32[]{:S(2)}, u32[]{:S(2)}) collective-permute-start(bf16[128,256]{1,0:T(8,128)(2,1)S(1)} %collective-permute-done.11), channel_id=1, source_target_pairs={{0,112},{16,0},{32,16},{48,32},{64,48},{80,64},{96,80},{112,96},{1... | collective-permute-start | bytes 196616 | tf_op jit(solution)/shard_map/ppermute | solution.py:202
  33.2 4.3 %collective-permute-start.14 = (bf16[128,256]{1,0:T(8,128)(2,1)S(1)}, bf16[128,256]{1,0:T(8,128)(2,1)S(1)}, u32[]{:S(2)}, u32[]{:S(2)}) collective-permute-start(bf16[128,256]{1,0:T(8,128)(2,1)S(1)} %collective-permute-done.12), channel_id=1, source_target_pairs={{0,16},{16,32},{32,48},{48,64},{64,80},{80,96},{96,112},{112,0},{1... | collective-permute-start | bytes 196616 | tf_op jit(solution)/shard_map/ppermute | solution.py:199
  33.2 4.3 %collective-permute-start.15 = (bf16[128,256]{1,0:T(8,128)(2,1)S(1)}, bf16[128,256]{1,0:T(8,128)(2,1)S(1)}, u32[]{:S(2)}, u32[]{:S(2)}) collective-permute-start(bf16[128,256]{1,0:T(8,128)(2,1)S(1)} %collective-permute-done.13), channel_id=1, source_target_pairs={{0,112},{16,0},{32,16},{48,32},{64,48},{80,64},{96,80},{112,96},{1... | collective-permute-start | bytes 196616 | tf_op jit(solution)/shard_map/ppermute | solution.py:202
  41.9 12.2 %collective-permute-start.17 = (bf16[1024,256]{1,0:T(8,128)(2,1)S(1)}, bf16[1024,256]{1,0:T(8,128)(2,1)S(1)}, u32[]{:S(2)}, u32[]{:S(2)}) collective-permute-start(bf16[1024,256]{1,0:T(8,128)(2,1)S(1)} %constant_dynamic-update-slice_fusion.4), channel_id=1, source_target_pairs={{0,4},{4,8},{8,12},{12,0},{1,5},{5,9},{9,13},{13,1},{2,6},{6,10},{... | collective-permute-start | bytes 1572872 | tf_op jit(solution)/shard_map/ppermute | solution.py:199
  42.3 17.6 %collective-permute-start.18 = (bf16[1024,256]{1,0:T(8,128)(2,1)S(1)}, bf16[1024,256]{1,0:T(8,128)(2,1)S(1)}, u32[]{:S(2)}, u32[]{:S(2)}) collective-permute-start(bf16[1024,256]{1,0:T(8,128)(2,1)S(1)} %constant_dynamic-update-slice_fusion.4), channel_id=1, source_target_pairs={{0,12},{4,0},{8,4},{12,8},{1,13},{5,1},{9,5},{13,9},{2,14},{6,2},{... | collective-permute-start | bytes 1572872 | tf_op jit(solution)/shard_map/ppermute | solution.py:202
  44.6 6.4 %collective-permute-start.5 = (bf16[512,256]{1,0:T(8,128)(2,1)S(1)}, bf16[512,256]{1,0:T(8,128)(2,1)S(1)}, u32[]{:S(2)}, u32[]{:S(2)}) collective-permute-start(bf16[512,256]{1,0:T(8,128)(2,1)S(1)} %collective-permute-done.3), channel_id=1, source_target_pairs={{0,16},{16,32},{32,48},{48,64},{64,80},{80,96},{96,112},{112,0},{1... | collective-permute-start | bytes 786440 | tf_op jit(solution)/shard_map/ppermute | solution.py:199
  44.6 6.4 %collective-permute-start.6 = (bf16[512,256]{1,0:T(8,128)(2,1)S(1)}, bf16[512,256]{1,0:T(8,128)(2,1)S(1)}, u32[]{:S(2)}, u32[]{:S(2)}) collective-permute-start(bf16[512,256]{1,0:T(8,128)(2,1)S(1)} %collective-permute-done.4), channel_id=1, source_target_pairs={{0,112},{16,0},{32,16},{48,32},{64,48},{80,64},{96,80},{112,96},{1... | collective-permute-start | bytes 786440 | tf_op jit(solution)/shard_map/ppermute | solution.py:202
  51.0 8.8 %collective-permute-start.7 = (bf16[512,256]{1,0:T(8,128)(2,1)S(1)}, bf16[512,256]{1,0:T(8,128)(2,1)S(1)}, u32[]{:S(2)}, u32[]{:S(2)}) collective-permute-start(bf16[512,256]{1,0:T(8,128)(2,1)S(1)} %collective-permute-done.5), channel_id=1, source_target_pairs={{0,16},{16,32},{32,48},{48,64},{64,80},{80,96},{96,112},{112,0},{1... | collective-permute-start | bytes 786440 | tf_op jit(solution)/shard_map/ppermute | solution.py:199
  51.1 8.9 %collective-permute-start.8 = (bf16[512,256]{1,0:T(8,128)(2,1)S(1)}, bf16[512,256]{1,0:T(8,128)(2,1)S(1)}, u32[]{:S(2)}, u32[]{:S(2)}) collective-permute-start(bf16[512,256]{1,0:T(8,128)(2,1)S(1)} %collective-permute-done.6), channel_id=1, source_target_pairs={{0,112},{16,0},{32,16},{48,32},{64,48},{80,64},{96,80},{112,96},{1... | collective-permute-start | bytes 786440 | tf_op jit(solution)/shard_map/ppermute | solution.py:202
  54.1 14.6 %collective-permute-start.19 = (bf16[1024,256]{1,0:T(8,128)(2,1)S(1)}, bf16[1024,256]{1,0:T(8,128)(2,1)S(1)}, u32[]{:S(2)}, u32[]{:S(2)}) collective-permute-start(bf16[1024,256]{1,0:T(8,128)(2,1)S(1)} %collective-permute-done.17), channel_id=1, source_target_pairs={{0,4},{4,8},{8,12},{12,0},{1,5},{5,9},{9,13},{13,1},{2,6},{6,10},{... | collective-permute-start | bytes 1572872 | tf_op jit(solution)/shard_map/ppermute | solution.py:199
  59.9 8.7 %collective-permute-start.9 = (bf16[512,256]{1,0:T(8,128)(2,1)S(1)}, bf16[512,256]{1,0:T(8,128)(2,1)S(1)}, u32[]{:S(2)}, u32[]{:S(2)}) collective-permute-start(bf16[512,256]{1,0:T(8,128)(2,1)S(1)} %collective-permute-done.7), channel_id=1, source_target_pairs={{0,16},{16,32},{32,48},{48,64},{64,80},{80,96},{96,112},{112,0},{1... | collective-permute-start | bytes 786440 | tf_op jit(solution)/shard_map/ppermute | solution.py:199
  88.5 15.6 %collective-permute-start.21 = (f32[4,512]{1,0:T(4,128)S(1)}, f32[4,512]{1,0:T(4,128)S(1)}, u32[]{:S(2)}, u32[]{:S(2)}) collective-permute-start(f32[4,512]{1,0:T(4,128)S(1)} %pad_maximum_fusion), channel_id=1, source_target_pairs={{0,128},{1,129},{2,130},{3,131},{4,132},{5,133},{6,134},{7,135},{8... | collective-permute-start | bytes 24584 | tf_op jit(solution)/shard_map/ppermute | solution.py:265
  92.2 14.1 %collective-permute-start.22 = (bf16[2,512,128]{2,1,0:T(8,128)(2,1)S(1)}, bf16[2,512,128]{2,1,0:T(8,128)(2,1)S(1)}, u32[]{:S(2)}, u32[]{:S(2)}) collective-permute-start(bf16[2,512,128]{2,1,0:T(8,128)(2,1)S(1)} %convert_element_type.40), channel_id=1, source_target_pairs={{0,128},{1,129},{2,130},{3,131},{4,132},{5,133},{6,134},{7,135},{8... | collective-permute-start | bytes 786440 | tf_op jit(solution)/shard_map/ppermute | solution.py:264
  111.9 7.9 %collective-permute-start.23 = (bf16[2,32,4096]{2,1,0:T(8,128)(2,1)S(1)}, bf16[2,32,4096]{2,1,0:T(8,128)(2,1)}, u32[]{:S(2)}, u32[]{:S(2)}) collective-permute-start(bf16[2,32,4096]{2,1,0:T(8,128)(2,1)S(1)} %bitcast_convert_fusion), channel_id=1, source_target_pairs={{0,1},{1,0},{2,3},{3,2},{4,5},{5,4},{6,7},{7,6},{8,9},{9,8},{10,11... | collective-permute-start | bytes 1572872 | tf_op jit(solution)/shard_map/ppermute | solution.py:230
  121.0 9.0 %collective-permute-start.24 = (bf16[32,4096]{1,0:T(8,128)(2,1)S(1)}, bf16[32,4096]{1,0:T(8,128)(2,1)S(1)}, u32[]{:S(2)}, u32[]{:S(2)}) collective-permute-start(bf16[32,4096]{1,0:T(8,128)(2,1)S(1)} %bitcast_convert_fusion.1), channel_id=1, source_target_pairs={{0,2},{2,0},{1,3},{3,1},{4,6},{6,4},{5,7},{7,5},{8,10},{10,8},{9,1... | collective-permute-start | bytes 786440 | tf_op jit(solution)/shard_map/ppermute | solution.py:235
  (8 other events, 35.7 us)

commit v15 on v11

--- a/solution.py
+++ b/solution.py
@@ -14,7 +14,8 @@
 NEGATIVE = -1e30
 
 
-def attention_kernel(table_ref, meta_ref, q_ref, k_ref, v_ref, acc_ref, peak_ref, total_ref):
+def attention_kernel(table_ref, meta_ref, q_ref, k_ref, v_ref, acc_ref, peak_ref, total_ref,
+                     send_ref, stats_ref):
     g = pl.program_id(0)
     step = pl.program_id(1)
     blocks = pl.num_programs(1)
@@ -77,6 +78,12 @@
         )
         update(allowed[None])
 
+    @pl.when(step == blocks - 1)
+    def _():
+        send_ref[...] = acc_ref[...].astype(send_ref.dtype)
+        stats_ref[0, 0:1, :] = jnp.transpose(peak_ref[0])
+        stats_ref[0, 1:2, :] = jnp.transpose(total_ref[0])
+
 
 def block_table(row_base, row_count, key_offset, key_count, roles, sinks, windows):
     blocks = key_count // KEY_BLOCK
@@ -123,6 +130,8 @@
             jax.ShapeDtypeStruct(stacked.shape, jnp.float32),
             jax.ShapeDtypeStruct((local_heads, stack_rows, 1), jnp.float32),
             jax.ShapeDtypeStruct((local_heads, stack_rows, 1), jnp.float32),
+            jax.ShapeDtypeStruct(stacked.shape, jnp.bfloat16),
+            jax.ShapeDtypeStruct((local_heads, 2, stack_rows), jnp.float32),
         ),
         grid_spec=pltpu.PrefetchScalarGridSpec(
             num_scalar_prefetch=2,
@@ -136,6 +145,8 @@
                 pl.BlockSpec((1, stack_rows, HD), lambda g, s, t, m: (g, 0, 0)),
                 pl.BlockSpec((1, stack_rows, 1), lambda g, s, t, m: (g, 0, 0)),
                 pl.BlockSpec((1, stack_rows, 1), lambda g, s, t, m: (g, 0, 0)),
+                pl.BlockSpec((1, stack_rows, HD), lambda g, s, t, m: (g, 0, 0)),
+                pl.BlockSpec((1, 2, stack_rows), lambda g, s, t, m: (g, 0, 0)),
             ),
         ),
         compiler_params=pltpu.CompilerParams(
@@ -241,20 +252,17 @@
         partner * row_count, row_count, key_offset, both.shape[0],
         roles_here, sinks_here, windows_here,
     )
-    acc_p, peak_p, total_p = attend(partner_queries, both, table, meta)
-    stats_p = jnp.concatenate(
-        [peak_p.reshape(local_heads, -1), total_p.reshape(local_heads, -1)], axis=0
-    )
-    acc_p = lax.ppermute(acc_p.astype(jnp.bfloat16), "xh", [(0, 1)])
+    _, _, _, acc_p, stats_p = attend(partner_queries, both, table, meta)
+    acc_p = lax.ppermute(acc_p, "xh", [(0, 1)])
     stats_p = lax.ppermute(stats_p, "xh", [(0, 1)])
     table, meta = block_table(
         ctx * row_count, row_count, key_offset, both.shape[0],
         roles_here, sinks_here, windows_here,
     )
-    own = attend(stack_heads(queries, local_heads), both, table, meta)
+    own = attend(stack_heads(queries, local_heads), both, table, meta)[:3]
     received = half == 1
-    peak_b = jnp.where(received, stats_p[:local_heads], NEGATIVE)[:, :, None]
-    total_b = jnp.where(received, stats_p[local_heads:], 0.0)[:, :, None]
+    peak_b = jnp.where(received, stats_p[:, 0], NEGATIVE)[:, :, None]
+    total_b = jnp.where(received, stats_p[:, 1], 0.0)[:, :, None]
     acc_b = jnp.where(received, acc_p.astype(jnp.float32), 0.0)
     attended = merge(own, (acc_b, peak_b, total_b), row_count)
     partial = jnp.dot(attended, out_weight, preferred_element_type=jnp.float32)

time: 127 us -> 122 us (0.961)
  other arithmetic: 13.4 us -> 7.91 us
  local copies, waits for them, and re-layouts: 18.7 us -> 20.7 us
  Pallas kernels: 23.7 us -> 25.6 us
  starting transfers between devices: 27.9 us -> 26.4 us
  waiting for transfers between devices: 37.2 us -> 35.9 us
    ppermute x1, starting transfers between devices: 6.35 us -> 2.35 us  [scatter_sum(): got = lax.ppermute(give.astype(jnp.bfloat16), 'core', [(0, 1), (1, 0)])]
    ppermute x1, starting transfers between devices: 0.09 us -> 2.62 us  [scatter_sum(): got = lax.ppermute(give.astype(jnp.bfloat16), 'xl', [(0, 1), (1, 0)])]
    pallas_call x2 -> x0, other arithmetic: 2.51 us -> none  [attend(): pl.pallas_call(attention_kernel, out_shape=(jax.ShapeDtypeStruct(stacked....]
    pallas_call x0 -> x2, local copies, waits for them, and re-layouts: none -> 2.46 us  [attend(): pl.pallas_call(attention_kernel, out_shape=(jax.ShapeDtypeStruct(stacked....]
    pallas_call x2, Pallas kernels: 23.7 us -> 25.6 us  [attend(): pl.pallas_call(attention_kernel, out_shape=(jax.ShapeDtypeStruct(stacked....]
    exp x1 -> x0, other arithmetic: 1.75 us -> none  [merge(): scale_a = jnp.exp(peak_a - peak)]
  transfers between devices with their start and end apart: 15 -> 15, of which waited for: 7 -> 7; matrix products, arithmetic and copies ran while one was open for 19% -> 19% of each run, Pallas kernels for 8% -> 9%
where the time goes in v15:
time: 122 us
  waiting for transfers between devices  35.9 us (29%)
  starting transfers between devices  26.4 us (22%)
  Pallas kernels  25.6 us (21%)
  local copies, waits for them, and re-layouts  20.7 us (17%)
  other arithmetic  7.91 us (6%)
  matrix products  4.64 us (4%)
    ppermute x4, waiting for transfers between devices, gather_both_ways(): forward = lax.ppermute(forward, axis, right)  27.1 us
    pallas_call x2, Pallas kernels, attend(): pl.pallas_call(attention_kernel, out_shape=(jax.ShapeDtypeStruct(stacked....  25.6 us
    ppermute x3, starting transfers between devices, gather_both_ways(): backward = lax.ppermute(backward, axis, left)  9.81 us
    dynamic_update_slice x12, local copies, waits for them, and re-layouts, place(): return lax.dynamic_update_slice(result, piece, (origin * piece.shape[0], 0))  6.71 us
    ppermute x1, waiting for transfers between devices, scatter_sum(): got = lax.ppermute(give.astype(jnp.bfloat16), 'xl', [(0, 1), (1, 0)])  6.38 us
    ppermute x3, starting transfers between devices, gather_ring(): lax.ppermute(block, axis, [(i, (i + shift) % size) for i in range(size)])  5.81 us
    dot_general x1, matrix products, per_device(): partial = jnp.dot(attended, out_weight, preferred_element_type=jnp.float32)  4.64 us
    ppermute x1, starting transfers between devices, scatter_sum(): got = lax.ppermute(give.astype(jnp.bfloat16), 'xl', [(0, 1), (1, 0)])  2.62 us
  transfers between devices with their start and end apart: 15, of which 7 were waited for; matrix products, arithmetic and copies ran while one was open for 19% of the time, Pallas kernels for 9%

profile of v15, /device:TPU:1, one launch (start us, length us, event | category | flops | bytes accessed | tf_op | source)
XLA Modules:
  0.0 121.7 jit_solution(9307538636732961373)
XLA Ops:
  1.7 2.1 %collective-permute-start = (bf16[128,512]{1,0:T(8,128)(2,1)S(1)}, bf16[128,512]{1,0:T(8,128)(2,1)S(1)}, u32[]{:S(2)}, u32[]{:S(2)}) collective-permute-start(bf16[128,512]{1,0:T(8,128)(2,1)S(1)} %constant_dynamic-update-slice_fusion), channel_id=1, source_target_pairs={{0,4},{4,8},{8,12},{12,0},{1,5},{5,9},{9,13},{13,1},{2,6},{6,10},{... | collective-permute-start | bytes 393224 | tf_op jit(solution)/shard_map/ppermute | solution.py:194
  3.8 2.6 %collective-permute-start.1 = (bf16[128,512]{1,0:T(8,128)(2,1)S(1)}, bf16[128,512]{1,0:T(8,128)(2,1)S(1)}, u32[]{:S(2)}, u32[]{:S(2)}) collective-permute-start(bf16[128,512]{1,0:T(8,128)(2,1)S(1)} %constant_dynamic-update-slice_fusion), channel_id=1, source_target_pairs={{0,8},{4,12},{8,0},{12,4},{1,9},{5,13},{9,1},{13,5},{2,10},{6,14},... | collective-permute-start | bytes 393224 | tf_op jit(solution)/shard_map/ppermute | solution.py:194
  8.7 1.3 %collective-permute-start.10 = (bf16[2,512,128]{2,1,0:T(8,128)(2,1)S(1)}, bf16[2,512,128]{2,1,0:T(8,128)(2,1)}, u32[]{:S(2)}, u32[]{:S(2)}) collective-permute-start(bf16[2,512,128]{2,1,0:T(8,128)(2,1)S(1)} %bitcast.96), channel_id=1, source_target_pairs={{128,0},{129,1},{130,2},{131,3},{132,4},{133,5},{134,6},{135,7},{1... | collective-permute-start | bytes 786440 | tf_op jit(solution)/shard_map/ppermute | solution.py:246
  15.7 1.7 %collective-permute-start.3 = (bf16[512,512]{1,0:T(8,128)(2,1)S(1)}, bf16[512,512]{1,0:T(8,128)(2,1)S(1)}, u32[]{:S(2)}, u32[]{:S(2)}) collective-permute-start(bf16[512,512]{1,0:T(8,128)(2,1)S(1)} %constant_dynamic-update-slice_fusion.10), channel_id=1, source_target_pairs={{0,16},{16,32},{32,48},{48,64},{64,80},{80,96},{96,112},{112,0},{1... | collective-permute-start | bytes 1572872 | tf_op jit(solution)/shard_map/ppermute | solution.py:209
  18.3 4.0 %collective-permute-start.4 = (bf16[512,512]{1,0:T(8,128)(2,1)S(1)}, bf16[512,512]{1,0:T(8,128)(2,1)S(1)}, u32[]{:S(2)}, u32[]{:S(2)}) collective-permute-start(bf16[512,512]{1,0:T(8,128)(2,1)S(1)} %constant_dynamic-update-slice_fusion.10), channel_id=1, source_target_pairs={{0,112},{16,0},{32,16},{48,32},{64,48},{80,64},{96,80},{112,96},{1... | collective-permute-start | bytes 1572872 | tf_op jit(solution)/shard_map/ppermute | solution.py:212
  22.9 9.3 %collective-permute-done.3 = bf16[512,512]{1,0:T(8,128)(2,1)S(1)} collective-permute-done((bf16[512,512]{1,0:T(8,128)(2,1)S(1)}, bf16[512,512]{1,0:T(8,128)(2,1)S(1)}, u32[]{:S(2)}, u32[]{:S(2)}) %collective-permute-start.3) | collective-permute-done | bytes 524320 | tf_op jit(solution)/shard_map/ppermute | solution.py:209
  32.2 3.2 %collective-permute-start.6 = (bf16[512,512]{1,0:T(8,128)(2,1)S(1)}, bf16[512,512]{1,0:T(8,128)(2,1)S(1)}, u32[]{:S(2)}, u32[]{:S(2)}) collective-permute-start(bf16[512,512]{1,0:T(8,128)(2,1)S(1)} %collective-permute-done.4), channel_id=1, source_target_pairs={{0,112},{16,0},{32,16},{48,32},{64,48},{80,64},{96,80},{112,96},{1... | collective-permute-start | bytes 1572872 | tf_op jit(solution)/shard_map/ppermute | solution.py:212
  35.5 9.1 %collective-permute-done.5 = bf16[512,512]{1,0:T(8,128)(2,1)S(1)} collective-permute-done((bf16[512,512]{1,0:T(8,128)(2,1)S(1)}, bf16[512,512]{1,0:T(8,128)(2,1)S(1)}, u32[]{:S(2)}, u32[]{:S(2)}) %collective-permute-start.5) | collective-permute-done | bytes 524320 | tf_op jit(solution)/shard_map/ppermute | solution.py:209
  46.6 2.2 %broadcast_in_dim.93 = bf16[4096,512]{1,0:T(8,128)(2,1)} broadcast(bf16[]{:T(256)} %constant.155.clone.1), dimensions={} | broadcast | bytes 4194306 | tf_op jit(solution)/shard_map/broadcast_in_dim | solution.py:204
  49.7 2.7 %collective-permute-start.8 = (bf16[512,512]{1,0:T(8,128)(2,1)S(1)}, bf16[512,512]{1,0:T(8,128)(2,1)S(1)}, u32[]{:S(2)}, u32[]{:S(2)}) collective-permute-start(bf16[512,512]{1,0:T(8,128)(2,1)S(1)} %collective-permute-done.6), channel_id=1, source_target_pairs={{0,112},{16,0},{32,16},{48,32},{64,48},{80,64},{96,80},{112,96},{1... | collective-permute-start | bytes 1572872 | tf_op jit(solution)/shard_map/ppermute | solution.py:212
  53.2 3.0 %collective-permute-done.7 = bf16[512,512]{1,0:T(8,128)(2,1)S(1)} collective-permute-done((bf16[512,512]{1,0:T(8,128)(2,1)S(1)}, bf16[512,512]{1,0:T(8,128)(2,1)S(1)}, u32[]{:S(2)}, u32[]{:S(2)}) %collective-permute-start.7) | collective-permute-done | bytes 524320 | tf_op jit(solution)/shard_map/ppermute | solution.py:209
  61.0 5.7 %collective-permute-done.9 = bf16[512,512]{1,0:T(8,128)(2,1)S(1)} collective-permute-done((bf16[512,512]{1,0:T(8,128)(2,1)S(1)}, bf16[512,512]{1,0:T(8,128)(2,1)S(1)}, u32[]{:S(2)}, u32[]{:S(2)}) %collective-permute-start.9) | collective-permute-done | bytes 524320 | tf_op jit(solution)/shard_map/ppermute | solution.py:209
  67.6 15.0 %shard_map.74 = (f32[2,512,128]{2,1,0:T(8,128)}, f32[2,512,1]{2,1,0:T(8,128)}, f32[2,512,1]{2,1,0:T(8,128)}, bf16[2,512,128]{2,1,0:T(8,128)(2,1)}, f32[2,2,512]{2,1,0:T(2,128)}) custom-call(s32[2,4]{1,0:T(2,128)} %pad_add_fusion.3.table_ref, s32[2,8]{1,0:T(2,128)} %pad.8.meta_ref, bf16[2,512,128]{2,1,0:T(8,128)(2,1)} %collective-permute-done.10.q_ref, ...), custom_call_target="tpu_custom_call" | custom-call | tf_op jit(solution)/shard_map/pallas_call | solution.py:127
  82.6 1.3 %collective-permute-start.11 = (f32[2,2,512]{2,1,0:T(2,128)}, f32[2,2,512]{2,1,0:T(2,128)S(1)}, u32[]{:S(2)}, u32[]{:S(2)}) collective-permute-start(f32[2,2,512]{2,1,0:T(2,128)} %get-tuple-element.20), channel_id=1, source_target_pairs={{0,128},{1,129},{2,130},{3,131},{4,132},{5,133},{6,134},{7,135},{8... | collective-permute-start | bytes 24584 | tf_op jit(solution)/shard_map/ppermute | solution.py:257
  83.9 1.5 %collective-permute-start.12 = (bf16[2,512,128]{2,1,0:T(8,128)(2,1)}, bf16[2,512,128]{2,1,0:T(8,128)(2,1)S(1)}, u32[]{:S(2)}, u32[]{:S(2)}) collective-permute-start(bf16[2,512,128]{2,1,0:T(8,128)(2,1)} %get-tuple-element.21), channel_id=1, source_target_pairs={{0,128},{1,129},{2,130},{3,131},{4,132},{5,133},{6,134},{7,135},{8... | collective-permute-start | bytes 786440 | tf_op jit(solution)/shard_map/ppermute | solution.py:256
  86.8 10.6 %shard_map.73 = (f32[2,512,128]{2,1,0:T(8,128)}, f32[2,512,1]{2,1,0:T(8,128)}, f32[2,512,1]{2,1,0:T(8,128)}, bf16[2,512,128]{2,1,0:T(8,128)(2,1)}, f32[2,2,512]{2,1,0:T(2,128)}) custom-call(s32[2,4]{1,0:T(2,128)} %pad_add_fusion.2.table_ref, s32[2,8]{1,0:T(2,128)} %pad.7.meta_ref, bf16[2,512,128]{2,1,0:T(8,128)(2,1)} %bitcast.97, ...), custom_call_target="tpu_custom_call" | custom-call | tf_op jit(solution)/shard_map/pallas_call | solution.py:127
  97.5 1.2 %copy.74 = f32[2,512,1]{1,2,0:T(1,128)S(1)} copy(f32[2,512,1]{2,1,0:T(8,128)} %get-tuple-element.18) | data formatting | bytes 8192 | tf_op jit(solution)/shard_map/pallas_call | solution.py:127
  98.7 1.2 %copy.75 = f32[2,512,1]{1,2,0:T(1,128)S(1)} copy(f32[2,512,1]{2,1,0:T(8,128)} %get-tuple-element.22) | data formatting | bytes 8192 | tf_op jit(solution)/shard_map/pallas_call | solution.py:127
  100.0 1.5 %divide_convert_fusion = bf16[2,512,128]{2,1,0:T(8,128)(2,1)S(1)} fusion(bf16[2,512,128]{2,1,0:T(8,128)(2,1)S(1)} %collective-permute-done.12, f32[2,512,128]{2,1,0:T(8,128)} %get-tuple-element.17, f32[2,512]{1,0:T(2,128)S(1)} %bitcast.99, f32[2,512]{1,0:T(2,128)S(1)} %bitcast.100, f32[2,512]{1,0:T(2,128)S(1)} %bitcast.101, pred[]{:T(512)S(6)} %eq.20), kind=kLoop, calls=%fused_computation.13 | loop fusion | flops 917504 | bytes 1060865 | tf_op jit(solution)/shard_map/convert_element_type | solution.py:176
  101.9 4.6 %fusion = f32[2,2,32,4096]{3,2,1,0:T(8,128)S(1)} fusion(bf16[2,2,32,1024]{3,2,1,0:T(8,128)(2,1)S(1)} %dot_general.5, bf16[1024,4096]{1,0:T(8,128)(2,1)} %param.18), kind=kOutput, calls=%fused_computation.4 | convolution fusion | flops 1073741824 | bytes 10747904 | tf_op jit(solution)/shard_map/dot_general | solution.py:268
  106.7 2.4 %collective-permute-start.13 = (bf16[2,32,4096]{2,1,0:T(8,128)(2,1)S(1)}, bf16[2,32,4096]{2,1,0:T(8,128)(2,1)}, u32[]{:S(2)}, u32[]{:S(2)}) collective-permute-start(bf16[2,32,4096]{2,1,0:T(8,128)(2,1)S(1)} %bitcast_convert_fusion), channel_id=1, source_target_pairs={{0,1},{1,0},{2,3},{3,2},{4,5},{5,4},{6,7},{7,6},{8,9},{9,8},{10,11... | collective-permute-start | bytes 1572872 | tf_op jit(solution)/shard_map/ppermute | solution.py:224
  109.0 1.7 %collective-permute-done.13 = bf16[2,32,4096]{2,1,0:T(8,128)(2,1)} collective-permute-done((bf16[2,32,4096]{2,1,0:T(8,128)(2,1)S(1)}, bf16[2,32,4096]{2,1,0:T(8,128)(2,1)}, u32[]{:S(2)}, u32[]{:S(2)}) %collective-permute-start.13) | collective-permute-done | bytes 524320 | tf_op jit(solution)/shard_map/ppermute | solution.py:224
  111.9 2.6 %collective-permute-start.14 = (bf16[32,4096]{1,0:T(8,128)(2,1)S(1)}, bf16[32,4096]{1,0:T(8,128)(2,1)S(1)}, u32[]{:S(2)}, u32[]{:S(2)}) collective-permute-start(bf16[32,4096]{1,0:T(8,128)(2,1)S(1)} %bitcast_convert_fusion.1), channel_id=1, source_target_pairs={{0,2},{2,0},{1,3},{3,1},{4,6},{6,4},{5,7},{7,5},{8,10},{10,8},{9,1... | collective-permute-start | bytes 786440 | tf_op jit(solution)/shard_map/ppermute | solution.py:229
  114.5 6.4 %collective-permute-done.14 = bf16[32,4096]{1,0:T(8,128)(2,1)S(1)} collective-permute-done((bf16[32,4096]{1,0:T(8,128)(2,1)S(1)}, bf16[32,4096]{1,0:T(8,128)(2,1)S(1)}, u32[]{:S(2)}, u32[]{:S(2)}) %collective-permute-start.14) | collective-permute-done | bytes 262176 | tf_op jit(solution)/shard_map/ppermute | solution.py:229
  (102 shorter events, 24.3 us)
Async XLA Ops:
  0.0 35.4 %copy-start.1 = (s32[8]{0:T(128)S(1)}, s32[8]{0:T(128)}, u32[]{:S(2)}) copy-start(s32[8]{0:T(128)} %param.19) | copy-start | bytes 100
  0.0 44.6 %copy-start.2 = (s32[8]{0:T(128)S(1)}, s32[8]{0:T(128)}, u32[]{:S(2)}) copy-start(s32[8]{0:T(128)} %param.20) | copy-start | bytes 100
  1.7 13.9 %collective-permute-start = (bf16[128,512]{1,0:T(8,128)(2,1)S(1)}, bf16[128,512]{1,0:T(8,128)(2,1)S(1)}, u32[]{:S(2)}, u32[]{:S(2)}) collective-permute-start(bf16[128,512]{1,0:T(8,128)(2,1)S(1)} %constant_dynamic-update-slice_fusion), channel_id=1, source_target_pairs={{0,4},{4,8},{8,12},{12,0},{1,5},{5,9},{9,13},{13,1},{2,6},{6,10},{... | collective-permute-start | bytes 393224 | tf_op jit(solution)/shard_map/ppermute | solution.py:194
  3.8 11.8 %collective-permute-start.1 = (bf16[128,512]{1,0:T(8,128)(2,1)S(1)}, bf16[128,512]{1,0:T(8,128)(2,1)S(1)}, u32[]{:S(2)}, u32[]{:S(2)}) collective-permute-start(bf16[128,512]{1,0:T(8,128)(2,1)S(1)} %constant_dynamic-update-slice_fusion), channel_id=1, source_target_pairs={{0,8},{4,12},{8,0},{12,4},{1,9},{5,13},{9,1},{13,5},{2,10},{6,14},... | collective-permute-start | bytes 393224 | tf_op jit(solution)/shard_map/ppermute | solution.py:194
  6.5 9.2 %collective-permute-start.2 = (bf16[128,512]{1,0:T(8,128)(2,1)S(1)}, bf16[128,512]{1,0:T(8,128)(2,1)S(1)}, u32[]{:S(2)}, u32[]{:S(2)}) collective-permute-start(bf16[128,512]{1,0:T(8,128)(2,1)S(1)} %constant_dynamic-update-slice_fusion), channel_id=1, source_target_pairs={{0,12},{4,0},{8,4},{12,8},{1,13},{5,1},{9,5},{13,9},{2,14},{6,2},{... | collective-permute-start | bytes 393224 | tf_op jit(solution)/shard_map/ppermute | solution.py:194
  8.7 40.1 %copy-start = (bf16[128,2,4,128]{3,0,2,1:T(8,128)(2,1)}, bf16[128,2,4,128]{3,0,2,1:T(8,128)(2,1)S(1)}, u32[]{:S(2)}) copy-start(bf16[128,2,4,128]{3,0,2,1:T(8,128)(2,1)S(1)} %copy.63) | copy-start | bytes 786436
  8.7 58.9 %collective-permute-start.10 = (bf16[2,512,128]{2,1,0:T(8,128)(2,1)S(1)}, bf16[2,512,128]{2,1,0:T(8,128)(2,1)}, u32[]{:S(2)}, u32[]{:S(2)}) collective-permute-start(bf16[2,512,128]{2,1,0:T(8,128)(2,1)S(1)} %bitcast.96), channel_id=1, source_target_pairs={{128,0},{129,1},{130,2},{131,3},{132,4},{133,5},{134,6},{135,7},{1... | collective-permute-start | bytes 786440 | tf_op jit(solution)/shard_map/ppermute | solution.py:246
  15.7 16.4 %collective-permute-start.3 = (bf16[512,512]{1,0:T(8,128)(2,1)S(1)}, bf16[512,512]{1,0:T(8,128)(2,1)S(1)}, u32[]{:S(2)}, u32[]{:S(2)}) collective-permute-start(bf16[512,512]{1,0:T(8,128)(2,1)S(1)} %constant_dynamic-update-slice_fusion.10), channel_id=1, source_target_pairs={{0,16},{16,32},{32,48},{48,64},{64,80},{80,96},{96,112},{112,0},{1... | collective-permute-start | bytes 1572872 | tf_op jit(solution)/shard_map/ppermute | solution.py:209
  18.3 13.9 %collective-permute-start.4 = (bf16[512,512]{1,0:T(8,128)(2,1)S(1)}, bf16[512,512]{1,0:T(8,128)(2,1)S(1)}, u32[]{:S(2)}, u32[]{:S(2)}) collective-permute-start(bf16[512,512]{1,0:T(8,128)(2,1)S(1)} %constant_dynamic-update-slice_fusion.10), channel_id=1, source_target_pairs={{0,112},{16,0},{32,16},{48,32},{64,48},{80,64},{96,80},{112,96},{1... | collective-permute-start | bytes 1572872 | tf_op jit(solution)/shard_map/ppermute | solution.py:212
  32.1 12.5 %collective-permute-start.5 = (bf16[512,512]{1,0:T(8,128)(2,1)S(1)}, bf16[512,512]{1,0:T(8,128)(2,1)S(1)}, u32[]{:S(2)}, u32[]{:S(2)}) collective-permute-start(bf16[512,512]{1,0:T(8,128)(2,1)S(1)} %collective-permute-done.3), channel_id=1, source_target_pairs={{0,16},{16,32},{32,48},{48,64},{64,80},{80,96},{96,112},{112,0},{1... | collective-permute-start | bytes 1572872 | tf_op jit(solution)/shard_map/ppermute | solution.py:209
  32.2 17.5 %collective-permute-start.6 = (bf16[512,512]{1,0:T(8,128)(2,1)S(1)}, bf16[512,512]{1,0:T(8,128)(2,1)S(1)}, u32[]{:S(2)}, u32[]{:S(2)}) collective-permute-start(bf16[512,512]{1,0:T(8,128)(2,1)S(1)} %collective-permute-done.4), channel_id=1, source_target_pairs={{0,112},{16,0},{32,16},{48,32},{64,48},{80,64},{96,80},{112,96},{1... | collective-permute-start | bytes 1572872 | tf_op jit(solution)/shard_map/ppermute | solution.py:212
  44.6 11.5 %collective-permute-start.7 = (bf16[512,512]{1,0:T(8,128)(2,1)S(1)}, bf16[512,512]{1,0:T(8,128)(2,1)S(1)}, u32[]{:S(2)}, u32[]{:S(2)}) collective-permute-start(bf16[512,512]{1,0:T(8,128)(2,1)S(1)} %collective-permute-done.5), channel_id=1, source_target_pairs={{0,16},{16,32},{32,48},{48,64},{64,80},{80,96},{96,112},{112,0},{1... | collective-permute-start | bytes 1572872 | tf_op jit(solution)/shard_map/ppermute | solution.py:209
  49.7 10.5 %collective-permute-start.8 = (bf16[512,512]{1,0:T(8,128)(2,1)S(1)}, bf16[512,512]{1,0:T(8,128)(2,1)S(1)}, u32[]{:S(2)}, u32[]{:S(2)}) collective-permute-start(bf16[512,512]{1,0:T(8,128)(2,1)S(1)} %collective-permute-done.6), channel_id=1, source_target_pairs={{0,112},{16,0},{32,16},{48,32},{64,48},{80,64},{96,80},{112,96},{1... | collective-permute-start | bytes 1572872 | tf_op jit(solution)/shard_map/ppermute | solution.py:212
  56.1 10.6 %collective-permute-start.9 = (bf16[512,512]{1,0:T(8,128)(2,1)S(1)}, bf16[512,512]{1,0:T(8,128)(2,1)S(1)}, u32[]{:S(2)}, u32[]{:S(2)}) collective-permute-start(bf16[512,512]{1,0:T(8,128)(2,1)S(1)} %collective-permute-done.7), channel_id=1, source_target_pairs={{0,16},{16,32},{32,48},{48,64},{64,80},{80,96},{96,112},{112,0},{1... | collective-permute-start | bytes 1572872 | tf_op jit(solution)/shard_map/ppermute | solution.py:209
  82.6 17.4 %collective-permute-start.11 = (f32[2,2,512]{2,1,0:T(2,128)}, f32[2,2,512]{2,1,0:T(2,128)S(1)}, u32[]{:S(2)}, u32[]{:S(2)}) collective-permute-start(f32[2,2,512]{2,1,0:T(2,128)} %get-tuple-element.20), channel_id=1, source_target_pairs={{0,128},{1,129},{2,130},{3,131},{4,132},{5,133},{6,134},{7,135},{8... | collective-permute-start | bytes 24584 | tf_op jit(solution)/shard_map/ppermute | solution.py:257
  83.9 16.2 %collective-permute-start.12 = (bf16[2,512,128]{2,1,0:T(8,128)(2,1)}, bf16[2,512,128]{2,1,0:T(8,128)(2,1)S(1)}, u32[]{:S(2)}, u32[]{:S(2)}) collective-permute-start(bf16[2,512,128]{2,1,0:T(8,128)(2,1)} %get-tuple-element.21), channel_id=1, source_target_pairs={{0,128},{1,129},{2,130},{3,131},{4,132},{5,133},{6,134},{7,135},{8... | collective-permute-start | bytes 786440 | tf_op jit(solution)/shard_map/ppermute | solution.py:256
  106.7 4.0 %collective-permute-start.13 = (bf16[2,32,4096]{2,1,0:T(8,128)(2,1)S(1)}, bf16[2,32,4096]{2,1,0:T(8,128)(2,1)}, u32[]{:S(2)}, u32[]{:S(2)}) collective-permute-start(bf16[2,32,4096]{2,1,0:T(8,128)(2,1)S(1)} %bitcast_convert_fusion), channel_id=1, source_target_pairs={{0,1},{1,0},{2,3},{3,2},{4,5},{5,4},{6,7},{7,6},{8,9},{9,8},{10,11... | collective-permute-start | bytes 1572872 | tf_op jit(solution)/shard_map/ppermute | solution.py:224
  111.9 9.0 %collective-permute-start.14 = (bf16[32,4096]{1,0:T(8,128)(2,1)S(1)}, bf16[32,4096]{1,0:T(8,128)(2,1)S(1)}, u32[]{:S(2)}, u32[]{:S(2)}) collective-permute-start(bf16[32,4096]{1,0:T(8,128)(2,1)S(1)} %bitcast_convert_fusion.1), channel_id=1, source_target_pairs={{0,2},{2,0},{1,3},{3,1},{4,6},{6,4},{5,7},{7,5},{8,10},{10,8},{9,1... | collective-permute-start | bytes 786440 | tf_op jit(solution)/shard_map/ppermute | solution.py:229

commit v16 on v15

--- a/solution.py
+++ b/solution.py
@@ -85,17 +85,18 @@
         stats_ref[0, 1:2, :] = jnp.transpose(total_ref[0])
 
 
-def block_table(row_base, row_count, key_offset, key_count, roles, sinks, windows):
+def block_table(row_bases, row_count, key_offset, key_count, roles, sinks, windows):
     blocks = key_count // KEY_BLOCK
     first = key_offset + jnp.arange(blocks, dtype=jnp.int32) * KEY_BLOCK
     last_key = first + KEY_BLOCK - 1
+    row_base = row_bases[:, None]
     last_row = row_base + row_count - 1
-    causal = first <= last_row
+    causal = first[None, :] <= last_row
     reach = last_key[None, :] >= row_base - windows[:, None] + 1
     sunk = first[None, :] < sinks[:, None]
     retrieval = roles[:, None] == 1
-    needed = causal[None, :] & (retrieval | reach | sunk)
-    whole = (last_key <= row_base)[None, :] & (
+    needed = causal & (retrieval | reach | sunk)
+    whole = (last_key[None, :] <= row_base) & (
         retrieval
         | (last_key[None, :] < sinks[:, None])
         | (last_row - first[None, :] < windows[:, None])
@@ -112,7 +113,7 @@
             roles,
             sinks,
             windows,
-            jnp.broadcast_to(row_base, count.shape),
+            row_bases,
             jnp.broadcast_to(key_offset, count.shape),
         ],
         axis=1,
@@ -248,17 +249,21 @@
     both = gather_ring(both, "y")
     both = gather_both_ways(both, "z")
     key_offset = half * both.shape[0]
-    table, meta = block_table(
-        partner * row_count, row_count, key_offset, both.shape[0],
-        roles_here, sinks_here, windows_here,
-    )
+    row_bases = jnp.concatenate(
+        [jnp.broadcast_to(partner * row_count, (local_heads,)),
+         jnp.broadcast_to(ctx * row_count, (local_heads,))]
+    ).astype(jnp.int32)
+    tables, metas = block_table(
+        row_bases, row_count, key_offset, both.shape[0],
+        jnp.concatenate([roles_here, roles_here]),
+        jnp.concatenate([sinks_here, sinks_here]),
+        jnp.concatenate([windows_here, windows_here]),
+    )
+    table, meta = tables[:local_heads], metas[:local_heads]
     _, _, _, acc_p, stats_p = attend(partner_queries, both, table, meta)
     acc_p = lax.ppermute(acc_p, "xh", [(0, 1)])
     stats_p = lax.ppermute(stats_p, "xh", [(0, 1)])
-    table, meta = block_table(
-        ctx * row_count, row_count, key_offset, both.shape[0],
-        roles_here, sinks_here, windows_here,
-    )
+    table, meta = tables[local_heads:], metas[local_heads:]
     own = attend(stack_heads(queries, local_heads), both, table, meta)[:3]
     received = half == 1
     peak_b = jnp.where(received, stats_p[:, 0], NEGATIVE)[:, :, None]

time: 122 us -> 120 us (0.984)
  other arithmetic: 7.91 us -> 4.9 us
  Pallas kernels: 25.6 us -> 24.3 us
    ppermute x1, starting transfers between devices: 2.35 us -> 5.02 us  [scatter_sum(): got = lax.ppermute(give.astype(jnp.bfloat16), 'core', [(0, 1), (1, 0)])]
    ppermute x4, waiting for transfers between devices: 27.1 us -> 29 us  [gather_both_ways(): forward = lax.ppermute(forward, axis, right)]
    dynamic_slice x0 -> x2, local copies, waits for them, and re-layouts: none -> 1.46 us  [the longest x1 0.73 us: per_device(): windows_here = lax.dynamic_slice_in_dim(window_len, first_head, local_heads)]
    ppermute x1, starting transfers between devices: 2.62 us -> 1.3 us  [scatter_sum(): got = lax.ppermute(give.astype(jnp.bfloat16), 'xl', [(0, 1), (1, 0)])]
    pallas_call x2, Pallas kernels: 25.6 us -> 24.3 us  [attend(): pl.pallas_call(attention_kernel, out_shape=(jax.ShapeDtypeStruct(stacked....]
  transfers between devices with their start and end apart: 15 -> 15, of which waited for: 7 -> 6; matrix products, arithmetic and copies ran while one was open for 19% -> 17% of each run, Pallas kernels for 9% -> 9%
where the time goes in v16:
time: 120 us; the launch traced here: 119 us
  waiting for transfers between devices  37 us (31%)
  starting transfers between devices  27.3 us (23%)
  Pallas kernels  24.3 us (20%)
  local copies, waits for them, and re-layouts  20.5 us (17%)
  other arithmetic  4.9 us (4%)
  matrix products  4.64 us (4%)
    ppermute x4, waiting for transfers between devices, gather_both_ways(): forward = lax.ppermute(forward, axis, right)  29 us
    pallas_call x2, Pallas kernels, attend(): pl.pallas_call(attention_kernel, out_shape=(jax.ShapeDtypeStruct(stacked....  24.3 us
    ppermute x3, starting transfers between devices, gather_both_ways(): backward = lax.ppermute(backward, axis, left)  9.35 us
    dynamic_update_slice x12, local copies, waits for them, and re-layouts, place(): return lax.dynamic_update_slice(result, piece, (origin * piece.shape[0], 0))  6.78 us
    ppermute x1, waiting for transfers between devices, scatter_sum(): got = lax.ppermute(give.astype(jnp.bfloat16), 'xl', [(0, 1), (1, 0)])  6.31 us
    ppermute x3, starting transfers between devices, gather_ring(): lax.ppermute(block, axis, [(i, (i + shift) % size) for i in range(size)])  5.81 us
    ppermute x1, starting transfers between devices, scatter_sum(): got = lax.ppermute(give.astype(jnp.bfloat16), 'core', [(0, 1), (1, 0)])  5.02 us
    dot_general x1, matrix products, per_device(): partial = jnp.dot(attended, out_weight, preferred_element_type=jnp.float32)  4.64 us
  transfers between devices with their start and end apart: 15, of which 6 were waited for; matrix products, arithmetic and copies ran while one was open for 17% of the time, Pallas kernels for 9%

profile of v16, /device:TPU:1, one launch (start us, length us, event | category | flops | bytes accessed | tf_op | source)
XLA Modules:
  0.0 119.1 jit_solution(360662895830438798)
XLA Ops:
  1.7 2.1 %collective-permute-start = (bf16[128,512]{1,0:T(8,128)(2,1)S(1)}, bf16[128,512]{1,0:T(8,128)(2,1)S(1)}, u32[]{:S(2)}, u32[]{:S(2)}) collective-permute-start(bf16[128,512]{1,0:T(8,128)(2,1)S(1)} %constant_dynamic-update-slice_fusion), channel_id=1, source_target_pairs={{0,4},{4,8},{8,12},{12,0},{1,5},{5,9},{9,13},{13,1},{2,6},{6,10},{... | collective-permute-start | bytes 393224 | tf_op jit(solution)/shard_map/ppermute | solution.py:195
  3.8 2.6 %collective-permute-start.1 = (bf16[128,512]{1,0:T(8,128)(2,1)S(1)}, bf16[128,512]{1,0:T(8,128)(2,1)S(1)}, u32[]{:S(2)}, u32[]{:S(2)}) collective-permute-start(bf16[128,512]{1,0:T(8,128)(2,1)S(1)} %constant_dynamic-update-slice_fusion), channel_id=1, source_target_pairs={{0,8},{4,12},{8,0},{12,4},{1,9},{5,13},{9,1},{13,5},{2,10},{6,14},... | collective-permute-start | bytes 393224 | tf_op jit(solution)/shard_map/ppermute | solution.py:195
  8.7 1.3 %collective-permute-start.10 = (bf16[2,512,128]{2,1,0:T(8,128)(2,1)S(1)}, bf16[2,512,128]{2,1,0:T(8,128)(2,1)}, u32[]{:S(2)}, u32[]{:S(2)}) collective-permute-start(bf16[2,512,128]{2,1,0:T(8,128)(2,1)S(1)} %bitcast.72), channel_id=1, source_target_pairs={{128,0},{129,1},{130,2},{131,3},{132,4},{133,5},{134,6},{135,7},{1... | collective-permute-start | bytes 786440 | tf_op jit(solution)/shard_map/ppermute | solution.py:247
  14.7 1.7 %collective-permute-start.3 = (bf16[512,512]{1,0:T(8,128)(2,1)S(1)}, bf16[512,512]{1,0:T(8,128)(2,1)S(1)}, u32[]{:S(2)}, u32[]{:S(2)}) collective-permute-start(bf16[512,512]{1,0:T(8,128)(2,1)S(1)} %constant_dynamic-update-slice_fusion.10), channel_id=1, source_target_pairs={{0,16},{16,32},{32,48},{48,64},{64,80},{80,96},{96,112},{112,0},{1... | collective-permute-start | bytes 1572872 | tf_op jit(solution)/shard_map/ppermute | solution.py:210
  16.6 4.0 %collective-permute-start.4 = (bf16[512,512]{1,0:T(8,128)(2,1)S(1)}, bf16[512,512]{1,0:T(8,128)(2,1)S(1)}, u32[]{:S(2)}, u32[]{:S(2)}) collective-permute-start(bf16[512,512]{1,0:T(8,128)(2,1)S(1)} %constant_dynamic-update-slice_fusion.10), channel_id=1, source_target_pairs={{0,112},{16,0},{32,16},{48,32},{64,48},{80,64},{96,80},{112,96},{1... | collective-permute-start | bytes 1572872 | tf_op jit(solution)/shard_map/ppermute | solution.py:213
  20.9 10.1 %collective-permute-done.3 = bf16[512,512]{1,0:T(8,128)(2,1)S(1)} collective-permute-done((bf16[512,512]{1,0:T(8,128)(2,1)S(1)}, bf16[512,512]{1,0:T(8,128)(2,1)S(1)}, u32[]{:S(2)}, u32[]{:S(2)}) %collective-permute-start.3) | collective-permute-done | bytes 524320 | tf_op jit(solution)/shard_map/ppermute | solution.py:210
  32.0 2.7 %collective-permute-start.6 = (bf16[512,512]{1,0:T(8,128)(2,1)S(1)}, bf16[512,512]{1,0:T(8,128)(2,1)S(1)}, u32[]{:S(2)}, u32[]{:S(2)}) collective-permute-start(bf16[512,512]{1,0:T(8,128)(2,1)S(1)} %collective-permute-done.4), channel_id=1, source_target_pairs={{0,112},{16,0},{32,16},{48,32},{64,48},{80,64},{96,80},{112,96},{1... | collective-permute-start | bytes 1572872 | tf_op jit(solution)/shard_map/ppermute | solution.py:213
  35.3 8.2 %collective-permute-done.5 = bf16[512,512]{1,0:T(8,128)(2,1)S(1)} collective-permute-done((bf16[512,512]{1,0:T(8,128)(2,1)S(1)}, bf16[512,512]{1,0:T(8,128)(2,1)S(1)}, u32[]{:S(2)}, u32[]{:S(2)}) %collective-permute-start.5) | collective-permute-done | bytes 524320 | tf_op jit(solution)/shard_map/ppermute | solution.py:210
  44.2 2.2 %broadcast_in_dim.78 = bf16[4096,512]{1,0:T(8,128)(2,1)} broadcast(bf16[]{:T(256)} %constant.164.clone.1), dimensions={} | broadcast | bytes 4194306 | tf_op jit(solution)/shard_map/broadcast_in_dim | solution.py:205
  47.3 2.6 %collective-permute-start.8 = (bf16[512,512]{1,0:T(8,128)(2,1)S(1)}, bf16[512,512]{1,0:T(8,128)(2,1)S(1)}, u32[]{:S(2)}, u32[]{:S(2)}) collective-permute-start(bf16[512,512]{1,0:T(8,128)(2,1)S(1)} %collective-permute-done.6), channel_id=1, source_target_pairs={{0,112},{16,0},{32,16},{48,32},{64,48},{80,64},{96,80},{112,96},{1... | collective-permute-start | bytes 1572872 | tf_op jit(solution)/shard_map/ppermute | solution.py:213
  50.7 4.3 %collective-permute-done.7 = bf16[512,512]{1,0:T(8,128)(2,1)S(1)} collective-permute-done((bf16[512,512]{1,0:T(8,128)(2,1)S(1)}, bf16[512,512]{1,0:T(8,128)(2,1)S(1)}, u32[]{:S(2)}, u32[]{:S(2)}) %collective-permute-start.7) | collective-permute-done | bytes 524320 | tf_op jit(solution)/shard_map/ppermute | solution.py:210
  59.3 6.4 %collective-permute-done.9 = bf16[512,512]{1,0:T(8,128)(2,1)S(1)} collective-permute-done((bf16[512,512]{1,0:T(8,128)(2,1)S(1)}, bf16[512,512]{1,0:T(8,128)(2,1)S(1)}, u32[]{:S(2)}, u32[]{:S(2)}) %collective-permute-start.9) | collective-permute-done | bytes 524320 | tf_op jit(solution)/shard_map/ppermute | solution.py:210
  66.5 13.7 %shard_map.74 = (f32[2,512,128]{2,1,0:T(8,128)}, f32[2,512,1]{2,1,0:T(8,128)}, f32[2,512,1]{2,1,0:T(8,128)}, bf16[2,512,128]{2,1,0:T(8,128)(2,1)}, f32[2,2,512]{2,1,0:T(2,128)}) custom-call(s32[2,4]{1,0:T(2,128)} %get-tuple-element.51.table_ref, s32[2,8]{1,0:T(2,128)} %get-tuple-element.49.meta_ref, bf16[2,512,128]{2,1,0:T(8,128)(2,1)} %collective-permute-done.10.q_ref, ...), custom_call_target="tpu_custom_call" | custom-call | tf_op jit(solution)/shard_map/pallas_call | solution.py:128
  80.2 1.3 %collective-permute-start.12 = (bf16[2,512,128]{2,1,0:T(8,128)(2,1)}, bf16[2,512,128]{2,1,0:T(8,128)(2,1)S(1)}, u32[]{:S(2)}, u32[]{:S(2)}) collective-permute-start(bf16[2,512,128]{2,1,0:T(8,128)(2,1)} %get-tuple-element.17), channel_id=1, source_target_pairs={{0,128},{1,129},{2,130},{3,131},{4,132},{5,133},{6,134},{7,135},{8... | collective-permute-start | bytes 786440 | tf_op jit(solution)/shard_map/ppermute | solution.py:264
  81.5 1.5 %collective-permute-start.11 = (f32[2,2,512]{2,1,0:T(2,128)}, f32[2,2,512]{2,1,0:T(2,128)S(1)}, u32[]{:S(2)}, u32[]{:S(2)}) collective-permute-start(f32[2,2,512]{2,1,0:T(2,128)} %get-tuple-element.16), channel_id=1, source_target_pairs={{0,128},{1,129},{2,130},{3,131},{4,132},{5,133},{6,134},{7,135},{8... | collective-permute-start | bytes 24584 | tf_op jit(solution)/shard_map/ppermute | solution.py:265
  83.0 10.7 %shard_map.73 = (f32[2,512,128]{2,1,0:T(8,128)}, f32[2,512,1]{2,1,0:T(8,128)}, f32[2,512,1]{2,1,0:T(8,128)}, bf16[2,512,128]{2,1,0:T(8,128)(2,1)}, f32[2,2,512]{2,1,0:T(2,128)}) custom-call(s32[2,4]{1,0:T(2,128)} %get-tuple-element.50.table_ref, s32[2,8]{1,0:T(2,128)} %get-tuple-element.48.meta_ref, bf16[2,512,128]{2,1,0:T(8,128)(2,1)} %bitcast.73, ...), custom_call_target="tpu_custom_call" | custom-call | tf_op jit(solution)/shard_map/pallas_call | solution.py:128
  93.7 1.2 %copy.48 = f32[2,512,1]{1,2,0:T(1,128)S(1)} copy(f32[2,512,1]{2,1,0:T(8,128)} %get-tuple-element.15) | data formatting | bytes 8192 | tf_op jit(solution)/shard_map/pallas_call | solution.py:128
  94.9 1.2 %copy.49 = f32[2,512,1]{1,2,0:T(1,128)S(1)} copy(f32[2,512,1]{2,1,0:T(8,128)} %get-tuple-element.18) | data formatting | bytes 8192 | tf_op jit(solution)/shard_map/pallas_call | solution.py:128
  96.2 1.5 %divide_convert_fusion = bf16[2,512,128]{2,1,0:T(8,128)(2,1)S(1)} fusion(bf16[2,512,128]{2,1,0:T(8,128)(2,1)S(1)} %collective-permute-done.12, f32[2,512,128]{2,1,0:T(8,128)} %get-tuple-element.14, f32[2,512]{1,0:T(2,128)S(1)} %bitcast.75, f32[2,512]{1,0:T(2,128)S(1)} %bitcast.76, f32[2,512]{1,0:T(2,128)S(1)} %bitcast.77, pred[]{:T(512)S(6)} %eq.23), kind=kLoop, calls=%fused_computation.11 | loop fusion | flops 917504 | bytes 1060865 | tf_op jit(solution)/shard_map/convert_element_type | solution.py:177
  98.1 4.6 %fusion = f32[2,2,32,4096]{3,2,1,0:T(8,128)S(1)} fusion(bf16[2,2,32,1024]{3,2,1,0:T(8,128)(2,1)S(1)} %dot_general.5, bf16[1024,4096]{1,0:T(8,128)(2,1)} %param.14), kind=kOutput, calls=%fused_computation.2 | convolution fusion | flops 1073741824 | bytes 10747904 | tf_op jit(solution)/shard_map/dot_general | solution.py:273
  102.9 5.0 %collective-permute-start.13 = (bf16[2,32,4096]{2,1,0:T(8,128)(2,1)S(1)}, bf16[2,32,4096]{2,1,0:T(8,128)(2,1)}, u32[]{:S(2)}, u32[]{:S(2)}) collective-permute-start(bf16[2,32,4096]{2,1,0:T(8,128)(2,1)S(1)} %bitcast_convert_fusion), channel_id=1, source_target_pairs={{0,1},{1,0},{2,3},{3,2},{4,5},{5,4},{6,7},{7,6},{8,9},{9,8},{10,11... | collective-permute-start | bytes 1572872 | tf_op jit(solution)/shard_map/ppermute | solution.py:225
  107.9 1.7 %collective-permute-done.13 = bf16[2,32,4096]{2,1,0:T(8,128)(2,1)} collective-permute-done((bf16[2,32,4096]{2,1,0:T(8,128)(2,1)S(1)}, bf16[2,32,4096]{2,1,0:T(8,128)(2,1)}, u32[]{:S(2)}, u32[]{:S(2)}) %collective-permute-start.13) | collective-permute-done | bytes 524320 | tf_op jit(solution)/shard_map/ppermute | solution.py:225
  110.7 1.3 %collective-permute-start.14 = (bf16[32,4096]{1,0:T(8,128)(2,1)S(1)}, bf16[32,4096]{1,0:T(8,128)(2,1)S(1)}, u32[]{:S(2)}, u32[]{:S(2)}) collective-permute-start(bf16[32,4096]{1,0:T(8,128)(2,1)S(1)} %bitcast_convert_fusion.1), channel_id=1, source_target_pairs={{0,2},{2,0},{1,3},{3,1},{4,6},{6,4},{5,7},{7,5},{8,10},{10,8},{9,1... | collective-permute-start | bytes 786440 | tf_op jit(solution)/shard_map/ppermute | solution.py:230
  112.0 6.3 %collective-permute-done.14 = bf16[32,4096]{1,0:T(8,128)(2,1)S(1)} collective-permute-done((bf16[32,4096]{1,0:T(8,128)(2,1)S(1)}, bf16[32,4096]{1,0:T(8,128)(2,1)S(1)}, u32[]{:S(2)}, u32[]{:S(2)}) %collective-permute-start.14) | collective-permute-done | bytes 262176 | tf_op jit(solution)/shard_map/ppermute | solution.py:230
  (83 shorter events, 20.3 us)
Async XLA Ops:
  1.7 12.9 %collective-permute-start = (bf16[128,512]{1,0:T(8,128)(2,1)S(1)}, bf16[128,512]{1,0:T(8,128)(2,1)S(1)}, u32[]{:S(2)}, u32[]{:S(2)}) collective-permute-start(bf16[128,512]{1,0:T(8,128)(2,1)S(1)} %constant_dynamic-update-slice_fusion), channel_id=1, source_target_pairs={{0,4},{4,8},{8,12},{12,0},{1,5},{5,9},{9,13},{13,1},{2,6},{6,10},{... | collective-permute-start | bytes 393224 | tf_op jit(solution)/shard_map/ppermute | solution.py:195
  3.8 10.8 %collective-permute-start.1 = (bf16[128,512]{1,0:T(8,128)(2,1)S(1)}, bf16[128,512]{1,0:T(8,128)(2,1)S(1)}, u32[]{:S(2)}, u32[]{:S(2)}) collective-permute-start(bf16[128,512]{1,0:T(8,128)(2,1)S(1)} %constant_dynamic-update-slice_fusion), channel_id=1, source_target_pairs={{0,8},{4,12},{8,0},{12,4},{1,9},{5,13},{9,1},{13,5},{2,10},{6,14},... | collective-permute-start | bytes 393224 | tf_op jit(solution)/shard_map/ppermute | solution.py:195
  6.4 8.2 %collective-permute-start.2 = (bf16[128,512]{1,0:T(8,128)(2,1)S(1)}, bf16[128,512]{1,0:T(8,128)(2,1)S(1)}, u32[]{:S(2)}, u32[]{:S(2)}) collective-permute-start(bf16[128,512]{1,0:T(8,128)(2,1)S(1)} %constant_dynamic-update-slice_fusion), channel_id=1, source_target_pairs={{0,12},{4,0},{8,4},{12,8},{1,13},{5,1},{9,5},{13,9},{2,14},{6,2},{... | collective-permute-start | bytes 393224 | tf_op jit(solution)/shard_map/ppermute | solution.py:195
  8.7 38.6 %copy-start = (bf16[128,2,4,128]{3,0,2,1:T(8,128)(2,1)}, bf16[128,2,4,128]{3,0,2,1:T(8,128)(2,1)S(1)}, u32[]{:S(2)}) copy-start(bf16[128,2,4,128]{3,0,2,1:T(8,128)(2,1)S(1)} %copy.46) | copy-start | bytes 786436
  8.7 57.8 %collective-permute-start.10 = (bf16[2,512,128]{2,1,0:T(8,128)(2,1)S(1)}, bf16[2,512,128]{2,1,0:T(8,128)(2,1)}, u32[]{:S(2)}, u32[]{:S(2)}) collective-permute-start(bf16[2,512,128]{2,1,0:T(8,128)(2,1)S(1)} %bitcast.72), channel_id=1, source_target_pairs={{128,0},{129,1},{130,2},{131,3},{132,4},{133,5},{134,6},{135,7},{1... | collective-permute-start | bytes 786440 | tf_op jit(solution)/shard_map/ppermute | solution.py:247
  14.7 16.4 %collective-permute-start.3 = (bf16[512,512]{1,0:T(8,128)(2,1)S(1)}, bf16[512,512]{1,0:T(8,128)(2,1)S(1)}, u32[]{:S(2)}, u32[]{:S(2)}) collective-permute-start(bf16[512,512]{1,0:T(8,128)(2,1)S(1)} %constant_dynamic-update-slice_fusion.10), channel_id=1, source_target_pairs={{0,16},{16,32},{32,48},{48,64},{64,80},{80,96},{96,112},{112,0},{1... | collective-permute-start | bytes 1572872 | tf_op jit(solution)/shard_map/ppermute | solution.py:210
  16.6 15.4 %collective-permute-start.4 = (bf16[512,512]{1,0:T(8,128)(2,1)S(1)}, bf16[512,512]{1,0:T(8,128)(2,1)S(1)}, u32[]{:S(2)}, u32[]{:S(2)}) collective-permute-start(bf16[512,512]{1,0:T(8,128)(2,1)S(1)} %constant_dynamic-update-slice_fusion.10), channel_id=1, source_target_pairs={{0,112},{16,0},{32,16},{48,32},{64,48},{80,64},{96,80},{112,96},{1... | collective-permute-start | bytes 1572872 | tf_op jit(solution)/shard_map/ppermute | solution.py:213
  31.0 12.5 %collective-permute-start.5 = (bf16[512,512]{1,0:T(8,128)(2,1)S(1)}, bf16[512,512]{1,0:T(8,128)(2,1)S(1)}, u32[]{:S(2)}, u32[]{:S(2)}) collective-permute-start(bf16[512,512]{1,0:T(8,128)(2,1)S(1)} %collective-permute-done.3), channel_id=1, source_target_pairs={{0,16},{16,32},{32,48},{48,64},{64,80},{80,96},{96,112},{112,0},{1... | collective-permute-start | bytes 1572872 | tf_op jit(solution)/shard_map/ppermute | solution.py:210
  32.0 15.3 %collective-permute-start.6 = (bf16[512,512]{1,0:T(8,128)(2,1)S(1)}, bf16[512,512]{1,0:T(8,128)(2,1)S(1)}, u32[]{:S(2)}, u32[]{:S(2)}) collective-permute-start(bf16[512,512]{1,0:T(8,128)(2,1)S(1)} %collective-permute-done.4), channel_id=1, source_target_pairs={{0,112},{16,0},{32,16},{48,32},{64,48},{80,64},{96,80},{112,96},{1... | collective-permute-start | bytes 1572872 | tf_op jit(solution)/shard_map/ppermute | solution.py:213
  43.5 11.5 %collective-permute-start.7 = (bf16[512,512]{1,0:T(8,128)(2,1)S(1)}, bf16[512,512]{1,0:T(8,128)(2,1)S(1)}, u32[]{:S(2)}, u32[]{:S(2)}) collective-permute-start(bf16[512,512]{1,0:T(8,128)(2,1)S(1)} %collective-permute-done.5), channel_id=1, source_target_pairs={{0,16},{16,32},{32,48},{48,64},{64,80},{80,96},{96,112},{112,0},{1... | collective-permute-start | bytes 1572872 | tf_op jit(solution)/shard_map/ppermute | solution.py:210
  47.3 11.2 %collective-permute-start.8 = (bf16[512,512]{1,0:T(8,128)(2,1)S(1)}, bf16[512,512]{1,0:T(8,128)(2,1)S(1)}, u32[]{:S(2)}, u32[]{:S(2)}) collective-permute-start(bf16[512,512]{1,0:T(8,128)(2,1)S(1)} %collective-permute-done.6), channel_id=1, source_target_pairs={{0,112},{16,0},{32,16},{48,32},{64,48},{80,64},{96,80},{112,96},{1... | collective-permute-start | bytes 1572872 | tf_op jit(solution)/shard_map/ppermute | solution.py:213
  55.1 10.6 %collective-permute-start.9 = (bf16[512,512]{1,0:T(8,128)(2,1)S(1)}, bf16[512,512]{1,0:T(8,128)(2,1)S(1)}, u32[]{:S(2)}, u32[]{:S(2)}) collective-permute-start(bf16[512,512]{1,0:T(8,128)(2,1)S(1)} %collective-permute-done.7), channel_id=1, source_target_pairs={{0,16},{16,32},{32,48},{48,64},{64,80},{80,96},{96,112},{112,0},{1... | collective-permute-start | bytes 1572872 | tf_op jit(solution)/shard_map/ppermute | solution.py:210
  80.2 16.0 %collective-permute-start.12 = (bf16[2,512,128]{2,1,0:T(8,128)(2,1)}, bf16[2,512,128]{2,1,0:T(8,128)(2,1)S(1)}, u32[]{:S(2)}, u32[]{:S(2)}) collective-permute-start(bf16[2,512,128]{2,1,0:T(8,128)(2,1)} %get-tuple-element.17), channel_id=1, source_target_pairs={{0,128},{1,129},{2,130},{3,131},{4,132},{5,133},{6,134},{7,135},{8... | collective-permute-start | bytes 786440 | tf_op jit(solution)/shard_map/ppermute | solution.py:264
  81.5 14.7 %collective-permute-start.11 = (f32[2,2,512]{2,1,0:T(2,128)}, f32[2,2,512]{2,1,0:T(2,128)S(1)}, u32[]{:S(2)}, u32[]{:S(2)}) collective-permute-start(f32[2,2,512]{2,1,0:T(2,128)} %get-tuple-element.16), channel_id=1, source_target_pairs={{0,128},{1,129},{2,130},{3,131},{4,132},{5,133},{6,134},{7,135},{8... | collective-permute-start | bytes 24584 | tf_op jit(solution)/shard_map/ppermute | solution.py:265
  102.9 6.7 %collective-permute-start.13 = (bf16[2,32,4096]{2,1,0:T(8,128)(2,1)S(1)}, bf16[2,32,4096]{2,1,0:T(8,128)(2,1)}, u32[]{:S(2)}, u32[]{:S(2)}) collective-permute-start(bf16[2,32,4096]{2,1,0:T(8,128)(2,1)S(1)} %bitcast_convert_fusion), channel_id=1, source_target_pairs={{0,1},{1,0},{2,3},{3,2},{4,5},{5,4},{6,7},{7,6},{8,9},{9,8},{10,11... | collective-permute-start | bytes 1572872 | tf_op jit(solution)/shard_map/ppermute | solution.py:225
  110.7 7.6 %collective-permute-start.14 = (bf16[32,4096]{1,0:T(8,128)(2,1)S(1)}, bf16[32,4096]{1,0:T(8,128)(2,1)S(1)}, u32[]{:S(2)}, u32[]{:S(2)}) collective-permute-start(bf16[32,4096]{1,0:T(8,128)(2,1)S(1)} %bitcast_convert_fusion.1), channel_id=1, source_target_pairs={{0,2},{2,0},{1,3},{3,1},{4,6},{6,4},{5,7},{7,5},{8,10},{10,8},{9,1... | collective-permute-start | bytes 786440 | tf_op jit(solution)/shard_map/ppermute | solution.py:230

commit v17 on v16

--- a/solution.py
+++ b/solution.py
@@ -197,12 +197,11 @@
     return result
 
 
-def gather_both_ways(block, axis):
+def gather_both_ways(block, axis, result):
     size = lax.axis_size(axis)
     here = lax.axis_index(axis)
     right = [(i, (i + 1) % size) for i in range(size)]
     left = [(i, (i - 1) % size) for i in range(size)]
-    result = jnp.zeros((size * block.shape[0], block.shape[1]), block.dtype)
     result = place(result, block, here)
     forward = block
     backward = block
@@ -244,10 +243,15 @@
     roles_here = lax.dynamic_slice_in_dim(head_role, first_head, local_heads)
     sinks_here = lax.dynamic_slice_in_dim(sink_len, first_head, local_heads)
     windows_here = lax.dynamic_slice_in_dim(window_len, first_head, local_heads)
-    partner_queries = lax.ppermute(stack_heads(queries, local_heads), "xh", [(1, 0)])
+    blank = jnp.broadcast_to(
+        key_states[0, 0] * 0,
+        (lax.axis_size("z") * lax.axis_size("y") * key_states.shape[0], 2 * key_states.shape[1]),
+    )
+    blank, own_queries = lax.optimization_barrier((blank, stack_heads(queries, local_heads)))
+    partner_queries = lax.ppermute(own_queries, "xh", [(1, 0)])
     both = jnp.concatenate([key_states, value_states], axis=1)
     both = gather_ring(both, "y")
-    both = gather_both_ways(both, "z")
+    both = gather_both_ways(both, "z", blank)
     key_offset = half * both.shape[0]
     row_bases = jnp.concatenate(
         [jnp.broadcast_to(partner * row_count, (local_heads,)),

time: 120 us -> 123 us (1.025)
  waiting for transfers between devices: 37 us -> 40.5 us
    ppermute x4, waiting for transfers between devices: 29 us -> 31.3 us  [gather_both_ways(): forward = lax.ppermute(forward, axis, right)]
    ppermute x1, starting transfers between devices: 5.02 us -> 6.35 us  [scatter_sum(): got = lax.ppermute(give.astype(jnp.bfloat16), 'core', [(0, 1), (1, 0)])]
  transfers between devices with their start and end apart: 15 -> 15, of which waited for: 6 -> 6; matrix products, arithmetic and copies ran while one was open for 17% -> 16% of each run, Pallas kernels for 9% -> 9%
where the time goes in v17:
time: 123 us
  waiting for transfers between devices  40.5 us (33%)
  starting transfers between devices  27.4 us (22%)
  Pallas kernels  24.3 us (20%)
  local copies, waits for them, and re-layouts  19.8 us (16%)
  other arithmetic  4.9 us (4%)
  matrix products  4.64 us (4%)
    ppermute x4, waiting for transfers between devices, gather_both_ways(): forward = lax.ppermute(forward, axis, right)  31.3 us
    pallas_call x2, Pallas kernels, attend(): pl.pallas_call(attention_kernel, out_shape=(jax.ShapeDtypeStruct(stacked....  24.3 us
    ppermute x3, starting transfers between devices, gather_both_ways(): backward = lax.ppermute(backward, axis, left)  9.34 us
    ppermute x1, waiting for transfers between devices, scatter_sum(): got = lax.ppermute(give.astype(jnp.bfloat16), 'xl', [(0, 1), (1, 0)])  7.5 us
    dynamic_update_slice x12, local copies, waits for them, and re-layouts, place(): return lax.dynamic_update_slice(result, piece, (origin * piece.shape[0], 0))  6.77 us
    ppermute x1, starting transfers between devices, scatter_sum(): got = lax.ppermute(give.astype(jnp.bfloat16), 'core', [(0, 1), (1, 0)])  6.35 us
    ppermute x3, starting transfers between devices, gather_ring(): lax.ppermute(block, axis, [(i, (i + shift) % size) for i in range(size)])  5.81 us
    dot_general x1, matrix products, per_device(): partial = jnp.dot(attended, out_weight, preferred_element_type=jnp.float32)  4.64 us
  transfers between devices with their start and end apart: 15, of which 6 were waited for; matrix products, arithmetic and copies ran while one was open for 16% of the time, Pallas kernels for 9%

profile of v17, /device:TPU:1, one launch (start us, length us, event | category | flops | bytes accessed | tf_op | source)
XLA Modules:
  0.0 122.6 jit_solution(3473233754526823579)
XLA Ops:
  1.7 2.1 %collective-permute-start = (bf16[128,512]{1,0:T(8,128)(2,1)S(1)}, bf16[128,512]{1,0:T(8,128)(2,1)S(1)}, u32[]{:S(2)}, u32[]{:S(2)}) collective-permute-start(bf16[128,512]{1,0:T(8,128)(2,1)S(1)} %constant_dynamic-update-slice_fusion), channel_id=1, source_target_pairs={{0,4},{4,8},{8,12},{12,0},{1,5},{5,9},{9,13},{13,1},{2,6},{6,10},{... | collective-permute-start | bytes 393224 | tf_op jit(solution)/shard_map/ppermute | solution.py:195
  3.9 2.6 %collective-permute-start.1 = (bf16[128,512]{1,0:T(8,128)(2,1)S(1)}, bf16[128,512]{1,0:T(8,128)(2,1)S(1)}, u32[]{:S(2)}, u32[]{:S(2)}) collective-permute-start(bf16[128,512]{1,0:T(8,128)(2,1)S(1)} %constant_dynamic-update-slice_fusion), channel_id=1, source_target_pairs={{0,8},{4,12},{8,0},{12,4},{1,9},{5,13},{9,1},{13,5},{2,10},{6,14},... | collective-permute-start | bytes 393224 | tf_op jit(solution)/shard_map/ppermute | solution.py:195
  7.6 1.2 slice.23
  10.6 2.2 %broadcast_in_dim.78 = bf16[4096,512]{1,0:T(8,128)(2,1)} broadcast(bf16[]{:T(256)} %bitcast.11), dimensions={} | broadcast | bytes 4194306 | tf_op jit(solution)/shard_map/broadcast_in_dim | solution.py:246
  12.8 1.3 %collective-permute-start.10 = (bf16[2,512,128]{2,1,0:T(8,128)(2,1)S(1)}, bf16[2,512,128]{2,1,0:T(8,128)(2,1)}, u32[]{:S(2)}, u32[]{:S(2)}) collective-permute-start(bf16[2,512,128]{2,1,0:T(8,128)(2,1)S(1)} %bitcast.73), channel_id=1, source_target_pairs={{128,0},{129,1},{130,2},{131,3},{132,4},{133,5},{134,6},{135,7},{1... | collective-permute-start | bytes 786440 | tf_op jit(solution)/shard_map/ppermute | solution.py:251
  16.9 1.7 %collective-permute-start.3 = (bf16[512,512]{1,0:T(8,128)(2,1)S(1)}, bf16[512,512]{1,0:T(8,128)(2,1)S(1)}, u32[]{:S(2)}, u32[]{:S(2)}) collective-permute-start(bf16[512,512]{1,0:T(8,128)(2,1)S(1)} %constant_dynamic-update-slice_fusion.10), channel_id=1, source_target_pairs={{0,16},{16,32},{32,48},{48,64},{64,80},{80,96},{96,112},{112,0},{1... | collective-permute-start | bytes 1572872 | tf_op jit(solution)/shard_map/ppermute | solution.py:209
  18.8 4.0 %collective-permute-start.4 = (bf16[512,512]{1,0:T(8,128)(2,1)S(1)}, bf16[512,512]{1,0:T(8,128)(2,1)S(1)}, u32[]{:S(2)}, u32[]{:S(2)}) collective-permute-start(bf16[512,512]{1,0:T(8,128)(2,1)S(1)} %constant_dynamic-update-slice_fusion.10), channel_id=1, source_target_pairs={{0,112},{16,0},{32,16},{48,32},{64,48},{80,64},{96,80},{112,96},{1... | collective-permute-start | bytes 1572872 | tf_op jit(solution)/shard_map/ppermute | solution.py:212
  23.1 10.1 %collective-permute-done.3 = bf16[512,512]{1,0:T(8,128)(2,1)S(1)} collective-permute-done((bf16[512,512]{1,0:T(8,128)(2,1)S(1)}, bf16[512,512]{1,0:T(8,128)(2,1)S(1)}, u32[]{:S(2)}, u32[]{:S(2)}) %collective-permute-start.3) | collective-permute-done | bytes 524320 | tf_op jit(solution)/shard_map/ppermute | solution.py:209
  34.2 2.7 %collective-permute-start.6 = (bf16[512,512]{1,0:T(8,128)(2,1)S(1)}, bf16[512,512]{1,0:T(8,128)(2,1)S(1)}, u32[]{:S(2)}, u32[]{:S(2)}) collective-permute-start(bf16[512,512]{1,0:T(8,128)(2,1)S(1)} %collective-permute-done.4), channel_id=1, source_target_pairs={{0,112},{16,0},{32,16},{48,32},{64,48},{80,64},{96,80},{112,96},{1... | collective-permute-start | bytes 1572872 | tf_op jit(solution)/shard_map/ppermute | solution.py:212
  37.5 8.2 %collective-permute-done.5 = bf16[512,512]{1,0:T(8,128)(2,1)S(1)} collective-permute-done((bf16[512,512]{1,0:T(8,128)(2,1)S(1)}, bf16[512,512]{1,0:T(8,128)(2,1)S(1)}, u32[]{:S(2)}, u32[]{:S(2)}) %collective-permute-start.5) | collective-permute-done | bytes 524320 | tf_op jit(solution)/shard_map/ppermute | solution.py:209
  47.3 2.6 %collective-permute-start.8 = (bf16[512,512]{1,0:T(8,128)(2,1)S(1)}, bf16[512,512]{1,0:T(8,128)(2,1)S(1)}, u32[]{:S(2)}, u32[]{:S(2)}) collective-permute-start(bf16[512,512]{1,0:T(8,128)(2,1)S(1)} %collective-permute-done.6), channel_id=1, source_target_pairs={{0,112},{16,0},{32,16},{48,32},{64,48},{80,64},{96,80},{112,96},{1... | collective-permute-start | bytes 1572872 | tf_op jit(solution)/shard_map/ppermute | solution.py:212
  50.7 6.5 %collective-permute-done.7 = bf16[512,512]{1,0:T(8,128)(2,1)S(1)} collective-permute-done((bf16[512,512]{1,0:T(8,128)(2,1)S(1)}, bf16[512,512]{1,0:T(8,128)(2,1)S(1)}, u32[]{:S(2)}, u32[]{:S(2)}) %collective-permute-start.7) | collective-permute-done | bytes 524320 | tf_op jit(solution)/shard_map/ppermute | solution.py:209
  61.4 6.4 %collective-permute-done.9 = bf16[512,512]{1,0:T(8,128)(2,1)S(1)} collective-permute-done((bf16[512,512]{1,0:T(8,128)(2,1)S(1)}, bf16[512,512]{1,0:T(8,128)(2,1)S(1)}, u32[]{:S(2)}, u32[]{:S(2)}) %collective-permute-start.9) | collective-permute-done | bytes 524320 | tf_op jit(solution)/shard_map/ppermute | solution.py:209
  68.7 13.7 %shard_map.74 = (f32[2,512,128]{2,1,0:T(8,128)}, f32[2,512,1]{2,1,0:T(8,128)}, f32[2,512,1]{2,1,0:T(8,128)}, bf16[2,512,128]{2,1,0:T(8,128)(2,1)}, f32[2,2,512]{2,1,0:T(2,128)}) custom-call(s32[2,4]{1,0:T(2,128)} %get-tuple-element.55.table_ref, s32[2,8]{1,0:T(2,128)} %get-tuple-element.53.meta_ref, bf16[2,512,128]{2,1,0:T(8,128)(2,1)} %collective-permute-done.10.q_ref, ...), custom_call_target="tpu_custom_call" | custom-call | tf_op jit(solution)/shard_map/pallas_call | solution.py:128
  82.4 1.3 %collective-permute-start.12 = (bf16[2,512,128]{2,1,0:T(8,128)(2,1)}, bf16[2,512,128]{2,1,0:T(8,128)(2,1)S(1)}, u32[]{:S(2)}, u32[]{:S(2)}) collective-permute-start(bf16[2,512,128]{2,1,0:T(8,128)(2,1)} %get-tuple-element.21), channel_id=1, source_target_pairs={{0,128},{1,129},{2,130},{3,131},{4,132},{5,133},{6,134},{7,135},{8... | collective-permute-start | bytes 786440 | tf_op jit(solution)/shard_map/ppermute | solution.py:268
  83.7 1.5 %collective-permute-start.11 = (f32[2,2,512]{2,1,0:T(2,128)}, f32[2,2,512]{2,1,0:T(2,128)S(1)}, u32[]{:S(2)}, u32[]{:S(2)}) collective-permute-start(f32[2,2,512]{2,1,0:T(2,128)} %get-tuple-element.20), channel_id=1, source_target_pairs={{0,128},{1,129},{2,130},{3,131},{4,132},{5,133},{6,134},{7,135},{8... | collective-permute-start | bytes 24584 | tf_op jit(solution)/shard_map/ppermute | solution.py:269
  85.2 10.7 %shard_map.73 = (f32[2,512,128]{2,1,0:T(8,128)}, f32[2,512,1]{2,1,0:T(8,128)}, f32[2,512,1]{2,1,0:T(8,128)}, bf16[2,512,128]{2,1,0:T(8,128)(2,1)}, f32[2,2,512]{2,1,0:T(2,128)}) custom-call(s32[2,4]{1,0:T(2,128)} %get-tuple-element.54.table_ref, s32[2,8]{1,0:T(2,128)} %get-tuple-element.52.meta_ref, bf16[2,512,128]{2,1,0:T(8,128)(2,1)} %bitcast.74, ...), custom_call_target="tpu_custom_call" | custom-call | tf_op jit(solution)/shard_map/pallas_call | solution.py:128
  95.9 1.2 copy.48
  97.1 1.2 %copy.49 = f32[2,512,1]{1,2,0:T(1,128)S(1)} copy(f32[2,512,1]{2,1,0:T(8,128)} %get-tuple-element.22) | data formatting | bytes 8192 | tf_op jit(solution)/shard_map/pallas_call | solution.py:128
  98.4 1.5 %divide_convert_fusion = bf16[2,512,128]{2,1,0:T(8,128)(2,1)S(1)} fusion(bf16[2,512,128]{2,1,0:T(8,128)(2,1)S(1)} %collective-permute-done.12, f32[2,512,128]{2,1,0:T(8,128)} %get-tuple-element.17, f32[2,512]{1,0:T(2,128)S(1)} %bitcast.76, f32[2,512]{1,0:T(2,128)S(1)} %bitcast.77, f32[2,512]{1,0:T(2,128)S(1)} %bitcast.78, pred[]{:T(512)S(6)} %eq.23), kind=kLoop, calls=%fused_computation.11 | loop fusion | flops 917504 | bytes 1060865 | tf_op jit(solution)/shard_map/convert_element_type | solution.py:177
  100.3 4.6 %fusion = f32[2,2,32,4096]{3,2,1,0:T(8,128)S(1)} fusion(bf16[2,2,32,1024]{3,2,1,0:T(8,128)(2,1)S(1)} %dot_general.5, bf16[1024,4096]{1,0:T(8,128)(2,1)} %param.14), kind=kOutput, calls=%fused_computation.2 | convolution fusion | flops 1073741824 | bytes 10747904 | tf_op jit(solution)/shard_map/dot_general | solution.py:277
  105.0 6.4 %collective-permute-start.13 = (bf16[2,32,4096]{2,1,0:T(8,128)(2,1)S(1)}, bf16[2,32,4096]{2,1,0:T(8,128)(2,1)}, u32[]{:S(2)}, u32[]{:S(2)}) collective-permute-start(bf16[2,32,4096]{2,1,0:T(8,128)(2,1)S(1)} %bitcast_convert_fusion), channel_id=1, source_target_pairs={{0,1},{1,0},{2,3},{3,2},{4,5},{5,4},{6,7},{7,6},{8,9},{9,8},{10,11... | collective-permute-start | bytes 1572872 | tf_op jit(solution)/shard_map/ppermute | solution.py:224
  111.4 1.7 %collective-permute-done.13 = bf16[2,32,4096]{2,1,0:T(8,128)(2,1)} collective-permute-done((bf16[2,32,4096]{2,1,0:T(8,128)(2,1)S(1)}, bf16[2,32,4096]{2,1,0:T(8,128)(2,1)}, u32[]{:S(2)}, u32[]{:S(2)}) %collective-permute-start.13) | collective-permute-done | bytes 524320 | tf_op jit(solution)/shard_map/ppermute | solution.py:224
  114.4 7.5 %collective-permute-done.14 = bf16[32,4096]{1,0:T(8,128)(2,1)S(1)} collective-permute-done((bf16[32,4096]{1,0:T(8,128)(2,1)S(1)}, bf16[32,4096]{1,0:T(8,128)(2,1)S(1)}, u32[]{:S(2)}, u32[]{:S(2)}) %collective-permute-start.14) | collective-permute-done | bytes 262176 | tf_op jit(solution)/shard_map/ppermute | solution.py:229
  (90 shorter events, 18.5 us)
Async XLA Ops:
  0.0 14.1 %copy-start.1 = (s32[8]{0:T(128)S(1)}, s32[8]{0:T(128)}, u32[]{:S(2)}) copy-start(s32[8]{0:T(128)} %param.17) | copy-start | bytes 100
  0.0 14.2 %copy-start.2 = (s32[8]{0:T(128)S(1)}, s32[8]{0:T(128)}, u32[]{:S(2)}) copy-start(s32[8]{0:T(128)} %param.16) | copy-start | bytes 100
  0.0 14.4 %copy-start.3 = (s32[8]{0:T(128)S(1)}, s32[8]{0:T(128)}, u32[]{:S(2)}) copy-start(s32[8]{0:T(128)} %param.15) | copy-start | bytes 100
  1.7 15.0 %collective-permute-start = (bf16[128,512]{1,0:T(8,128)(2,1)S(1)}, bf16[128,512]{1,0:T(8,128)(2,1)S(1)}, u32[]{:S(2)}, u32[]{:S(2)}) collective-permute-start(bf16[128,512]{1,0:T(8,128)(2,1)S(1)} %constant_dynamic-update-slice_fusion), channel_id=1, source_target_pairs={{0,4},{4,8},{8,12},{12,0},{1,5},{5,9},{9,13},{13,1},{2,6},{6,10},{... | collective-permute-start | bytes 393224 | tf_op jit(solution)/shard_map/ppermute | solution.py:195
  3.9 12.9 %collective-permute-start.1 = (bf16[128,512]{1,0:T(8,128)(2,1)S(1)}, bf16[128,512]{1,0:T(8,128)(2,1)S(1)}, u32[]{:S(2)}, u32[]{:S(2)}) collective-permute-start(bf16[128,512]{1,0:T(8,128)(2,1)S(1)} %constant_dynamic-update-slice_fusion), channel_id=1, source_target_pairs={{0,8},{4,12},{8,0},{12,4},{1,9},{5,13},{9,1},{13,5},{2,10},{6,14},... | collective-permute-start | bytes 393224 | tf_op jit(solution)/shard_map/ppermute | solution.py:195
  6.5 10.3 %collective-permute-start.2 = (bf16[128,512]{1,0:T(8,128)(2,1)S(1)}, bf16[128,512]{1,0:T(8,128)(2,1)S(1)}, u32[]{:S(2)}, u32[]{:S(2)}) collective-permute-start(bf16[128,512]{1,0:T(8,128)(2,1)S(1)} %constant_dynamic-update-slice_fusion), channel_id=1, source_target_pairs={{0,12},{4,0},{8,4},{12,8},{1,13},{5,1},{9,5},{13,9},{2,14},{6,2},{... | collective-permute-start | bytes 393224 | tf_op jit(solution)/shard_map/ppermute | solution.py:195
  9.9 37.4 %copy-start = (bf16[128,2,4,128]{3,0,2,1:T(8,128)(2,1)}, bf16[128,2,4,128]{3,0,2,1:T(8,128)(2,1)S(1)}, u32[]{:S(2)}) copy-start(bf16[128,2,4,128]{3,0,2,1:T(8,128)(2,1)S(1)} %copy.46) | copy-start | bytes 786436
  12.8 55.9 %collective-permute-start.10 = (bf16[2,512,128]{2,1,0:T(8,128)(2,1)S(1)}, bf16[2,512,128]{2,1,0:T(8,128)(2,1)}, u32[]{:S(2)}, u32[]{:S(2)}) collective-permute-start(bf16[2,512,128]{2,1,0:T(8,128)(2,1)S(1)} %bitcast.73), channel_id=1, source_target_pairs={{128,0},{129,1},{130,2},{131,3},{132,4},{133,5},{134,6},{135,7},{1... | collective-permute-start | bytes 786440 | tf_op jit(solution)/shard_map/ppermute | solution.py:251
  16.9 16.4 %collective-permute-start.3 = (bf16[512,512]{1,0:T(8,128)(2,1)S(1)}, bf16[512,512]{1,0:T(8,128)(2,1)S(1)}, u32[]{:S(2)}, u32[]{:S(2)}) collective-permute-start(bf16[512,512]{1,0:T(8,128)(2,1)S(1)} %constant_dynamic-update-slice_fusion.10), channel_id=1, source_target_pairs={{0,16},{16,32},{32,48},{48,64},{64,80},{80,96},{96,112},{112,0},{1... | collective-permute-start | bytes 1572872 | tf_op jit(solution)/shard_map/ppermute | solution.py:209
  18.8 15.4 %collective-permute-start.4 = (bf16[512,512]{1,0:T(8,128)(2,1)S(1)}, bf16[512,512]{1,0:T(8,128)(2,1)S(1)}, u32[]{:S(2)}, u32[]{:S(2)}) collective-permute-start(bf16[512,512]{1,0:T(8,128)(2,1)S(1)} %constant_dynamic-update-slice_fusion.10), channel_id=1, source_target_pairs={{0,112},{16,0},{32,16},{48,32},{64,48},{80,64},{96,80},{112,96},{1... | collective-permute-start | bytes 1572872 | tf_op jit(solution)/shard_map/ppermute | solution.py:212
  33.2 12.5 %collective-permute-start.5 = (bf16[512,512]{1,0:T(8,128)(2,1)S(1)}, bf16[512,512]{1,0:T(8,128)(2,1)S(1)}, u32[]{:S(2)}, u32[]{:S(2)}) collective-permute-start(bf16[512,512]{1,0:T(8,128)(2,1)S(1)} %collective-permute-done.3), channel_id=1, source_target_pairs={{0,16},{16,32},{32,48},{48,64},{64,80},{80,96},{96,112},{112,0},{1... | collective-permute-start | bytes 1572872 | tf_op jit(solution)/shard_map/ppermute | solution.py:209
  34.2 13.1 %collective-permute-start.6 = (bf16[512,512]{1,0:T(8,128)(2,1)S(1)}, bf16[512,512]{1,0:T(8,128)(2,1)S(1)}, u32[]{:S(2)}, u32[]{:S(2)}) collective-permute-start(bf16[512,512]{1,0:T(8,128)(2,1)S(1)} %collective-permute-done.4), channel_id=1, source_target_pairs={{0,112},{16,0},{32,16},{48,32},{64,48},{80,64},{96,80},{112,96},{1... | collective-permute-start | bytes 1572872 | tf_op jit(solution)/shard_map/ppermute | solution.py:212
  45.7 11.5 %collective-permute-start.7 = (bf16[512,512]{1,0:T(8,128)(2,1)S(1)}, bf16[512,512]{1,0:T(8,128)(2,1)S(1)}, u32[]{:S(2)}, u32[]{:S(2)}) collective-permute-start(bf16[512,512]{1,0:T(8,128)(2,1)S(1)} %collective-permute-done.5), channel_id=1, source_target_pairs={{0,16},{16,32},{32,48},{48,64},{64,80},{80,96},{96,112},{112,0},{1... | collective-permute-start | bytes 1572872 | tf_op jit(solution)/shard_map/ppermute | solution.py:209
  47.3 13.3 %collective-permute-start.8 = (bf16[512,512]{1,0:T(8,128)(2,1)S(1)}, bf16[512,512]{1,0:T(8,128)(2,1)S(1)}, u32[]{:S(2)}, u32[]{:S(2)}) collective-permute-start(bf16[512,512]{1,0:T(8,128)(2,1)S(1)} %collective-permute-done.6), channel_id=1, source_target_pairs={{0,112},{16,0},{32,16},{48,32},{64,48},{80,64},{96,80},{112,96},{1... | collective-permute-start | bytes 1572872 | tf_op jit(solution)/shard_map/ppermute | solution.py:212
  57.2 10.6 %collective-permute-start.9 = (bf16[512,512]{1,0:T(8,128)(2,1)S(1)}, bf16[512,512]{1,0:T(8,128)(2,1)S(1)}, u32[]{:S(2)}, u32[]{:S(2)}) collective-permute-start(bf16[512,512]{1,0:T(8,128)(2,1)S(1)} %collective-permute-done.7), channel_id=1, source_target_pairs={{0,16},{16,32},{32,48},{48,64},{64,80},{80,96},{96,112},{112,0},{1... | collective-permute-start | bytes 1572872 | tf_op jit(solution)/shard_map/ppermute | solution.py:209
  82.4 16.0 %collective-permute-start.12 = (bf16[2,512,128]{2,1,0:T(8,128)(2,1)}, bf16[2,512,128]{2,1,0:T(8,128)(2,1)S(1)}, u32[]{:S(2)}, u32[]{:S(2)}) collective-permute-start(bf16[2,512,128]{2,1,0:T(8,128)(2,1)} %get-tuple-element.21), channel_id=1, source_target_pairs={{0,128},{1,129},{2,130},{3,131},{4,132},{5,133},{6,134},{7,135},{8... | collective-permute-start | bytes 786440 | tf_op jit(solution)/shard_map/ppermute | solution.py:268
  83.7 14.7 %collective-permute-start.11 = (f32[2,2,512]{2,1,0:T(2,128)}, f32[2,2,512]{2,1,0:T(2,128)S(1)}, u32[]{:S(2)}, u32[]{:S(2)}) collective-permute-start(f32[2,2,512]{2,1,0:T(2,128)} %get-tuple-element.20), channel_id=1, source_target_pairs={{0,128},{1,129},{2,130},{3,131},{4,132},{5,133},{6,134},{7,135},{8... | collective-permute-start | bytes 24584 | tf_op jit(solution)/shard_map/ppermute | solution.py:269
  105.0 8.0 %collective-permute-start.13 = (bf16[2,32,4096]{2,1,0:T(8,128)(2,1)S(1)}, bf16[2,32,4096]{2,1,0:T(8,128)(2,1)}, u32[]{:S(2)}, u32[]{:S(2)}) collective-permute-start(bf16[2,32,4096]{2,1,0:T(8,128)(2,1)S(1)} %bitcast_convert_fusion), channel_id=1, source_target_pairs={{0,1},{1,0},{2,3},{3,2},{4,5},{5,4},{6,7},{7,6},{8,9},{9,8},{10,11... | collective-permute-start | bytes 1572872 | tf_op jit(solution)/shard_map/ppermute | solution.py:224
  114.3 7.6 %collective-permute-start.14 = (bf16[32,4096]{1,0:T(8,128)(2,1)S(1)}, bf16[32,4096]{1,0:T(8,128)(2,1)S(1)}, u32[]{:S(2)}, u32[]{:S(2)}) collective-permute-start(bf16[32,4096]{1,0:T(8,128)(2,1)S(1)} %bitcast_convert_fusion.1), channel_id=1, source_target_pairs={{0,2},{2,0},{1,3},{3,1},{4,6},{6,4},{5,7},{7,5},{8,10},{10,8},{9,1... | collective-permute-start | bytes 786440 | tf_op jit(solution)/shard_map/ppermute | solution.py:229

commit v18 on v16

--- a/solution.py
+++ b/solution.py
@@ -223,11 +223,11 @@
     keep = jnp.take(parts, core, axis=1)
     give = jnp.take(parts, 1 - core, axis=1)
     got = lax.ppermute(give.astype(jnp.bfloat16), "core", [(0, 1), (1, 0)])
-    summed = keep + got.astype(jnp.float32)
     xl = lax.axis_index("xl")
-    keep = jnp.take(summed, xl, axis=0)
-    give = jnp.take(summed, 1 - xl, axis=0)
-    got = lax.ppermute(give.astype(jnp.bfloat16), "xl", [(0, 1), (1, 0)])
+    give = jnp.take(keep, 1 - xl, axis=0) + jnp.take(got, 1 - xl, axis=0).astype(jnp.float32)
+    sent = lax.ppermute(give.astype(jnp.bfloat16), "xl", [(0, 1), (1, 0)])
+    keep = jnp.take(keep, xl, axis=0) + jnp.take(got, xl, axis=0).astype(jnp.float32)
+    got = sent
     return (keep + got.astype(jnp.float32)).astype(jnp.bfloat16)
 
 

time: 120 us -> 122 us (1.017)
  other arithmetic: 4.9 us -> 6.6 us
  transfers between devices with their start and end apart: 15 -> 15, of which waited for: 6 -> 6; matrix products, arithmetic and copies ran while one was open for 17% -> 16% of each run, Pallas kernels for 9% -> 9%
where the time goes in v18:
time: 122 us; the launch traced here: 121 us
  waiting for transfers between devices  37.2 us (30%)
  starting transfers between devices  27.2 us (22%)
  Pallas kernels  24.3 us (20%)
  local copies, waits for them, and re-layouts  20.5 us (17%)
  other arithmetic  6.6 us (5%)
  matrix products  4.64 us (4%)
    ppermute x4, waiting for transfers between devices, gather_both_ways(): forward = lax.ppermute(forward, axis, right)  29 us
    pallas_call x2, Pallas kernels, attend(): pl.pallas_call(attention_kernel, out_shape=(jax.ShapeDtypeStruct(stacked....  24.3 us
    ppermute x3, starting transfers between devices, gather_both_ways(): backward = lax.ppermute(backward, axis, left)  9.35 us
    dynamic_update_slice x12, local copies, waits for them, and re-layouts, place(): return lax.dynamic_update_slice(result, piece, (origin * piece.shape[0], 0))  6.78 us
    ppermute x1, waiting for transfers between devices, scatter_sum(): sent = lax.ppermute(give.astype(jnp.bfloat16), 'xl', [(0, 1), (1, 0)])  6.31 us
    ppermute x3, starting transfers between devices, gather_ring(): lax.ppermute(block, axis, [(i, (i + shift) % size) for i in range(size)])  5.81 us
    ppermute x1, starting transfers between devices, scatter_sum(): got = lax.ppermute(give.astype(jnp.bfloat16), 'core', [(0, 1), (1, 0)])  4.93 us
    dot_general x1, matrix products, per_device(): partial = jnp.dot(attended, out_weight, preferred_element_type=jnp.float32)  4.64 us
  transfers between devices with their start and end apart: 15, of which 6 were waited for; matrix products, arithmetic and copies ran while one was open for 16% of the time, Pallas kernels for 9%

profile of v18, /device:TPU:1, one launch (start us, length us, event | category | flops | bytes accessed | tf_op | source)
XLA Modules:
  0.0 120.9 jit_solution(10172560085412671036)
XLA Ops:
  1.7 2.1 %collective-permute-start = (bf16[128,512]{1,0:T(8,128)(2,1)S(1)}, bf16[128,512]{1,0:T(8,128)(2,1)S(1)}, u32[]{:S(2)}, u32[]{:S(2)}) collective-permute-start(bf16[128,512]{1,0:T(8,128)(2,1)S(1)} %constant_dynamic-update-slice_fusion), channel_id=1, source_target_pairs={{0,4},{4,8},{8,12},{12,0},{1,5},{5,9},{9,13},{13,1},{2,6},{6,10},{... | collective-permute-start | bytes 393224 | tf_op jit(solution)/shard_map/ppermute | solution.py:195
  3.8 2.6 %collective-permute-start.1 = (bf16[128,512]{1,0:T(8,128)(2,1)S(1)}, bf16[128,512]{1,0:T(8,128)(2,1)S(1)}, u32[]{:S(2)}, u32[]{:S(2)}) collective-permute-start(bf16[128,512]{1,0:T(8,128)(2,1)S(1)} %constant_dynamic-update-slice_fusion), channel_id=1, source_target_pairs={{0,8},{4,12},{8,0},{12,4},{1,9},{5,13},{9,1},{13,5},{2,10},{6,14},... | collective-permute-start | bytes 393224 | tf_op jit(solution)/shard_map/ppermute | solution.py:195
  8.7 1.3 %collective-permute-start.10 = (bf16[2,512,128]{2,1,0:T(8,128)(2,1)S(1)}, bf16[2,512,128]{2,1,0:T(8,128)(2,1)}, u32[]{:S(2)}, u32[]{:S(2)}) collective-permute-start(bf16[2,512,128]{2,1,0:T(8,128)(2,1)S(1)} %bitcast.76), channel_id=1, source_target_pairs={{128,0},{129,1},{130,2},{131,3},{132,4},{133,5},{134,6},{135,7},{1... | collective-permute-start | bytes 786440 | tf_op jit(solution)/shard_map/ppermute | solution.py:247
  14.7 1.7 %collective-permute-start.3 = (bf16[512,512]{1,0:T(8,128)(2,1)S(1)}, bf16[512,512]{1,0:T(8,128)(2,1)S(1)}, u32[]{:S(2)}, u32[]{:S(2)}) collective-permute-start(bf16[512,512]{1,0:T(8,128)(2,1)S(1)} %constant_dynamic-update-slice_fusion.10), channel_id=1, source_target_pairs={{0,16},{16,32},{32,48},{48,64},{64,80},{80,96},{96,112},{112,0},{1... | collective-permute-start | bytes 1572872 | tf_op jit(solution)/shard_map/ppermute | solution.py:210
  16.6 4.0 %collective-permute-start.4 = (bf16[512,512]{1,0:T(8,128)(2,1)S(1)}, bf16[512,512]{1,0:T(8,128)(2,1)S(1)}, u32[]{:S(2)}, u32[]{:S(2)}) collective-permute-start(bf16[512,512]{1,0:T(8,128)(2,1)S(1)} %constant_dynamic-update-slice_fusion.10), channel_id=1, source_target_pairs={{0,112},{16,0},{32,16},{48,32},{64,48},{80,64},{96,80},{112,96},{1... | collective-permute-start | bytes 1572872 | tf_op jit(solution)/shard_map/ppermute | solution.py:213
  20.9 10.1 %collective-permute-done.3 = bf16[512,512]{1,0:T(8,128)(2,1)S(1)} collective-permute-done((bf16[512,512]{1,0:T(8,128)(2,1)S(1)}, bf16[512,512]{1,0:T(8,128)(2,1)S(1)}, u32[]{:S(2)}, u32[]{:S(2)}) %collective-permute-start.3) | collective-permute-done | bytes 524320 | tf_op jit(solution)/shard_map/ppermute | solution.py:210
  32.0 2.7 %collective-permute-start.6 = (bf16[512,512]{1,0:T(8,128)(2,1)S(1)}, bf16[512,512]{1,0:T(8,128)(2,1)S(1)}, u32[]{:S(2)}, u32[]{:S(2)}) collective-permute-start(bf16[512,512]{1,0:T(8,128)(2,1)S(1)} %collective-permute-done.4), channel_id=1, source_target_pairs={{0,112},{16,0},{32,16},{48,32},{64,48},{80,64},{96,80},{112,96},{1... | collective-permute-start | bytes 1572872 | tf_op jit(solution)/shard_map/ppermute | solution.py:213
  35.3 8.2 %collective-permute-done.5 = bf16[512,512]{1,0:T(8,128)(2,1)S(1)} collective-permute-done((bf16[512,512]{1,0:T(8,128)(2,1)S(1)}, bf16[512,512]{1,0:T(8,128)(2,1)S(1)}, u32[]{:S(2)}, u32[]{:S(2)}) %collective-permute-start.5) | collective-permute-done | bytes 524320 | tf_op jit(solution)/shard_map/ppermute | solution.py:210
  44.2 2.2 %broadcast_in_dim.87 = bf16[4096,512]{1,0:T(8,128)(2,1)} broadcast(bf16[]{:T(256)} %constant.175.clone.1), dimensions={} | broadcast | bytes 4194306 | tf_op jit(solution)/shard_map/broadcast_in_dim | solution.py:205
  47.3 2.6 %collective-permute-start.8 = (bf16[512,512]{1,0:T(8,128)(2,1)S(1)}, bf16[512,512]{1,0:T(8,128)(2,1)S(1)}, u32[]{:S(2)}, u32[]{:S(2)}) collective-permute-start(bf16[512,512]{1,0:T(8,128)(2,1)S(1)} %collective-permute-done.6), channel_id=1, source_target_pairs={{0,112},{16,0},{32,16},{48,32},{64,48},{80,64},{96,80},{112,96},{1... | collective-permute-start | bytes 1572872 | tf_op jit(solution)/shard_map/ppermute | solution.py:213
  50.7 4.3 %collective-permute-done.7 = bf16[512,512]{1,0:T(8,128)(2,1)S(1)} collective-permute-done((bf16[512,512]{1,0:T(8,128)(2,1)S(1)}, bf16[512,512]{1,0:T(8,128)(2,1)S(1)}, u32[]{:S(2)}, u32[]{:S(2)}) %collective-permute-start.7) | collective-permute-done | bytes 524320 | tf_op jit(solution)/shard_map/ppermute | solution.py:210
  59.3 6.4 %collective-permute-done.9 = bf16[512,512]{1,0:T(8,128)(2,1)S(1)} collective-permute-done((bf16[512,512]{1,0:T(8,128)(2,1)S(1)}, bf16[512,512]{1,0:T(8,128)(2,1)S(1)}, u32[]{:S(2)}, u32[]{:S(2)}) %collective-permute-start.9) | collective-permute-done | bytes 524320 | tf_op jit(solution)/shard_map/ppermute | solution.py:210
  66.5 13.7 %shard_map.74 = (f32[2,512,128]{2,1,0:T(8,128)}, f32[2,512,1]{2,1,0:T(8,128)}, f32[2,512,1]{2,1,0:T(8,128)}, bf16[2,512,128]{2,1,0:T(8,128)(2,1)}, f32[2,2,512]{2,1,0:T(2,128)}) custom-call(s32[2,4]{1,0:T(2,128)} %get-tuple-element.63.table_ref, s32[2,8]{1,0:T(2,128)} %get-tuple-element.61.meta_ref, bf16[2,512,128]{2,1,0:T(8,128)(2,1)} %collective-permute-done.10.q_ref, ...), custom_call_target="tpu_custom_call" | custom-call | tf_op jit(solution)/shard_map/pallas_call | solution.py:128
  80.2 1.3 %collective-permute-start.12 = (bf16[2,512,128]{2,1,0:T(8,128)(2,1)}, bf16[2,512,128]{2,1,0:T(8,128)(2,1)S(1)}, u32[]{:S(2)}, u32[]{:S(2)}) collective-permute-start(bf16[2,512,128]{2,1,0:T(8,128)(2,1)} %get-tuple-element.18), channel_id=1, source_target_pairs={{0,128},{1,129},{2,130},{3,131},{4,132},{5,133},{6,134},{7,135},{8... | collective-permute-start | bytes 786440 | tf_op jit(solution)/shard_map/ppermute | solution.py:264
  81.5 1.5 %collective-permute-start.11 = (f32[2,2,512]{2,1,0:T(2,128)}, f32[2,2,512]{2,1,0:T(2,128)S(1)}, u32[]{:S(2)}, u32[]{:S(2)}) collective-permute-start(f32[2,2,512]{2,1,0:T(2,128)} %get-tuple-element.17), channel_id=1, source_target_pairs={{0,128},{1,129},{2,130},{3,131},{4,132},{5,133},{6,134},{7,135},{8... | collective-permute-start | bytes 24584 | tf_op jit(solution)/shard_map/ppermute | solution.py:265
  83.0 10.7 %shard_map.73 = (f32[2,512,128]{2,1,0:T(8,128)}, f32[2,512,1]{2,1,0:T(8,128)}, f32[2,512,1]{2,1,0:T(8,128)}, bf16[2,512,128]{2,1,0:T(8,128)(2,1)}, f32[2,2,512]{2,1,0:T(2,128)}) custom-call(s32[2,4]{1,0:T(2,128)} %get-tuple-element.62.table_ref, s32[2,8]{1,0:T(2,128)} %get-tuple-element.60.meta_ref, bf16[2,512,128]{2,1,0:T(8,128)(2,1)} %bitcast.77, ...), custom_call_target="tpu_custom_call" | custom-call | tf_op jit(solution)/shard_map/pallas_call | solution.py:128
  94.9 1.2 %copy.49 = f32[2,512,1]{1,2,0:T(1,128)S(1)} copy(f32[2,512,1]{2,1,0:T(8,128)} %get-tuple-element.19) | data formatting | bytes 8192 | tf_op jit(solution)/shard_map/pallas_call | solution.py:128
  96.2 1.5 %divide_convert_fusion = bf16[2,512,128]{2,1,0:T(8,128)(2,1)S(1)} fusion(bf16[2,512,128]{2,1,0:T(8,128)(2,1)S(1)} %collective-permute-done.12, f32[2,512,128]{2,1,0:T(8,128)} %get-tuple-element.15, f32[2,512]{1,0:T(2,128)S(1)} %bitcast.79, f32[2,512]{1,0:T(2,128)S(1)} %bitcast.80, f32[2,512]{1,0:T(2,128)S(1)} %bitcast.81, pred[]{:T(512)S(6)} %eq.23), kind=kLoop, calls=%fused_computation.12 | loop fusion | flops 917504 | bytes 1060865 | tf_op jit(solution)/shard_map/convert_element_type | solution.py:177
  98.1 4.6 %fusion = f32[2,2,32,4096]{3,2,1,0:T(8,128)S(1)} fusion(bf16[2,2,32,1024]{3,2,1,0:T(8,128)(2,1)S(1)} %dot_general.5, bf16[1024,4096]{1,0:T(8,128)(2,1)} %param.16), kind=kOutput, calls=%fused_computation.2 | convolution fusion | flops 1073741824 | bytes 10747904 | tf_op jit(solution)/shard_map/dot_general | solution.py:273
  103.6 4.9 %collective-permute-start.13 = (bf16[2,32,4096]{2,1,0:T(8,128)(2,1)}, bf16[2,32,4096]{2,1,0:T(8,128)(2,1)}, u32[]{:S(2)}, u32[]{:S(2)}) collective-permute-start(bf16[2,32,4096]{2,1,0:T(8,128)(2,1)} %bitcast_convert_fusion), channel_id=1, source_target_pairs={{0,1},{1,0},{2,3},{3,2},{4,5},{5,4},{6,7},{7,6},{8,9},{9,8},{10,11... | collective-permute-start | bytes 1572872 | tf_op jit(solution)/shard_map/ppermute | solution.py:225
  108.6 1.8 %collective-permute-done.13 = bf16[2,32,4096]{2,1,0:T(8,128)(2,1)} collective-permute-done((bf16[2,32,4096]{2,1,0:T(8,128)(2,1)}, bf16[2,32,4096]{2,1,0:T(8,128)(2,1)}, u32[]{:S(2)}, u32[]{:S(2)}) %collective-permute-start.13) | collective-permute-done | bytes 524320 | tf_op jit(solution)/shard_map/ppermute | solution.py:225
  111.5 1.3 %collective-permute-start.14 = (bf16[32,4096]{1,0:T(8,128)(2,1)S(1)}, bf16[32,4096]{1,0:T(8,128)(2,1)S(1)}, u32[]{:S(2)}, u32[]{:S(2)}) collective-permute-start(bf16[32,4096]{1,0:T(8,128)(2,1)S(1)} %fusion.3), channel_id=1, source_target_pairs={{0,2},{2,0},{1,3},{3,1},{4,6},{6,4},{5,7},{7,5},{8,10},{10,8},{9,1... | collective-permute-start | bytes 786440 | tf_op jit(solution)/shard_map/ppermute | solution.py:228
  112.8 6.3 %collective-permute-done.14 = bf16[32,4096]{1,0:T(8,128)(2,1)S(1)} collective-permute-done((bf16[32,4096]{1,0:T(8,128)(2,1)S(1)}, bf16[32,4096]{1,0:T(8,128)(2,1)S(1)}, u32[]{:S(2)}, u32[]{:S(2)}) %collective-permute-start.14) | collective-permute-done | bytes 262176 | tf_op jit(solution)/shard_map/ppermute | solution.py:228
  119.1 1.8 %fusion.5 = bf16[32,4096]{1,0:T(8,128)(2,1)} fusion(f32[2,32,4096]{2,1,0:T(8,128)S(1)} %fusion.2, s32[]{:T(128)S(6)} %select_n.226, bf16[32,4096]{1,0:T(8,128)(2,1)S(1)} %collective-permute-done.14, bf16[2,32,4096]{2,1,0:T(8,128)(2,1)} %collective-permute-done.13, pred[]{:T(512)S(6)} %and.103), kind=kLoop, calls=%fused_computation.11 | loop fusion | flops 917504 | bytes 1310725 | tf_op jit(solution)/shard_map/convert_element_type | solution.py:231
  (83 shorter events, 21.5 us)
Async XLA Ops:
  1.7 12.9 %collective-permute-start = (bf16[128,512]{1,0:T(8,128)(2,1)S(1)}, bf16[128,512]{1,0:T(8,128)(2,1)S(1)}, u32[]{:S(2)}, u32[]{:S(2)}) collective-permute-start(bf16[128,512]{1,0:T(8,128)(2,1)S(1)} %constant_dynamic-update-slice_fusion), channel_id=1, source_target_pairs={{0,4},{4,8},{8,12},{12,0},{1,5},{5,9},{9,13},{13,1},{2,6},{6,10},{... | collective-permute-start | bytes 393224 | tf_op jit(solution)/shard_map/ppermute | solution.py:195
  3.8 10.8 %collective-permute-start.1 = (bf16[128,512]{1,0:T(8,128)(2,1)S(1)}, bf16[128,512]{1,0:T(8,128)(2,1)S(1)}, u32[]{:S(2)}, u32[]{:S(2)}) collective-permute-start(bf16[128,512]{1,0:T(8,128)(2,1)S(1)} %constant_dynamic-update-slice_fusion), channel_id=1, source_target_pairs={{0,8},{4,12},{8,0},{12,4},{1,9},{5,13},{9,1},{13,5},{2,10},{6,14},... | collective-permute-start | bytes 393224 | tf_op jit(solution)/shard_map/ppermute | solution.py:195
  6.4 8.2 %collective-permute-start.2 = (bf16[128,512]{1,0:T(8,128)(2,1)S(1)}, bf16[128,512]{1,0:T(8,128)(2,1)S(1)}, u32[]{:S(2)}, u32[]{:S(2)}) collective-permute-start(bf16[128,512]{1,0:T(8,128)(2,1)S(1)} %constant_dynamic-update-slice_fusion), channel_id=1, source_target_pairs={{0,12},{4,0},{8,4},{12,8},{1,13},{5,1},{9,5},{13,9},{2,14},{6,2},{... | collective-permute-start | bytes 393224 | tf_op jit(solution)/shard_map/ppermute | solution.py:195
  8.7 38.6 %copy-start = (bf16[128,2,4,128]{3,0,2,1:T(8,128)(2,1)}, bf16[128,2,4,128]{3,0,2,1:T(8,128)(2,1)S(1)}, u32[]{:S(2)}) copy-start(bf16[128,2,4,128]{3,0,2,1:T(8,128)(2,1)S(1)} %copy.46) | copy-start | bytes 786436
  8.7 57.8 %collective-permute-start.10 = (bf16[2,512,128]{2,1,0:T(8,128)(2,1)S(1)}, bf16[2,512,128]{2,1,0:T(8,128)(2,1)}, u32[]{:S(2)}, u32[]{:S(2)}) collective-permute-start(bf16[2,512,128]{2,1,0:T(8,128)(2,1)S(1)} %bitcast.76), channel_id=1, source_target_pairs={{128,0},{129,1},{130,2},{131,3},{132,4},{133,5},{134,6},{135,7},{1... | collective-permute-start | bytes 786440 | tf_op jit(solution)/shard_map/ppermute | solution.py:247
  14.7 16.4 %collective-permute-start.3 = (bf16[512,512]{1,0:T(8,128)(2,1)S(1)}, bf16[512,512]{1,0:T(8,128)(2,1)S(1)}, u32[]{:S(2)}, u32[]{:S(2)}) collective-permute-start(bf16[512,512]{1,0:T(8,128)(2,1)S(1)} %constant_dynamic-update-slice_fusion.10), channel_id=1, source_target_pairs={{0,16},{16,32},{32,48},{48,64},{64,80},{80,96},{96,112},{112,0},{1... | collective-permute-start | bytes 1572872 | tf_op jit(solution)/shard_map/ppermute | solution.py:210
  16.6 15.4 %collective-permute-start.4 = (bf16[512,512]{1,0:T(8,128)(2,1)S(1)}, bf16[512,512]{1,0:T(8,128)(2,1)S(1)}, u32[]{:S(2)}, u32[]{:S(2)}) collective-permute-start(bf16[512,512]{1,0:T(8,128)(2,1)S(1)} %constant_dynamic-update-slice_fusion.10), channel_id=1, source_target_pairs={{0,112},{16,0},{32,16},{48,32},{64,48},{80,64},{96,80},{112,96},{1... | collective-permute-start | bytes 1572872 | tf_op jit(solution)/shard_map/ppermute | solution.py:213
  31.0 12.5 %collective-permute-start.5 = (bf16[512,512]{1,0:T(8,128)(2,1)S(1)}, bf16[512,512]{1,0:T(8,128)(2,1)S(1)}, u32[]{:S(2)}, u32[]{:S(2)}) collective-permute-start(bf16[512,512]{1,0:T(8,128)(2,1)S(1)} %collective-permute-done.3), channel_id=1, source_target_pairs={{0,16},{16,32},{32,48},{48,64},{64,80},{80,96},{96,112},{112,0},{1... | collective-permute-start | bytes 1572872 | tf_op jit(solution)/shard_map/ppermute | solution.py:210
  32.0 15.3 %collective-permute-start.6 = (bf16[512,512]{1,0:T(8,128)(2,1)S(1)}, bf16[512,512]{1,0:T(8,128)(2,1)S(1)}, u32[]{:S(2)}, u32[]{:S(2)}) collective-permute-start(bf16[512,512]{1,0:T(8,128)(2,1)S(1)} %collective-permute-done.4), channel_id=1, source_target_pairs={{0,112},{16,0},{32,16},{48,32},{64,48},{80,64},{96,80},{112,96},{1... | collective-permute-start | bytes 1572872 | tf_op jit(solution)/shard_map/ppermute | solution.py:213
  43.5 11.5 %collective-permute-start.7 = (bf16[512,512]{1,0:T(8,128)(2,1)S(1)}, bf16[512,512]{1,0:T(8,128)(2,1)S(1)}, u32[]{:S(2)}, u32[]{:S(2)}) collective-permute-start(bf16[512,512]{1,0:T(8,128)(2,1)S(1)} %collective-permute-done.5), channel_id=1, source_target_pairs={{0,16},{16,32},{32,48},{48,64},{64,80},{80,96},{96,112},{112,0},{1... | collective-permute-start | bytes 1572872 | tf_op jit(solution)/shard_map/ppermute | solution.py:210
  47.3 11.2 %collective-permute-start.8 = (bf16[512,512]{1,0:T(8,128)(2,1)S(1)}, bf16[512,512]{1,0:T(8,128)(2,1)S(1)}, u32[]{:S(2)}, u32[]{:S(2)}) collective-permute-start(bf16[512,512]{1,0:T(8,128)(2,1)S(1)} %collective-permute-done.6), channel_id=1, source_target_pairs={{0,112},{16,0},{32,16},{48,32},{64,48},{80,64},{96,80},{112,96},{1... | collective-permute-start | bytes 1572872 | tf_op jit(solution)/shard_map/ppermute | solution.py:213
  55.1 10.6 %collective-permute-start.9 = (bf16[512,512]{1,0:T(8,128)(2,1)S(1)}, bf16[512,512]{1,0:T(8,128)(2,1)S(1)}, u32[]{:S(2)}, u32[]{:S(2)}) collective-permute-start(bf16[512,512]{1,0:T(8,128)(2,1)S(1)} %collective-permute-done.7), channel_id=1, source_target_pairs={{0,16},{16,32},{32,48},{48,64},{64,80},{80,96},{96,112},{112,0},{1... | collective-permute-start | bytes 1572872 | tf_op jit(solution)/shard_map/ppermute | solution.py:210
  80.2 16.0 %collective-permute-start.12 = (bf16[2,512,128]{2,1,0:T(8,128)(2,1)}, bf16[2,512,128]{2,1,0:T(8,128)(2,1)S(1)}, u32[]{:S(2)}, u32[]{:S(2)}) collective-permute-start(bf16[2,512,128]{2,1,0:T(8,128)(2,1)} %get-tuple-element.18), channel_id=1, source_target_pairs={{0,128},{1,129},{2,130},{3,131},{4,132},{5,133},{6,134},{7,135},{8... | collective-permute-start | bytes 786440 | tf_op jit(solution)/shard_map/ppermute | solution.py:264
  81.5 14.7 %collective-permute-start.11 = (f32[2,2,512]{2,1,0:T(2,128)}, f32[2,2,512]{2,1,0:T(2,128)S(1)}, u32[]{:S(2)}, u32[]{:S(2)}) collective-permute-start(f32[2,2,512]{2,1,0:T(2,128)} %get-tuple-element.17), channel_id=1, source_target_pairs={{0,128},{1,129},{2,130},{3,131},{4,132},{5,133},{6,134},{7,135},{8... | collective-permute-start | bytes 24584 | tf_op jit(solution)/shard_map/ppermute | solution.py:265
  103.6 6.8 %collective-permute-start.13 = (bf16[2,32,4096]{2,1,0:T(8,128)(2,1)}, bf16[2,32,4096]{2,1,0:T(8,128)(2,1)}, u32[]{:S(2)}, u32[]{:S(2)}) collective-permute-start(bf16[2,32,4096]{2,1,0:T(8,128)(2,1)} %bitcast_convert_fusion), channel_id=1, source_target_pairs={{0,1},{1,0},{2,3},{3,2},{4,5},{5,4},{6,7},{7,6},{8,9},{9,8},{10,11... | collective-permute-start | bytes 1572872 | tf_op jit(solution)/shard_map/ppermute | solution.py:225
  111.5 7.6 %collective-permute-start.14 = (bf16[32,4096]{1,0:T(8,128)(2,1)S(1)}, bf16[32,4096]{1,0:T(8,128)(2,1)S(1)}, u32[]{:S(2)}, u32[]{:S(2)}) collective-permute-start(bf16[32,4096]{1,0:T(8,128)(2,1)S(1)} %fusion.3), channel_id=1, source_target_pairs={{0,2},{2,0},{1,3},{3,1},{4,6},{6,4},{5,7},{7,5},{8,10},{10,8},{9,1... | collective-permute-start | bytes 786440 | tf_op jit(solution)/shard_map/ppermute | solution.py:228
